TPU v7x, 32 devices: a whole 2x2x4 slice. The times are simulated.
32 devices in a mesh: groups: 2 (over y), trial: 4 (over x, core), dp: 4 (over z).
Axes of the slice: x: 2, y: 2, z: 4, core: 2. Of those that a mesh axis runs over, the one named last changes fastest.
Arguments:
- features: bfloat16 [8, 4, 592, 1536], P(('groups', 'dp'), 'trial'), parts along dimension 0, may hold values from -6 to 6
- owner: int32 [8], P(('groups', 'dp')), parts along dimension 0, may hold values from 0 to 3
- dilation_index: int32 [4], P('trial'), may hold values from 0 to 3
- labels: int32 [8, 592], P(('groups', 'dp')), parts along dimension 0, may hold values from 0 to 149
- input_weight: bfloat16 [4, 1536, 512], P('trial'), may hold values from -0.15625 to 0.15625
- taps: float32 [4, 9, 512], P('trial'), may hold values from -2 to 2
- output_weight: bfloat16 [4, 512, 150], P('trial'), may hold values from -1.0546875 to 1.0546875
Outputs:
- grad_in: float32 [8, 1536, 512], P(('groups', 'trial'), 'dp'), parts along dimension 0
- grad_taps: float32 [8, 9, 512], P(('groups', 'trial')), parts along dimension 0
- grad_out: float32 [8, 512, 150], P(('groups', 'trial'), 'dp'), parts along dimension 0
- noise_norms: float32 [8, 2, 3], P(('groups', 'trial')), parts along dimension 0
There are 2 independent parts, one for each index of `groups`. A program takes and returns all parts, laid end to end along the dimension named above; an argument that names none is the same for every part. Nothing has to cross between parts.
All inputs are finite; a program needn't handle non-finite values.
Results may differ from a plain program's by a relative error of at most 0.0015.
The roundings to bfloat16 on the way count: a program that leaves them out, or rounds other values in their place, can miss the bound.
Values may be sent and summed in bfloat16 or wider, within the bound.
No kernel may reach another device: no remote copies, remote signals or barrier semaphores. Data moves between devices by JAX's collectives and lax.ppermute only.
A program may use at most 64 MiB of HBM per device.

v0:
```python
import jax
import jax.numpy as jnp
from jax import lax
from jax.sharding import PartitionSpec as P

PC = 37


def broadcast(block, axis, source):
    block = jnp.where(lax.axis_index(axis) == source, block, jnp.zeros_like(block))
    return lax.psum(block, axis)


def gelu_parts(value):
    inner = 0.7978845608 * (value + 0.044715 * value * value * value)
    tanh_val = jnp.tanh(inner)
    out_val = 0.5 * value * (1.0 + tanh_val)
    slope = 0.5 * (1.0 + tanh_val) + 0.5 * value * (1.0 - tanh_val * tanh_val) * 0.7978845608 * (
        1.0 + 3.0 * 0.044715 * value * value
    )
    return (out_val, slope)


def head_backward(xrows, label_row, weight_in, tap_table, weight_out, dilation_rate):
    rows_count = xrows.shape[0]
    hidden_width = weight_in.shape[1]
    classes = weight_out.shape[1]
    slab_rows = rows_count // PC
    pre = jnp.dot(xrows, weight_in, preferred_element_type=jnp.float32).reshape(
        slab_rows, PC, hidden_width
    )
    padded = jnp.pad(pre, ((4, 4), (4, 4), (0, 0)))
    zero_idx = jnp.int32(0)
    shifted = []
    for off_a in (-1, 0, 1):
        for off_b in (-1, 0, 1):
            start_a = 4 + dilation_rate * off_a
            start_b = 4 + dilation_rate * off_b
            shifted.append(
                lax.dynamic_slice(
                    padded, (start_a, start_b, zero_idx), (slab_rows, PC, hidden_width)
                )
            )
    yval = shifted[0] * tap_table[0]
    for index in range(1, 9):
        yval = yval + shifted[index] * tap_table[index]
    act, slope = gelu_parts(yval)
    hid = act.astype(jnp.bfloat16).reshape(rows_count, hidden_width)
    logits = jnp.dot(hid, weight_out, preferred_element_type=jnp.float32)
    prob = jax.nn.softmax(logits, axis=-1)
    onehot = (label_row[:, None] == jnp.arange(classes, dtype=jnp.int32)[None, :]).astype(
        jnp.float32
    )
    dlog = (prob - onehot).astype(jnp.bfloat16)
    g_out = jnp.dot(hid.T, dlog, preferred_element_type=jnp.float32)
    dhid = jnp.dot(dlog, weight_out.T, preferred_element_type=jnp.float32).reshape(
        slab_rows, PC, hidden_width
    )
    dyval = dhid * slope
    g_taps = jnp.stack([jnp.sum(dyval * shifted[index], axis=(0, 1)) for index in range(9)])
    padded_dy = jnp.pad(dyval, ((4, 4), (4, 4), (0, 0)))
    dpre = jnp.zeros((slab_rows, PC, hidden_width), jnp.float32)
    index = 0
    for off_a in (-1, 0, 1):
        for off_b in (-1, 0, 1):
            start_a = 4 - dilation_rate * off_a
            start_b = 4 - dilation_rate * off_b
            dpre = dpre + tap_table[index] * lax.dynamic_slice(
                padded_dy, (start_a, start_b, zero_idx), (slab_rows, PC, hidden_width)
            )
            index += 1
    dpre = dpre.astype(jnp.bfloat16).reshape(rows_count, hidden_width)
    return (g_taps, g_out, dpre)


def per_device(features, owner, dilation_index, labels, input_weight, taps, output_weight):
    xrows = broadcast(features[0, 0], "trial", owner[0])
    dilation_rate = dilation_index[0] + 1
    g_taps, g_out, dpre = head_backward(
        xrows, labels[0], input_weight[0], taps[0], output_weight[0], dilation_rate
    )
    g_in = jnp.dot(xrows.T, dpre, preferred_element_type=jnp.float32)
    share_in, share_out = (
        lax.psum_scatter(g_in, "dp", scatter_dimension=0, tiled=True),
        lax.psum_scatter(g_out, "dp", scatter_dimension=0, tiled=True),
    )
    local = jnp.stack([jnp.sum(g_in * g_in), jnp.sum(g_taps * g_taps), jnp.sum(g_out * g_out)])
    share_sq = jnp.stack([jnp.sum(share_in * share_in), jnp.sum(share_out * share_out)])
    total_taps, squares = lax.psum((g_taps, local), "dp")
    share_total = lax.psum(share_sq, "dp")
    totals = jnp.stack([share_total[0], jnp.sum(total_taps * total_taps), share_total[1]])
    norms = jnp.log(1e-12 + jnp.stack([squares, totals]))
    return (share_in[None], total_taps[None], share_out[None], norms[None])


def solution(mesh):
    placed = (
        P(("groups", "dp"), "trial", None, None),
        P(("groups", "dp")),
        P("trial"),
        P(("groups", "dp"), None),
        P("trial", None, None),
        P("trial", None, None),
        P("trial", None, None),
    )
    return jax.shard_map(
        per_device,
        mesh=mesh,
        in_specs=placed,
        out_specs=(
            P(("groups", "trial"), "dp", None),
            P(("groups", "trial"), None, None),
            P(("groups", "trial"), "dp", None),
            P(("groups", "trial"), None, None),
        ),
        check_vma=False,
    )
```

profile of v0, /device:TPU:0, one launch (start us, length us, event | category | flops | bytes accessed | tf_op | source)
XLA Modules:
  0.0 185.1 jit_solution(14359373586882467331)
XLA Ops:
  7.2 0.0 copy-start
  7.2 0.0 all-reduce.5.cloned.1.call-start
  8.0 1.4 select_bitcast_fusion
  9.4 0.0 all-reduce.5.cloned.1.call-update
  9.4 0.0 reduce-scatter.5.cloned.1.call-start
  10.1 0.6 reduce
  10.7 0.6 fusion.29
  11.3 49.4 %all-reduce.5.cloned.1.call-done = bf16[592,1536]{1,0:T(8,128)(2,1)} async-done(((bf16[592,1536]{1,0:T(8,128)(2,1)}), bf16[592,1536]{1,0:T(8,128)(2,1)}) %all-reduce.5.cloned.1.call-update) | async-done | bytes 1818640 | tf_op jit(solution)/shard_map/psum | solution.py:11
  60.8 1.8 dot_general.19
  62.5 0.0 copy-start.4
  62.6 0.0 copy-start.6
  62.6 0.0 copy-start.8
  62.6 0.0 copy-start.10
  62.6 0.0 copy-start.12
  62.6 1.2 fusion
  63.9 4.0 %multiply_convert_fusion = (bf16[16,37,512]{2,1,0:T(8,128)(2,1)S(1)}, f32[16,37,512]{2,1,0:T(8,128)}) fusion(f32[512]{0:T(512)S(1)} %bitcast.83, s32[]{:T(128)S(6)} %select_n.57, s32[]{:T(128)S(6)} %select_n.56, f32[512]{0:T(512)S(1)} %bitcast.85, f32[512]{0:T(512)S(1)} %bitcast.71, s32[]{:T(128)S(6)} %select_n.55, f32[512]{0:T(512)S(1)} %bitcast.73, ...), kind=kLoop, calls=%fused_computation.54 | loop fusion | flops 7880704 | bytes 3049488 | tf_op jit(solution)/shard_map/convert_element_type | solution.py:48
  67.9 0.2 reshape.104
  68.1 0.7 copy-done.2
  68.8 0.4 fusion.31
  69.2 0.1 fusion.24
  69.2 0.1 subtract_convert_fusion
  69.4 1.6 multiply_reduce_fusion.11
  71.0 0.2 copy.13
  71.1 0.0 reduce-scatter.5.cloned.1.call-update
  71.2 0.0 reduce-scatter.3.cloned.1.call-start
  71.2 0.1 dot_general.22
  71.3 0.0 copy-start.5
  71.3 0.0 copy-start.7
  71.4 7.3 %multiply_reduce_fusion.1 = (f32[512]{0:T(512)S(1)}, f32[512]{0:T(512)S(1)}, f32[512]{0:T(512)S(1)}, f32[512]{0:T(512)S(1)}, f32[512]{0:T(512)S(1)}, /*index=5*/...) fusion(s32[]{:T(128)S(6)} %select_n.57, s32[]{:T(128)S(6)} %select_n.56, ...), kind=kOutput, calls=%fused_computation.45 | convolution fusion | flops 101838336 | bytes 3986896 | tf_op jit(solution)/shard_map/dot_general | solution.py:56
  78.8 2.5 %fusion.16 = bf16[16,37,512]{2,1,0:T(8,128)(2,1)S(1)} fusion(s32[]{:T(128)S(6)} %select_n.58, s32[]{:T(128)S(6)} %select_n.59, f32[16,37,512]{2,1,0:T(8,128)S(1)} %get-tuple-element.39, s32[]{:T(128)S(6)} %select_n.60, s32[]{:T(128)S(6)} %select_n.61, f32[512]{0:T(512)S(1)} %bitcast.84, f32[512]{0:T(512)S(1)} %bitcast.86, f32[512]{0:T(512)S(1)} %bitcast.72, ...), kind=kLoop, calls=%fused_computation.37 | loop fusion | flops 5455872 | bytes 1837072 | tf_op jit(solution)/shard_map/convert_element_type | solution.py:72
  81.2 0.2 reshape.105
  81.4 5.2 %multiply_reduce_fusion = (f32[]{:T(128)}, f32[1536,512]{1,0:T(8,128)}) fusion(bf16[592,1536]{1,0:T(8,128)(2,1)} %all-reduce.5.cloned.1.call-done, bf16[592,512]{1,0:T(8,128)(2,1)S(1)} %reshape.105), kind=kOutput, calls=%fused_computation.16 | convolution fusion | flops 932708352 | bytes 5570564 | tf_op jit(solution)/shard_map/dot_general | solution.py:82
  86.6 0.0 reduce-scatter.3.cloned.1.call-update
  86.7 0.1 stack.75
  86.7 0.6 multiply_reduce_fusion.14
  87.3 2.0 %maximum_bitcast_fusion = f32[1,1,3]{2,1,0:T(1,128)S(1)} fusion(f32[1]{0:T(128)} %bitcast.40, f32[1]{0:T(128)} %bitcast.39, f32[1]{0:T(128)} %bitcast.38), kind=kLoop, calls=%fused_computation.70 | loop fusion | flops 6 | bytes 24 | tf_op jit(solution)/shard_map/stack | solution.py:92
  89.3 2.0 %reduce-scatter.5.cloned.1.call-done = f32[128,150]{0,1:T(8,128)} async-done(((f32[512,150]{0,1:T(8,128)}), f32[128,150]{0,1:T(8,128)}) %reduce-scatter.5.cloned.1.call-update) | async-done | bytes 76816 | tf_op jit(solution)/shard_map/reduce_scatter | solution.py:85
  91.3 1.6 copy.14
  92.9 1.5 multiply_reduce_fusion.12
  94.4 58.3 %reduce-scatter.3.cloned.1.call-done = f32[384,512]{1,0:T(8,128)} async-done(((f32[1536,512]{1,0:T(8,128)}), f32[384,512]{1,0:T(8,128)}) %reduce-scatter.3.cloned.1.call-update) | async-done | bytes 786448 | tf_op jit(solution)/shard_map/reduce_scatter | solution.py:84
  152.8 1.9 %multiply_reduce_fusion.10 = f32[]{:T(128)} fusion(f32[384,512]{1,0:T(8,128)} %reduce-scatter.3.cloned.1.call-done), kind=kLoop, calls=%fused_computation.56 | loop fusion | flops 393215 | bytes 786436 | tf_op jit(solution)/shard_map/reduce_sum | solution.py:88
  154.7 1.4 pad_maximum_fusion
  156.1 18.1 %all-reduce.2 = (f32[9,512]{1,0:T(8,128)S(1)}, f32[2]{0:T(128)S(1)}, f32[1,1,3]{2,1,0:T(1,128)S(1)}) all-reduce(f32[9,512]{1,0:T(8,128)S(1)} %stack.75, f32[2]{0:T(128)S(1)} %pad_maximum_fusion, f32[1,1,3]{2,1,0:T(1,128)S(1)} %maximum_bitcast_fusion), channel_id=1, replica_groups=mesh['groups'=2,'trial'=4,'dp'=4] {'dp'}, use_global_device_ids=true, to_apply=%region_13.14 | all-reduce | flops 4613 | bytes 36904 | tf_op jit(solution)/shard_map/psum | solution.py:89
  174.2 0.6 multiply_reduce_fusion.13
  174.8 0.6 broadcast_in_dim.18
  175.4 0.7 fusion.30
  176.0 2.0 %maximum_bitcast_fusion.1 = f32[1,1,3]{2,1,0:T(1,128)S(1)} fusion(f32[1]{0:T(128)} %get-tuple-element.36, f32[1]{0:T(128)} %bitcast.44, f32[1]{0:T(128)} %get-tuple-element.35), kind=kLoop, calls=%fused_computation.72 | loop fusion | flops 6 | bytes 24 | tf_op jit(solution)/shard_map/stack | solution.py:92
  178.0 0.6 fusion.28
  (23 shorter events, 0.0 us)
Async XLA Ops:
  7.2 55.4 %copy-start = (bf16[1,1536,512]{2,1,0:T(8,128)(2,1)S(1)}, bf16[1,1536,512]{2,1,0:T(8,128)(2,1)}, u32[]{:S(2)}) copy-start(bf16[1,1536,512]{2,1,0:T(8,128)(2,1)} %param.11) | copy-start | bytes 4718596
  7.2 53.6 %all-reduce.5.cloned.1.call-start = ((), (), s32[]{:S(2)}) async-start(), calls=%async_computation.2 | async-start | bytes 3637248 | tf_op jit(solution)/shard_map/psum | solution.py:11
  9.4 0.8 copy-start.15
  9.4 1.4 copy-start.3
  9.4 81.9 %reduce-scatter.5.cloned.1.call-start = ((), (), s32[]{:S(2)}) async-start(), calls=%async_computation.4 | async-start | bytes 389120 | tf_op jit(solution)/shard_map/reduce_scatter | solution.py:85
  62.5 1.3 copy-start.4
  62.6 1.3 copy-start.6
  62.6 1.3 copy-start.8
  62.6 1.3 copy-start.10
  62.6 1.3 copy-start.12
  63.8 4.1 %copy-start.1 = (f32[16,37,512]{2,1,0:T(8,128)}, f32[16,37,512]{2,1,0:T(8,128)S(1)}, u32[]{:S(2)}) copy-start(f32[16,37,512]{2,1,0:T(8,128)S(1)} %fusion) | copy-start | bytes 3637252
  67.9 0.9 copy-start.2
  67.9 1.4 copy-start.14
  71.2 81.6 %reduce-scatter.3.cloned.1.call-start = ((), (), s32[]{:S(2)}) async-start(), calls=%async_computation.3 | async-start | bytes 3932160 | tf_op jit(solution)/shard_map/reduce_scatter | solution.py:84
  71.3 7.4 %copy-start.5 = (f32[1,1,512]{2,0,1:T(1,128)S(1)}, f32[1,1,512]{2,0,1:T(1,128)}, u32[]{:S(2)}) copy-start(f32[1,1,512]{2,0,1:T(1,128)} %get-tuple-element.30) | copy-start | bytes 6148
  71.3 7.4 %copy-start.7 = (f32[1,1,512]{2,0,1:T(1,128)S(1)}, f32[1,1,512]{2,0,1:T(1,128)}, u32[]{:S(2)}) copy-start(f32[1,1,512]{2,0,1:T(1,128)} %get-tuple-element.31) | copy-start | bytes 6148
  71.4 7.4 %copy-start.9 = (f32[1,1,512]{2,0,1:T(1,128)S(1)}, f32[1,1,512]{2,0,1:T(1,128)}, u32[]{:S(2)}) copy-start(f32[1,1,512]{2,0,1:T(1,128)} %get-tuple-element.32) | copy-start | bytes 6148
  71.4 7.4 %copy-start.11 = (f32[1,1,512]{2,0,1:T(1,128)S(1)}, f32[1,1,512]{2,0,1:T(1,128)}, u32[]{:S(2)}) copy-start(f32[1,1,512]{2,0,1:T(1,128)} %get-tuple-element.33) | copy-start | bytes 6148
  71.4 7.4 %copy-start.13 = (f32[1,1,512]{2,0,1:T(1,128)S(1)}, f32[1,1,512]{2,0,1:T(1,128)}, u32[]{:S(2)}) copy-start(f32[1,1,512]{2,0,1:T(1,128)} %get-tuple-element.34) | copy-start | bytes 6148
Sparse Core Ops, SparseCore 0:
  10.4 50.3 all-reduce.4
  71.3 19.9 reduce-scatter.4
  94.2 58.5 reduce-scatter.2
where the time goes:
time: 185 us
  waiting for transfers between devices  110 us (59%)
  other arithmetic  19.3 us (10%)
  blocking collectives  18.1 us (10%)
  matrix products  15.7 us (8%)
  between operations  15.5 us (8%)
  local copies, waits for them, and re-layouts  6.75 us (4%)
    reduce_scatter x1, waiting for transfers between devices, per_device(): lax.psum_scatter(g_in, 'dp', scatter_dimension=0, tiled=True)  58.3 us
    psum x1, waiting for transfers between devices, broadcast(): return lax.psum(block, axis)  49.4 us
    psum x1, blocking collectives, per_device(): total_taps, squares = lax.psum((g_taps, local), 'dp')  18.1 us
    dot_general x1, matrix products, head_backward(): jnp.dot(dlog, weight_out.T, preferred_element_type=jnp.float32)  7.31 us
    dot_general x1, matrix products, per_device(): g_in = jnp.dot(xrows.T, dpre, preferred_element_type=jnp.float32)  5.19 us
    convert_element_type x1, other arithmetic, head_backward(): hid = act.astype(jnp.bfloat16).reshape(rows_count, hidden_width)  4.01 us
    another operation x2, other arithmetic, per_device(): norms = jnp.log(1e-12 + jnp.stack([squares, totals]))  3.98 us
  transfers between devices with their start and end apart: 3, of which 3 were waited for; matrix products, arithmetic and copies ran while one was open for 12% of the time, Pallas kernels for 0%

commit v1 on v0

--- a/solution.py
+++ b/solution.py
@@ -6,9 +6,30 @@
 PC = 37
 
 
-def broadcast(block, axis, source):
-    block = jnp.where(lax.axis_index(axis) == source, block, jnp.zeros_like(block))
-    return lax.psum(block, axis)
+def broadcast(block, axis, size, source):
+    if size != 4:
+        block = jnp.where(lax.axis_index(axis) == source, block, jnp.zeros_like(block))
+        return lax.psum(block, axis)
+    me = lax.axis_index(axis)
+    core = me % 2
+    mate = [(0, 1), (1, 0), (2, 3), (3, 2)]
+    across = [(0, 2), (2, 0), (1, 3), (3, 1)]
+    width = block.shape[1] // 2
+    low, high = block[:, :width], block[:, width:]
+    got = lax.ppermute(jnp.where(core == 0, high, low), axis, mate)
+    kept = jnp.where(core == 0, low, high)
+    held = jnp.where(source % 2 == core, kept, got)
+    other = lax.ppermute(held, axis, across)
+    here = (source // 2) == (me // 2)
+    back_held = lax.ppermute(held, axis, mate)
+    back_other = lax.ppermute(other, axis, mate)
+    first = jnp.where(here, held, other)
+    second = jnp.where(here, back_held, back_other)
+    return jnp.where(
+        core == 0,
+        jnp.concatenate([first, second], axis=1),
+        jnp.concatenate([second, first], axis=1),
+    )
 
 
 def gelu_parts(value):
@@ -73,27 +94,59 @@
     return (g_taps, g_out, dpre)
 
 
-def per_device(features, owner, dilation_index, labels, input_weight, taps, output_weight):
-    xrows = broadcast(features[0, 0], "trial", owner[0])
+def shift(value, step, size):
+    return lax.ppermute(value, "dp", [(i, (i + step) % size) for i in range(size)])
+
+
+def per_device(dp, trials, features, owner, dilation_index, labels, input_weight, taps, output_weight):
+    xrows = broadcast(features[0, 0], "trial", trials, owner[0])
     dilation_rate = dilation_index[0] + 1
     g_taps, g_out, dpre = head_backward(
         xrows, labels[0], input_weight[0], taps[0], output_weight[0], dilation_rate
     )
-    g_in = jnp.dot(xrows.T, dpre, preferred_element_type=jnp.float32)
-    share_in, share_out = (
-        lax.psum_scatter(g_in, "dp", scatter_dimension=0, tiled=True),
-        lax.psum_scatter(g_out, "dp", scatter_dimension=0, tiled=True),
-    )
-    local = jnp.stack([jnp.sum(g_in * g_in), jnp.sum(g_taps * g_taps), jnp.sum(g_out * g_out)])
+    me = lax.axis_index("dp")
+    depth = xrows.shape[1] // dp
+    depth_out = g_out.shape[0] // dp
+
+    def block(array, index, size, axis):
+        return lax.dynamic_slice_in_dim(array, index * size, size, axis)
+
+    share_out = block(g_out, me, depth_out, 0)
+    for step in range(1, dp):
+        share_out = share_out + shift(block(g_out, (me + step) % dp, depth_out, 0), step, dp)
+    share_in = None
+    norm_in = 0.0
+    got = []
+    for step in list(range(1, dp)) + [0]:
+        part = jnp.dot(
+            block(xrows, (me + step) % dp, depth, 1).T, dpre, preferred_element_type=jnp.float32
+        )
+        norm_in = norm_in + jnp.sum(part * part)
+        if step:
+            got.append(shift(part.astype(jnp.bfloat16), step, dp))
+        else:
+            share_in = part
+    local = jnp.stack([norm_in, jnp.sum(g_taps * g_taps), jnp.sum(g_out * g_out)])
+    packed = jnp.concatenate([g_taps, jnp.zeros((7, g_taps.shape[1]), jnp.float32)])
+    packed = packed.at[9, :3].set(local)
+    total = packed
+    for step in range(1, dp):
+        total = total + shift(packed, step, dp)
+    total_taps, squares = total[:9], total[9, :3]
+    for value in got:
+        share_in = share_in + value.astype(jnp.float32)
     share_sq = jnp.stack([jnp.sum(share_in * share_in), jnp.sum(share_out * share_out)])
-    total_taps, squares = lax.psum((g_taps, local), "dp")
-    share_total = lax.psum(share_sq, "dp")
-    totals = jnp.stack([share_total[0], jnp.sum(total_taps * total_taps), share_total[1]])
+    share_sq = jnp.broadcast_to(jnp.pad(share_sq, (0, 126))[None], (8, 128))
+    share_total = share_sq
+    for step in range(1, dp):
+        share_total = share_total + shift(share_sq, step, dp)
+    totals = jnp.stack([share_total[0, 0], jnp.sum(total_taps * total_taps), share_total[0, 1]])
     norms = jnp.log(1e-12 + jnp.stack([squares, totals]))
     return (share_in[None], total_taps[None], share_out[None], norms[None])
 
 
 def solution(mesh):
+    dp, trials = mesh.shape["dp"], mesh.shape["trial"]
     placed = (
         P(("groups", "dp"), "trial", None, None),
         P(("groups", "dp")),
@@ -103,8 +156,12 @@
         P("trial", None, None),
         P("trial", None, None),
     )
+
+    def step(*args):
+        return per_device(dp, trials, *args)
+
     return jax.shard_map(
-        per_device,
+        step,
         mesh=mesh,
         in_specs=placed,
         out_specs=(

time: 185 us -> 141 us (0.76)
  waiting for transfers between devices: 110 us -> 42.4 us
  starting transfers between devices: 0.12 us -> 27.6 us
  blocking collectives: 18.1 us -> 0 us
  between operations: 15.5 us -> 5.12 us
  other arithmetic: 19.3 us -> 28.6 us
  local copies, waits for them, and re-layouts: 6.75 us -> 14.4 us
  matrix products: 15.7 us -> 22.5 us
    reduce_scatter x2 -> x0, waiting for transfers between devices: 60.3 us -> none  [the longest x1 58.3 us: per_device(): lax.psum_scatter(g_in, 'dp', scatter_dimension=0, tiled=True)]
    psum x1 -> x0, waiting for transfers between devices: 49.4 us -> none  [broadcast(): return lax.psum(block, axis)]
    ppermute x0 -> x16, waiting for transfers between devices: none -> 42.4 us  [the longest x12 21.1 us: shift(): lax.ppermute(value, 'dp', [(i, (i + step) % size) for i in range(size)])]
    ppermute x0 -> x16, starting transfers between devices: none -> 27.6 us  [the longest x12 24.3 us: shift(): lax.ppermute(value, 'dp', [(i, (i + step) % size) for i in range(size)])]
    psum x1 -> x0, blocking collectives: 18.1 us -> none  [per_device(): total_taps, squares = lax.psum((g_taps, local), 'dp')]
    select_n x1 -> x5, other arithmetic: 1.38 us -> 9.19 us  [the longest x1 2.64 us: broadcast(): got = lax.ppermute(jnp.where(core == 0, high, low), axis, mate)]
    dot_general x1 -> x4, matrix products: 5.19 us -> 8.26 us  [per_device(): jnp.dot(block(xrows, (me + step) % dp, depth, 1).T, dpre, preferred_eleme...]
    concatenate x0 -> x3, local copies, waits for them, and re-layouts: none -> 2.59 us  [the longest x2 2.53 us: broadcast(): jnp.concatenate([first, second], axis=1)]
  transfers between devices with their start and end apart: 3 -> 16, of which waited for: 3 -> 5; matrix products, arithmetic and copies ran while one was open for 12% -> 22% of each run, Pallas kernels for 0% -> 0%
where the time goes in v1:
time: 141 us
  waiting for transfers between devices  42.4 us (30%)
  other arithmetic  28.6 us (20%)
  starting transfers between devices  27.6 us (20%)
  matrix products  22.5 us (16%)
  local copies, waits for them, and re-layouts  14.4 us (10%)
  between operations  5.12 us (4%)
    ppermute x12, starting transfers between devices, shift(): lax.ppermute(value, 'dp', [(i, (i + step) % size) for i in range(size)])  24.3 us
    ppermute x12, waiting for transfers between devices, shift(): lax.ppermute(value, 'dp', [(i, (i + step) % size) for i in range(size)])  21.1 us
    ppermute x1, waiting for transfers between devices, broadcast(): other = lax.ppermute(held, axis, across)  19.6 us
    dot_general x4, matrix products, per_device(): jnp.dot(block(xrows, (me + step) % dp, depth, 1).T, dpre, preferred_eleme...  8.26 us
    dot_general x1, matrix products, head_backward(): jnp.dot(dlog, weight_out.T, preferred_element_type=jnp.float32)  7.79 us
    convert_element_type x1, other arithmetic, head_backward(): hid = act.astype(jnp.bfloat16).reshape(rows_count, hidden_width)  4.19 us
    dot_general x1, matrix products, head_backward(): jnp.dot(xrows, weight_in, preferred_element_type=jnp.float32)  3.34 us
    convert_element_type x1, other arithmetic, head_backward(): dpre = dpre.astype(jnp.bfloat16).reshape(rows_count, hidden_width)  3.29 us
  transfers between devices with their start and end apart: 16, of which 5 were waited for; matrix products, arithmetic and copies ran while one was open for 22% of the time, Pallas kernels for 0%

profile of v1, /device:TPU:0, one launch (start us, length us, event | category | flops | bytes accessed | tf_op | source)
XLA Modules:
  0.0 140.7 jit_solution(7016211090659684727)
XLA Ops:
  0.7 2.6 %broadcast_select_fusion = bf16[592,768]{1,0:T(8,128)(2,1)} fusion(pred[]{:T(512)S(6)} %eq.36, bf16[592,1536]{1,0:T(8,128)(2,1)} %bitcast.75), kind=kLoop, calls=%fused_computation.63 | loop fusion | flops 454656 | bytes 2727937 | tf_op jit(solution)/shard_map/jit(_where)/select_n | solution.py:19
  4.5 1.7 %collective-permute-done = bf16[592,768]{1,0:T(8,128)(2,1)} collective-permute-done((bf16[592,768]{1,0:T(8,128)(2,1)}, bf16[592,768]{1,0:T(8,128)(2,1)}, u32[]{:S(2)}, u32[]{:S(2)}) %collective-permute-start) | collective-permute-done | bytes 909344 | tf_op jit(solution)/shard_map/ppermute | solution.py:19
  6.2 2.3 %select_select_fusion = bf16[592,768]{1,0:T(8,128)(2,1)} fusion(bf16[592,768]{1,0:T(8,128)(2,1)} %collective-permute-done, pred[]{:T(512)S(6)} %eq.36, pred[]{:T(512)S(6)} %eq.38, bf16[592,1536]{1,0:T(8,128)(2,1)S(1)} %bitcast.76), kind=kLoop, calls=%fused_computation.62 | loop fusion | flops 909312 | bytes 3637250 | tf_op jit(solution)/shard_map/jit(_where)/select_n | solution.py:21
  8.5 2.9 %collective-permute-start.1 = (bf16[592,768]{1,0:T(8,128)(2,1)}, bf16[592,768]{1,0:T(8,128)(2,1)}, u32[]{:S(2)}, u32[]{:S(2)}) collective-permute-start(bf16[592,768]{1,0:T(8,128)(2,1)} %select_select_fusion), channel_id=1, source_target_pairs={{0,8},{8,0},{4,12},{12,4},{1,9},{9,1},{5,13},{13,5},{2,10},{10,2},... | collective-permute-start | bytes 2727944 | tf_op jit(solution)/shard_map/ppermute | solution.py:22
  11.3 19.6 %collective-permute-done.1 = bf16[592,768]{1,0:T(8,128)(2,1)} collective-permute-done((bf16[592,768]{1,0:T(8,128)(2,1)}, bf16[592,768]{1,0:T(8,128)(2,1)}, u32[]{:S(2)}, u32[]{:S(2)}) %collective-permute-start.1) | collective-permute-done | bytes 909344 | tf_op jit(solution)/shard_map/ppermute | solution.py:22
  31.7 0.6 reduce.2
  32.4 1.3 broadcast_select_fusion.2
  33.6 1.2 concatenate.31
  34.9 1.0 copy-done.8
  35.9 1.3 broadcast_select_fusion.1
  37.1 1.3 concatenate.32
  38.4 3.3 %fusion = f32[16,37,512]{2,1,0:T(8,128)S(1)} fusion(bf16[16,37,768]{2,1,0:T(8,128)(2,1)} %concatenate.32, bf16[16,37,768]{2,1,0:T(8,128)(2,1)} %concatenate.31, pred[]{:T(512)S(6)} %eq.36, bf16[1,1536,512]{2,1,0:T(8,128)(2,1)S(1)} %copy-done), kind=kOutput, calls=%fused_computation.17 | convolution fusion | flops 939319296 | bytes 4603905 | tf_op jit(solution)/shard_map/dot_general | solution.py:50
  41.8 4.2 %multiply_convert_fusion = (bf16[16,37,512]{2,1,0:T(8,128)(2,1)}, f32[16,37,512]{2,1,0:T(8,128)}) fusion(f32[512]{0:T(512)S(1)} %bitcast.92, s32[]{:T(128)S(6)} %select_n.166, s32[]{:T(128)S(6)} %select_n.165, f32[512]{0:T(512)S(1)} %bitcast.94, f32[512]{0:T(512)S(1)} %bitcast.80, s32[]{:T(128)S(6)} %select_n.164, f32[512]{0:T(512)S(1)} %bitcast.82, ...), kind=kLoop, calls=%fused_computation.60 | loop fusion | flops 7880704 | bytes 3049488 | tf_op jit(solution)/shard_map/convert_element_type | solution.py:69
  46.0 2.2 %reshape.136 = bf16[592,512]{1,0:T(8,128)(2,1)} reshape(bf16[16,37,512]{2,1,0:T(8,128)(2,1)} %get-tuple-element.37) | data formatting | bytes 1212416 | tf_op jit(solution)/shard_map/reshape | solution.py:69
  48.2 1.5 %fusion.52 = (f32[592]{0:T(1024)S(1)}, f32[592,150]{0,1:T(8,128)S(1)}) fusion(bf16[592,512]{1,0:T(8,128)(2,1)} %reshape.136, bf16[1,512,150]{1,2,0:T(8,128)(2,1)S(1)} %copy-done.9), kind=kOutput, calls=%fused_computation.113 | convolution fusion | flops 91019408 | bytes 1117376 | tf_op jit(solution)/shard_map/dot_general | solution.py:70
  49.9 0.7 copy-done.5
  50.6 1.7 %multiply_reduce_fusion.14 = (f32[]{:T(128)}, f32[512,150]{0,1:T(8,128)}) fusion(bf16[592,512]{1,0:T(8,128)(2,1)S(1)} %copy-done.2, bf16[592,150]{0,1:T(8,128)(2,1)S(1)} %subtract_convert_fusion), kind=kOutput, calls=%fused_computation.84 | convolution fusion | flops 91084800 | bytes 1091012 | tf_op jit(solution)/shard_map/dot_general | solution.py:76
  52.3 1.8 %copy.13 = bf16[592,150]{1,0:T(8,128)(2,1)} copy(bf16[592,150]{0,1:T(8,128)(2,1)} %copy-done.5) | data formatting | bytes 355200 | tf_op jit(solution)/shard_map/convert_element_type | solution.py:75
  54.1 1.7 %maximum_select_fusion.2 = bf16[592,1536]{1,0:T(8,128)(2,1)} fusion(bf16[592,768]{1,0:T(8,128)(2,1)S(1)} %broadcast_select_fusion.1, bf16[592,768]{1,0:T(8,128)(2,1)S(1)} %broadcast_select_fusion.2, pred[]{:T(512)S(6)} %eq.36), kind=kLoop, calls=%fused_computation.26 | loop fusion | flops 8183808 | bytes 3637249 | tf_op jit(solution)/shard_map/jit(_where)/select_n | solution.py:28
  55.8 0.7 constant_dynamic-slice_fusion
  56.5 2.5 %collective-permute-start.10 = (f32[128,150]{0,1:T(8,128)}, f32[128,150]{0,1:T(8,128)}, u32[]{:S(2)}, u32[]{:S(2)}) collective-permute-start(f32[128,150]{0,1:T(8,128)} %get-tuple-element.46), channel_id=1, source_target_pairs={{0,1},{1,2},{2,3},{3,0},{4,5},{5,6},{6,7},{7,4},{8,9},{9,10},{10,1... | collective-permute-start | bytes 230408 | tf_op jit(solution)/shard_map/ppermute | solution.py:98
  59.0 1.9 %collective-permute-start.11 = (f32[128,150]{0,1:T(8,128)}, f32[128,150]{0,1:T(8,128)}, u32[]{:S(2)}, u32[]{:S(2)}) collective-permute-start(f32[128,150]{0,1:T(8,128)} %get-tuple-element.48), channel_id=1, source_target_pairs={{0,2},{1,3},{2,0},{3,1},{4,6},{5,7},{6,4},{7,5},{8,10},{9,11},{10,... | collective-permute-start | bytes 230408 | tf_op jit(solution)/shard_map/ppermute | solution.py:98
  60.9 1.1 dot_general.28
  62.1 7.8 %multiply_reduce_fusion = (f32[512]{0:T(512)}, f32[512]{0:T(512)}, f32[512]{0:T(512)}, f32[512]{0:T(512)}, f32[512]{0:T(512)}, /*index=5*/f32[512]{0:T(512)}, f3...) fusion(s32[]{:T(128)S(6)} %select_n.166, s32[]{:T(128)S(6)} %select_n.165, ...), kind=kOutput, calls=%fused_computation.51 | convolution fusion | flops 101838336 | bytes 3986896 | tf_op jit(solution)/shard_map/dot_general | solution.py:77
  69.9 3.3 %fusion.22 = bf16[16,37,512]{2,1,0:T(8,128)(2,1)} fusion(s32[]{:T(128)S(6)} %select_n.167, s32[]{:T(128)S(6)} %select_n.168, f32[16,37,512]{2,1,0:T(8,128)S(1)} %get-tuple-element.67, s32[]{:T(128)S(6)} %select_n.169, s32[]{:T(128)S(6)} %select_n.170, f32[512]{0:T(512)S(1)} %bitcast.93, f32[512]{0:T(512)S(1)} %bitcast.95, f32[512]{0:T(512)S(1)} %bitcast.81, ...), kind=kLoop, calls=%fused_computation.43 | loop fusion | flops 5455872 | bytes 1837072 | tf_op jit(solution)/shard_map/convert_element_type | solution.py:93
  73.2 2.1 %reshape.137 = bf16[592,512]{1,0:T(8,128)(2,1)} reshape(bf16[16,37,512]{2,1,0:T(8,128)(2,1)} %fusion.22) | data formatting | bytes 1212416 | tf_op jit(solution)/shard_map/reshape | solution.py:93
  75.3 3.0 %multiply_reduce_fusion.13 = (f32[]{:T(128)}, bf16[384,512]{1,0:T(8,128)(2,1)}) fusion(bf16[592,512]{1,0:T(8,128)(2,1)} %reshape.137, bf16[592,1536]{1,0:T(8,128)(2,1)S(1)} %copy-done.3, s32[]{:T(128)S(6)} %select_n.172), kind=kOutput, calls=%fused_computation.70 | convolution fusion | flops 233373696 | bytes 1454088 | tf_op jit(solution)/shard_map/dot_general | solution.py:121
  78.4 1.9 %multiply_reduce_fusion.12 = (f32[]{:T(128)}, bf16[384,512]{1,0:T(8,128)(2,1)}) fusion(bf16[592,512]{1,0:T(8,128)(2,1)S(1)} %copy-done.4, bf16[592,1536]{1,0:T(8,128)(2,1)S(1)} %copy-done.3, s32[]{:T(128)S(6)} %select_n.174), kind=kOutput, calls=%fused_computation.69 | convolution fusion | flops 233373696 | bytes 1454088 | tf_op jit(solution)/shard_map/dot_general | solution.py:121
  80.2 2.6 %collective-permute-start.5 = (bf16[384,512]{1,0:T(8,128)(2,1)}, bf16[384,512]{1,0:T(8,128)(2,1)}, u32[]{:S(2)}, u32[]{:S(2)}) collective-permute-start(bf16[384,512]{1,0:T(8,128)(2,1)} %get-tuple-element.43), channel_id=1, source_target_pairs={{0,2},{1,3},{2,0},{3,1},{4,6},{5,7},{6,4},{7,5},{8,10},{9,11},{10,... | collective-permute-start | bytes 1179656 | tf_op jit(solution)/shard_map/ppermute | solution.py:98
  82.8 1.9 %multiply_reduce_fusion.11 = (f32[]{:T(128)}, bf16[384,512]{1,0:T(8,128)(2,1)}) fusion(bf16[592,512]{1,0:T(8,128)(2,1)S(1)} %copy-done.4, bf16[592,1536]{1,0:T(8,128)(2,1)S(1)} %copy-done.3, s32[]{:T(128)S(6)} %select_n.176), kind=kOutput, calls=%fused_computation.68 | convolution fusion | flops 233373696 | bytes 1454088 | tf_op jit(solution)/shard_map/dot_general | solution.py:121
  84.7 1.4 collective-permute-start.6
  86.1 1.5 %fusion.36 = f32[384,512]{1,0:T(8,128)S(1)} fusion(bf16[592,512]{1,0:T(8,128)(2,1)S(1)} %copy-done.4, bf16[592,1536]{1,0:T(8,128)(2,1)} %maximum_select_fusion.2, s32[]{:T(128)S(6)} %select_n.160), kind=kOutput, calls=%fused_computation.78 | convolution fusion | flops 232783872 | bytes 1847300 | tf_op jit(solution)/shard_map/dot_general | solution.py:121
  90.3 0.7 multiply_reduce_fusion.17
  91.0 19.1 %collective-permute-done.12 = f32[128,150]{0,1:T(8,128)S(1)} collective-permute-done((f32[128,150]{0,1:T(8,128)S(1)}, f32[128,150]{0,1:T(8,128)S(1)}, u32[]{:S(2)}, u32[]{:S(2)}) %collective-permute-start.12) | collective-permute-done | bytes 76832 | tf_op jit(solution)/shard_map/ppermute | solution.py:98
  110.1 1.7 %multiply_reduce_fusion.15 = (f32[]{:T(128)}, f32[128,150]{0,1:T(8,128)S(1)}) fusion(f32[128,150]{0,1:T(8,128)S(1)} %collective-permute-done.12, f32[128,150]{0,1:T(8,128)} %collective-permute-done.11, f32[128,150]{0,1:T(8,128)} %collective-permute-done.10, f32[512,150]{0,1:T(8,128)} %get-tuple-element.69, s32[]{:T(128)S(6)} %select_n.177), kind=kLoop, calls=%fused_computation.88 | loop fusion | flops 95999 | bytes 384008 | tf_op jit(solution)/shard_map/reduce_sum | solution.py:138
  111.7 0.7 copy.14
  112.4 2.9 %multiply_reduce_fusion.9 = (f32[]{:T(128)}, f32[]{:T(128)}, f32[1,384,512]{2,1,0:T(8,128)}) fusion(bf16[384,512]{1,0:T(8,128)(2,1)S(1)} %collective-permute-done.6, bf16[384,512]{1,0:T(8,128)(2,1)} %collective-permute-done.5, f32[384,512]{1,0:T(8,128)S(1)} %fusion.36, bf16[384,512]{1,0:T(8,128)(2,1)} %collective-permute-done.4), kind=kLoop, calls=%fused_computation.66 | loop fusion | flops 1966078 | bytes 2752520 | tf_op jit(solution)/shard_map/reduce_sum | solution.py:138
  115.3 1.4 fusion.48
  116.7 9.1 %collective-permute-start.13 = (f32[8,128]{1,0:T(8,128)S(1)}, f32[8,128]{1,0:T(8,128)S(1)}, u32[]{:S(2)}, u32[]{:S(2)}) collective-permute-start(f32[8,128]{1,0:T(8,128)S(1)} %broadcast_in_dim.26), channel_id=1, source_target_pairs={{0,1},{1,2},{2,3},{3,0},{4,5},{5,6},{6,7},{7,4},{8,9},{9,10},{10,1... | collective-permute-start | bytes 12296 | tf_op jit(solution)/shard_map/ppermute | solution.py:98
  125.8 2.4 %collective-permute-start.15 = (f32[8,128]{1,0:T(8,128)S(1)}, f32[8,128]{1,0:T(8,128)S(1)}, u32[]{:S(2)}, u32[]{:S(2)}) collective-permute-start(f32[8,128]{1,0:T(8,128)S(1)} %broadcast_in_dim.26), channel_id=1, source_target_pairs={{0,3},{1,0},{2,1},{3,2},{4,7},{5,4},{6,5},{7,6},{8,11},{9,8},{10,9... | collective-permute-start | bytes 12296 | tf_op jit(solution)/shard_map/ppermute | solution.py:98
  128.9 1.4 maximum_bitcast_fusion
  130.5 2.5 %collective-permute-start.8 = (f32[16,512]{1,0:T(8,128)S(1)}, f32[16,512]{1,0:T(8,128)S(1)}, u32[]{:S(2)}, u32[]{:S(2)}) collective-permute-start(f32[16,512]{1,0:T(8,128)S(1)} %scatter.4), channel_id=1, source_target_pairs={{0,2},{1,3},{2,0},{3,1},{4,6},{5,7},{6,4},{7,5},{8,10},{9,11},{10,... | collective-permute-start | bytes 98312 | tf_op jit(solution)/shard_map/ppermute | solution.py:98
  133.0 1.3 collective-permute-start.9
  134.9 1.4 collective-permute-done.7
  136.3 0.6 collective-permute-done.9
  136.9 0.6 multiply_reduce_fusion.16
  137.5 0.6 broadcast_in_dim.24
  138.2 1.9 %maximum_bitcast_fusion.1 = f32[1,1,3]{2,1,0:T(1,128)S(1)} fusion(f32[1]{0:T(128)} %bitcast.47, f32[1]{0:T(128)} %bitcast.46, f32[1]{0:T(128)} %bitcast.45), kind=kLoop, calls=%fused_computation.109 | loop fusion | flops 6 | bytes 24 | tf_op jit(solution)/shard_map/stack | solution.py:144
  (103 shorter events, 2.9 us)
Async XLA Ops:
  0.6 37.8 %copy-start = (bf16[1,1536,512]{2,1,0:T(8,128)(2,1)S(1)}, bf16[1,1536,512]{2,1,0:T(8,128)(2,1)}, u32[]{:S(2)}) copy-start(bf16[1,1536,512]{2,1,0:T(8,128)(2,1)} %param.13) | copy-start | bytes 4718596
  0.7 5.5 %copy-start.1 = (bf16[1,1,592,1536]{3,2,1,0:T(8,128)(2,1)S(1)}, bf16[1,1,592,1536]{3,2,1,0:T(8,128)(2,1)}, u32[]{:S(2)}) copy-start(bf16[1,1,592,1536]{3,2,1,0:T(8,128)(2,1)} %param.9) | copy-start | bytes 5455876
  3.3 2.9 %collective-permute-start = (bf16[592,768]{1,0:T(8,128)(2,1)}, bf16[592,768]{1,0:T(8,128)(2,1)}, u32[]{:S(2)}, u32[]{:S(2)}) collective-permute-start(bf16[592,768]{1,0:T(8,128)(2,1)} %broadcast_select_fusion), channel_id=1, source_target_pairs={{0,4},{4,0},{8,12},{12,8},{1,5},{5,1},{9,13},{13,9},{2,6},{6,2},{1... | collective-permute-start | bytes 2727944 | tf_op jit(solution)/shard_map/ppermute | solution.py:19
  4.4 27.2 %copy-start.36 = (s32[1,592]{1,0:T(1,128)S(1)}, s32[1,592]{1,0:T(1,128)}, u32[]{:S(2)}) copy-start(s32[1,592]{1,0:T(1,128)} %param.12) | copy-start | bytes 7108
  4.5 27.8 %copy-start.11 = (f32[1,9,512]{2,0,1:T(1,128)S(1)}, f32[1,9,512]{2,0,1:T(1,128)}, u32[]{:S(2)}) copy-start(f32[1,9,512]{2,0,1:T(1,128)} %param.14) | copy-start | bytes 55300
  8.5 22.5 %collective-permute-start.1 = (bf16[592,768]{1,0:T(8,128)(2,1)}, bf16[592,768]{1,0:T(8,128)(2,1)}, u32[]{:S(2)}, u32[]{:S(2)}) collective-permute-start(bf16[592,768]{1,0:T(8,128)(2,1)} %select_select_fusion), channel_id=1, source_target_pairs={{0,8},{8,0},{4,12},{12,4},{1,9},{9,1},{5,13},{13,5},{2,10},{10,2},... | collective-permute-start | bytes 2727944 | tf_op jit(solution)/shard_map/ppermute | solution.py:22
  11.3 23.6 %collective-permute-start.2 = (bf16[592,768]{1,0:T(8,128)(2,1)}, bf16[592,768]{1,0:T(8,128)(2,1)S(1)}, u32[]{:S(2)}, u32[]{:S(2)}) collective-permute-start(bf16[592,768]{1,0:T(8,128)(2,1)} %select_select_fusion), channel_id=1, source_target_pairs={{0,4},{4,0},{8,12},{12,8},{1,5},{5,1},{9,13},{13,9},{2,6},{6,2},{1... | collective-permute-start | bytes 2727944 | tf_op jit(solution)/shard_map/ppermute | solution.py:24
  30.9 4.9 %collective-permute-start.3 = (bf16[592,768]{1,0:T(8,128)(2,1)}, bf16[592,768]{1,0:T(8,128)(2,1)}, u32[]{:S(2)}, u32[]{:S(2)}) collective-permute-start(bf16[592,768]{1,0:T(8,128)(2,1)} %collective-permute-done.1), channel_id=1, source_target_pairs={{0,4},{4,0},{8,12},{12,8},{1,5},{5,1},{9,13},{13,9},{2,6},{6,2},{1... | collective-permute-start | bytes 2727944 | tf_op jit(solution)/shard_map/ppermute | solution.py:25
  32.3 9.5 %copy-start.12 = (f32[1,1,512]{2,0,1:T(1,128)}, f32[1,1,512]{2,0,1:T(1,128)S(1)}, u32[]{:S(2)}) copy-start(f32[1,1,512]{2,0,1:T(1,128)S(1)} %get-tuple-element.53) | copy-start | bytes 6148
  32.3 9.5 %copy-start.14 = (f32[1,1,512]{2,0,1:T(1,128)}, f32[1,1,512]{2,0,1:T(1,128)S(1)}, u32[]{:S(2)}) copy-start(f32[1,1,512]{2,0,1:T(1,128)S(1)} %get-tuple-element.54) | copy-start | bytes 6148
  32.3 9.5 %copy-start.16 = (f32[1,1,512]{2,0,1:T(1,128)}, f32[1,1,512]{2,0,1:T(1,128)S(1)}, u32[]{:S(2)}) copy-start(f32[1,1,512]{2,0,1:T(1,128)S(1)} %get-tuple-element.55) | copy-start | bytes 6148
  32.3 9.5 %copy-start.18 = (f32[1,1,512]{2,0,1:T(1,128)}, f32[1,1,512]{2,0,1:T(1,128)S(1)}, u32[]{:S(2)}) copy-start(f32[1,1,512]{2,0,1:T(1,128)S(1)} %get-tuple-element.56) | copy-start | bytes 6148
  32.3 9.5 %copy-start.20 = (f32[1,1,512]{2,0,1:T(1,128)}, f32[1,1,512]{2,0,1:T(1,128)S(1)}, u32[]{:S(2)}) copy-start(f32[1,1,512]{2,0,1:T(1,128)S(1)} %get-tuple-element.57) | copy-start | bytes 6148
  32.3 9.5 %copy-start.22 = (f32[1,1,512]{2,0,1:T(1,128)}, f32[1,1,512]{2,0,1:T(1,128)S(1)}, u32[]{:S(2)}) copy-start(f32[1,1,512]{2,0,1:T(1,128)S(1)} %get-tuple-element.58) | copy-start | bytes 6148
  32.4 9.5 %copy-start.24 = (f32[1,1,512]{2,0,1:T(1,128)}, f32[1,1,512]{2,0,1:T(1,128)S(1)}, u32[]{:S(2)}) copy-start(f32[1,1,512]{2,0,1:T(1,128)S(1)} %get-tuple-element.59) | copy-start | bytes 6148
  41.8 4.3 %copy-start.6 = (f32[16,37,512]{2,1,0:T(8,128)}, f32[16,37,512]{2,1,0:T(8,128)S(1)}, u32[]{:S(2)}) copy-start(f32[16,37,512]{2,1,0:T(8,128)S(1)} %fusion) | copy-start | bytes 3637252
  48.2 2.4 %copy-start.2 = (bf16[592,512]{1,0:T(8,128)(2,1)S(1)}, bf16[592,512]{1,0:T(8,128)(2,1)}, u32[]{:S(2)}) copy-start(bf16[592,512]{1,0:T(8,128)(2,1)} %reshape.136) | copy-start | bytes 1818628
  56.5 33.2 %collective-permute-start.10 = (f32[128,150]{0,1:T(8,128)}, f32[128,150]{0,1:T(8,128)}, u32[]{:S(2)}, u32[]{:S(2)}) collective-permute-start(f32[128,150]{0,1:T(8,128)} %get-tuple-element.46), channel_id=1, source_target_pairs={{0,1},{1,2},{2,3},{3,0},{4,5},{5,6},{6,7},{7,4},{8,9},{9,10},{10,1... | collective-permute-start | bytes 230408 | tf_op jit(solution)/shard_map/ppermute | solution.py:98
  59.0 32.0 %collective-permute-start.11 = (f32[128,150]{0,1:T(8,128)}, f32[128,150]{0,1:T(8,128)}, u32[]{:S(2)}, u32[]{:S(2)}) collective-permute-start(f32[128,150]{0,1:T(8,128)} %get-tuple-element.48), channel_id=1, source_target_pairs={{0,2},{1,3},{2,0},{3,1},{4,6},{5,7},{6,4},{7,5},{8,10},{9,11},{10,... | collective-permute-start | bytes 230408 | tf_op jit(solution)/shard_map/ppermute | solution.py:98
  62.0 7.9 %copy-start.13 = (f32[1,1,512]{2,0,1:T(1,128)S(1)}, f32[1,1,512]{2,0,1:T(1,128)}, u32[]{:S(2)}) copy-start(f32[1,1,512]{2,0,1:T(1,128)} %copy-done.12) | copy-start | bytes 6148
  62.0 7.9 %copy-start.15 = (f32[1,1,512]{2,0,1:T(1,128)S(1)}, f32[1,1,512]{2,0,1:T(1,128)}, u32[]{:S(2)}) copy-start(f32[1,1,512]{2,0,1:T(1,128)} %copy-done.14) | copy-start | bytes 6148
  62.0 7.8 %copy-start.17 = (f32[1,1,512]{2,0,1:T(1,128)S(1)}, f32[1,1,512]{2,0,1:T(1,128)}, u32[]{:S(2)}) copy-start(f32[1,1,512]{2,0,1:T(1,128)} %copy-done.16) | copy-start | bytes 6148
  62.0 7.8 %copy-start.19 = (f32[1,1,512]{2,0,1:T(1,128)S(1)}, f32[1,1,512]{2,0,1:T(1,128)}, u32[]{:S(2)}) copy-start(f32[1,1,512]{2,0,1:T(1,128)} %copy-done.18) | copy-start | bytes 6148
  62.1 7.8 %copy-start.21 = (f32[1,1,512]{2,0,1:T(1,128)S(1)}, f32[1,1,512]{2,0,1:T(1,128)}, u32[]{:S(2)}) copy-start(f32[1,1,512]{2,0,1:T(1,128)} %copy-done.20) | copy-start | bytes 6148
  62.1 7.8 %copy-start.23 = (f32[1,1,512]{2,0,1:T(1,128)S(1)}, f32[1,1,512]{2,0,1:T(1,128)}, u32[]{:S(2)}) copy-start(f32[1,1,512]{2,0,1:T(1,128)} %copy-done.22) | copy-start | bytes 6148
  62.1 7.8 %copy-start.25 = (f32[1,1,512]{2,0,1:T(1,128)S(1)}, f32[1,1,512]{2,0,1:T(1,128)}, u32[]{:S(2)}) copy-start(f32[1,1,512]{2,0,1:T(1,128)} %copy-done.24) | copy-start | bytes 6148
  69.9 5.4 %copy-start.3 = (bf16[592,1536]{1,0:T(8,128)(2,1)S(1)}, bf16[592,1536]{1,0:T(8,128)(2,1)}, u32[]{:S(2)}) copy-start(bf16[592,1536]{1,0:T(8,128)(2,1)} %maximum_select_fusion.2) | copy-start | bytes 5455876
  75.3 3.0 %copy-start.4 = (bf16[592,512]{1,0:T(8,128)(2,1)S(1)}, bf16[592,512]{1,0:T(8,128)(2,1)}, u32[]{:S(2)}) copy-start(bf16[592,512]{1,0:T(8,128)(2,1)} %reshape.137) | copy-start | bytes 1818628
  78.4 34.1 %collective-permute-start.4 = (bf16[384,512]{1,0:T(8,128)(2,1)}, bf16[384,512]{1,0:T(8,128)(2,1)}, u32[]{:S(2)}, u32[]{:S(2)}) collective-permute-start(bf16[384,512]{1,0:T(8,128)(2,1)} %get-tuple-element.45), channel_id=1, source_target_pairs={{0,1},{1,2},{2,3},{3,0},{4,5},{5,6},{6,7},{7,4},{8,9},{9,10},{10,1... | collective-permute-start | bytes 1179656 | tf_op jit(solution)/shard_map/ppermute | solution.py:98
  80.2 32.2 %collective-permute-start.5 = (bf16[384,512]{1,0:T(8,128)(2,1)}, bf16[384,512]{1,0:T(8,128)(2,1)}, u32[]{:S(2)}, u32[]{:S(2)}) collective-permute-start(bf16[384,512]{1,0:T(8,128)(2,1)} %get-tuple-element.43), channel_id=1, source_target_pairs={{0,2},{1,3},{2,0},{3,1},{4,6},{5,7},{6,4},{7,5},{8,10},{9,11},{10,... | collective-permute-start | bytes 1179656 | tf_op jit(solution)/shard_map/ppermute | solution.py:98
  84.7 3.0 %copy-start.27 = (f32[512]{0:T(512)S(1)}, f32[512]{0:T(512)}, u32[]{:S(2)}) copy-start(f32[512]{0:T(512)} %get-tuple-element.24) | copy-start | bytes 6148
  84.7 3.0 %copy-start.28 = (f32[512]{0:T(512)S(1)}, f32[512]{0:T(512)}, u32[]{:S(2)}) copy-start(f32[512]{0:T(512)} %get-tuple-element.25) | copy-start | bytes 6148
  84.7 3.0 %copy-start.29 = (f32[512]{0:T(512)S(1)}, f32[512]{0:T(512)}, u32[]{:S(2)}) copy-start(f32[512]{0:T(512)} %get-tuple-element.26) | copy-start | bytes 6148
  84.7 3.0 %copy-start.30 = (f32[512]{0:T(512)S(1)}, f32[512]{0:T(512)}, u32[]{:S(2)}) copy-start(f32[512]{0:T(512)} %get-tuple-element.27) | copy-start | bytes 6148
  84.7 3.0 %copy-start.31 = (f32[512]{0:T(512)S(1)}, f32[512]{0:T(512)}, u32[]{:S(2)}) copy-start(f32[512]{0:T(512)} %get-tuple-element.28) | copy-start | bytes 6148
  84.7 3.0 %copy-start.32 = (f32[512]{0:T(512)S(1)}, f32[512]{0:T(512)}, u32[]{:S(2)}) copy-start(f32[512]{0:T(512)} %get-tuple-element.29) | copy-start | bytes 6148
  84.7 3.0 %copy-start.33 = (f32[512]{0:T(512)S(1)}, f32[512]{0:T(512)}, u32[]{:S(2)}) copy-start(f32[512]{0:T(512)} %get-tuple-element.30) | copy-start | bytes 6148
  84.7 3.0 %copy-start.34 = (f32[512]{0:T(512)S(1)}, f32[512]{0:T(512)}, u32[]{:S(2)}) copy-start(f32[512]{0:T(512)} %get-tuple-element.31) | copy-start | bytes 6148
  84.7 3.0 %copy-start.35 = (f32[512]{0:T(512)S(1)}, f32[512]{0:T(512)}, u32[]{:S(2)}) copy-start(f32[512]{0:T(512)} %get-tuple-element.32) | copy-start | bytes 6148
  84.7 5.0 %copy-start.10 = (f32[128,150]{0,1:T(8,128)S(1)}, f32[128,150]{0,1:T(8,128)}, u32[]{:S(2)}) copy-start(f32[128,150]{0,1:T(8,128)} %get-tuple-element.47) | copy-start | bytes 230404
  84.7 27.7 %collective-permute-start.6 = (bf16[384,512]{1,0:T(8,128)(2,1)}, bf16[384,512]{1,0:T(8,128)(2,1)S(1)}, u32[]{:S(2)}, u32[]{:S(2)}) collective-permute-start(bf16[384,512]{1,0:T(8,128)(2,1)} %get-tuple-element.41), channel_id=1, source_target_pairs={{0,3},{1,0},{2,1},{3,2},{4,7},{5,4},{6,5},{7,6},{8,11},{9,8},{10,9... | collective-permute-start | bytes 1179656 | tf_op jit(solution)/shard_map/ppermute | solution.py:98
  89.8 20.3 %collective-permute-start.12 = (f32[128,150]{0,1:T(8,128)S(1)}, f32[128,150]{0,1:T(8,128)S(1)}, u32[]{:S(2)}, u32[]{:S(2)}) collective-permute-start(f32[128,150]{0,1:T(8,128)S(1)} %copy-done.10), channel_id=1, source_target_pairs={{0,3},{1,0},{2,1},{3,2},{4,7},{5,4},{6,5},{7,6},{8,11},{9,8},{10,9... | collective-permute-start | bytes 230408 | tf_op jit(solution)/shard_map/ppermute | solution.py:98
  116.7 16.3 %collective-permute-start.13 = (f32[8,128]{1,0:T(8,128)S(1)}, f32[8,128]{1,0:T(8,128)S(1)}, u32[]{:S(2)}, u32[]{:S(2)}) collective-permute-start(f32[8,128]{1,0:T(8,128)S(1)} %broadcast_in_dim.26), channel_id=1, source_target_pairs={{0,1},{1,2},{2,3},{3,0},{4,5},{5,6},{6,7},{7,4},{8,9},{9,10},{10,1... | collective-permute-start | bytes 12296 | tf_op jit(solution)/shard_map/ppermute | solution.py:98
  125.8 8.5 %collective-permute-start.14 = (f32[8,128]{1,0:T(8,128)S(1)}, f32[8,128]{1,0:T(8,128)S(1)}, u32[]{:S(2)}, u32[]{:S(2)}) collective-permute-start(f32[8,128]{1,0:T(8,128)S(1)} %broadcast_in_dim.26), channel_id=1, source_target_pairs={{0,2},{1,3},{2,0},{3,1},{4,6},{5,7},{6,4},{7,5},{8,10},{9,11},{10,... | collective-permute-start | bytes 12296 | tf_op jit(solution)/shard_map/ppermute | solution.py:98
  125.8 8.5 %collective-permute-start.15 = (f32[8,128]{1,0:T(8,128)S(1)}, f32[8,128]{1,0:T(8,128)S(1)}, u32[]{:S(2)}, u32[]{:S(2)}) collective-permute-start(f32[8,128]{1,0:T(8,128)S(1)} %broadcast_in_dim.26), channel_id=1, source_target_pairs={{0,3},{1,0},{2,1},{3,2},{4,7},{5,4},{6,5},{7,6},{8,11},{9,8},{10,9... | collective-permute-start | bytes 12296 | tf_op jit(solution)/shard_map/ppermute | solution.py:98
  130.4 5.9 %collective-permute-start.7 = (f32[16,512]{1,0:T(8,128)S(1)}, f32[16,512]{1,0:T(8,128)S(1)}, u32[]{:S(2)}, u32[]{:S(2)}) collective-permute-start(f32[16,512]{1,0:T(8,128)S(1)} %scatter.4), channel_id=1, source_target_pairs={{0,1},{1,2},{2,3},{3,0},{4,5},{5,6},{6,7},{7,4},{8,9},{9,10},{10,1... | collective-permute-start | bytes 98312 | tf_op jit(solution)/shard_map/ppermute | solution.py:98
  130.5 5.8 %collective-permute-start.8 = (f32[16,512]{1,0:T(8,128)S(1)}, f32[16,512]{1,0:T(8,128)S(1)}, u32[]{:S(2)}, u32[]{:S(2)}) collective-permute-start(f32[16,512]{1,0:T(8,128)S(1)} %scatter.4), channel_id=1, source_target_pairs={{0,2},{1,3},{2,0},{3,1},{4,6},{5,7},{6,4},{7,5},{8,10},{9,11},{10,... | collective-permute-start | bytes 98312 | tf_op jit(solution)/shard_map/ppermute | solution.py:98
  133.0 3.9 %collective-permute-start.9 = (f32[16,512]{1,0:T(8,128)S(1)}, f32[16,512]{1,0:T(8,128)S(1)}, u32[]{:S(2)}, u32[]{:S(2)}) collective-permute-start(f32[16,512]{1,0:T(8,128)S(1)} %scatter.4), channel_id=1, source_target_pairs={{0,3},{1,0},{2,1},{3,2},{4,7},{5,4},{6,5},{7,6},{8,11},{9,8},{10,9... | collective-permute-start | bytes 98312 | tf_op jit(solution)/shard_map/ppermute | solution.py:98
  (5 other events, 7.1 us)

commit v2 on v1

v2 whole, which is shorter than its diff:
```python
import functools

import jax
import jax.numpy as jnp
from jax import lax
from jax.experimental import pallas as pl
from jax.experimental.pallas import tpu as pltpu
from jax.sharding import PartitionSpec as P

PC = 37
LANES = 128
STEP = 32
REACH = 4
OFFSETS = [(a, b) for a in (-1, 0, 1) for b in (-1, 0, 1)]
X_LIMIT = 6.0


def pieces(block, axis, size, source):
    if size != 4:
        block = jnp.where(lax.axis_index(axis) == source, block, jnp.zeros_like(block))
        block = lax.psum(block, axis)
        width = block.shape[1] // 2
        low, high = block[:, :width], block[:, width:]
        zero = jnp.int32(0)
        return zero + 1, zero, (low, low, high, high)
    me = lax.axis_index(axis)
    core = me % 2
    mate = [(0, 1), (1, 0), (2, 3), (3, 2)]
    across = [(0, 2), (2, 0), (1, 3), (3, 1)]
    width = block.shape[1] // 2
    low, high = block[:, :width], block[:, width:]
    got = lax.ppermute(jnp.where(core == 0, high, low), axis, mate)
    kept = jnp.where(core == 0, low, high)
    held = jnp.where(source % 2 == core, kept, got)
    other = lax.ppermute(held, axis, across)
    here = ((source // 2) == (me // 2)).astype(jnp.int32)
    back_held = lax.ppermute(held, axis, mate)
    back_other = lax.ppermute(other, axis, mate)
    return here, core, (held, other, back_held, back_other)


def gelu_parts(value):
    inner = 0.7978845608 * (value + 0.044715 * value * value * value)
    tanh_val = jnp.tanh(inner)
    out_val = 0.5 * value * (1.0 + tanh_val)
    slope = 0.5 * (1.0 + tanh_val) + 0.5 * value * (1.0 - tanh_val * tanh_val) * 0.7978845608 * (
        1.0 + 3.0 * 0.044715 * value * value
    )
    return (out_val, slope)


def head_kernel(
    dp,
    classes,
    scalars,
    held,
    other,
    back_held,
    back_other,
    weight_in,
    taps,
    weight_out,
    onehot,
    after,
    before,
    x_out,
    dpre_out,
    stats_out,
    *rest,
):
    packs = rest[:dp]
    x_vmem, pre, dys, slope, hid, dlog, gout, sem_in, sem_out = rest[dp:]
    rows = x_vmem.shape[0]
    width = x_vmem.shape[1] // 2
    hidden = weight_in.shape[1]
    chunks = hidden // LANES
    guard = REACH * (PC + 1)
    padded = slope.shape[1]
    blocks = padded // STEP
    dil, here, core, me = scalars[0], scalars[1], scalars[2], scalars[3]

    def fetch(source, place, index):
        column = pl.multiple_of(place * width, LANES)
        return pltpu.make_async_copy(source, x_vmem.at[:, pl.ds(column, width)], sem_in.at[index])

    @pl.when(here == 1)
    def _():
        fetch(held, core, 0).start()
        fetch(back_held, 1 - core, 1).start()

    @pl.when(here == 0)
    def _():
        fetch(other, core, 0).start()
        fetch(back_other, 1 - core, 1).start()

    for shift in range(3):
        for c in range(chunks):
            for ref in (pre, dys):
                ref[shift, c, :guard, :] = jnp.zeros((guard, LANES), jnp.float32)
                tail = ref.shape[2] - guard - rows
                ref[shift, c, guard + rows :, :] = jnp.zeros((tail, LANES), jnp.float32)
    fetch(held, core, 0).wait()
    fetch(back_held, 1 - core, 1).wait()
    save = pltpu.make_async_copy(x_vmem, x_out, sem_out)
    save.start()

    masks = (after, None, before)
    for n in range(hidden // 256):
        value = jnp.dot(
            x_vmem[...], weight_in[:, 256 * n : 256 * n + 256], preferred_element_type=jnp.float32
        )
        for h in range(2):
            part = value[:, LANES * h : LANES * h + LANES]
            for shift in range(3):
                mask = (before, None, after)[shift]
                pre[shift, 2 * n + h, guard : guard + rows, :] = (
                    part if mask is None else part * mask[...]
                )

    starts = [dil * (PC * a + b) for a, b in OFFSETS]

    def forward(i, carry):
        row = pl.multiple_of(i * STEP, STEP)
        for c in range(chunks):
            total = None
            for k in range(9):
                term = (
                    pre[k % 3, c, pl.ds(guard + row + starts[k], STEP), :]
                    * taps[k : k + 1, LANES * c : LANES * c + LANES]
                )
                total = term if total is None else total + term
            act, grad = gelu_parts(total)
            slope[c, pl.ds(row, STEP), :] = grad
            hid[pl.ds(row, STEP), LANES * c : LANES * c + LANES] = act.astype(jnp.bfloat16)
        return carry

    lax.fori_loop(0, blocks, forward, 0)

    logits = jnp.dot(hid[:rows, :], weight_out[...], preferred_element_type=jnp.float32)
    lane = lax.broadcasted_iota(jnp.int32, logits.shape, 1)
    logits = jnp.where(lane < classes, logits, -1e30)
    peak = jnp.max(logits, axis=1, keepdims=True)
    power = jnp.exp(logits - peak)
    prob = power / jnp.sum(power, axis=1, keepdims=True)
    dlog[...] = (prob - onehot[...].astype(jnp.float32)).astype(jnp.bfloat16)

    gout[...] = lax.dot_general(
        hid[:rows, :], dlog[...], (((0,), (0,)), ((), ())), preferred_element_type=jnp.float32
    )
    for n in range(hidden // 256):
        value = lax.dot_general(
            dlog[...],
            weight_out[256 * n : 256 * n + 256, :],
            (((1,), (1,)), ((), ())),
            preferred_element_type=jnp.float32,
        )
        for h in range(2):
            c = 2 * n + h
            part = value[:, LANES * h : LANES * h + LANES] * slope[c, :rows, :]
            for shift in range(3):
                mask = (after, None, before)[shift]
                dys[shift, c, guard : guard + rows, :] = part if mask is None else part * mask[...]

    def fold(value):
        return jnp.sum(value.reshape(STEP // 8, 8, LANES), axis=0)

    biggest = jnp.zeros((8, LANES), jnp.float32)
    for c in range(chunks):
        column = slice(LANES * c, LANES * c + LANES)

        def backward(i, carry):
            row = pl.multiple_of(i * STEP, STEP)
            sums, top = carry
            dy = dys[1, c, pl.ds(guard + row, STEP), :]
            total = None
            out = []
            for k in range(9):
                out.append(sums[k] + fold(dy * pre[k % 3, c, pl.ds(guard + row + starts[k], STEP), :]))
                term = (
                    dys[k % 3, c, pl.ds(guard + row - starts[k], STEP), :]
                    * taps[k : k + 1, column]
                )
                total = term if total is None else total + term
            dpre_out[pl.ds(row, STEP), column] = total.astype(jnp.bfloat16)
            size = jnp.max(jnp.abs(total).reshape(STEP // 8, 8, LANES), axis=0)
            return tuple(out), jnp.maximum(top, size)

        zeros = tuple(jnp.zeros((8, LANES), jnp.float32) for _ in range(9))
        sums, biggest = lax.fori_loop(0, blocks, backward, (zeros, biggest))
        square = jnp.zeros((1, LANES), jnp.float32)
        for k in range(9):
            value = jnp.sum(sums[k], axis=0, keepdims=True)
            square = square + value * value
            for pack in packs:
                pack[depth_of(packs) + 2 * k + c // 2, LANES * (c % 2) : LANES * (c % 2) + LANES] = value[0]
        stats_out[0:1, column] = square
    depth = hidden // dp
    top = jnp.full((1, 256), jnp.max(biggest), jnp.float32)
    for s in range(dp):
        place = lax.rem(me + s, dp)
        packs[s][:depth, :] = gout[pl.ds(pl.multiple_of(place * depth, 8), depth), :]
        packs[s][depth + 18 : depth + 19, :] = top
    stats_out[1:2, :256] = jnp.sum(gout[...] * gout[...], axis=0, keepdims=True)
    save.wait()


def depth_of(packs):
    return packs[0].shape[0] - 24


def head_backward(dp, here, core, me, halves, onehot, weight_in, taps, weight_out, dil, masks):
    rows = onehot.shape[0]
    hidden = weight_in.shape[1]
    chunks = hidden // LANES
    padded = pl.cdiv(rows, STEP) * STEP
    guard = REACH * (PC + 1)
    depth = hidden // dp
    scalars = jnp.stack([dil, here, core, me]).astype(jnp.int32)
    vmem = pl.BlockSpec(memory_space=pltpu.VMEM)
    anywhere = pl.BlockSpec(memory_space=pl.ANY)
    classes = weight_out.shape[1]
    weight_out = jnp.pad(weight_out, ((0, 0), (0, 256 - classes)))
    span = 2 * guard + padded
    return pl.pallas_call(
        functools.partial(head_kernel, dp, classes),
        out_shape=[
            jax.ShapeDtypeStruct((rows, weight_in.shape[0]), jnp.bfloat16),
            jax.ShapeDtypeStruct((padded, hidden), jnp.bfloat16),
            jax.ShapeDtypeStruct((8, hidden), jnp.float32),
        ]
        + [jax.ShapeDtypeStruct((depth + 24, 256), jnp.float32)] * dp,
        in_specs=[pl.BlockSpec(memory_space=pltpu.SMEM)] + [anywhere] * 4 + [vmem] * 6,
        out_specs=[anywhere, vmem, vmem] + [vmem] * dp,
        scratch_shapes=[
            pltpu.VMEM((rows, weight_in.shape[0]), jnp.bfloat16),
            pltpu.VMEM((3, chunks, span, LANES), jnp.float32),
            pltpu.VMEM((3, chunks, span, LANES), jnp.float32),
            pltpu.VMEM((chunks, padded, LANES), jnp.float32),
            pltpu.VMEM((padded, hidden), jnp.bfloat16),
            pltpu.VMEM((rows, 256), jnp.bfloat16),
            pltpu.VMEM((hidden, 256), jnp.float32),
            pltpu.SemaphoreType.DMA((2,)),
            pltpu.SemaphoreType.DMA,
        ],
        compiler_params=pltpu.CompilerParams(vmem_limit_bytes=48 * 1024 * 1024),
        name="head",
    )(scalars, *halves, weight_in, taps, weight_out, onehot, *masks)


def shift(value, step, size):
    return lax.ppermute(value, "dp", [(i, (i + step) % size) for i in range(size)])


def per_device(dp, trials, features, owner, dilation_index, labels, input_weight, taps, output_weight):
    here, core, halves = pieces(features[0, 0], "trial", trials, owner[0])
    me = lax.axis_index("dp")
    dil = dilation_index[0] + 1
    rows = features.shape[2]
    onehot = (labels[0][:, None] == jnp.arange(256, dtype=jnp.int32)[None, :]).astype(jnp.bfloat16)
    column = lax.broadcasted_iota(jnp.int32, (rows, LANES), 0) % PC
    before = (column < PC - dil).astype(jnp.float32)
    after = (column >= dil).astype(jnp.float32)
    xrows, dpre, stats, *packs = head_backward(
        dp, here, core, me, halves, onehot, input_weight[0], taps[0], output_weight[0], dil, (after, before)
    )
    dpre = dpre[:rows]
    classes = output_weight.shape[2]
    depth = xrows.shape[1] // dp
    depth_out = input_weight.shape[2] // dp
    sent = [shift(packs[s], s, dp) for s in range(1, dp)]
    limit = X_LIMIT * rows
    room = 32768.0 / limit

    def bound(pack):
        return jnp.maximum(pack[depth_out + 18, 0], 1e-30)

    scale = room / bound(packs[0])
    norm_in = 0.0
    got = []
    share_in = None
    for step in list(range(1, dp)) + [0]:
        place = (me + step) % dp
        part = jnp.dot(
            lax.dynamic_slice_in_dim(xrows, place * depth, depth, 1).T,
            dpre,
            preferred_element_type=jnp.float32,
        )
        norm_in = norm_in + jnp.sum(part * part)
        if step:
            got.append(shift((part * scale).astype(jnp.float16), step, dp))
        else:
            share_in = part
    total = packs[0]
    for pack in sent:
        total = total + pack
    share_out = total[:depth_out, :classes]
    total_taps = total[depth_out : depth_out + 18].reshape(9, -1)
    for value, pack in zip(got, sent):
        share_in = share_in + value.astype(jnp.float32) * (bound(pack) * (1.0 / room))
    line = jnp.stack(
        [
            jnp.sum(share_in * share_in),
            jnp.sum(share_out * share_out),
            norm_in,
            jnp.sum(stats[0]),
            jnp.sum(stats[1, :256]),
        ]
    )
    line = jnp.broadcast_to(jnp.pad(line, (0, 123))[None], (8, 128))
    whole = line
    for step in range(1, dp):
        whole = whole + shift(line, step, dp)
    totals = jnp.stack([whole[0, 0], jnp.sum(total_taps * total_taps), whole[0, 1]])
    norms = jnp.log(1e-12 + jnp.stack([whole[0, 2:5], totals]))
    return (share_in[None], total_taps[None], share_out[None], norms[None])


def solution(mesh):
    dp, trials = mesh.shape["dp"], mesh.shape["trial"]
    placed = (
        P(("groups", "dp"), "trial", None, None),
        P(("groups", "dp")),
        P("trial"),
        P(("groups", "dp"), None),
        P("trial", None, None),
        P("trial", None, None),
        P("trial", None, None),
    )

    def step(*args):
        return per_device(dp, trials, *args)

    return jax.shard_map(
        step,
        mesh=mesh,
        in_specs=placed,
        out_specs=(
            P(("groups", "trial"), "dp", None),
            P(("groups", "trial"), None, None),
            P(("groups", "trial"), "dp", None),
            P(("groups", "trial"), None, None),
        ),
        check_vma=False,
    )
```

time: 141 us -> 118 us (0.84)
  other arithmetic: 28.6 us -> 7.59 us
  matrix products: 22.5 us -> 10.1 us
  waiting for transfers between devices: 42.4 us -> 52.8 us
  Pallas kernels: 0 us -> 9.02 us
  local copies, waits for them, and re-layouts: 14.4 us -> 6.85 us
  starting transfers between devices: 27.6 us -> 23.5 us
  between operations: 5.12 us -> 7.51 us
    dot_general x8 -> x4, matrix products: 22.5 us -> 10.1 us  [per_device(): jnp.dot(lax.dynamic_slice_in_dim(xrows, place * depth, depth, 1).T, dpre,...]
    ppermute x12 -> x9, waiting for transfers between devices: 21.1 us -> 31.1 us  [shift(): lax.ppermute(value, 'dp', [(i, (i + step) % size) for i in range(size)])]
    pallas_call x0 -> x1, Pallas kernels: none -> 9.02 us  [head_backward(): pl.pallas_call(functools.partial(head_kernel, dp, classes), out_shape=[ja...]
    select_n x5 -> x2, other arithmetic: 9.19 us -> 1.87 us  [the longest x1 1.67 us: pieces(): got = lax.ppermute(jnp.where(core == 0, high, low), axis, mate)]
    convert_element_type x3 -> x2, other arithmetic: 7.59 us -> 0.45 us  [the longest x1 0.3 us: per_device(): before = (column < PC - dil).astype(jnp.float32)]
    ppermute x12 -> x9, starting transfers between devices: 24.3 us -> 18.6 us  [shift(): lax.ppermute(value, 'dp', [(i, (i + step) % size) for i in range(size)])]
    reshape x2 -> x0, local copies, waits for them, and re-layouts: 4.27 us -> none  [the longest x1 2.15 us: head_backward(): hid = act.astype(jnp.bfloat16).reshape(rows_count, hidden_width)]
    another operation x2 -> x3, local copies, waits for them, and re-layouts: 0.06 us -> 3.25 us  [the longest x1 2.55 us: per_device(): jnp.stack([jnp.sum(share_in * share_in), jnp.sum(share_out * share_out),...]
  transfers between devices with their start and end apart: 16 -> 13, of which waited for: 5 -> 7; matrix products, arithmetic and copies ran while one was open for 22% -> 7% of each run, Pallas kernels for 0% -> 0%
where the time goes in v2:
time: 118 us; the launch traced here: 117 us
  waiting for transfers between devices  52.8 us (45%)
  starting transfers between devices  23.5 us (20%)
  matrix products  10.1 us (9%)
  Pallas kernels  9.02 us (8%)
  other arithmetic  7.59 us (6%)
  between operations  7.51 us (6%)
  local copies, waits for them, and re-layouts  6.85 us (6%)
    ppermute x9, waiting for transfers between devices, shift(): lax.ppermute(value, 'dp', [(i, (i + step) % size) for i in range(size)])  31.1 us
    ppermute x1, waiting for transfers between devices, pieces(): other = lax.ppermute(held, axis, across)  19.4 us
    ppermute x9, starting transfers between devices, shift(): lax.ppermute(value, 'dp', [(i, (i + step) % size) for i in range(size)])  18.6 us
    dot_general x4, matrix products, per_device(): jnp.dot(lax.dynamic_slice_in_dim(xrows, place * depth, depth, 1).T, dpre,...  10.1 us
    pallas_call x1, Pallas kernels, head_backward(): pl.pallas_call(functools.partial(head_kernel, dp, classes), out_shape=[ja...  9.02 us
    ppermute x1, starting transfers between devices, pieces(): other = lax.ppermute(held, axis, across)  2.92 us
    another operation x1, local copies, waits for them, and re-layouts, per_device(): jnp.stack([jnp.sum(share_in * share_in), jnp.sum(share_out * share_out),...  2.55 us
  transfers between devices with their start and end apart: 13, of which 7 were waited for; matrix products, arithmetic and copies ran while one was open for 7% of the time, Pallas kernels for 0%

profile of v2, /device:TPU:0, one launch (start us, length us, event | category | flops | bytes accessed | tf_op | source)
XLA Modules:
  0.0 117.3 jit_solution(15537600205194876342)
XLA Ops:
  0.7 1.7 %broadcast_select_fusion = bf16[592,768]{1,0:T(8,128)(2,1)S(1)} fusion(pred[]{:T(512)S(6)} %eq.36, bf16[592,1536]{1,0:T(8,128)(2,1)} %bitcast.36), kind=kLoop, calls=%fused_computation.1 | loop fusion | flops 454656 | bytes 2727937 | tf_op jit(solution)/shard_map/jit(_where)/select_n | solution.py:32
  2.3 0.5 collective-permute-start
  3.5 0.0 copy-start.2
  3.5 0.0 copy-start.4
  3.6 1.5 %collective-permute-done = bf16[592,768]{1,0:T(8,128)(2,1)} collective-permute-done((bf16[592,768]{1,0:T(8,128)(2,1)S(1)}, bf16[592,768]{1,0:T(8,128)(2,1)}, u32[]{:S(2)}, u32[]{:S(2)}) %collective-permute-start) | collective-permute-done | bytes 909344 | tf_op jit(solution)/shard_map/ppermute | solution.py:32
  5.1 0.2 select_select_fusion.held
  5.3 2.9 %collective-permute-start.1 = (bf16[592,768]{1,0:T(8,128)(2,1)S(1)}, bf16[592,768]{1,0:T(8,128)(2,1)S(1)}, u32[]{:S(2)}, u32[]{:S(2)}) collective-permute-start(bf16[592,768]{1,0:T(8,128)(2,1)S(1)} %select_select_fusion.held), channel_id=1, source_target_pairs={{0,8},{8,0},{4,12},{12,4},{1,9},{9,1},{5,13},{13,5},{2,10},{10,2},... | collective-permute-start | bytes 2727944 | tf_op jit(solution)/shard_map/ppermute | solution.py:35
  8.2 1.0 collective-permute-start.2
  9.2 19.4 %collective-permute-done.1.other = bf16[592,768]{1,0:T(8,128)(2,1)S(1)} collective-permute-done((bf16[592,768]{1,0:T(8,128)(2,1)S(1)}, bf16[592,768]{1,0:T(8,128)(2,1)S(1)}, u32[]{:S(2)}, u32[]{:S(2)}) %collective-permute-start.1) | collective-permute-done | bytes 909344 | tf_op jit(solution)/shard_map/ppermute | solution.py:35
  28.7 0.4 collective-permute-start.3
  29.7 0.1 copy.14
  30.0 0.1 pad_add_fusion.scalars
  30.1 0.1 fusion.onehot
  30.2 0.3 fusion.14
  30.6 0.7 collective-permute-done.3.back_other
  31.3 9.0 %head.1 = (bf16[592,1536]{1,0:T(8,128)(2,1)}, bf16[608,512]{1,0:T(8,128)(2,1)S(1)}, f32[8,512]{1,0:T(8,128)S(1)}, f32[152,256]{1,0:T(8,128)S(1)}, f32[152,256]{1...) custom-call(s32[4]{0:T(128)S(1)} %pad_add_fusion.scalars, bf16[592,768]{1,0:T(8,128)(2,1)S(1)} %select_select_fusion.held, ...), custom_call_target="tpu_custom_call" | custom-call | tf_op jit(solution)/shard_map/head/pallas_call | solution.py:224
  40.3 0.5 slice.45
  41.8 2.9 %multiply_reduce_fusion.3 = (f32[]{:T(128)}, f16[384,512]{1,0:T(8,128)(2,1)}) fusion(f32[]{:T(128)} %bitcast.8, bf16[608,512]{1,0:T(8,128)(2,1)S(1)} %get-tuple-element.12, bf16[592,1536]{1,0:T(8,128)(2,1)} %get-tuple-element.11, s32[]{:T(128)S(6)} %select_n.85), kind=kOutput, calls=%fused_computation.5 | convolution fusion | flops 233570304 | bytes 1454600 | tf_op jit(solution)/shard_map/dot_general | solution.py:283
  44.7 1.8 %multiply_reduce_fusion.2 = (f32[]{:T(128)}, f16[384,512]{1,0:T(8,128)(2,1)}) fusion(f32[]{:T(128)} %bitcast.8, bf16[608,512]{1,0:T(8,128)(2,1)S(1)} %get-tuple-element.12, bf16[592,1536]{1,0:T(8,128)(2,1)S(1)} %copy-done.5, s32[]{:T(128)S(6)} %select_n.87), kind=kOutput, calls=%fused_computation.4 | convolution fusion | flops 233570304 | bytes 1454092 | tf_op jit(solution)/shard_map/dot_general | solution.py:283
  46.5 3.7 %collective-permute-start.7 = (f32[152,256]{1,0:T(8,128)S(1)}, f32[152,256]{1,0:T(8,128)S(1)}, u32[]{:S(2)}, u32[]{:S(2)}) collective-permute-start(f32[152,256]{1,0:T(8,128)S(1)} %get-tuple-element.15), channel_id=1, source_target_pairs={{0,2},{1,3},{2,0},{3,1},{4,6},{5,7},{6,4},{7,5},{8,10},{9,11},{10,... | collective-permute-start | bytes 466952 | tf_op jit(solution)/shard_map/ppermute | solution.py:251
  50.2 1.9 %multiply_reduce_fusion.1 = (f32[]{:T(128)}, f16[384,512]{1,0:T(8,128)(2,1)}) fusion(f32[]{:T(128)} %bitcast.8, bf16[608,512]{1,0:T(8,128)(2,1)S(1)} %get-tuple-element.12, bf16[592,1536]{1,0:T(8,128)(2,1)S(1)} %copy-done.5, s32[]{:T(128)S(6)} %select_n.89), kind=kOutput, calls=%fused_computation.3 | convolution fusion | flops 233570304 | bytes 1454092 | tf_op jit(solution)/shard_map/dot_general | solution.py:283
  52.1 1.2 %collective-permute-start.4 = (f16[384,512]{1,0:T(8,128)(2,1)}, f16[384,512]{1,0:T(8,128)(2,1)S(1)}, u32[]{:S(2)}, u32[]{:S(2)}) collective-permute-start(f16[384,512]{1,0:T(8,128)(2,1)} %get-tuple-element.34), channel_id=1, source_target_pairs={{0,1},{1,2},{2,3},{3,0},{4,5},{5,6},{6,7},{7,4},{8,9},{9,10},{10,1... | collective-permute-start | bytes 1179656 | tf_op jit(solution)/shard_map/ppermute | solution.py:251
  53.3 0.7 collective-permute-start.6
  54.0 1.9 %collective-permute-start.9 = (f32[152,256]{1,0:T(8,128)S(1)}, f32[152,256]{1,0:T(8,128)S(1)}, u32[]{:S(2)}, u32[]{:S(2)}) collective-permute-start(f32[152,256]{1,0:T(8,128)S(1)} %get-tuple-element.16), channel_id=1, source_target_pairs={{0,3},{1,0},{2,1},{3,2},{4,7},{5,4},{6,5},{7,6},{8,11},{9,8},{10,9... | collective-permute-start | bytes 466952 | tf_op jit(solution)/shard_map/ppermute | solution.py:251
  55.9 0.6 collective-permute-start.5
  56.5 0.7 slice_reduce_fusion
  57.1 18.1 %collective-permute-done.7 = f32[152,256]{1,0:T(8,128)S(1)} collective-permute-done((f32[152,256]{1,0:T(8,128)S(1)}, f32[152,256]{1,0:T(8,128)S(1)}, u32[]{:S(2)}, u32[]{:S(2)}) %collective-permute-start.7) | collective-permute-done | bytes 155680 | tf_op jit(solution)/shard_map/ppermute | solution.py:251
  75.3 0.6 slice_reduce_fusion.1
  77.8 0.5 slice.59
  78.9 0.5 slice.60
  80.1 1.2 %collective-permute-done.5 = f32[152,256]{1,0:T(8,128)S(1)} collective-permute-done((f32[152,256]{1,0:T(8,128)S(1)}, f32[152,256]{1,0:T(8,128)S(1)}, u32[]{:S(2)}, u32[]{:S(2)}) %collective-permute-start.5) | collective-permute-done | bytes 155680 | tf_op jit(solution)/shard_map/ppermute | solution.py:251
  81.3 0.5 slice.58
  82.5 0.1 add_add_fusion
  82.5 0.7 multiply_reduce_fusion.5
  83.2 4.0 %collective-permute-done.6 = f16[384,512]{1,0:T(8,128)(2,1)} collective-permute-done((f16[384,512]{1,0:T(8,128)(2,1)}, f16[384,512]{1,0:T(8,128)(2,1)}, u32[]{:S(2)}, u32[]{:S(2)}) %collective-permute-start.6) | collective-permute-done | bytes 393248 | tf_op jit(solution)/shard_map/ppermute | solution.py:251
  87.2 7.8 %collective-permute-done.8 = f16[384,512]{1,0:T(8,128)(2,1)} collective-permute-done((f16[384,512]{1,0:T(8,128)(2,1)}, f16[384,512]{1,0:T(8,128)(2,1)}, u32[]{:S(2)}, u32[]{:S(2)}) %collective-permute-start.8) | collective-permute-done | bytes 393248 | tf_op jit(solution)/shard_map/ppermute | solution.py:251
  94.9 3.5 %multiply_reduce_fusion = (f32[]{:T(128)}, f32[]{:T(128)}, f32[1,384,512]{2,1,0:T(8,128)}) fusion(f32[]{:T(128)} %bitcast.11, f16[384,512]{1,0:T(8,128)(2,1)} %collective-permute-done.8, f32[]{:T(128)} %bitcast.10, f16[384,512]{1,0:T(8,128)(2,1)} %collective-permute-done.6, f32[]{:T(128)} %bitcast.9, f16[384,512]{1,0:T(8,128)(2,1)S(1)} %collective-permute-done.4, ...), kind=kOutput, calls=%fused_computation.2 | convolution fusion | flops 235339776 | bytes 3028492 | tf_op jit(solution)/shard_map/dot_general | solution.py:283
  99.0 2.6 %stack.58 = f32[5]{0:T(128)S(1)} concatenate(f32[1]{0:T(128)} %bitcast.14, f32[1]{0:T(128)} %bitcast.15, f32[1]{0:T(128)} %bitcast.16, f32[1]{0:T(128)} %bitcast.17, f32[1]{0:T(128)} %bitcast.18), dimensions={0} | concatenate | bytes 40 | tf_op jit(solution)/shard_map/stack | solution.py:300
  101.6 5.7 %collective-permute-start.10 = (f32[8,128]{1,0:T(8,128)S(1)}, f32[8,128]{1,0:T(8,128)S(1)}, u32[]{:S(2)}, u32[]{:S(2)}) collective-permute-start(f32[8,128]{1,0:T(8,128)S(1)} %broadcast_in_dim.16), channel_id=1, source_target_pairs={{0,1},{1,2},{2,3},{3,0},{4,5},{5,6},{6,7},{7,4},{8,9},{9,10},{10,1... | collective-permute-start | bytes 12296 | tf_op jit(solution)/shard_map/ppermute | solution.py:251
  107.2 2.0 %collective-permute-start.11 = (f32[8,128]{1,0:T(8,128)S(1)}, f32[8,128]{1,0:T(8,128)S(1)}, u32[]{:S(2)}, u32[]{:S(2)}) collective-permute-start(f32[8,128]{1,0:T(8,128)S(1)} %broadcast_in_dim.16), channel_id=1, source_target_pairs={{0,2},{1,3},{2,0},{3,1},{4,6},{5,7},{6,4},{7,5},{8,10},{9,11},{10,... | collective-permute-start | bytes 12296 | tf_op jit(solution)/shard_map/ppermute | solution.py:251
  109.3 2.8 %collective-permute-start.12 = (f32[8,128]{1,0:T(8,128)S(1)}, f32[8,128]{1,0:T(8,128)S(1)}, u32[]{:S(2)}, u32[]{:S(2)}) collective-permute-start(f32[8,128]{1,0:T(8,128)S(1)} %broadcast_in_dim.16), channel_id=1, source_target_pairs={{0,3},{1,0},{2,1},{3,2},{4,7},{5,4},{6,5},{7,6},{8,11},{9,8},{10,9... | collective-permute-start | bytes 12296 | tf_op jit(solution)/shard_map/ppermute | solution.py:251
  112.1 0.6 multiply_reduce_fusion.6
  112.7 0.7 copy.16
  113.4 0.6 broadcast_in_dim_reshape.4
  114.1 0.6 fusion.25
  114.7 0.1 slice_bitcast_fusion.1
  114.8 2.0 %maximum_bitcast_fusion = f32[1,1,3]{2,1,0:T(1,128)S(1)} fusion(f32[1]{0:T(128)} %bitcast.22, f32[1]{0:T(128)} %bitcast.21, f32[1]{0:T(128)} %bitcast.20), kind=kLoop, calls=%fused_computation.49 | loop fusion | flops 6 | bytes 24 | tf_op jit(solution)/shard_map/stack | solution.py:314
  116.7 0.6 fusion.19
  (25 shorter events, 0.1 us)
Async XLA Ops:
  0.6 4.4 %copy-start.1 = (bf16[1,1,592,1536]{3,2,1,0:T(8,128)(2,1)S(1)}, bf16[1,1,592,1536]{3,2,1,0:T(8,128)(2,1)}, u32[]{:S(2)}) copy-start(bf16[1,1,592,1536]{3,2,1,0:T(8,128)(2,1)} %param.7) | copy-start | bytes 5455876
  2.3 2.7 %collective-permute-start = (bf16[592,768]{1,0:T(8,128)(2,1)S(1)}, bf16[592,768]{1,0:T(8,128)(2,1)}, u32[]{:S(2)}, u32[]{:S(2)}) collective-permute-start(bf16[592,768]{1,0:T(8,128)(2,1)S(1)} %broadcast_select_fusion), channel_id=1, source_target_pairs={{0,4},{4,0},{8,12},{12,8},{1,5},{5,1},{9,13},{13,9},{2,6},{6,2},{1... | collective-permute-start | bytes 2727944 | tf_op jit(solution)/shard_map/ppermute | solution.py:32
  3.5 26.2 %copy-start.2 = (bf16[1,512,150]{1,2,0:T(8,128)(2,1)S(1)}, bf16[1,512,150]{1,2,0:T(8,128)(2,1)}, u32[]{:S(2)}) copy-start(bf16[1,512,150]{1,2,0:T(8,128)(2,1)} %param.13) | copy-start | bytes 460804
  3.5 26.3 %copy-start.4 = (s32[1,592]{1,0:T(1,128)S(1)}, s32[1,592]{1,0:T(1,128)}, u32[]{:S(2)}) copy-start(s32[1,592]{1,0:T(1,128)} %param.10) | copy-start | bytes 7108
  3.5 26.3 %copy-start.3 = (f32[1,9,512]{2,0,1:T(1,128)S(1)}, f32[1,9,512]{2,0,1:T(1,128)}, u32[]{:S(2)}) copy-start(f32[1,9,512]{2,0,1:T(1,128)} %param.12) | copy-start | bytes 55300
  5.3 23.4 %collective-permute-start.1 = (bf16[592,768]{1,0:T(8,128)(2,1)S(1)}, bf16[592,768]{1,0:T(8,128)(2,1)S(1)}, u32[]{:S(2)}, u32[]{:S(2)}) collective-permute-start(bf16[592,768]{1,0:T(8,128)(2,1)S(1)} %select_select_fusion.held), channel_id=1, source_target_pairs={{0,8},{8,0},{4,12},{12,4},{1,9},{9,1},{5,13},{13,5},{2,10},{10,2},... | collective-permute-start | bytes 2727944 | tf_op jit(solution)/shard_map/ppermute | solution.py:35
  8.2 22.4 %collective-permute-start.2 = (bf16[592,768]{1,0:T(8,128)(2,1)S(1)}, bf16[592,768]{1,0:T(8,128)(2,1)S(1)}, u32[]{:S(2)}, u32[]{:S(2)}) collective-permute-start(bf16[592,768]{1,0:T(8,128)(2,1)S(1)} %select_select_fusion.held), channel_id=1, source_target_pairs={{0,4},{4,0},{8,12},{12,8},{1,5},{5,1},{9,13},{13,9},{2,6},{6,2},{1... | collective-permute-start | bytes 2727944 | tf_op jit(solution)/shard_map/ppermute | solution.py:37
  28.7 2.6 %collective-permute-start.3 = (bf16[592,768]{1,0:T(8,128)(2,1)S(1)}, bf16[592,768]{1,0:T(8,128)(2,1)}, u32[]{:S(2)}, u32[]{:S(2)}) collective-permute-start(bf16[592,768]{1,0:T(8,128)(2,1)S(1)} %collective-permute-done.1.other), channel_id=1, source_target_pairs={{0,4},{4,0},{8,12},{12,8},{1,5},{5,1},{9,13},{13,9},{2,6},{6,2},{1... | collective-permute-start | bytes 2727944 | tf_op jit(solution)/shard_map/ppermute | solution.py:38
  40.3 9.9 %copy-start = (bf16[608,512]{1,0:T(8,128)(2,1)}, bf16[608,512]{1,0:T(8,128)(2,1)S(1)}, u32[]{:S(2)}) copy-start(bf16[608,512]{1,0:T(8,128)(2,1)S(1)} %get-tuple-element.12) | copy-start | bytes 1867780
  40.3 4.4 %copy-start.5 = (bf16[592,1536]{1,0:T(8,128)(2,1)S(1)}, bf16[592,1536]{1,0:T(8,128)(2,1)}, u32[]{:S(2)}) copy-start(bf16[592,1536]{1,0:T(8,128)(2,1)} %get-tuple-element.11) | copy-start | bytes 5455876
  46.5 28.8 %collective-permute-start.7 = (f32[152,256]{1,0:T(8,128)S(1)}, f32[152,256]{1,0:T(8,128)S(1)}, u32[]{:S(2)}, u32[]{:S(2)}) collective-permute-start(f32[152,256]{1,0:T(8,128)S(1)} %get-tuple-element.15), channel_id=1, source_target_pairs={{0,2},{1,3},{2,0},{3,1},{4,6},{5,7},{6,4},{7,5},{8,10},{9,11},{10,... | collective-permute-start | bytes 466952 | tf_op jit(solution)/shard_map/ppermute | solution.py:251
  52.1 31.1 %collective-permute-start.4 = (f16[384,512]{1,0:T(8,128)(2,1)}, f16[384,512]{1,0:T(8,128)(2,1)S(1)}, u32[]{:S(2)}, u32[]{:S(2)}) collective-permute-start(f16[384,512]{1,0:T(8,128)(2,1)} %get-tuple-element.34), channel_id=1, source_target_pairs={{0,1},{1,2},{2,3},{3,0},{4,5},{5,6},{6,7},{7,4},{8,9},{9,10},{10,1... | collective-permute-start | bytes 1179656 | tf_op jit(solution)/shard_map/ppermute | solution.py:251
  53.3 33.9 %collective-permute-start.6 = (f16[384,512]{1,0:T(8,128)(2,1)}, f16[384,512]{1,0:T(8,128)(2,1)}, u32[]{:S(2)}, u32[]{:S(2)}) collective-permute-start(f16[384,512]{1,0:T(8,128)(2,1)} %get-tuple-element.32), channel_id=1, source_target_pairs={{0,2},{1,3},{2,0},{3,1},{4,6},{5,7},{6,4},{7,5},{8,10},{9,11},{10,... | collective-permute-start | bytes 1179656 | tf_op jit(solution)/shard_map/ppermute | solution.py:251
  54.0 25.0 %collective-permute-start.9 = (f32[152,256]{1,0:T(8,128)S(1)}, f32[152,256]{1,0:T(8,128)S(1)}, u32[]{:S(2)}, u32[]{:S(2)}) collective-permute-start(f32[152,256]{1,0:T(8,128)S(1)} %get-tuple-element.16), channel_id=1, source_target_pairs={{0,3},{1,0},{2,1},{3,2},{4,7},{5,4},{6,5},{7,6},{8,11},{9,8},{10,9... | collective-permute-start | bytes 466952 | tf_op jit(solution)/shard_map/ppermute | solution.py:251
  55.9 25.4 %collective-permute-start.5 = (f32[152,256]{1,0:T(8,128)S(1)}, f32[152,256]{1,0:T(8,128)S(1)}, u32[]{:S(2)}, u32[]{:S(2)}) collective-permute-start(f32[152,256]{1,0:T(8,128)S(1)} %get-tuple-element.14), channel_id=1, source_target_pairs={{0,1},{1,2},{2,3},{3,0},{4,5},{5,6},{6,7},{7,4},{8,9},{9,10},{10,1... | collective-permute-start | bytes 466952 | tf_op jit(solution)/shard_map/ppermute | solution.py:251
  75.3 19.7 %collective-permute-start.8 = (f16[384,512]{1,0:T(8,128)(2,1)}, f16[384,512]{1,0:T(8,128)(2,1)}, u32[]{:S(2)}, u32[]{:S(2)}) collective-permute-start(f16[384,512]{1,0:T(8,128)(2,1)} %get-tuple-element.30), channel_id=1, source_target_pairs={{0,3},{1,0},{2,1},{3,2},{4,7},{5,4},{6,5},{7,6},{8,11},{9,8},{10,9... | collective-permute-start | bytes 1179656 | tf_op jit(solution)/shard_map/ppermute | solution.py:251
  101.6 12.5 %collective-permute-start.10 = (f32[8,128]{1,0:T(8,128)S(1)}, f32[8,128]{1,0:T(8,128)S(1)}, u32[]{:S(2)}, u32[]{:S(2)}) collective-permute-start(f32[8,128]{1,0:T(8,128)S(1)} %broadcast_in_dim.16), channel_id=1, source_target_pairs={{0,1},{1,2},{2,3},{3,0},{4,5},{5,6},{6,7},{7,4},{8,9},{9,10},{10,1... | collective-permute-start | bytes 12296 | tf_op jit(solution)/shard_map/ppermute | solution.py:251
  107.2 6.8 %collective-permute-start.11 = (f32[8,128]{1,0:T(8,128)S(1)}, f32[8,128]{1,0:T(8,128)S(1)}, u32[]{:S(2)}, u32[]{:S(2)}) collective-permute-start(f32[8,128]{1,0:T(8,128)S(1)} %broadcast_in_dim.16), channel_id=1, source_target_pairs={{0,2},{1,3},{2,0},{3,1},{4,6},{5,7},{6,4},{7,5},{8,10},{9,11},{10,... | collective-permute-start | bytes 12296 | tf_op jit(solution)/shard_map/ppermute | solution.py:251
  109.3 4.8 %collective-permute-start.12 = (f32[8,128]{1,0:T(8,128)S(1)}, f32[8,128]{1,0:T(8,128)S(1)}, u32[]{:S(2)}, u32[]{:S(2)}) collective-permute-start(f32[8,128]{1,0:T(8,128)S(1)} %broadcast_in_dim.16), channel_id=1, source_target_pairs={{0,3},{1,0},{2,1},{3,2},{4,7},{5,4},{6,5},{7,6},{8,11},{9,8},{10,9... | collective-permute-start | bytes 12296 | tf_op jit(solution)/shard_map/ppermute | solution.py:251

commit v3 on v2

--- a/solution.py
+++ b/solution.py
@@ -75,8 +75,6 @@
     hidden = weight_in.shape[1]
     chunks = hidden // LANES
     guard = REACH * (PC + 1)
-    padded = slope.shape[1]
-    blocks = padded // STEP
     dil, here, core, me = scalars[0], scalars[1], scalars[2], scalars[3]
 
     def fetch(source, place, index):
@@ -119,24 +117,30 @@
 
     starts = [dil * (PC * a + b) for a, b in OFFSETS]
 
-    def forward(i, carry):
-        row = pl.multiple_of(i * STEP, STEP)
+    def forward(row, count):
         for c in range(chunks):
             total = None
             for k in range(9):
                 term = (
-                    pre[k % 3, c, pl.ds(guard + row + starts[k], STEP), :]
+                    pre[k % 3, c, pl.ds(guard + row + starts[k], count), :]
                     * taps[k : k + 1, LANES * c : LANES * c + LANES]
                 )
                 total = term if total is None else total + term
             act, grad = gelu_parts(total)
-            slope[c, pl.ds(row, STEP), :] = grad
-            hid[pl.ds(row, STEP), LANES * c : LANES * c + LANES] = act.astype(jnp.bfloat16)
-        return carry
-
-    lax.fori_loop(0, blocks, forward, 0)
-
-    logits = jnp.dot(hid[:rows, :], weight_out[...], preferred_element_type=jnp.float32)
+            slope[c, pl.ds(row, count), :] = grad
+            hid[pl.ds(row, count), LANES * c : LANES * c + LANES] = act.astype(jnp.bfloat16)
+
+    whole = rows // STEP
+    left = rows - whole * STEP
+
+    @pl.loop(0, whole)
+    def _(i):
+        forward(pl.multiple_of(i * STEP, STEP), STEP)
+
+    if left:
+        forward(whole * STEP, left)
+
+    logits = jnp.dot(hid[...], weight_out[...], preferred_element_type=jnp.float32)
     lane = lax.broadcasted_iota(jnp.int32, logits.shape, 1)
     logits = jnp.where(lane < classes, logits, -1e30)
     peak = jnp.max(logits, axis=1, keepdims=True)
@@ -145,7 +149,7 @@
     dlog[...] = (prob - onehot[...].astype(jnp.float32)).astype(jnp.bfloat16)
 
     gout[...] = lax.dot_general(
-        hid[:rows, :], dlog[...], (((0,), (0,)), ((), ())), preferred_element_type=jnp.float32
+        dlog[...], hid[...], (((0,), (0,)), ((), ())), preferred_element_type=jnp.float32
     )
     for n in range(hidden // 256):
         value = lax.dot_general(
@@ -156,89 +160,113 @@
         )
         for h in range(2):
             c = 2 * n + h
-            part = value[:, LANES * h : LANES * h + LANES] * slope[c, :rows, :]
+            part = value[:, LANES * h : LANES * h + LANES] * slope[c]
             for shift in range(3):
                 mask = (after, None, before)[shift]
                 dys[shift, c, guard : guard + rows, :] = part if mask is None else part * mask[...]
 
     def fold(value):
-        return jnp.sum(value.reshape(STEP // 8, 8, LANES), axis=0)
-
+        return jnp.sum(value.reshape(-1, 8, LANES), axis=0)
+
+    rows_out = class_rows(classes)
     biggest = jnp.zeros((8, LANES), jnp.float32)
+    taps_square = jnp.zeros((1, LANES), jnp.float32)
     for c in range(chunks):
         column = slice(LANES * c, LANES * c + LANES)
 
-        def backward(i, carry):
-            row = pl.multiple_of(i * STEP, STEP)
+        def backward(row, count, carry):
             sums, top = carry
-            dy = dys[1, c, pl.ds(guard + row, STEP), :]
+            dy = dys[1, c, pl.ds(guard + row, count), :]
             total = None
             out = []
             for k in range(9):
-                out.append(sums[k] + fold(dy * pre[k % 3, c, pl.ds(guard + row + starts[k], STEP), :]))
+                out.append(sums[k] + fold(dy * pre[k % 3, c, pl.ds(guard + row + starts[k], count), :]))
                 term = (
-                    dys[k % 3, c, pl.ds(guard + row - starts[k], STEP), :]
-                    * taps[k : k + 1, column]
+                    dys[k % 3, c, pl.ds(guard + row - starts[k], count), :] * taps[k : k + 1, column]
                 )
                 total = term if total is None else total + term
-            dpre_out[pl.ds(row, STEP), column] = total.astype(jnp.bfloat16)
-            size = jnp.max(jnp.abs(total).reshape(STEP // 8, 8, LANES), axis=0)
+            dpre_out[pl.ds(row, count), column] = total.astype(jnp.bfloat16)
+            size = jnp.max(jnp.abs(total).reshape(-1, 8, LANES), axis=0)
             return tuple(out), jnp.maximum(top, size)
 
         zeros = tuple(jnp.zeros((8, LANES), jnp.float32) for _ in range(9))
-        sums, biggest = lax.fori_loop(0, blocks, backward, (zeros, biggest))
-        square = jnp.zeros((1, LANES), jnp.float32)
+        carry = lax.fori_loop(
+            0,
+            whole,
+            lambda i, carry: backward(pl.multiple_of(i * STEP, STEP), STEP, carry),
+            (zeros, biggest),
+        )
+        if left:
+            carry = backward(whole * STEP, left, carry)
+        sums, biggest = carry
         for k in range(9):
             value = jnp.sum(sums[k], axis=0, keepdims=True)
-            square = square + value * value
+            taps_square = taps_square + value * value
+            row = rows_out + chunks * k + c
             for pack in packs:
-                pack[depth_of(packs) + 2 * k + c // 2, LANES * (c % 2) : LANES * (c % 2) + LANES] = value[0]
-        stats_out[0:1, column] = square
+                pack[row : row + 1, :] = value
+    top = jnp.full((1, LANES), jnp.max(biggest), jnp.float32)
     depth = hidden // dp
-    top = jnp.full((1, 256), jnp.max(biggest), jnp.float32)
+    row = rows_out + 9 * chunks
     for s in range(dp):
-        place = lax.rem(me + s, dp)
-        packs[s][:depth, :] = gout[pl.ds(pl.multiple_of(place * depth, 8), depth), :]
-        packs[s][depth + 18 : depth + 19, :] = top
-    stats_out[1:2, :256] = jnp.sum(gout[...] * gout[...], axis=0, keepdims=True)
+        packs[s][row : row + 1, :] = top
+        if depth % LANES == 0:
+            place = pl.multiple_of((me ^ s) * depth, depth)
+            packs[s][:rows_out, :] = gout[:rows_out, pl.ds(place, depth)]
+    if depth % LANES:
+        for at in range(dp):
+
+            @pl.when(me == at)
+            def _(at=at):
+                for s in range(dp):
+                    place = (at ^ s) * depth
+                    packs[s][:rows_out, :depth] = gout[:rows_out, place : place + depth]
+    stats_out[...] = jnp.zeros(stats_out.shape, jnp.float32)
+    stats_out[0:1, :] = taps_square
+    square = jnp.sum(gout[...] * gout[...], axis=0, keepdims=True)
+    for c in range(chunks):
+        stats_out[1 + c : 2 + c, :] = square[:, LANES * c : LANES * c + LANES]
     save.wait()
 
 
-def depth_of(packs):
-    return packs[0].shape[0] - 24
+def class_rows(classes):
+    return (classes + 7) // 8 * 8
+
+
+def pack_rows(classes, chunks):
+    return class_rows(classes) + (9 * chunks + 8) // 8 * 8
 
 
 def head_backward(dp, here, core, me, halves, onehot, weight_in, taps, weight_out, dil, masks):
     rows = onehot.shape[0]
-    hidden = weight_in.shape[1]
+    wide, hidden = weight_in.shape
     chunks = hidden // LANES
-    padded = pl.cdiv(rows, STEP) * STEP
     guard = REACH * (PC + 1)
-    depth = hidden // dp
     scalars = jnp.stack([dil, here, core, me]).astype(jnp.int32)
     vmem = pl.BlockSpec(memory_space=pltpu.VMEM)
     anywhere = pl.BlockSpec(memory_space=pl.ANY)
     classes = weight_out.shape[1]
     weight_out = jnp.pad(weight_out, ((0, 0), (0, 256 - classes)))
-    span = 2 * guard + padded
+    span = 2 * guard + rows
+    pack = jax.ShapeDtypeStruct((pack_rows(classes, chunks), LANES), jnp.float32)
     return pl.pallas_call(
         functools.partial(head_kernel, dp, classes),
         out_shape=[
-            jax.ShapeDtypeStruct((rows, weight_in.shape[0]), jnp.bfloat16),
-            jax.ShapeDtypeStruct((padded, hidden), jnp.bfloat16),
-            jax.ShapeDtypeStruct((8, hidden), jnp.float32),
+            jax.ShapeDtypeStruct((rows, wide), jnp.bfloat16),
+            jax.ShapeDtypeStruct((rows, hidden), jnp.bfloat16),
+            jax.ShapeDtypeStruct((8, LANES), jnp.float32),
         ]
-        + [jax.ShapeDtypeStruct((depth + 24, 256), jnp.float32)] * dp,
+        + [pack] * dp,
         in_specs=[pl.BlockSpec(memory_space=pltpu.SMEM)] + [anywhere] * 4 + [vmem] * 6,
         out_specs=[anywhere, vmem, vmem] + [vmem] * dp,
         scratch_shapes=[
-            pltpu.VMEM((rows, weight_in.shape[0]), jnp.bfloat16),
+            pltpu.VMEM((rows, wide), jnp.bfloat16),
             pltpu.VMEM((3, chunks, span, LANES), jnp.float32),
             pltpu.VMEM((3, chunks, span, LANES), jnp.float32),
-            pltpu.VMEM((chunks, padded, LANES), jnp.float32),
-            pltpu.VMEM((padded, hidden), jnp.bfloat16),
+            pltpu.VMEM((chunks, rows, LANES), jnp.float32),
+            pltpu.VMEM((rows, hidden), jnp.bfloat16),
             pltpu.VMEM((rows, 256), jnp.bfloat16),
-            pltpu.VMEM((hidden, 256), jnp.float32),
+            pltpu.VMEM((256, hidden), jnp.float32),
             pltpu.SemaphoreType.DMA((2,)),
             pltpu.SemaphoreType.DMA,
         ],
@@ -247,8 +275,69 @@
     )(scalars, *halves, weight_in, taps, weight_out, onehot, *masks)
 
 
-def shift(value, step, size):
-    return lax.ppermute(value, "dp", [(i, (i + step) % size) for i in range(size)])
+def sum_kernel(classes, dp, *refs):
+    parts, last, stats = refs[0], refs[1], refs[2]
+    packs = refs[3 : 3 + dp]
+    norms = refs[3 + dp : 3 + 2 * dp]
+    share_in, share_out, taps_out, line, turned = refs[3 + 2 * dp :]
+    depth = share_out.shape[0]
+    chunks = taps_out.shape[1] // LANES
+    rows_out = class_rows(classes)
+
+    def fold(value):
+        value = jnp.sum(value.reshape(-1, 8, value.shape[1]), axis=0)
+        return sum(value[:, LANES * c : LANES * c + LANES] for c in range(value.shape[1] // LANES))
+
+    total = parts[...] + last[...]
+    share_in[...] = total
+    line[0:8, :] = fold(total * total)
+    summed = packs[0][...]
+    for pack in packs[1:]:
+        summed = summed + pack[...]
+    turned[...] = jnp.zeros(turned.shape, jnp.float32)
+    turned[:rows_out, :] = summed[:rows_out, :]
+    flat = turned[...]
+    if depth < LANES:
+        keep = lax.broadcasted_iota(jnp.int32, flat.shape, 1) < depth
+        flat = jnp.where(keep, flat, 0.0)
+    line[8:16, :] = fold(flat * flat)
+    share_out[...] = flat.T[:depth, :classes]
+    square = jnp.zeros((1, LANES), jnp.float32)
+    for k in range(9):
+        for c in range(chunks):
+            row = rows_out + chunks * k + c
+            value = summed[row : row + 1, :]
+            taps_out[k : k + 1, LANES * c : LANES * c + LANES] = value
+            square = square + value * value
+    line[16:24, :] = stats[...]
+    line[24:32, :] = jnp.zeros((8, LANES), jnp.float32)
+    line[24:25, :] = square
+    line[25:26, :] = jnp.full((1, LANES), sum(norm[0] for norm in norms), jnp.float32)
+
+
+def norm_kernel(dp, chunks, *refs):
+    lines, out = refs[:dp], refs[dp]
+    total = lines[0][...]
+    for line in lines[1:]:
+        total = total + line[...]
+    values = [
+        jnp.max(total[25:26, :]),
+        jnp.sum(total[16:17, :]),
+        jnp.sum(total[17 : 17 + chunks, :]),
+        jnp.sum(total[0:8, :]),
+        jnp.sum(lines[0][24:25, :]),
+        jnp.sum(total[8:16, :]),
+    ]
+    row = lax.broadcasted_iota(jnp.int32, (8, LANES), 0)
+    lane = lax.broadcasted_iota(jnp.int32, (8, LANES), 1)
+    spread = jnp.zeros((8, LANES), jnp.float32)
+    for i, value in enumerate(values):
+        spread = jnp.where((row == i // 3) & (lane == i % 3), value, spread)
+    out[...] = jnp.log(1e-12 + spread)[:2, :3]
+
+
+def swap(value, step, size):
+    return lax.ppermute(value, "dp", [(i, i ^ step) for i in range(size)])
 
 
 def per_device(dp, trials, features, owner, dilation_index, labels, input_weight, taps, output_weight):
@@ -263,55 +352,56 @@
     xrows, dpre, stats, *packs = head_backward(
         dp, here, core, me, halves, onehot, input_weight[0], taps[0], output_weight[0], dil, (after, before)
     )
-    dpre = dpre[:rows]
     classes = output_weight.shape[2]
+    hidden = input_weight.shape[2]
+    chunks = hidden // LANES
     depth = xrows.shape[1] // dp
-    depth_out = input_weight.shape[2] // dp
-    sent = [shift(packs[s], s, dp) for s in range(1, dp)]
-    limit = X_LIMIT * rows
-    room = 32768.0 / limit
+    packs = packs[:1] + [swap(packs[s], s, dp) for s in range(1, dp)]
+    room = 32768.0 / (X_LIMIT * rows)
+    mark = class_rows(classes) + 9 * chunks
 
     def bound(pack):
-        return jnp.maximum(pack[depth_out + 18, 0], 1e-30)
+        return jnp.maximum(pack[mark, 0], 1e-30)
 
     scale = room / bound(packs[0])
-    norm_in = 0.0
+    norms = []
     got = []
-    share_in = None
     for step in list(range(1, dp)) + [0]:
-        place = (me + step) % dp
         part = jnp.dot(
-            lax.dynamic_slice_in_dim(xrows, place * depth, depth, 1).T,
+            lax.dynamic_slice_in_dim(xrows, (me ^ step) * depth, depth, 1).T,
             dpre,
             preferred_element_type=jnp.float32,
         )
-        norm_in = norm_in + jnp.sum(part * part)
+        norms.append(jnp.sum(part * part).reshape(1))
         if step:
-            got.append(shift((part * scale).astype(jnp.float16), step, dp))
-        else:
-            share_in = part
-    total = packs[0]
-    for pack in sent:
-        total = total + pack
-    share_out = total[:depth_out, :classes]
-    total_taps = total[depth_out : depth_out + 18].reshape(9, -1)
-    for value, pack in zip(got, sent):
-        share_in = share_in + value.astype(jnp.float32) * (bound(pack) * (1.0 / room))
-    line = jnp.stack(
-        [
-            jnp.sum(share_in * share_in),
-            jnp.sum(share_out * share_out),
-            norm_in,
-            jnp.sum(stats[0]),
-            jnp.sum(stats[1, :256]),
-        ]
-    )
-    line = jnp.broadcast_to(jnp.pad(line, (0, 123))[None], (8, 128))
-    whole = line
-    for step in range(1, dp):
-        whole = whole + shift(line, step, dp)
-    totals = jnp.stack([whole[0, 0], jnp.sum(total_taps * total_taps), whole[0, 1]])
-    norms = jnp.log(1e-12 + jnp.stack([whole[0, 2:5], totals]))
+            got.append(swap((part * scale).astype(jnp.float16), step, dp))
+    for step in range(1, dp - 1):
+        part = part + got[step - 1].astype(jnp.float32) * (bound(packs[step]) * (1.0 / room))
+        part = lax.optimization_barrier(part)
+    last = got[-1].astype(jnp.float32) * (bound(packs[-1]) * (1.0 / room))
+    vmem = pl.BlockSpec(memory_space=pltpu.VMEM)
+    smem = pl.BlockSpec(memory_space=pltpu.SMEM)
+    share_in, share_out, total_taps, line = pl.pallas_call(
+        functools.partial(sum_kernel, classes, dp),
+        out_shape=[
+            jax.ShapeDtypeStruct((depth, hidden), jnp.float32),
+            jax.ShapeDtypeStruct((hidden // dp, classes), jnp.float32),
+            jax.ShapeDtypeStruct((9, hidden), jnp.float32),
+            jax.ShapeDtypeStruct((32, LANES), jnp.float32),
+        ],
+        in_specs=[vmem] * (3 + dp) + [smem] * dp,
+        out_specs=[vmem] * 4,
+        scratch_shapes=[pltpu.VMEM((256, LANES), jnp.float32)],
+        name="sums",
+    )(part, last, stats, *packs, *norms)
+    lines = [line] + [swap(line, s, dp) for s in range(1, dp)]
+    norms = pl.pallas_call(
+        functools.partial(norm_kernel, dp, chunks),
+        out_shape=jax.ShapeDtypeStruct((2, 3), jnp.float32),
+        in_specs=[vmem] * dp,
+        out_specs=vmem,
+        name="norms",
+    )(*lines)
     return (share_in[None], total_taps[None], share_out[None], norms[None])
 
 

time: 118 us -> 106 us (0.90)
  Pallas kernels: 9.02 us -> 15.5 us
  waiting for transfers between devices: 52.8 us -> 47.3 us
  matrix products: 10.1 us -> 6.04 us
  other arithmetic: 7.59 us -> 4.47 us
  between operations: 7.51 us -> 4.85 us
  starting transfers between devices: 23.5 us -> 21.5 us
    pallas_call x0 -> x2, Pallas kernels: none -> 6.56 us  [the longest x1 5.09 us: per_device(): pl.pallas_call(functools.partial(sum_kernel, classes, dp), out_shape=[jax...]
    ppermute x9, waiting for transfers between devices: 31.1 us -> 25.6 us  [swap(): return lax.ppermute(value, 'dp', [(i, i ^ step) for i in range(size)])]
    dot_general x4, matrix products: 10.1 us -> 6.04 us  [per_device(): jnp.dot(lax.dynamic_slice_in_dim(xrows, (me ^ step) * depth, depth, 1).T,...]
    another operation x3 -> x0, local copies, waits for them, and re-layouts: 3.25 us -> none  [the longest x1 2.55 us: per_device(): jnp.stack([jnp.sum(share_in * share_in), jnp.sum(share_out * share_out),...]
    unnamed x15 -> x30, local copies, waits for them, and re-layouts: 0.9 us -> 4.05 us
    reduce_sum x4 -> x0, other arithmetic: 2.54 us -> none  [the longest x1 0.66 us: per_device(): jnp.sum(stats[0])]
    ppermute x9, starting transfers between devices: 18.6 us -> 16.6 us  [swap(): return lax.ppermute(value, 'dp', [(i, i ^ step) for i in range(size)])]
    another operation x1 -> x0, other arithmetic: 1.97 us -> none  [per_device(): norms = jnp.log(1e-12 + jnp.stack([whole[0, 2:5], totals]))]
  transfers between devices with their start and end apart: 13 -> 13, of which waited for: 7 -> 6; matrix products, arithmetic and copies ran while one was open for 7% -> 12% of each run, Pallas kernels for 0% -> 0%
where the time goes in v3:
time: 106 us
  waiting for transfers between devices  47.3 us (45%)
  starting transfers between devices  21.5 us (20%)
  Pallas kernels  15.5 us (15%)
  local copies, waits for them, and re-layouts  6.2 us (6%)
  matrix products  6.04 us (6%)
  between operations  4.85 us (5%)
  other arithmetic  4.47 us (4%)
    ppermute x9, waiting for transfers between devices, swap(): return lax.ppermute(value, 'dp', [(i, i ^ step) for i in range(size)])  25.6 us
    ppermute x1, waiting for transfers between devices, pieces(): other = lax.ppermute(held, axis, across)  19.4 us
    ppermute x9, starting transfers between devices, swap(): return lax.ppermute(value, 'dp', [(i, i ^ step) for i in range(size)])  16.6 us
    pallas_call x1, Pallas kernels, head_backward(): pl.pallas_call(functools.partial(head_kernel, dp, classes), out_shape=[ja...  8.91 us
    dot_general x4, matrix products, per_device(): jnp.dot(lax.dynamic_slice_in_dim(xrows, (me ^ step) * depth, depth, 1).T,...  6.04 us
    pallas_call x1, Pallas kernels, per_device(): pl.pallas_call(functools.partial(sum_kernel, classes, dp), out_shape=[jax...  5.09 us
    unnamed x30, local copies, waits for them, and re-layouts  4.05 us
    ppermute x1, starting transfers between devices, pieces(): other = lax.ppermute(held, axis, across)  2.92 us
  transfers between devices with their start and end apart: 13, of which 6 were waited for; matrix products, arithmetic and copies ran while one was open for 12% of the time, Pallas kernels for 0%

profile of v3, /device:TPU:0, one launch (start us, length us, event | category | flops | bytes accessed | tf_op | source)
XLA Modules:
  0.0 105.8 jit_solution(4024000162376406151)
XLA Ops:
  0.7 1.7 %broadcast_select_fusion = bf16[592,768]{1,0:T(8,128)(2,1)S(1)} fusion(pred[]{:T(512)S(6)} %eq.32, bf16[592,1536]{1,0:T(8,128)(2,1)} %bitcast.32), kind=kLoop, calls=%fused_computation.1 | loop fusion | flops 454656 | bytes 2727937 | tf_op jit(solution)/shard_map/jit(_where)/select_n | solution.py:32
  2.3 0.5 collective-permute-start
  3.5 0.0 copy-start.3
  3.5 0.0 copy-start.11
  3.5 0.0 copy-start.7
  3.6 1.5 %collective-permute-done = bf16[592,768]{1,0:T(8,128)(2,1)} collective-permute-done((bf16[592,768]{1,0:T(8,128)(2,1)S(1)}, bf16[592,768]{1,0:T(8,128)(2,1)}, u32[]{:S(2)}, u32[]{:S(2)}) %collective-permute-start) | collective-permute-done | bytes 909344 | tf_op jit(solution)/shard_map/ppermute | solution.py:32
  5.1 0.2 select_select_fusion.held
  5.3 2.9 %collective-permute-start.1 = (bf16[592,768]{1,0:T(8,128)(2,1)S(1)}, bf16[592,768]{1,0:T(8,128)(2,1)S(1)}, u32[]{:S(2)}, u32[]{:S(2)}) collective-permute-start(bf16[592,768]{1,0:T(8,128)(2,1)S(1)} %select_select_fusion.held), channel_id=1, source_target_pairs={{0,8},{8,0},{4,12},{12,4},{1,9},{9,1},{5,13},{13,5},{2,10},{10,2},... | collective-permute-start | bytes 2727944 | tf_op jit(solution)/shard_map/ppermute | solution.py:35
  8.2 1.0 collective-permute-start.2
  9.2 19.4 %collective-permute-done.1.other = bf16[592,768]{1,0:T(8,128)(2,1)S(1)} collective-permute-done((bf16[592,768]{1,0:T(8,128)(2,1)S(1)}, bf16[592,768]{1,0:T(8,128)(2,1)S(1)}, u32[]{:S(2)}, u32[]{:S(2)}) %collective-permute-start.1) | collective-permute-done | bytes 909344 | tf_op jit(solution)/shard_map/ppermute | solution.py:35
  28.7 0.4 collective-permute-start.3
  29.7 0.1 copy.11
  30.0 0.1 pad_add_fusion.scalars
  30.1 0.1 fusion.onehot
  30.2 0.3 fusion.10
  30.5 0.0 collective-permute-done.2.back_held
  30.6 0.7 collective-permute-done.3.back_other
  31.3 8.9 %head.1 = (bf16[592,1536]{1,0:T(8,128)(2,1)}, bf16[592,512]{1,0:T(8,128)(2,1)S(1)}, f32[8,128]{1,0:T(8,128)S(1)}, f32[192,128]{1,0:T(8,128)S(1)}, f32[192,128]{1...) custom-call(s32[4]{0:T(128)S(1)} %pad_add_fusion.scalars, bf16[592,768]{1,0:T(8,128)(2,1)S(1)} %select_select_fusion.held, ...), custom_call_target="tpu_custom_call" | custom-call | tf_op jit(solution)/shard_map/head/pallas_call | solution.py:252
  40.2 0.0 copy-start.1
  40.2 0.5 slice.20
  40.7 4.7 %collective-permute-start.9 = (f32[192,128]{1,0:T(8,128)S(1)}, f32[192,128]{1,0:T(8,128)S(1)}, u32[]{:S(2)}, u32[]{:S(2)}) collective-permute-start(f32[192,128]{1,0:T(8,128)S(1)} %get-tuple-element.20), channel_id=1, source_target_pairs={{0,3},{1,2},{2,1},{3,0},{4,7},{5,6},{6,5},{7,4},{8,11},{9,10},{10,... | collective-permute-start | bytes 294920 | tf_op jit(solution)/shard_map/ppermute | solution.py:340
  46.1 2.2 %multiply_reduce_fusion.3 = (f32[]{:T(128)}, f16[384,512]{1,0:T(8,128)(2,1)S(1)}) fusion(f32[]{:T(128)} %bitcast.8, bf16[592,512]{1,0:T(8,128)(2,1)S(1)} %get-tuple-element.16, bf16[592,1536]{1,0:T(8,128)(2,1)} %get-tuple-element.15, s32[]{:T(128)S(6)} %select_n.67), kind=kOutput, calls=%fused_computation.5 | convolution fusion | flops 233570304 | bytes 1454600 | tf_op jit(solution)/shard_map/dot_general | solution.py:370
  48.4 0.0 collective-permute-start.4
  48.4 1.2 %multiply_reduce_fusion.2 = (f32[]{:T(128)}, f16[384,512]{1,0:T(8,128)(2,1)S(1)}) fusion(f32[]{:T(128)} %bitcast.8, bf16[592,512]{1,0:T(8,128)(2,1)S(1)} %get-tuple-element.16, bf16[592,1536]{1,0:T(8,128)(2,1)S(1)} %copy-done.12, s32[]{:T(128)S(6)} %select_n.68), kind=kOutput, calls=%fused_computation.4 | convolution fusion | flops 233570304 | bytes 1454092 | tf_op jit(solution)/shard_map/dot_general | solution.py:370
  49.6 0.6 collective-permute-start.6
  50.3 1.5 %collective-permute-start.5 = (f32[192,128]{1,0:T(8,128)S(1)}, f32[192,128]{1,0:T(8,128)S(1)}, u32[]{:S(2)}, u32[]{:S(2)}) collective-permute-start(f32[192,128]{1,0:T(8,128)S(1)} %get-tuple-element.18), channel_id=1, source_target_pairs={{0,1},{1,0},{2,3},{3,2},{4,5},{5,4},{6,7},{7,6},{8,9},{9,8},{10,11... | collective-permute-start | bytes 294920 | tf_op jit(solution)/shard_map/ppermute | solution.py:340
  51.7 2.9 %collective-permute-start.7 = (f32[192,128]{1,0:T(8,128)S(1)}, f32[192,128]{1,0:T(8,128)S(1)}, u32[]{:S(2)}, u32[]{:S(2)}) collective-permute-start(f32[192,128]{1,0:T(8,128)S(1)} %get-tuple-element.19), channel_id=1, source_target_pairs={{0,2},{1,3},{2,0},{3,1},{4,6},{5,7},{6,4},{7,5},{8,10},{9,11},{10,... | collective-permute-start | bytes 294920 | tf_op jit(solution)/shard_map/ppermute | solution.py:340
  54.6 1.3 %multiply_reduce_fusion.1 = (f32[]{:T(128)}, f16[384,512]{1,0:T(8,128)(2,1)S(1)}) fusion(f32[]{:T(128)} %bitcast.8, bf16[592,512]{1,0:T(8,128)(2,1)S(1)} %get-tuple-element.16, bf16[592,1536]{1,0:T(8,128)(2,1)S(1)} %copy-done.12, s32[]{:T(128)S(6)} %select_n.69), kind=kOutput, calls=%fused_computation.3 | convolution fusion | flops 233570304 | bytes 1454092 | tf_op jit(solution)/shard_map/dot_general | solution.py:370
  55.9 0.1 collective-permute-start.8
  55.9 0.5 slice.28
  57.1 11.3 %collective-permute-done.5.refs_4_ = f32[192,128]{1,0:T(8,128)S(1)} collective-permute-done((f32[192,128]{1,0:T(8,128)S(1)}, f32[192,128]{1,0:T(8,128)S(1)}, u32[]{:S(2)}, u32[]{:S(2)}) %collective-permute-start.5) | collective-permute-done | bytes 98336 | tf_op jit(solution)/shard_map/ppermute | solution.py:340
  68.4 0.5 slice.26
  69.6 13.9 %collective-permute-done.7.refs_5_ = f32[192,128]{1,0:T(8,128)S(1)} collective-permute-done((f32[192,128]{1,0:T(8,128)S(1)}, f32[192,128]{1,0:T(8,128)S(1)}, u32[]{:S(2)}, u32[]{:S(2)}) %collective-permute-start.7) | collective-permute-done | bytes 98336 | tf_op jit(solution)/shard_map/ppermute | solution.py:340
  83.6 0.5 slice.27
  84.8 1.3 %multiply_reduce_fusion = (f32[]{:T(128)}, f32[384,512]{1,0:T(8,128)S(1)}) fusion(f32[]{:T(128)} %bitcast.9, f16[384,512]{1,0:T(8,128)(2,1)S(1)} %collective-permute-done.4, bf16[592,512]{1,0:T(8,128)(2,1)S(1)} %get-tuple-element.16, bf16[592,1536]{1,0:T(8,128)(2,1)S(1)} %copy-done.12, s32[]{:T(128)S(6)} %select_n.66), kind=kOutput, calls=%fused_computation.2 | convolution fusion | flops 233766912 | bytes 2240524 | tf_op jit(solution)/shard_map/dot_general | solution.py:370
  86.1 1.0 multiply_add_fusion.refs_0_
  87.1 1.0 convert_multiply_fusion.refs_1_
  88.1 5.1 %sums.1 = (f32[384,512]{1,0:T(8,128)}, f32[128,150]{1,0:T(8,128)}, f32[9,512]{1,0:T(8,128)}, f32[32,128]{1,0:T(8,128)}) custom-call(f32[384,512]{1,0:T(8,128)} %multiply_add_fusion.refs_0_, f32[384,512]{1,0:T(8,128)} %convert_multiply_fusion.refs_1_, f32[8,128]{1,0:T(8,128)} %copy-done.1, f32[192,128]{1,0:T(8,128)} %copy-done, f32[192,128]{1,0:T(8,128)} %copy-done.5, ...), custom_call_target="tpu_custom_call" | custom-call | tf_op jit(solution)/shard_map/sums/pallas_call | solution.py:384
  93.2 4.5 %collective-permute-start.10 = (f32[32,128]{1,0:T(8,128)}, f32[32,128]{1,0:T(8,128)S(1)}, u32[]{:S(2)}, u32[]{:S(2)}) collective-permute-start(f32[32,128]{1,0:T(8,128)} %get-tuple-element.25.refs_0_), channel_id=1, source_target_pairs={{0,1},{1,0},{2,3},{3,2},{4,5},{5,4},{6,7},{7,6},{8,9},{9,8},{10,11... | collective-permute-start | bytes 49160 | tf_op jit(solution)/shard_map/ppermute | solution.py:340
  97.7 0.1 collective-permute-start.11
  97.8 2.4 %collective-permute-start.12 = (f32[32,128]{1,0:T(8,128)}, f32[32,128]{1,0:T(8,128)S(1)}, u32[]{:S(2)}, u32[]{:S(2)}) collective-permute-start(f32[32,128]{1,0:T(8,128)} %get-tuple-element.25.refs_0_), channel_id=1, source_target_pairs={{0,3},{1,2},{2,1},{3,0},{4,7},{5,6},{6,5},{7,4},{8,11},{9,10},{10,... | collective-permute-start | bytes 49160 | tf_op jit(solution)/shard_map/ppermute | solution.py:340
  100.1 1.6 %copy.13 = f32[1,128,150]{1,0,2:T(1,128)} copy(f32[1,128,150]{2,1,0:T(8,128)} %bitcast.36) | data formatting | bytes 153600
  101.7 1.4 %copy.12 = f32[1,9,512]{2,0,1:T(1,128)} copy(f32[1,9,512]{2,1,0:T(8,128)} %bitcast.37) | data formatting | bytes 36864
  103.1 0.4 collective-permute-done.12.refs_3_
  103.5 0.2 copy-done.8
  103.7 0.0 copy-done.9
  103.7 0.6 copy-done.10
  104.3 1.5 %norms.1 = f32[2,3]{1,0:T(2,128)} custom-call(f32[32,128]{1,0:T(8,128)} %get-tuple-element.25.refs_0_, f32[32,128]{1,0:T(8,128)} %copy-done.8, f32[32,128]{1,0:T(8,128)} %copy-done.9, f32[32,128]{1,0:T(8,128)} %copy-done.10), custom_call_target="tpu_custom_call" | custom-call | tf_op jit(solution)/shard_map/norms/pallas_call | solution.py:398
  (30 shorter events, 0.1 us)
Async XLA Ops:
  0.6 4.4 %copy-start.2 = (bf16[1,1,592,1536]{3,2,1,0:T(8,128)(2,1)S(1)}, bf16[1,1,592,1536]{3,2,1,0:T(8,128)(2,1)}, u32[]{:S(2)}) copy-start(bf16[1,1,592,1536]{3,2,1,0:T(8,128)(2,1)} %param.7) | copy-start | bytes 5455876
  2.3 2.7 %collective-permute-start = (bf16[592,768]{1,0:T(8,128)(2,1)S(1)}, bf16[592,768]{1,0:T(8,128)(2,1)}, u32[]{:S(2)}, u32[]{:S(2)}) collective-permute-start(bf16[592,768]{1,0:T(8,128)(2,1)S(1)} %broadcast_select_fusion), channel_id=1, source_target_pairs={{0,4},{4,0},{8,12},{12,8},{1,5},{5,1},{9,13},{13,9},{2,6},{6,2},{1... | collective-permute-start | bytes 2727944 | tf_op jit(solution)/shard_map/ppermute | solution.py:32
  3.5 26.2 %copy-start.3 = (bf16[1,512,150]{1,2,0:T(8,128)(2,1)S(1)}, bf16[1,512,150]{1,2,0:T(8,128)(2,1)}, u32[]{:S(2)}) copy-start(bf16[1,512,150]{1,2,0:T(8,128)(2,1)} %param.13) | copy-start | bytes 460804
  3.5 26.3 %copy-start.11 = (s32[1,592]{1,0:T(1,128)S(1)}, s32[1,592]{1,0:T(1,128)}, u32[]{:S(2)}) copy-start(s32[1,592]{1,0:T(1,128)} %param.10) | copy-start | bytes 7108
  3.5 26.3 %copy-start.7 = (f32[1,9,512]{2,0,1:T(1,128)S(1)}, f32[1,9,512]{2,0,1:T(1,128)}, u32[]{:S(2)}) copy-start(f32[1,9,512]{2,0,1:T(1,128)} %param.12) | copy-start | bytes 55300
  5.3 23.4 %collective-permute-start.1 = (bf16[592,768]{1,0:T(8,128)(2,1)S(1)}, bf16[592,768]{1,0:T(8,128)(2,1)S(1)}, u32[]{:S(2)}, u32[]{:S(2)}) collective-permute-start(bf16[592,768]{1,0:T(8,128)(2,1)S(1)} %select_select_fusion.held), channel_id=1, source_target_pairs={{0,8},{8,0},{4,12},{12,4},{1,9},{9,1},{5,13},{13,5},{2,10},{10,2},... | collective-permute-start | bytes 2727944 | tf_op jit(solution)/shard_map/ppermute | solution.py:35
  8.2 22.3 %collective-permute-start.2 = (bf16[592,768]{1,0:T(8,128)(2,1)S(1)}, bf16[592,768]{1,0:T(8,128)(2,1)S(1)}, u32[]{:S(2)}, u32[]{:S(2)}) collective-permute-start(bf16[592,768]{1,0:T(8,128)(2,1)S(1)} %select_select_fusion.held), channel_id=1, source_target_pairs={{0,4},{4,0},{8,12},{12,8},{1,5},{5,1},{9,13},{13,9},{2,6},{6,2},{1... | collective-permute-start | bytes 2727944 | tf_op jit(solution)/shard_map/ppermute | solution.py:37
  28.7 2.6 %collective-permute-start.3 = (bf16[592,768]{1,0:T(8,128)(2,1)S(1)}, bf16[592,768]{1,0:T(8,128)(2,1)}, u32[]{:S(2)}, u32[]{:S(2)}) collective-permute-start(bf16[592,768]{1,0:T(8,128)(2,1)S(1)} %collective-permute-done.1.other), channel_id=1, source_target_pairs={{0,4},{4,0},{8,12},{12,8},{1,5},{5,1},{9,13},{13,9},{2,6},{6,2},{1... | collective-permute-start | bytes 2727944 | tf_op jit(solution)/shard_map/ppermute | solution.py:38
  40.2 9.4 %copy-start = (f32[192,128]{1,0:T(8,128)}, f32[192,128]{1,0:T(8,128)S(1)}, u32[]{:S(2)}) copy-start(f32[192,128]{1,0:T(8,128)S(1)} %get-tuple-element.17.refs_3_) | copy-start | bytes 294916
  40.2 9.4 %copy-start.1 = (f32[8,128]{1,0:T(8,128)}, f32[8,128]{1,0:T(8,128)S(1)}, u32[]{:S(2)}) copy-start(f32[8,128]{1,0:T(8,128)S(1)} %get-tuple-element.21.refs_2_) | copy-start | bytes 12292
  40.2 8.2 %copy-start.12 = (bf16[592,1536]{1,0:T(8,128)(2,1)S(1)}, bf16[592,1536]{1,0:T(8,128)(2,1)}, u32[]{:S(2)}) copy-start(bf16[592,1536]{1,0:T(8,128)(2,1)} %get-tuple-element.15) | copy-start | bytes 5455876
  40.7 15.1 %collective-permute-start.9 = (f32[192,128]{1,0:T(8,128)S(1)}, f32[192,128]{1,0:T(8,128)S(1)}, u32[]{:S(2)}, u32[]{:S(2)}) collective-permute-start(f32[192,128]{1,0:T(8,128)S(1)} %get-tuple-element.20), channel_id=1, source_target_pairs={{0,3},{1,2},{2,1},{3,0},{4,7},{5,6},{6,5},{7,4},{8,11},{9,10},{10,... | collective-permute-start | bytes 294920 | tf_op jit(solution)/shard_map/ppermute | solution.py:340
  48.4 36.4 %collective-permute-start.4 = (f16[384,512]{1,0:T(8,128)(2,1)S(1)}, f16[384,512]{1,0:T(8,128)(2,1)S(1)}, u32[]{:S(2)}, u32[]{:S(2)}) collective-permute-start(f16[384,512]{1,0:T(8,128)(2,1)S(1)} %get-tuple-element.37), channel_id=1, source_target_pairs={{0,1},{1,0},{2,3},{3,2},{4,5},{5,4},{6,7},{7,6},{8,9},{9,8},{10,11... | collective-permute-start | bytes 1179656 | tf_op jit(solution)/shard_map/ppermute | solution.py:340
  49.6 36.5 %collective-permute-start.6 = (f16[384,512]{1,0:T(8,128)(2,1)S(1)}, f16[384,512]{1,0:T(8,128)(2,1)S(1)}, u32[]{:S(2)}, u32[]{:S(2)}) collective-permute-start(f16[384,512]{1,0:T(8,128)(2,1)S(1)} %get-tuple-element.35), channel_id=1, source_target_pairs={{0,2},{1,3},{2,0},{3,1},{4,6},{5,7},{6,4},{7,5},{8,10},{9,11},{10,... | collective-permute-start | bytes 1179656 | tf_op jit(solution)/shard_map/ppermute | solution.py:340
  50.3 18.2 %collective-permute-start.5 = (f32[192,128]{1,0:T(8,128)S(1)}, f32[192,128]{1,0:T(8,128)S(1)}, u32[]{:S(2)}, u32[]{:S(2)}) collective-permute-start(f32[192,128]{1,0:T(8,128)S(1)} %get-tuple-element.18), channel_id=1, source_target_pairs={{0,1},{1,0},{2,3},{3,2},{4,5},{5,4},{6,7},{7,6},{8,9},{9,8},{10,11... | collective-permute-start | bytes 294920 | tf_op jit(solution)/shard_map/ppermute | solution.py:340
  51.7 31.9 %collective-permute-start.7 = (f32[192,128]{1,0:T(8,128)S(1)}, f32[192,128]{1,0:T(8,128)S(1)}, u32[]{:S(2)}, u32[]{:S(2)}) collective-permute-start(f32[192,128]{1,0:T(8,128)S(1)} %get-tuple-element.19), channel_id=1, source_target_pairs={{0,2},{1,3},{2,0},{3,1},{4,6},{5,7},{6,4},{7,5},{8,10},{9,11},{10,... | collective-permute-start | bytes 294920 | tf_op jit(solution)/shard_map/ppermute | solution.py:340
  55.9 31.3 %copy-start.4 = (f32[192,128]{1,0:T(8,128)}, f32[192,128]{1,0:T(8,128)S(1)}, u32[]{:S(2)}) copy-start(f32[192,128]{1,0:T(8,128)S(1)} %collective-permute-done.9.refs_6_) | copy-start | bytes 294916
  55.9 31.3 %collective-permute-start.8 = (f16[384,512]{1,0:T(8,128)(2,1)S(1)}, f16[384,512]{1,0:T(8,128)(2,1)S(1)}, u32[]{:S(2)}, u32[]{:S(2)}) collective-permute-start(f16[384,512]{1,0:T(8,128)(2,1)S(1)} %get-tuple-element.33), channel_id=1, source_target_pairs={{0,3},{1,2},{2,1},{3,0},{4,7},{5,6},{6,5},{7,4},{8,11},{9,10},{10,... | collective-permute-start | bytes 1179656 | tf_op jit(solution)/shard_map/ppermute | solution.py:340
  68.4 18.7 %copy-start.5 = (f32[192,128]{1,0:T(8,128)}, f32[192,128]{1,0:T(8,128)S(1)}, u32[]{:S(2)}) copy-start(f32[192,128]{1,0:T(8,128)S(1)} %collective-permute-done.5.refs_4_) | copy-start | bytes 294916
  83.6 3.6 %copy-start.6 = (f32[192,128]{1,0:T(8,128)}, f32[192,128]{1,0:T(8,128)S(1)}, u32[]{:S(2)}) copy-start(f32[192,128]{1,0:T(8,128)S(1)} %collective-permute-done.7.refs_5_) | copy-start | bytes 294916
  93.2 9.9 %collective-permute-start.10 = (f32[32,128]{1,0:T(8,128)}, f32[32,128]{1,0:T(8,128)S(1)}, u32[]{:S(2)}, u32[]{:S(2)}) collective-permute-start(f32[32,128]{1,0:T(8,128)} %get-tuple-element.25.refs_0_), channel_id=1, source_target_pairs={{0,1},{1,0},{2,3},{3,2},{4,5},{5,4},{6,7},{7,6},{8,9},{9,8},{10,11... | collective-permute-start | bytes 49160 | tf_op jit(solution)/shard_map/ppermute | solution.py:340
  97.7 5.4 %collective-permute-start.11 = (f32[32,128]{1,0:T(8,128)}, f32[32,128]{1,0:T(8,128)S(1)}, u32[]{:S(2)}, u32[]{:S(2)}) collective-permute-start(f32[32,128]{1,0:T(8,128)} %get-tuple-element.25.refs_0_), channel_id=1, source_target_pairs={{0,2},{1,3},{2,0},{3,1},{4,6},{5,7},{6,4},{7,5},{8,10},{9,11},{10,... | collective-permute-start | bytes 49160 | tf_op jit(solution)/shard_map/ppermute | solution.py:340
  97.8 5.7 %collective-permute-start.12 = (f32[32,128]{1,0:T(8,128)}, f32[32,128]{1,0:T(8,128)S(1)}, u32[]{:S(2)}, u32[]{:S(2)}) collective-permute-start(f32[32,128]{1,0:T(8,128)} %get-tuple-element.25.refs_0_), channel_id=1, source_target_pairs={{0,3},{1,2},{2,1},{3,0},{4,7},{5,6},{6,5},{7,4},{8,11},{9,10},{10,... | collective-permute-start | bytes 49160 | tf_op jit(solution)/shard_map/ppermute | solution.py:340
  103.1 0.6 copy-start.8
  103.1 0.6 copy-start.9
  103.7 0.6 copy-start.10

commit v4 on v3

v4 whole, which is shorter than its diff:
```python
import functools
import math

import jax
import jax.numpy as jnp
from jax import lax
from jax.experimental import pallas as pl
from jax.experimental.pallas import tpu as pltpu
from jax.sharding import PartitionSpec as P

PC = 37
LANES = 128
STEP = 32
REACH = 4
OFFSETS = [(a, b) for a in (-1, 0, 1) for b in (-1, 0, 1)]
X_LIMIT = 6.0
ROOM = 16384.0


def pieces(block, axis, size, source):
    if size != 4:
        block = jnp.where(lax.axis_index(axis) == source, block, jnp.zeros_like(block))
        block = lax.psum(block, axis)
        width = block.shape[1] // 2
        low, high = block[:, :width], block[:, width:]
        zero = jnp.int32(0)
        return zero + 1, zero, (low, low, high, high)
    me = lax.axis_index(axis)
    core = me % 2
    mate = [(0, 1), (1, 0), (2, 3), (3, 2)]
    across = [(0, 2), (2, 0), (1, 3), (3, 1)]
    width = block.shape[1] // 2
    low, high = block[:, :width], block[:, width:]
    got = lax.ppermute(jnp.where(core == 0, high, low), axis, mate)
    kept = jnp.where(core == 0, low, high)
    held = jnp.where(source % 2 == core, kept, got)
    other = lax.ppermute(held, axis, across)
    here = ((source // 2) == (me // 2)).astype(jnp.int32)
    back_held = lax.ppermute(held, axis, mate)
    back_other = lax.ppermute(other, axis, mate)
    return here, core, (held, other, back_held, back_other)


def gelu_parts(value):
    inner = 0.7978845608 * (value + 0.044715 * value * value * value)
    tanh_val = jnp.tanh(inner)
    out_val = 0.5 * value * (1.0 + tanh_val)
    slope = 0.5 * (1.0 + tanh_val) + 0.5 * value * (1.0 - tanh_val * tanh_val) * 0.7978845608 * (
        1.0 + 3.0 * 0.044715 * value * value
    )
    return (out_val, slope)


def exponent(size):
    size = jnp.maximum(jnp.full((1, LANES), size, jnp.float32), 1e-30)
    return jnp.clip(jnp.floor(jnp.log(ROOM / size) * (1.0 / math.log(2.0))), -100.0, 100.0)


def head_kernel(
    sizes,
    scalars,
    held,
    other,
    back_held,
    back_other,
    weight_in,
    taps,
    weight_out,
    onehot,
    after,
    before,
    x_out,
    dpre_out,
    gout,
    small,
    first,
    x_vmem,
    pre,
    dys,
    slope,
    hid,
    dlog,
    sem_in,
    sem_out,
):
    rows = x_vmem.shape[0]
    width = x_vmem.shape[1] // 2
    hidden = weight_in.shape[1]
    chunks = hidden // LANES
    guard = REACH * (PC + 1)
    dil, here, core = scalars[0], scalars[1], scalars[2]

    def fetch(source, place, index):
        column = pl.multiple_of(place * width, LANES)
        return pltpu.make_async_copy(source, x_vmem.at[:, pl.ds(column, width)], sem_in.at[index])

    @pl.when(here == 1)
    def _():
        fetch(held, core, 0).start()
        fetch(back_held, 1 - core, 1).start()

    @pl.when(here == 0)
    def _():
        fetch(other, core, 0).start()
        fetch(back_other, 1 - core, 1).start()

    for shift in range(3):
        for c in range(chunks):
            for ref in (pre, dys):
                ref[shift, c, :guard, :] = jnp.zeros((guard, LANES), jnp.float32)
                tail = ref.shape[2] - guard - rows
                ref[shift, c, guard + rows :, :] = jnp.zeros((tail, LANES), jnp.float32)
    fetch(held, core, 0).wait()
    fetch(back_held, 1 - core, 1).wait()
    save = pltpu.make_async_copy(x_vmem, x_out, sem_out)
    save.start()

    masks = (after, None, before)
    for n in range(hidden // 256):
        value = jnp.dot(
            x_vmem[...], weight_in[:, 256 * n : 256 * n + 256], preferred_element_type=jnp.float32
        )
        for h in range(2):
            part = value[:, LANES * h : LANES * h + LANES]
            for shift in range(3):
                mask = (before, None, after)[shift]
                pre[shift, 2 * n + h, guard : guard + rows, :] = (
                    part if mask is None else part * mask[...]
                )

    starts = [dil * (PC * a + b) for a, b in OFFSETS]

    def forward(row, count):
        for c in range(chunks):
            total = None
            for k in range(9):
                term = (
                    pre[k % 3, c, pl.ds(guard + row + starts[k], count), :]
                    * taps[k, :, LANES * c : LANES * c + LANES]
                )
                total = term if total is None else total + term
            act, grad = gelu_parts(total)
            slope[c, pl.ds(row, count), :] = grad
            hid[pl.ds(row, count), LANES * c : LANES * c + LANES] = act.astype(jnp.bfloat16)

    whole = rows // STEP
    left = rows - whole * STEP

    @pl.loop(0, whole)
    def _(i):
        forward(pl.multiple_of(i * STEP, STEP), STEP)

    if left:
        forward(whole * STEP, left)

    logits = lax.dot_general(
        hid[...], weight_out[...], (((1,), (1,)), ((), ())), preferred_element_type=jnp.float32
    )
    lane = lax.broadcasted_iota(jnp.int32, logits.shape, 1)
    logits = jnp.where(lane < sizes.classes, logits, -1e30)
    peak = jnp.max(logits, axis=1, keepdims=True)
    power = jnp.exp(logits - peak)
    prob = power / jnp.sum(power, axis=1, keepdims=True)
    dlog[...] = (prob - onehot[...].astype(jnp.float32)).astype(jnp.bfloat16)

    gout[...] = lax.dot_general(
        dlog[...], hid[...], (((0,), (0,)), ((), ())), preferred_element_type=jnp.float32
    )
    for n in range(hidden // 256):
        value = jnp.dot(
            dlog[...], weight_out[:, 256 * n : 256 * n + 256], preferred_element_type=jnp.float32
        )
        for h in range(2):
            c = 2 * n + h
            part = value[:, LANES * h : LANES * h + LANES] * slope[c]
            for shift in range(3):
                mask = (after, None, before)[shift]
                dys[shift, c, guard : guard + rows, :] = part if mask is None else part * mask[...]

    def fold(value):
        return jnp.sum(value.reshape(-1, 8, LANES), axis=0)

    biggest = jnp.zeros((8, LANES), jnp.float32)
    taps_biggest = jnp.zeros((1, LANES), jnp.float32)
    small[...] = jnp.zeros(small.shape, jnp.float32)
    taps_square = jnp.zeros((1, LANES), jnp.float32)
    for c in range(chunks):
        column = slice(LANES * c, LANES * c + LANES)

        def backward(row, count, carry):
            sums, top = carry
            dy = dys[1, c, pl.ds(guard + row, count), :]
            total = None
            out = []
            for k in range(9):
                out.append(sums[k] + fold(dy * pre[k % 3, c, pl.ds(guard + row + starts[k], count), :]))
                term = (
                    dys[k % 3, c, pl.ds(guard + row - starts[k], count), :] * taps[k, :, column]
                )
                total = term if total is None else total + term
            dpre_out[pl.ds(row, count), column] = total.astype(jnp.bfloat16)
            size = jnp.max(jnp.abs(total).reshape(-1, 8, LANES), axis=0)
            return tuple(out), jnp.maximum(top, size)

        zeros = tuple(jnp.zeros((8, LANES), jnp.float32) for _ in range(9))
        carry = lax.fori_loop(
            0,
            whole,
            lambda i, carry: backward(pl.multiple_of(i * STEP, STEP), STEP, carry),
            (zeros, biggest),
        )
        if left:
            carry = backward(whole * STEP, left, carry)
        sums, biggest = carry
        for k in range(9):
            value = jnp.sum(sums[k], axis=0, keepdims=True)
            taps_square = taps_square + value * value
            taps_biggest = jnp.maximum(taps_biggest, jnp.abs(value))
            small[k : k + 1, column] = value
    powers = (
        exponent(jnp.max(biggest) * (X_LIMIT * rows)),
        exponent(jnp.max(jnp.abs(gout[...]))),
        exponent(jnp.max(taps_biggest)),
    )
    for c in range(chunks):
        for i, power in enumerate(powers):
            small[9 + i : 10 + i, LANES * c : LANES * c + LANES] = power
    small[16:17, :LANES] = taps_square
    small[17:18, :] = jnp.sum(gout[...] * gout[...], axis=0, keepdims=True)
    if first.shape[0] == sizes.message:
        norm = message(sizes, scalars[3], x_vmem, dpre_out, gout, small, first, True)
        small[18:19, :LANES] = norm
    save.wait()


def message(sizes, place, x, dpre, gout, small, out, scaled):
    depth, depth_out = sizes.depth, sizes.depth_out
    column = pl.multiple_of(place * depth, LANES)
    block = lax.dot_general(
        x[:, pl.ds(column, depth)], dpre[...], (((0,), (0,)), ((), ())), preferred_element_type=jnp.float32
    )
    hidden = block.shape[1]
    chunks = hidden // LANES
    norm = jnp.sum(block * block, axis=0, keepdims=True)
    norm = sum(norm[:, LANES * c : LANES * c + LANES] for c in range(chunks))
    factors = [jnp.exp2(small[9 + i : 10 + i, :]) if scaled else 1.0 for i in range(3)]
    out[:depth, :] = block * factors[0]
    out[depth:, :] = jnp.zeros((out.shape[0] - depth, hidden), jnp.float32)
    column = pl.multiple_of(place * depth_out, LANES)
    for start, group in sizes.groups:
        value = gout[start : start + group, pl.ds(column, depth_out)]
        lane = start // sizes.group * LANES
        factor = factors[1][:, :LANES] if scaled else 1.0
        out[depth : depth + group, lane : lane + LANES] = value * factor
    row = depth + sizes.group
    out[row : row + 9, :] = small[0:9, :] * factors[2]
    if scaled:
        out[row + 9 : row + 12, :] = small[9:12, :]
    return norm


class Sizes:
    def __init__(self, wide, hidden, classes, dp):
        self.classes = classes
        self.depth = wide // dp
        self.depth_out = hidden // dp
        self.chunks = hidden // LANES
        self.class_rows = (classes + 7) // 8 * 8
        self.group = (self.class_rows // self.chunks + 7) // 8 * 8
        self.groups = [
            (at, min(self.group, self.class_rows - at)) for at in range(0, self.class_rows, self.group)
        ]
        self.message = self.depth + self.group + 16
        self.staged = dp == 4 and self.depth % LANES == 0 and self.depth_out == LANES


def head_backward(sizes, scalars, halves, onehot, weight_in, taps, weight_out, masks):
    rows = onehot.shape[0]
    wide, hidden = weight_in.shape
    chunks = hidden // LANES
    vmem = pl.BlockSpec(memory_space=pltpu.VMEM)
    anywhere = pl.BlockSpec(memory_space=pl.ANY)
    span = 2 * REACH * (PC + 1) + rows
    return pl.pallas_call(
        functools.partial(head_kernel, sizes),
        out_shape=[
            jax.ShapeDtypeStruct((rows, wide), jnp.bfloat16),
            jax.ShapeDtypeStruct((rows, hidden), jnp.bfloat16),
            jax.ShapeDtypeStruct((256, hidden), jnp.float32),
            jax.ShapeDtypeStruct((24, hidden), jnp.float32),
            jax.ShapeDtypeStruct((sizes.message if sizes.staged else 8, hidden), jnp.float32),
        ],
        in_specs=[pl.BlockSpec(memory_space=pltpu.SMEM)] + [anywhere] * 4 + [vmem] * 6,
        out_specs=[anywhere] + [vmem] * 4,
        scratch_shapes=[
            pltpu.VMEM((rows, wide), jnp.bfloat16),
            pltpu.VMEM((3, chunks, span, LANES), jnp.float32),
            pltpu.VMEM((3, chunks, span, LANES), jnp.float32),
            pltpu.VMEM((chunks, rows, LANES), jnp.float32),
            pltpu.VMEM((rows, hidden), jnp.bfloat16),
            pltpu.VMEM((rows, 256), jnp.bfloat16),
            pltpu.SemaphoreType.DMA((2,)),
            pltpu.SemaphoreType.DMA,
        ],
        compiler_params=pltpu.CompilerParams(vmem_limit_bytes=40 * 1024 * 1024),
        name="head",
    )(scalars, *halves, weight_in, taps, weight_out, onehot, *masks)


def blocks_kernel(sizes, scalars, x, dpre, gout, small, second, third, own, stats):
    norm = message(sizes, scalars[4], x, dpre, gout, small, second, True)
    norm = norm + message(sizes, scalars[5], x, dpre, gout, small, third, True)
    norm = norm + message(sizes, scalars[6], x, dpre, gout, small, own, False)
    stats[...] = jnp.zeros(stats.shape, jnp.float32)
    stats[0:1, :] = norm + small[18:19, :LANES]
    stats[1:2, :] = small[16:17, :LANES]
    for c in range(sizes.chunks):
        stats[2 + c : 3 + c, :] = small[17:18, LANES * c : LANES * c + LANES]


def sum_kernel(sizes, parts, last, stats, share_in, share_out, taps_out, line):
    depth, chunks = sizes.depth, sizes.chunks

    def fold(value):
        value = jnp.sum(value.reshape(-1, 8, value.shape[1]), axis=0)
        return sum(value[:, LANES * c : LANES * c + LANES] for c in range(value.shape[1] // LANES))

    mark = depth + sizes.group
    factors = [jnp.exp2(-last[mark + 9 + i : mark + 10 + i, :]) for i in range(3)]
    total = parts[:depth, :] + last[:depth, :] * factors[0]
    share_in[...] = total
    line[0:8, :] = fold(total * total)
    total = parts[depth:mark, :] + last[depth:mark, :] * factors[1]
    line[8:16, :] = fold(total * total)
    for start, group in sizes.groups:
        lane = start // sizes.group * LANES
        count = min(group, sizes.classes - start)
        share_out[start : start + count, 0, :] = total[:count, lane : lane + LANES]
    total = parts[mark : mark + 9, :] + last[mark : mark + 9, :] * factors[2]
    square = jnp.sum(total * total, axis=0, keepdims=True)
    for k in range(9):
        taps_out[k, :, :] = total[k : k + 1, :]
    line[16:24, :] = stats[...]
    line[24:32, :] = jnp.zeros((8, LANES), jnp.float32)
    line[24:25, :] = sum(square[:, LANES * c : LANES * c + LANES] for c in range(chunks))


def norm_kernel(dp, chunks, *refs):
    lines, out = refs[:dp], refs[dp]
    total = lines[0][...]
    for line in lines[1:]:
        total = total + line[...]
    values = [
        jnp.sum(total[16:17, :]),
        jnp.sum(total[17:18, :]),
        jnp.sum(total[18 : 18 + chunks, :]),
        jnp.sum(total[0:8, :]),
        jnp.sum(lines[0][24:25, :]),
        jnp.sum(total[8:16, :]),
    ]
    row = lax.broadcasted_iota(jnp.int32, (8, LANES), 0)
    lane = lax.broadcasted_iota(jnp.int32, (8, LANES), 1)
    spread = jnp.zeros((8, LANES), jnp.float32)
    for i, value in enumerate(values):
        spread = jnp.where((row == i // 3) & (lane == i % 3), value, spread)
    out[...] = jnp.log(1e-12 + spread)[:2, :3]


def permute(value, pairs):
    return lax.ppermute(value, "dp", pairs)


def by_row(sizes, shape, three):
    row = lax.broadcasted_iota(jnp.int32, shape, 0)
    return jnp.where(
        row < sizes.depth, three[0], jnp.where(row < sizes.depth + sizes.group, three[1], three[2])
    )


def staged_sums(sizes, me, scalars, xrows, dpre, gout, small, first):
    vmem = pl.BlockSpec(memory_space=pltpu.VMEM)
    smem = pl.BlockSpec(memory_space=pltpu.SMEM)
    hidden = dpre.shape[1]
    shape = (sizes.message, hidden)
    full = jax.ShapeDtypeStruct(shape, jnp.float32)
    lines = jax.ShapeDtypeStruct((8, LANES), jnp.float32)
    half = jnp.float16
    near = permute(first.astype(half), [(0, 1), (1, 0), (2, 3), (3, 2)])
    second, third, own, stats = pl.pallas_call(
        functools.partial(blocks_kernel, sizes),
        out_shape=[full, full, full, lines],
        in_specs=[smem] + [vmem] * 4,
        out_specs=[vmem] * 4,
        compiler_params=pltpu.CompilerParams(vmem_limit_bytes=16 * 1024 * 1024),
        name="blocks",
    )(scalars, xrows, dpre, gout, small)
    second = second.astype(half)
    middle = permute(second, [(1, 2), (2, 1)])
    end = (me == 0) | (me == 3)
    mark = sizes.depth + sizes.group + 9
    row = lax.broadcasted_iota(jnp.int32, shape, 0)

    def split(value):
        return [value[mark + i : mark + i + 1] for i in range(3)]

    mine, theirs = split(third), split(near.astype(jnp.float32))
    theirs = [jnp.where(end, a, b) for a, b in zip(mine, theirs)]
    common = [jnp.minimum(a, b) for a, b in zip(mine, theirs)]
    both = third * by_row(sizes, shape, [jnp.exp2(c - a) for a, c in zip(mine, common)])
    both = both + jnp.where(end, 0.0, near.astype(jnp.float32)) * by_row(
        sizes, shape, [jnp.exp2(c - b) for b, c in zip(theirs, common)]
    )
    for i in range(3):
        both = jnp.where(row == mark + i, common[i], both)
    far = permute(both.astype(half), [(0, 2), (2, 0), (1, 3), (3, 1)])
    edge = permute(second, [(0, 1), (3, 2)])

    def decode(value):
        value = value.astype(jnp.float32)
        return value * by_row(sizes, shape, [jnp.exp2(-v) for v in split(value)])

    parts = own + decode(jnp.where(end, near, middle)) + decode(edge)
    return parts, far.astype(jnp.float32), stats


def per_device(sizes, dp, trials, features, owner, dilation_index, labels, input_weight, taps, output_weight):
    here, core, halves = pieces(features[0, 0], "trial", trials, owner[0])
    me = lax.axis_index("dp")
    dil = dilation_index[0] + 1
    rows = features.shape[2]
    onehot = (labels[0][:, None] == jnp.arange(256, dtype=jnp.int32)[None, :]).astype(jnp.bfloat16)
    column = lax.broadcasted_iota(jnp.int32, (rows, LANES), 0) % PC
    before = (column < PC - dil).astype(jnp.float32)
    after = (column >= dil).astype(jnp.float32)
    classes, chunks = sizes.classes, sizes.chunks
    weight_out = jnp.pad(output_weight[0].T, ((0, 256 - classes), (0, 0)))
    high = me >= 2
    odd = me % 2
    to = [3 * (1 - odd), jnp.where(odd == 0, 1, 2), jnp.where(high, me - 2, me + 2), me]
    scalars = jnp.stack([dil, here, core] + to).astype(jnp.int32)
    xrows, dpre, gout, small, first = head_backward(
        sizes,
        scalars,
        halves,
        onehot,
        input_weight[0],
        taps[0][:, None, :],
        weight_out,
        (after, before),
    )
    if not sizes.staged:
        return general_sums(sizes, xrows, dpre, gout, small)
    parts, last, stats = staged_sums(sizes, me, scalars, xrows, dpre, gout, small, first)
    vmem = pl.BlockSpec(memory_space=pltpu.VMEM)
    hidden = dpre.shape[1]
    share_in, share_out, total_taps, line = pl.pallas_call(
        functools.partial(sum_kernel, sizes),
        out_shape=[
            jax.ShapeDtypeStruct((sizes.depth, hidden), jnp.float32),
            jax.ShapeDtypeStruct((classes, 1, sizes.depth_out), jnp.float32),
            jax.ShapeDtypeStruct((9, 1, hidden), jnp.float32),
            jax.ShapeDtypeStruct((32, LANES), jnp.float32),
        ],
        in_specs=[vmem] * 3,
        out_specs=[vmem] * 4,
        compiler_params=pltpu.CompilerParams(vmem_limit_bytes=8 * 1024 * 1024),
        name="sums",
    )(parts, last, stats)
    lines = [line] + [permute(line, [(i, i ^ s) for i in range(dp)]) for s in range(1, dp)]
    norms = pl.pallas_call(
        functools.partial(norm_kernel, dp, chunks),
        out_shape=jax.ShapeDtypeStruct((2, 3), jnp.float32),
        in_specs=[vmem] * dp,
        out_specs=vmem,
        compiler_params=pltpu.CompilerParams(vmem_limit_bytes=4 * 1024 * 1024),
        name="norms",
    )(*lines)
    share_out = jnp.transpose(share_out, (1, 2, 0))
    return (share_in[None], jnp.transpose(total_taps, (1, 0, 2)), share_out, norms[None])


def general_sums(sizes, xrows, dpre, gout, small):
    g_in = jnp.dot(xrows.T, dpre, preferred_element_type=jnp.float32)
    g_out = gout[: sizes.classes].T
    g_taps = small[:9]
    share_in = lax.psum_scatter(g_in, "dp", scatter_dimension=0, tiled=True)
    share_out = lax.psum_scatter(g_out, "dp", scatter_dimension=0, tiled=True)
    local = jnp.stack([jnp.sum(g_in * g_in), jnp.sum(g_taps * g_taps), jnp.sum(g_out * g_out)])
    share_sq = jnp.stack([jnp.sum(share_in * share_in), jnp.sum(share_out * share_out)])
    total_taps, squares, share_total = lax.psum((g_taps, local, share_sq), "dp")
    totals = jnp.stack([share_total[0], jnp.sum(total_taps * total_taps), share_total[1]])
    norms = jnp.log(1e-12 + jnp.stack([squares, totals]))
    return (share_in[None], total_taps[None], share_out[None], norms[None])


def solution(mesh):
    dp, trials = mesh.shape["dp"], mesh.shape["trial"]
    placed = (
        P(("groups", "dp"), "trial", None, None),
        P(("groups", "dp")),
        P("trial"),
        P(("groups", "dp"), None),
        P("trial", None, None),
        P("trial", None, None),
        P("trial", None, None),
    )

    def step(*args):
        (wide, hidden), classes = args[4].shape[1:], args[6].shape[2]
        return per_device(Sizes(wide, hidden, classes, dp), dp, trials, *args)

    return jax.shard_map(
        step,
        mesh=mesh,
        in_specs=placed,
        out_specs=(
            P(("groups", "trial"), "dp", None),
            P(("groups", "trial"), None, None),
            P(("groups", "trial"), "dp", None),
            P(("groups", "trial"), None, None),
        ),
        check_vma=False,
    )
```

time: 106 us -> 93.2 us (0.88)
  matrix products: 6.04 us -> 0 us
  local copies, waits for them, and re-layouts: 6.2 us -> 1.04 us
  waiting for transfers between devices: 47.3 us -> 51.5 us
  starting transfers between devices: 21.5 us -> 18.8 us
  between operations: 4.85 us -> 2.18 us
  Pallas kernels: 15.5 us -> 13.4 us
  other arithmetic: 4.47 us -> 5.9 us
    dot_general x4 -> x0, matrix products: 6.04 us -> none  [per_device(): jnp.dot(lax.dynamic_slice_in_dim(xrows, (me ^ step) * depth, depth, 1).T,...]
    unnamed x30 -> x6, local copies, waits for them, and re-layouts: 4.05 us -> 0.02 us
    ppermute x9 -> x7, waiting for transfers between devices: 25.6 us -> 29 us  [permute(): return lax.ppermute(value, 'dp', pairs)]
    slice x4 -> x0, local copies, waits for them, and re-layouts: 2.11 us -> none  [bound(): return jnp.maximum(pack[mark, 0], 1e-30)]
    convert_element_type x0 -> x6, other arithmetic: none -> 1.66 us  [the longest x1 1.19 us: staged_sums(): far = permute(both.astype(half), [(0, 2), (2, 0), (1, 3), (3, 1)])]
    select_n x1, other arithmetic: 0.2 us -> 1.68 us  [pieces(): held = jnp.where(source % 2 == core, kept, got)]
    pallas_call x2 -> x3, Pallas kernels: 14 us -> 12.7 us  [the longest x1 9.98 us: head_backward(): pl.pallas_call(functools.partial(head_kernel, sizes), out_shape=[jax.Shap...]
    ppermute x9 -> x7, starting transfers between devices: 16.6 us -> 15.4 us  [permute(): return lax.ppermute(value, 'dp', pairs)]
  transfers between devices with their start and end apart: 13 -> 11, of which waited for: 6 -> 9; matrix products, arithmetic and copies ran while one was open for 12% -> 4% of each run, Pallas kernels for 0% -> 0%
where the time goes in v4:
time: 93.2 us; the launch traced here: 92.9 us
  waiting for transfers between devices  51.5 us (55%)
  starting transfers between devices  18.8 us (20%)
  Pallas kernels  13.4 us (14%)
  other arithmetic  5.9 us (6%)
  between operations  2.18 us (2%)
  local copies, waits for them, and re-layouts  1.04 us (1%)
    ppermute x7, waiting for transfers between devices, permute(): return lax.ppermute(value, 'dp', pairs)  29 us
    ppermute x1, waiting for transfers between devices, pieces(): other = lax.ppermute(held, axis, across)  20.6 us
    ppermute x7, starting transfers between devices, permute(): return lax.ppermute(value, 'dp', pairs)  15.4 us
    pallas_call x1, Pallas kernels, head_backward(): pl.pallas_call(functools.partial(head_kernel, sizes), out_shape=[jax.Shap...  9.98 us
    ppermute x1, starting transfers between devices, pieces(): other = lax.ppermute(held, axis, across)  2.92 us
  transfers between devices with their start and end apart: 11, of which 9 were waited for; matrix products, arithmetic and copies ran while one was open for 4% of the time, Pallas kernels for 0%

profile of v4, /device:TPU:0, one launch (start us, length us, event | category | flops | bytes accessed | tf_op | source)
XLA Modules:
  0.0 92.9 jit_solution(10124611110946079289)
XLA Ops:
  0.6 1.5 %broadcast_select_fusion = bf16[592,768]{1,0:T(8,128)(2,1)S(1)} fusion(pred[]{:T(512)S(6)} %eq.64, bf16[592,1536]{1,0:T(8,128)(2,1)} %bitcast.39), kind=kLoop, calls=%fused_computation.1 | loop fusion | flops 454656 | bytes 2727937 | tf_op jit(solution)/shard_map/jit(_where)/select_n | solution.py:34
  2.2 0.5 collective-permute-start
  3.4 0.0 copy-start.2
  3.4 0.0 copy-start
  3.4 0.0 copy-start.1
  3.4 1.4 %collective-permute-done = bf16[592,768]{1,0:T(8,128)(2,1)S(1)} collective-permute-done((bf16[592,768]{1,0:T(8,128)(2,1)S(1)}, bf16[592,768]{1,0:T(8,128)(2,1)S(1)}, u32[]{:S(2)}, u32[]{:S(2)}) %collective-permute-start) | collective-permute-done | bytes 909344 | tf_op jit(solution)/shard_map/ppermute | solution.py:34
  4.8 1.7 %select_select_fusion.held = bf16[592,768]{1,0:T(8,128)(2,1)S(1)} fusion(bf16[592,768]{1,0:T(8,128)(2,1)S(1)} %collective-permute-done, pred[]{:T(512)S(6)} %eq.64, pred[]{:T(512)S(6)} %eq.63, bf16[592,1536]{1,0:T(8,128)(2,1)} %bitcast.40), kind=kLoop, calls=%fused_computation | loop fusion | flops 909312 | bytes 3637250 | tf_op jit(solution)/shard_map/jit(_where)/select_n | solution.py:36
  6.5 2.9 %collective-permute-start.1 = (bf16[592,768]{1,0:T(8,128)(2,1)S(1)}, bf16[592,768]{1,0:T(8,128)(2,1)}, u32[]{:S(2)}, u32[]{:S(2)}) collective-permute-start(bf16[592,768]{1,0:T(8,128)(2,1)S(1)} %select_select_fusion.held), channel_id=1, source_target_pairs={{0,8},{8,0},{4,12},{12,4},{1,9},{9,1},{5,13},{13,5},{2,10},{10,2},... | collective-permute-start | bytes 2727944 | tf_op jit(solution)/shard_map/ppermute | solution.py:37
  9.4 0.0 collective-permute-start.2
  9.4 20.6 %collective-permute-done.1.other = bf16[592,768]{1,0:T(8,128)(2,1)} collective-permute-done((bf16[592,768]{1,0:T(8,128)(2,1)S(1)}, bf16[592,768]{1,0:T(8,128)(2,1)}, u32[]{:S(2)}, u32[]{:S(2)}) %collective-permute-start.1) | collective-permute-done | bytes 909344 | tf_op jit(solution)/shard_map/ppermute | solution.py:37
  30.0 0.0 collective-permute-start.3
  30.6 0.0 copy-done.2
  30.7 0.9 %pad.4.weight_out = bf16[256,512]{1,0:T(8,128)(2,1)S(1)} pad(bf16[150,512]{1,0:T(8,128)(2,1)} %bitcast.41, bf16[]{:T(256)} %constant.72.clone.1), padding=0_106x0_0 | pad | bytes 415746 | tf_op jit(solution)/shard_map/jit(_pad)/pad | solution.py:436
  31.6 0.1 stack.32.scalars
  31.7 0.1 fusion.onehot
  31.9 0.3 fusion.2
  32.2 0.0 collective-permute-done.2.back_held
  32.2 0.6 collective-permute-done.3.back_other
  32.8 0.0 copy-done
  32.8 0.0 copy-done.1
  32.8 10.0 %head.1 = (bf16[592,1536]{1,0:T(8,128)(2,1)S(1)}, bf16[592,512]{1,0:T(8,128)(2,1)S(1)}, f32[256,512]{1,0:T(8,128)S(1)}, f32[24,512]{1,0:T(8,128)S(1)}, f32[440,512]{1,0:T(8,128)S(1)}) custom-call(s32[7]{0:T(128)S(1)} %stack.32.scalars, bf16[592,768]{1,0:T(8,128)(2,1)S(1)} %select_select_fusion.held, bf16[592,768]{1,0:T(8,128)(2,1)} %collective-permute-done.1.other, ...), custom_call_target="tpu_custom_call" | custom-call | tf_op jit(solution)/shard_map/head/pallas_call | solution.py:284
  42.8 1.7 %blocks.1 = (f32[440,512]{1,0:T(8,128)S(1)}, f32[440,512]{1,0:T(8,128)S(1)}, f32[440,512]{1,0:T(8,128)S(1)}, f32[8,128]{1,0:T(8,128)S(1)}) custom-call(s32[7]{0:T(128)S(1)} %stack.32.scalars, bf16[592,1536]{1,0:T(8,128)(2,1)S(1)} %get-tuple-element.17.x, bf16[592,512]{1,0:T(8,128)(2,1)S(1)} %get-tuple-element.18.dpre, ...), custom_call_target="tpu_custom_call" | custom-call | tf_op jit(solution)/shard_map/blocks/pallas_call | solution.py:389
  44.5 0.1 convert_element_type.38
  44.5 1.4 %collective-permute-start.5 = (f16[440,512]{1,0:T(8,128)(2,1)S(1)}, f16[440,512]{1,0:T(8,128)(2,1)}, u32[]{:S(2)}, u32[]{:S(2)}) collective-permute-start(f16[440,512]{1,0:T(8,128)(2,1)S(1)} %convert_element_type.38), channel_id=1, source_target_pairs={{1,2},{2,1},{5,6},{6,5},{9,10},{10,9},{13,14},{14,13},{17,18},{18,... | collective-permute-start | bytes 1351688 | tf_op jit(solution)/shard_map/ppermute | solution.py:370
  46.0 0.1 convert_element_type.37
  46.1 3.9 %collective-permute-start.4 = (f16[440,512]{1,0:T(8,128)(2,1)S(1)}, f16[440,512]{1,0:T(8,128)(2,1)S(1)}, u32[]{:S(2)}, u32[]{:S(2)}) collective-permute-start(f16[440,512]{1,0:T(8,128)(2,1)S(1)} %convert_element_type.37), channel_id=1, source_target_pairs={{0,1},{1,0},{2,3},{3,2},{4,5},{5,4},{6,7},{7,6},{8,9},{9,8},{10,11... | collective-permute-start | bytes 1351688 | tf_op jit(solution)/shard_map/ppermute | solution.py:370
  50.0 2.0 %collective-permute-start.6 = (f16[440,512]{1,0:T(8,128)(2,1)S(1)}, f16[440,512]{1,0:T(8,128)(2,1)S(1)}, u32[]{:S(2)}, u32[]{:S(2)}) collective-permute-start(f16[440,512]{1,0:T(8,128)(2,1)S(1)} %convert_element_type.38), channel_id=1, source_target_pairs={{0,1},{3,2},{4,5},{7,6},{8,9},{11,10},{12,13},{15,14},{16,17},{19,... | collective-permute-start | bytes 1351688 | tf_op jit(solution)/shard_map/ppermute | solution.py:370
  52.0 0.0 collective-permute-done.5
  52.0 8.7 %collective-permute-done.4 = f16[440,512]{1,0:T(8,128)(2,1)S(1)} collective-permute-done((f16[440,512]{1,0:T(8,128)(2,1)S(1)}, f16[440,512]{1,0:T(8,128)(2,1)S(1)}, u32[]{:S(2)}, u32[]{:S(2)}) %collective-permute-start.4) | collective-permute-done | bytes 450592 | tf_op jit(solution)/shard_map/ppermute | solution.py:370
  60.8 0.1 fusion.19
  61.0 1.2 %select_convert_fusion = f16[440,512]{1,0:T(8,128)(2,1)S(1)} fusion(f32[440,512]{1,0:T(8,128)S(1)} %get-tuple-element.24, f32[512]{0:T(512)S(1)} %bitcast.50, f32[512]{0:T(512)S(1)} %bitcast.49, f32[512]{0:T(512)S(1)} %bitcast.48, f32[512]{0:T(512)S(1)} %bitcast.47, f32[512]{0:T(512)S(1)} %bitcast.46, f32[512]{0:T(512)S(1)} %bitcast.45, f32[512]{0:T(512)S(1)} %bitcast.42, ...), kind=kLoop, calls=%fused_computation.2 | loop fusion | flops 2928640 | bytes 1822873 | tf_op jit(solution)/shard_map/convert_element_type | solution.py:415
  62.2 3.7 %collective-permute-start.7 = (f16[440,512]{1,0:T(8,128)(2,1)S(1)}, f16[440,512]{1,0:T(8,128)(2,1)S(1)}, u32[]{:S(2)}, u32[]{:S(2)}) collective-permute-start(f16[440,512]{1,0:T(8,128)(2,1)S(1)} %select_convert_fusion), channel_id=1, source_target_pairs={{0,2},{2,0},{1,3},{3,1},{4,6},{6,4},{5,7},{7,5},{8,10},{10,8},{9,1... | collective-permute-start | bytes 1351688 | tf_op jit(solution)/shard_map/ppermute | solution.py:370
  65.8 4.6 %collective-permute-done.6 = f16[440,512]{1,0:T(8,128)(2,1)S(1)} collective-permute-done((f16[440,512]{1,0:T(8,128)(2,1)S(1)}, f16[440,512]{1,0:T(8,128)(2,1)S(1)}, u32[]{:S(2)}, u32[]{:S(2)}) %collective-permute-start.6) | collective-permute-done | bytes 450592 | tf_op jit(solution)/shard_map/ppermute | solution.py:370
  70.4 0.1 convert_element_type.40
  70.6 0.4 multiply_add_fusion.parts
  71.0 13.2 %collective-permute-done.7 = f16[440,512]{1,0:T(8,128)(2,1)S(1)} collective-permute-done((f16[440,512]{1,0:T(8,128)(2,1)S(1)}, f16[440,512]{1,0:T(8,128)(2,1)S(1)}, u32[]{:S(2)}, u32[]{:S(2)}) %collective-permute-start.7) | collective-permute-done | bytes 450592 | tf_op jit(solution)/shard_map/ppermute | solution.py:370
  84.2 0.1 convert_element_type.43.last
  84.3 1.1 %sums.1 = (f32[384,512]{1,0:T(8,128)}, f32[150,1,128]{2,1,0:T(1,128)}, f32[9,1,512]{2,1,0:T(1,128)}, f32[32,128]{1,0:T(8,128)S(1)}) custom-call(f32[440,512]{1,0:T(8,128)S(1)} %multiply_add_fusion.parts, f32[440,512]{1,0:T(8,128)S(1)} %convert_element_type.43.last, f32[8,128]{1,0:T(8,128)S(1)} %get-tuple-element.25.stats), custom_call_target="tpu_custom_call" | custom-call | tf_op jit(solution)/shard_map/sums/pallas_call | solution.py:456
  85.4 2.2 %collective-permute-start.10 = (f32[32,128]{1,0:T(8,128)S(1)}, f32[32,128]{1,0:T(8,128)S(1)}, u32[]{:S(2)}, u32[]{:S(2)}) collective-permute-start(f32[32,128]{1,0:T(8,128)S(1)} %get-tuple-element.29.refs_0_), channel_id=1, source_target_pairs={{0,3},{1,2},{2,1},{3,0},{4,7},{5,6},{6,5},{7,4},{8,11},{9,10},{10,... | collective-permute-start | bytes 49160 | tf_op jit(solution)/shard_map/ppermute | solution.py:370
  87.6 0.0 collective-permute-start.8
  87.6 2.2 %collective-permute-start.9 = (f32[32,128]{1,0:T(8,128)S(1)}, f32[32,128]{1,0:T(8,128)S(1)}, u32[]{:S(2)}, u32[]{:S(2)}) collective-permute-start(f32[32,128]{1,0:T(8,128)S(1)} %get-tuple-element.29.refs_0_), channel_id=1, source_target_pairs={{0,2},{1,3},{2,0},{3,1},{4,6},{5,7},{6,4},{7,5},{8,10},{9,11},{10,... | collective-permute-start | bytes 49160 | tf_op jit(solution)/shard_map/ppermute | solution.py:370
  89.8 1.1 %collective-permute-done.10.refs_3_ = f32[32,128]{1,0:T(8,128)S(1)} collective-permute-done((f32[32,128]{1,0:T(8,128)S(1)}, f32[32,128]{1,0:T(8,128)S(1)}, u32[]{:S(2)}, u32[]{:S(2)}) %collective-permute-start.10) | collective-permute-done | bytes 16416 | tf_op jit(solution)/shard_map/ppermute | solution.py:370
  90.9 0.4 collective-permute-done.8.refs_1_
  91.3 0.9 collective-permute-done.9.refs_2_
  92.2 0.7 norms.1
  (10 shorter events, 0.2 us)
Async XLA Ops:
  2.2 2.6 %collective-permute-start = (bf16[592,768]{1,0:T(8,128)(2,1)S(1)}, bf16[592,768]{1,0:T(8,128)(2,1)S(1)}, u32[]{:S(2)}, u32[]{:S(2)}) collective-permute-start(bf16[592,768]{1,0:T(8,128)(2,1)S(1)} %broadcast_select_fusion), channel_id=1, source_target_pairs={{0,4},{4,0},{8,12},{12,8},{1,5},{5,1},{9,13},{13,9},{2,6},{6,2},{1... | collective-permute-start | bytes 2727944 | tf_op jit(solution)/shard_map/ppermute | solution.py:34
  3.4 27.3 %copy-start.2 = (s32[1,592]{1,0:T(1,128)S(1)}, s32[1,592]{1,0:T(1,128)}, u32[]{:S(2)}) copy-start(s32[1,592]{1,0:T(1,128)} %param.10) | copy-start | bytes 7108
  3.4 29.4 %copy-start = (bf16[1,1536,512]{2,1,0:T(8,128)(2,1)S(1)}, bf16[1,1536,512]{2,1,0:T(8,128)(2,1)}, u32[]{:S(2)}) copy-start(bf16[1,1536,512]{2,1,0:T(8,128)(2,1)} %param.11) | copy-start | bytes 4718596
  3.4 29.4 %copy-start.1 = (f32[1,9,512]{2,0,1:T(1,128)S(1)}, f32[1,9,512]{2,0,1:T(1,128)}, u32[]{:S(2)}) copy-start(f32[1,9,512]{2,0,1:T(1,128)} %param.12) | copy-start | bytes 55300
  6.5 23.5 %collective-permute-start.1 = (bf16[592,768]{1,0:T(8,128)(2,1)S(1)}, bf16[592,768]{1,0:T(8,128)(2,1)}, u32[]{:S(2)}, u32[]{:S(2)}) collective-permute-start(bf16[592,768]{1,0:T(8,128)(2,1)S(1)} %select_select_fusion.held), channel_id=1, source_target_pairs={{0,8},{8,0},{4,12},{12,4},{1,9},{9,1},{5,13},{13,5},{2,10},{10,2},... | collective-permute-start | bytes 2727944 | tf_op jit(solution)/shard_map/ppermute | solution.py:37
  9.4 22.8 %collective-permute-start.2 = (bf16[592,768]{1,0:T(8,128)(2,1)S(1)}, bf16[592,768]{1,0:T(8,128)(2,1)}, u32[]{:S(2)}, u32[]{:S(2)}) collective-permute-start(bf16[592,768]{1,0:T(8,128)(2,1)S(1)} %select_select_fusion.held), channel_id=1, source_target_pairs={{0,4},{4,0},{8,12},{12,8},{1,5},{5,1},{9,13},{13,9},{2,6},{6,2},{1... | collective-permute-start | bytes 2727944 | tf_op jit(solution)/shard_map/ppermute | solution.py:39
  30.0 2.8 %collective-permute-start.3 = (bf16[592,768]{1,0:T(8,128)(2,1)}, bf16[592,768]{1,0:T(8,128)(2,1)}, u32[]{:S(2)}, u32[]{:S(2)}) collective-permute-start(bf16[592,768]{1,0:T(8,128)(2,1)} %collective-permute-done.1.other), channel_id=1, source_target_pairs={{0,4},{4,0},{8,12},{12,8},{1,5},{5,1},{9,13},{13,9},{2,6},{6,2},{1... | collective-permute-start | bytes 2727944 | tf_op jit(solution)/shard_map/ppermute | solution.py:40
  44.5 7.5 %collective-permute-start.5 = (f16[440,512]{1,0:T(8,128)(2,1)S(1)}, f16[440,512]{1,0:T(8,128)(2,1)}, u32[]{:S(2)}, u32[]{:S(2)}) collective-permute-start(f16[440,512]{1,0:T(8,128)(2,1)S(1)} %convert_element_type.38), channel_id=1, source_target_pairs={{1,2},{2,1},{5,6},{6,5},{9,10},{10,9},{13,14},{14,13},{17,18},{18,... | collective-permute-start | bytes 1351688 | tf_op jit(solution)/shard_map/ppermute | solution.py:370
  46.1 14.7 %collective-permute-start.4 = (f16[440,512]{1,0:T(8,128)(2,1)S(1)}, f16[440,512]{1,0:T(8,128)(2,1)S(1)}, u32[]{:S(2)}, u32[]{:S(2)}) collective-permute-start(f16[440,512]{1,0:T(8,128)(2,1)S(1)} %convert_element_type.37), channel_id=1, source_target_pairs={{0,1},{1,0},{2,3},{3,2},{4,5},{5,4},{6,7},{7,6},{8,9},{9,8},{10,11... | collective-permute-start | bytes 1351688 | tf_op jit(solution)/shard_map/ppermute | solution.py:370
  50.0 20.4 %collective-permute-start.6 = (f16[440,512]{1,0:T(8,128)(2,1)S(1)}, f16[440,512]{1,0:T(8,128)(2,1)S(1)}, u32[]{:S(2)}, u32[]{:S(2)}) collective-permute-start(f16[440,512]{1,0:T(8,128)(2,1)S(1)} %convert_element_type.38), channel_id=1, source_target_pairs={{0,1},{3,2},{4,5},{7,6},{8,9},{11,10},{12,13},{15,14},{16,17},{19,... | collective-permute-start | bytes 1351688 | tf_op jit(solution)/shard_map/ppermute | solution.py:370
  62.2 22.0 %collective-permute-start.7 = (f16[440,512]{1,0:T(8,128)(2,1)S(1)}, f16[440,512]{1,0:T(8,128)(2,1)S(1)}, u32[]{:S(2)}, u32[]{:S(2)}) collective-permute-start(f16[440,512]{1,0:T(8,128)(2,1)S(1)} %select_convert_fusion), channel_id=1, source_target_pairs={{0,2},{2,0},{1,3},{3,1},{4,6},{6,4},{5,7},{7,5},{8,10},{10,8},{9,1... | collective-permute-start | bytes 1351688 | tf_op jit(solution)/shard_map/ppermute | solution.py:370
  85.4 5.5 %collective-permute-start.10 = (f32[32,128]{1,0:T(8,128)S(1)}, f32[32,128]{1,0:T(8,128)S(1)}, u32[]{:S(2)}, u32[]{:S(2)}) collective-permute-start(f32[32,128]{1,0:T(8,128)S(1)} %get-tuple-element.29.refs_0_), channel_id=1, source_target_pairs={{0,3},{1,2},{2,1},{3,0},{4,7},{5,6},{6,5},{7,4},{8,11},{9,10},{10,... | collective-permute-start | bytes 49160 | tf_op jit(solution)/shard_map/ppermute | solution.py:370
  87.6 3.7 %collective-permute-start.8 = (f32[32,128]{1,0:T(8,128)S(1)}, f32[32,128]{1,0:T(8,128)S(1)}, u32[]{:S(2)}, u32[]{:S(2)}) collective-permute-start(f32[32,128]{1,0:T(8,128)S(1)} %get-tuple-element.29.refs_0_), channel_id=1, source_target_pairs={{0,1},{1,0},{2,3},{3,2},{4,5},{5,4},{6,7},{7,6},{8,9},{9,8},{10,11... | collective-permute-start | bytes 49160 | tf_op jit(solution)/shard_map/ppermute | solution.py:370
  87.6 4.6 %collective-permute-start.9 = (f32[32,128]{1,0:T(8,128)S(1)}, f32[32,128]{1,0:T(8,128)S(1)}, u32[]{:S(2)}, u32[]{:S(2)}) collective-permute-start(f32[32,128]{1,0:T(8,128)S(1)} %get-tuple-element.29.refs_0_), channel_id=1, source_target_pairs={{0,2},{1,3},{2,0},{3,1},{4,6},{5,7},{6,4},{7,5},{8,10},{9,11},{10,... | collective-permute-start | bytes 49160 | tf_op jit(solution)/shard_map/ppermute | solution.py:370

commit v5 on v4

--- a/solution.py
+++ b/solution.py
@@ -18,27 +18,92 @@
 
 
 def pieces(block, axis, size, source):
+    width = block.shape[1] // 2
     if size != 4:
         block = jnp.where(lax.axis_index(axis) == source, block, jnp.zeros_like(block))
         block = lax.psum(block, axis)
-        width = block.shape[1] // 2
         low, high = block[:, :width], block[:, width:]
         zero = jnp.int32(0)
-        return zero + 1, zero, (low, low, high, high)
+        return zero + 1, zero, (width,), (low, low, high, high)
     me = lax.axis_index(axis)
     core = me % 2
     mate = [(0, 1), (1, 0), (2, 3), (3, 2)]
     across = [(0, 2), (2, 0), (1, 3), (3, 1)]
-    width = block.shape[1] // 2
-    low, high = block[:, :width], block[:, width:]
-    got = lax.ppermute(jnp.where(core == 0, high, low), axis, mate)
-    kept = jnp.where(core == 0, low, high)
-    held = jnp.where(source % 2 == core, kept, got)
-    other = lax.ppermute(held, axis, across)
     here = ((source // 2) == (me // 2)).astype(jnp.int32)
-    back_held = lax.ppermute(held, axis, mate)
-    back_other = lax.ppermute(other, axis, mate)
-    return here, core, (held, other, back_held, back_other)
+    widths = split_width(width)
+    rows = block.shape[0]
+    switches = jnp.stack([core, (source % 2 == core).astype(jnp.int32)]).astype(jnp.int32)
+    smem = pl.BlockSpec(memory_space=pltpu.SMEM)
+    vmem = pl.BlockSpec(memory_space=pltpu.VMEM)
+    anywhere = pl.BlockSpec(memory_space=pl.ANY)
+    hbm = pl.BlockSpec(memory_space=pltpu.MemorySpace.HBM)
+    sent = pl.pallas_call(
+        give_kernel,
+        out_shape=jax.ShapeDtypeStruct((rows, width), block.dtype),
+        in_specs=[smem, hbm],
+        out_specs=vmem,
+        scratch_shapes=[pltpu.SemaphoreType.DMA],
+        compiler_params=pltpu.CompilerParams(vmem_limit_bytes=4 * 1024 * 1024),
+        name="give",
+    )(switches, block)
+    got = lax.ppermute(sent, axis, mate)
+    held = pl.pallas_call(
+        functools.partial(hold_kernel, widths),
+        out_shape=[jax.ShapeDtypeStruct((rows, piece), block.dtype) for piece in widths],
+        in_specs=[smem, hbm, anywhere],
+        out_specs=[vmem] * len(widths),
+        scratch_shapes=[pltpu.SemaphoreType.DMA((len(widths),))],
+        compiler_params=pltpu.CompilerParams(vmem_limit_bytes=4 * 1024 * 1024),
+        name="hold",
+    )(switches, block, got)
+    values = []
+    for piece in held:
+        other = lax.ppermute(piece, axis, across)
+        back_held = lax.ppermute(piece, axis, mate)
+        back_other = lax.ppermute(other, axis, mate)
+        values += [piece, other, back_held, back_other]
+    return here, core, widths, tuple(values)
+
+
+def give_kernel(switches, block, out, sem):
+    width = out.shape[1]
+    column = pl.multiple_of((1 - switches[0]) * width, LANES)
+    copy = pltpu.make_async_copy(block.at[:, pl.ds(column, width)], out, sem)
+    copy.start()
+    copy.wait()
+
+
+def hold_kernel(widths, switches, block, got, *rest):
+    outs, sem = rest[:-1], rest[-1]
+    width = got.shape[1]
+    column = switches[0] * width
+    starts = [sum(widths[:i]) for i in range(len(widths))]
+
+    def copy(i, own):
+        if own:
+            source = block.at[:, pl.ds(pl.multiple_of(column + starts[i], LANES), widths[i])]
+        else:
+            source = got.at[:, pl.ds(starts[i], widths[i])]
+        return pltpu.make_async_copy(source, outs[i], sem.at[i])
+
+    @pl.when(switches[1] == 1)
+    def _():
+        for i in range(len(widths)):
+            copy(i, True).start()
+
+    @pl.when(switches[1] == 0)
+    def _():
+        for i in range(len(widths)):
+            copy(i, False).start()
+
+    for i in range(len(widths)):
+        copy(i, False).wait()
+
+
+def split_width(width):
+    tiles = width // LANES
+    last = max(tiles // 3, 1)
+    return tuple(LANES * n for n in (tiles - last, last) if n > 0)
 
 
 def gelu_parts(value):
@@ -58,31 +123,14 @@
 
 def head_kernel(
     sizes,
+    widths,
     scalars,
-    held,
-    other,
-    back_held,
-    back_other,
-    weight_in,
-    taps,
-    weight_out,
-    onehot,
-    after,
-    before,
-    x_out,
-    dpre_out,
-    gout,
-    small,
-    first,
-    x_vmem,
-    pre,
-    dys,
-    slope,
-    hid,
-    dlog,
-    sem_in,
-    sem_out,
+    *refs,
 ):
+    halves, refs = refs[: 4 * len(widths)], refs[4 * len(widths) :]
+    weight_in, taps, weight_out, onehot, after, before = refs[:6]
+    x_out, dpre_out, gout, small, first, early = refs[6:12]
+    x_vmem, pre, dys, slope, hid, dlog, sem_in, sem_out = refs[12:]
     rows = x_vmem.shape[0]
     width = x_vmem.shape[1] // 2
     hidden = weight_in.shape[1]
@@ -90,19 +138,23 @@
     guard = REACH * (PC + 1)
     dil, here, core = scalars[0], scalars[1], scalars[2]
 
-    def fetch(source, place, index):
-        column = pl.multiple_of(place * width, LANES)
-        return pltpu.make_async_copy(source, x_vmem.at[:, pl.ds(column, width)], sem_in.at[index])
+    def fetch(kind, index):
+        place = core if kind < 2 else 1 - core
+        column = pl.multiple_of(place * width + sum(widths[:index]), LANES)
+        target = x_vmem.at[:, pl.ds(column, widths[index])]
+        return pltpu.make_async_copy(halves[4 * index + kind], target, sem_in.at[index, kind // 2])
 
     @pl.when(here == 1)
     def _():
-        fetch(held, core, 0).start()
-        fetch(back_held, 1 - core, 1).start()
+        for index in range(len(widths)):
+            fetch(0, index).start()
+            fetch(2, index).start()
 
     @pl.when(here == 0)
     def _():
-        fetch(other, core, 0).start()
-        fetch(back_other, 1 - core, 1).start()
+        for index in range(len(widths)):
+            fetch(1, index).start()
+            fetch(3, index).start()
 
     for shift in range(3):
         for c in range(chunks):
@@ -110,8 +162,9 @@
                 ref[shift, c, :guard, :] = jnp.zeros((guard, LANES), jnp.float32)
                 tail = ref.shape[2] - guard - rows
                 ref[shift, c, guard + rows :, :] = jnp.zeros((tail, LANES), jnp.float32)
-    fetch(held, core, 0).wait()
-    fetch(back_held, 1 - core, 1).wait()
+    for index in range(len(widths)):
+        fetch(0, index).wait()
+        fetch(2, index).wait()
     save = pltpu.make_async_copy(x_vmem, x_out, sem_out)
     save.start()
 
@@ -229,6 +282,7 @@
     small[17:18, :] = jnp.sum(gout[...] * gout[...], axis=0, keepdims=True)
     if first.shape[0] == sizes.message:
         norm = message(sizes, scalars[3], x_vmem, dpre_out, gout, small, first, True)
+        norm = norm + message(sizes, scalars[4], x_vmem, dpre_out, gout, small, early, True)
         small[18:19, :LANES] = norm
     save.wait()
 
@@ -274,7 +328,7 @@
         self.staged = dp == 4 and self.depth % LANES == 0 and self.depth_out == LANES
 
 
-def head_backward(sizes, scalars, halves, onehot, weight_in, taps, weight_out, masks):
+def head_backward(sizes, widths, scalars, halves, onehot, weight_in, taps, weight_out, masks):
     rows = onehot.shape[0]
     wide, hidden = weight_in.shape
     chunks = hidden // LANES
@@ -282,16 +336,16 @@
     anywhere = pl.BlockSpec(memory_space=pl.ANY)
     span = 2 * REACH * (PC + 1) + rows
     return pl.pallas_call(
-        functools.partial(head_kernel, sizes),
+        functools.partial(head_kernel, sizes, widths),
         out_shape=[
             jax.ShapeDtypeStruct((rows, wide), jnp.bfloat16),
             jax.ShapeDtypeStruct((rows, hidden), jnp.bfloat16),
             jax.ShapeDtypeStruct((256, hidden), jnp.float32),
             jax.ShapeDtypeStruct((24, hidden), jnp.float32),
-            jax.ShapeDtypeStruct((sizes.message if sizes.staged else 8, hidden), jnp.float32),
-        ],
-        in_specs=[pl.BlockSpec(memory_space=pltpu.SMEM)] + [anywhere] * 4 + [vmem] * 6,
-        out_specs=[anywhere] + [vmem] * 4,
+        ]
+        + [jax.ShapeDtypeStruct((sizes.message if sizes.staged else 8, hidden), jnp.float32)] * 2,
+        in_specs=[pl.BlockSpec(memory_space=pltpu.SMEM)] + [anywhere] * len(halves) + [vmem] * 6,
+        out_specs=[anywhere] + [vmem] * 5,
         scratch_shapes=[
             pltpu.VMEM((rows, wide), jnp.bfloat16),
             pltpu.VMEM((3, chunks, span, LANES), jnp.float32),
@@ -299,17 +353,16 @@
             pltpu.VMEM((chunks, rows, LANES), jnp.float32),
             pltpu.VMEM((rows, hidden), jnp.bfloat16),
             pltpu.VMEM((rows, 256), jnp.bfloat16),
-            pltpu.SemaphoreType.DMA((2,)),
+            pltpu.SemaphoreType.DMA((len(widths), 2)),
             pltpu.SemaphoreType.DMA,
         ],
-        compiler_params=pltpu.CompilerParams(vmem_limit_bytes=40 * 1024 * 1024),
+        compiler_params=pltpu.CompilerParams(vmem_limit_bytes=30 * 1024 * 1024),
         name="head",
     )(scalars, *halves, weight_in, taps, weight_out, onehot, *masks)
 
 
-def blocks_kernel(sizes, scalars, x, dpre, gout, small, second, third, own, stats):
-    norm = message(sizes, scalars[4], x, dpre, gout, small, second, True)
-    norm = norm + message(sizes, scalars[5], x, dpre, gout, small, third, True)
+def blocks_kernel(sizes, scalars, x, dpre, gout, small, late, own, stats):
+    norm = message(sizes, scalars[5], x, dpre, gout, small, late, True)
     norm = norm + message(sizes, scalars[6], x, dpre, gout, small, own, False)
     stats[...] = jnp.zeros(stats.shape, jnp.float32)
     stats[0:1, :] = norm + small[18:19, :LANES]
@@ -370,6 +423,28 @@
     return lax.ppermute(value, "dp", pairs)
 
 
+def add_kernel(sizes, scalars, mine, theirs, out):
+    depth, group = sizes.depth, sizes.group
+    mark = depth + group
+    end = (scalars[6] == 0) | (scalars[6] == 3)
+
+    @pl.when(end)
+    def _():
+        out[...] = mine[...]
+
+    @pl.when(jnp.logical_not(end))
+    def _():
+        for i, (start, stop) in enumerate(((0, depth), (depth, mark), (mark, mark + 9))):
+            at = mark + 9 + i
+            a, b = mine[at : at + 1, :], theirs[at : at + 1, :]
+            common = jnp.minimum(a, b)
+            out[start:stop, :] = mine[start:stop, :] * jnp.exp2(common - a) + theirs[
+                start:stop, :
+            ] * jnp.exp2(common - b)
+            out[at : at + 1, :] = common
+        out[mark + 12 :, :] = mine[mark + 12 :, :]
+
+
 def by_row(sizes, shape, three):
     row = lax.broadcasted_iota(jnp.int32, shape, 0)
     return jnp.where(
@@ -377,7 +452,7 @@
     )
 
 
-def staged_sums(sizes, me, scalars, xrows, dpre, gout, small, first):
+def staged_sums(sizes, me, scalars, xrows, dpre, gout, small, first, early):
     vmem = pl.BlockSpec(memory_space=pltpu.VMEM)
     smem = pl.BlockSpec(memory_space=pltpu.SMEM)
     hidden = dpre.shape[1]
@@ -386,45 +461,50 @@
     lines = jax.ShapeDtypeStruct((8, LANES), jnp.float32)
     half = jnp.float16
     near = permute(first.astype(half), [(0, 1), (1, 0), (2, 3), (3, 2)])
-    second, third, own, stats = pl.pallas_call(
+    early = early.astype(half)
+    middle = permute(early, [(1, 2), (2, 1)])
+    skip = permute(early, [(0, 2), (3, 1)])
+    late, own, stats = pl.pallas_call(
         functools.partial(blocks_kernel, sizes),
-        out_shape=[full, full, full, lines],
+        out_shape=[full, full, lines],
         in_specs=[smem] + [vmem] * 4,
-        out_specs=[vmem] * 4,
+        out_specs=[vmem] * 3,
         compiler_params=pltpu.CompilerParams(vmem_limit_bytes=16 * 1024 * 1024),
+        cost_estimate=pl.CostEstimate(
+            flops=4 * sizes.depth * dpre.shape[0] * hidden,
+            bytes_accessed=2 * xrows.size + 2 * dpre.size + 8 * sizes.message * hidden,
+            transcendentals=0,
+        ),
         name="blocks",
     )(scalars, xrows, dpre, gout, small)
-    second = second.astype(half)
-    middle = permute(second, [(1, 2), (2, 1)])
     end = (me == 0) | (me == 3)
     mark = sizes.depth + sizes.group + 9
-    row = lax.broadcasted_iota(jnp.int32, shape, 0)
+    both = pl.pallas_call(
+        functools.partial(add_kernel, sizes),
+        out_shape=full,
+        in_specs=[smem, vmem, vmem],
+        out_specs=vmem,
+        compiler_params=pltpu.CompilerParams(vmem_limit_bytes=8 * 1024 * 1024),
+        name="add",
+    )(scalars, late, near.astype(jnp.float32))
+    both = both.astype(half)
+    near, skip, middle, _ = lax.optimization_barrier((near, skip, middle, both))
+    far = permute(both, [(0, 1), (3, 2), (1, 3), (2, 0)])
 
     def split(value):
         return [value[mark + i : mark + i + 1] for i in range(3)]
 
-    mine, theirs = split(third), split(near.astype(jnp.float32))
-    theirs = [jnp.where(end, a, b) for a, b in zip(mine, theirs)]
-    common = [jnp.minimum(a, b) for a, b in zip(mine, theirs)]
-    both = third * by_row(sizes, shape, [jnp.exp2(c - a) for a, c in zip(mine, common)])
-    both = both + jnp.where(end, 0.0, near.astype(jnp.float32)) * by_row(
-        sizes, shape, [jnp.exp2(c - b) for b, c in zip(theirs, common)]
-    )
-    for i in range(3):
-        both = jnp.where(row == mark + i, common[i], both)
-    far = permute(both.astype(half), [(0, 2), (2, 0), (1, 3), (3, 1)])
-    edge = permute(second, [(0, 1), (3, 2)])
 
     def decode(value):
         value = value.astype(jnp.float32)
         return value * by_row(sizes, shape, [jnp.exp2(-v) for v in split(value)])
 
-    parts = own + decode(jnp.where(end, near, middle)) + decode(edge)
+    parts = own + decode(jnp.where(end, near, skip)) + decode(middle)
     return parts, far.astype(jnp.float32), stats
 
 
 def per_device(sizes, dp, trials, features, owner, dilation_index, labels, input_weight, taps, output_weight):
-    here, core, halves = pieces(features[0, 0], "trial", trials, owner[0])
+    here, core, widths, halves = pieces(features[0, 0], "trial", trials, owner[0])
     me = lax.axis_index("dp")
     dil = dilation_index[0] + 1
     rows = features.shape[2]
@@ -436,10 +516,13 @@
     weight_out = jnp.pad(output_weight[0].T, ((0, 256 - classes), (0, 0)))
     high = me >= 2
     odd = me % 2
-    to = [3 * (1 - odd), jnp.where(odd == 0, 1, 2), jnp.where(high, me - 2, me + 2), me]
+    end = (me == 0) | (me == 3)
+    step, jump = jnp.where(odd == 0, 1, 2), jnp.where(high, me - 2, me + 2)
+    to = [3 * (1 - odd), jnp.where(end, jump, step), jnp.where(end, step, jump), me]
     scalars = jnp.stack([dil, here, core] + to).astype(jnp.int32)
-    xrows, dpre, gout, small, first = head_backward(
+    xrows, dpre, gout, small, first, early = head_backward(
         sizes,
+        widths,
         scalars,
         halves,
         onehot,
@@ -450,7 +533,7 @@
     )
     if not sizes.staged:
         return general_sums(sizes, xrows, dpre, gout, small)
-    parts, last, stats = staged_sums(sizes, me, scalars, xrows, dpre, gout, small, first)
+    parts, last, stats = staged_sums(sizes, me, scalars, xrows, dpre, gout, small, first, early)
     vmem = pl.BlockSpec(memory_space=pltpu.VMEM)
     hidden = dpre.shape[1]
     share_in, share_out, total_taps, line = pl.pallas_call(

time: 93.2 us -> 90.7 us (0.973)
  other arithmetic: 5.9 us -> 1.66 us
  Pallas kernels: 13.4 us -> 15.2 us
    select_n x2 -> x0, other arithmetic: 3.23 us -> none  [the longest x1 1.68 us: pieces(): held = jnp.where(source % 2 == core, kept, got)]
    pallas_call x1 -> x4, Pallas kernels: 9.98 us -> 12 us  [the longest x1 10.1 us: head_backward(): pl.pallas_call(functools.partial(head_kernel, sizes, widths), out_shape=[...]
    ppermute x7, starting transfers between devices: 15.4 us -> 13.7 us  [permute(): return lax.ppermute(value, 'dp', pairs)]
    unnamed x6 -> x10, local copies, waits for them, and re-layouts: 0.02 us -> 1.52 us
    convert_element_type x3, other arithmetic: 1.39 us -> 0.23 us  [the longest x1 0.1 us: staged_sums(): near.astype(jnp.float32)]
    ppermute x3 -> x5, waiting for transfers between devices: 22 us -> 20.9 us  [the longest x2 18.8 us: pieces(): other = lax.ppermute(piece, axis, across)]
    ppermute x3 -> x5, starting transfers between devices: 3.44 us -> 4.17 us  [the longest x2 3.15 us: pieces(): other = lax.ppermute(piece, axis, across)]
  transfers between devices with their start and end apart: 11 -> 14, of which waited for: 9 -> 9; matrix products, arithmetic and copies ran while one was open for 4% -> 2% of each run, Pallas kernels for 0% -> 2%
where the time goes in v5:
time: 90.7 us; the launch traced here: 90.6 us
  waiting for transfers between devices  52 us (57%)
  starting transfers between devices  17.9 us (20%)
  Pallas kernels  15.2 us (17%)
  between operations  2.28 us (3%)
  other arithmetic  1.66 us (2%)
  local copies, waits for them, and re-layouts  1.63 us (2%)
    ppermute x7, waiting for transfers between devices, permute(): return lax.ppermute(value, 'dp', pairs)  29.6 us
    ppermute x2, waiting for transfers between devices, pieces(): other = lax.ppermute(piece, axis, across)  18.8 us
    ppermute x7, starting transfers between devices, permute(): return lax.ppermute(value, 'dp', pairs)  13.7 us
    pallas_call x1, Pallas kernels, head_backward(): pl.pallas_call(functools.partial(head_kernel, sizes, widths), out_shape=[...  10.1 us
    ppermute x2, starting transfers between devices, pieces(): other = lax.ppermute(piece, axis, across)  3.15 us
    ppermute x1, waiting for transfers between devices, pieces(): got = lax.ppermute(sent, axis, mate)  2.09 us
  transfers between devices with their start and end apart: 14, of which 9 were waited for; matrix products, arithmetic and copies ran while one was open for 2% of the time, Pallas kernels for 2%

profile of v5, /device:TPU:0, one launch (start us, length us, event | category | flops | bytes accessed | tf_op | source)
XLA Modules:
  0.0 90.6 jit_solution(12293679239255822854)
XLA Ops:
  1.3 0.1 pad_add_fusion.switches
  1.4 1.5 %copy-done = bf16[1,1,592,1536]{3,2,1,0:T(8,128)(2,1)S(1)} copy-done((bf16[1,1,592,1536]{3,2,1,0:T(8,128)(2,1)S(1)}, bf16[1,1,592,1536]{3,2,1,0:T(8,128)(2,1)}, u32[]{:S(2)}) %copy-start) | copy-done | bytes 1818648
  2.9 0.6 give.1
  3.5 0.0 copy-start.4
  3.5 0.0 copy-start.3
  3.5 0.0 copy-start.1
  3.5 0.0 copy-start.2
  3.6 0.5 collective-permute-start
  4.1 2.1 %collective-permute-done.got = bf16[592,768]{1,0:T(8,128)(2,1)S(1)} collective-permute-done((bf16[592,768]{1,0:T(8,128)(2,1)S(1)}, bf16[592,768]{1,0:T(8,128)(2,1)S(1)}, u32[]{:S(2)}, u32[]{:S(2)}) %collective-permute-start) | collective-permute-done | bytes 909344 | tf_op jit(solution)/shard_map/ppermute | solution.py:49
  6.2 0.6 hold.1
  6.8 2.9 %collective-permute-start.1 = (bf16[592,512]{1,0:T(8,128)(2,1)S(1)}, bf16[592,512]{1,0:T(8,128)(2,1)S(1)}, u32[]{:S(2)}, u32[]{:S(2)}) collective-permute-start(bf16[592,512]{1,0:T(8,128)(2,1)S(1)} %get-tuple-element.22.refs_0_), channel_id=1, source_target_pairs={{0,8},{8,0},{4,12},{12,4},{1,9},{9,1},{5,13},{13,5},{2,10},{10,2},... | collective-permute-start | bytes 1818632 | tf_op jit(solution)/shard_map/ppermute | solution.py:61
  9.7 0.0 collective-permute-start.2
  9.7 0.2 collective-permute-start.4
  10.0 14.2 %collective-permute-done.1.refs_1_ = bf16[592,512]{1,0:T(8,128)(2,1)S(1)} collective-permute-done((bf16[592,512]{1,0:T(8,128)(2,1)S(1)}, bf16[592,512]{1,0:T(8,128)(2,1)S(1)}, u32[]{:S(2)}, u32[]{:S(2)}) %collective-permute-start.1) | collective-permute-done | bytes 606240 | tf_op jit(solution)/shard_map/ppermute | solution.py:61
  24.2 0.0 collective-permute-start.3
  25.0 0.1 stack.42.scalars
  25.1 0.1 fusion.refs_11_
  25.3 0.5 collective-permute-start.5
  25.8 4.6 %collective-permute-done.4.refs_5_ = bf16[592,256]{1,0:T(8,128)(2,1)} collective-permute-done((bf16[592,256]{1,0:T(8,128)(2,1)S(1)}, bf16[592,256]{1,0:T(8,128)(2,1)}, u32[]{:S(2)}, u32[]{:S(2)}) %collective-permute-start.4) | collective-permute-done | bytes 303136 | tf_op jit(solution)/shard_map/ppermute | solution.py:61
  30.3 0.0 collective-permute-start.6
  30.3 0.3 fusion.2
  30.7 0.0 collective-permute-done.2.refs_2_
  30.7 1.5 %collective-permute-done.6.refs_7_ = bf16[592,256]{1,0:T(8,128)(2,1)S(1)} collective-permute-done((bf16[592,256]{1,0:T(8,128)(2,1)}, bf16[592,256]{1,0:T(8,128)(2,1)S(1)}, u32[]{:S(2)}, u32[]{:S(2)}) %collective-permute-start.6) | collective-permute-done | bytes 303136 | tf_op jit(solution)/shard_map/ppermute | solution.py:63
  32.1 10.1 %head.1 = (bf16[592,1536]{1,0:T(8,128)(2,1)S(1)}, bf16[592,512]{1,0:T(8,128)(2,1)S(1)}, f32[256,512]{1,0:T(8,128)S(1)}, f32[24,512]{1,0:T(8,128)S(1)}, f32[440,512]{1,0:T(8,128)S(1)}, /*index=5*/f32[440,512]{1,0:T(8,128)S(1)}) custom-call(s32[7]{0:T(128)S(1)} %stack.42.scalars, bf16[592,512]{1,0:T(8,128)(2,1)S(1)} %get-tuple-element.22.refs_0_, ...), custom_call_target="tpu_custom_call" | custom-call | tf_op jit(solution)/shard_map/head/pallas_call | solution.py:338
  42.3 0.1 convert_element_type.37
  42.4 1.9 %collective-permute-start.7 = (f16[440,512]{1,0:T(8,128)(2,1)S(1)}, f16[440,512]{1,0:T(8,128)(2,1)S(1)}, u32[]{:S(2)}, u32[]{:S(2)}) collective-permute-start(f16[440,512]{1,0:T(8,128)(2,1)S(1)} %convert_element_type.37), channel_id=1, source_target_pairs={{0,1},{1,0},{2,3},{3,2},{4,5},{5,4},{6,7},{7,6},{8,9},{9,8},{10,11... | collective-permute-start | bytes 1351688 | tf_op jit(solution)/shard_map/ppermute | solution.py:423
  44.2 0.1 convert_element_type.38
  44.3 4.4 %collective-permute-start.8 = (f16[440,512]{1,0:T(8,128)(2,1)S(1)}, f16[440,512]{1,0:T(8,128)(2,1)S(1)}, u32[]{:S(2)}, u32[]{:S(2)}) collective-permute-start(f16[440,512]{1,0:T(8,128)(2,1)S(1)} %convert_element_type.38), channel_id=1, source_target_pairs={{0,2},{3,1},{4,6},{7,5},{8,10},{11,9},{12,14},{15,13},{16,18},{19,... | collective-permute-start | bytes 1351688 | tf_op jit(solution)/shard_map/ppermute | solution.py:423
  48.8 0.7 collective-permute-start.9
  49.5 1.4 %blocks.1 = (f32[440,512]{1,0:T(8,128)S(1)}, f32[440,512]{1,0:T(8,128)S(1)}, f32[8,128]{1,0:T(8,128)S(1)}) custom-call(s32[7]{0:T(128)S(1)} %stack.42.scalars, bf16[592,1536]{1,0:T(8,128)(2,1)S(1)} %get-tuple-element.24.x, bf16[592,512]{1,0:T(8,128)(2,1)S(1)} %get-tuple-element.25.dpre, f32[256,512]{1,0:T(8,128)S(1)} %get-tuple-element.26.gout, ...), custom_call_target="tpu_custom_call" | custom-call | flops 465567744 | bytes 4227072 | tf_op jit(solution)/shard_map/blocks/pallas_call | solution.py:467
  50.9 4.3 %collective-permute-done.7 = f16[440,512]{1,0:T(8,128)(2,1)S(1)} collective-permute-done((f16[440,512]{1,0:T(8,128)(2,1)S(1)}, f16[440,512]{1,0:T(8,128)(2,1)S(1)}, u32[]{:S(2)}, u32[]{:S(2)}) %collective-permute-start.7) | collective-permute-done | bytes 450592 | tf_op jit(solution)/shard_map/ppermute | solution.py:423
  55.2 0.1 convert_element_type.39.theirs
  55.3 0.6 add.55
  55.9 0.1 convert_element_type.40
  56.0 2.3 %collective-permute-start.10 = (f16[440,512]{1,0:T(8,128)(2,1)S(1)}, f16[440,512]{1,0:T(8,128)(2,1)S(1)}, u32[]{:S(2)}, u32[]{:S(2)}) collective-permute-start(f16[440,512]{1,0:T(8,128)(2,1)S(1)} %convert_element_type.40), channel_id=1, source_target_pairs={{0,1},{3,2},{1,3},{2,0},{4,5},{7,6},{5,7},{6,4},{8,9},{11,10},{9,1... | collective-permute-start | bytes 1351688 | tf_op jit(solution)/shard_map/ppermute | solution.py:423
  58.3 6.3 %collective-permute-done.8 = f16[440,512]{1,0:T(8,128)(2,1)S(1)} collective-permute-done((f16[440,512]{1,0:T(8,128)(2,1)S(1)}, f16[440,512]{1,0:T(8,128)(2,1)S(1)}, u32[]{:S(2)}, u32[]{:S(2)}) %collective-permute-start.8) | collective-permute-done | bytes 450592 | tf_op jit(solution)/shard_map/ppermute | solution.py:423
  64.6 0.0 collective-permute-done.9
  64.6 0.1 select_convert_fusion
  64.8 0.1 convert_element_type.42
  64.9 0.4 multiply_add_fusion.parts
  65.4 14.6 %collective-permute-done.10 = f16[440,512]{1,0:T(8,128)(2,1)S(1)} collective-permute-done((f16[440,512]{1,0:T(8,128)(2,1)S(1)}, f16[440,512]{1,0:T(8,128)(2,1)S(1)}, u32[]{:S(2)}, u32[]{:S(2)}) %collective-permute-start.10) | collective-permute-done | bytes 450592 | tf_op jit(solution)/shard_map/ppermute | solution.py:423
  80.0 0.1 convert_element_type.43.last
  80.1 1.1 %sums.1 = (f32[384,512]{1,0:T(8,128)}, f32[150,1,128]{2,1,0:T(1,128)}, f32[9,1,512]{2,1,0:T(1,128)}, f32[32,128]{1,0:T(8,128)S(1)}) custom-call(f32[440,512]{1,0:T(8,128)S(1)} %multiply_add_fusion.parts, f32[440,512]{1,0:T(8,128)S(1)} %convert_element_type.43.last, f32[8,128]{1,0:T(8,128)S(1)} %get-tuple-element.35.stats), custom_call_target="tpu_custom_call" | custom-call | tf_op jit(solution)/shard_map/sums/pallas_call | solution.py:539
  81.2 3.2 %collective-permute-start.12 = (f32[32,128]{1,0:T(8,128)S(1)}, f32[32,128]{1,0:T(8,128)S(1)}, u32[]{:S(2)}, u32[]{:S(2)}) collective-permute-start(f32[32,128]{1,0:T(8,128)S(1)} %get-tuple-element.39.refs_0_), channel_id=1, source_target_pairs={{0,2},{1,3},{2,0},{3,1},{4,6},{5,7},{6,4},{7,5},{8,10},{9,11},{10,... | collective-permute-start | bytes 49160 | tf_op jit(solution)/shard_map/ppermute | solution.py:423
  84.4 1.2 %collective-permute-start.13 = (f32[32,128]{1,0:T(8,128)S(1)}, f32[32,128]{1,0:T(8,128)S(1)}, u32[]{:S(2)}, u32[]{:S(2)}) collective-permute-start(f32[32,128]{1,0:T(8,128)S(1)} %get-tuple-element.39.refs_0_), channel_id=1, source_target_pairs={{0,3},{1,2},{2,1},{3,0},{4,7},{5,6},{6,5},{7,4},{8,11},{9,10},{10,... | collective-permute-start | bytes 49160 | tf_op jit(solution)/shard_map/ppermute | solution.py:423
  85.6 0.5 collective-permute-done.12.refs_2_
  86.1 3.8 %collective-permute-done.13.refs_3_ = f32[32,128]{1,0:T(8,128)S(1)} collective-permute-done((f32[32,128]{1,0:T(8,128)S(1)}, f32[32,128]{1,0:T(8,128)S(1)}, u32[]{:S(2)}, u32[]{:S(2)}) %collective-permute-start.13) | collective-permute-done | bytes 16416 | tf_op jit(solution)/shard_map/ppermute | solution.py:423
  89.9 0.7 norms.1
  (16 shorter events, 0.1 us)
Async XLA Ops:
  1.4 1.5 %copy-start = (bf16[1,1,592,1536]{3,2,1,0:T(8,128)(2,1)S(1)}, bf16[1,1,592,1536]{3,2,1,0:T(8,128)(2,1)}, u32[]{:S(2)}) copy-start(bf16[1,1,592,1536]{3,2,1,0:T(8,128)(2,1)} %param.7) | copy-start | bytes 5455876
  3.5 21.4 %copy-start.4 = (s32[1,592]{1,0:T(1,128)S(1)}, s32[1,592]{1,0:T(1,128)}, u32[]{:S(2)}) copy-start(s32[1,592]{1,0:T(1,128)} %param.10) | copy-start | bytes 7108
  3.5 21.5 %copy-start.3 = (bf16[1,512,150]{1,2,0:T(8,128)(2,1)S(1)}, bf16[1,512,150]{1,2,0:T(8,128)(2,1)}, u32[]{:S(2)}) copy-start(bf16[1,512,150]{1,2,0:T(8,128)(2,1)} %param.13) | copy-start | bytes 460804
  3.5 28.6 %copy-start.1 = (bf16[1,1536,512]{2,1,0:T(8,128)(2,1)S(1)}, bf16[1,1536,512]{2,1,0:T(8,128)(2,1)}, u32[]{:S(2)}) copy-start(bf16[1,1536,512]{2,1,0:T(8,128)(2,1)} %param.11) | copy-start | bytes 4718596
  3.5 28.6 %copy-start.2 = (f32[1,9,512]{2,0,1:T(1,128)S(1)}, f32[1,9,512]{2,0,1:T(1,128)}, u32[]{:S(2)}) copy-start(f32[1,9,512]{2,0,1:T(1,128)} %param.12) | copy-start | bytes 55300
  3.6 2.6 %collective-permute-start = (bf16[592,768]{1,0:T(8,128)(2,1)S(1)}, bf16[592,768]{1,0:T(8,128)(2,1)S(1)}, u32[]{:S(2)}, u32[]{:S(2)}) collective-permute-start(bf16[592,768]{1,0:T(8,128)(2,1)S(1)} %give.1), channel_id=1, source_target_pairs={{0,4},{4,0},{8,12},{12,8},{1,5},{5,1},{9,13},{13,9},{2,6},{6,2},{1... | collective-permute-start | bytes 2727944 | tf_op jit(solution)/shard_map/ppermute | solution.py:49
  6.8 17.4 %collective-permute-start.1 = (bf16[592,512]{1,0:T(8,128)(2,1)S(1)}, bf16[592,512]{1,0:T(8,128)(2,1)S(1)}, u32[]{:S(2)}, u32[]{:S(2)}) collective-permute-start(bf16[592,512]{1,0:T(8,128)(2,1)S(1)} %get-tuple-element.22.refs_0_), channel_id=1, source_target_pairs={{0,8},{8,0},{4,12},{12,4},{1,9},{9,1},{5,13},{13,5},{2,10},{10,2},... | collective-permute-start | bytes 1818632 | tf_op jit(solution)/shard_map/ppermute | solution.py:61
  9.7 20.9 %collective-permute-start.2 = (bf16[592,512]{1,0:T(8,128)(2,1)S(1)}, bf16[592,512]{1,0:T(8,128)(2,1)}, u32[]{:S(2)}, u32[]{:S(2)}) collective-permute-start(bf16[592,512]{1,0:T(8,128)(2,1)S(1)} %get-tuple-element.22.refs_0_), channel_id=1, source_target_pairs={{0,4},{4,0},{8,12},{12,8},{1,5},{5,1},{9,13},{13,9},{2,6},{6,2},{1... | collective-permute-start | bytes 1818632 | tf_op jit(solution)/shard_map/ppermute | solution.py:62
  9.7 20.6 %collective-permute-start.4 = (bf16[592,256]{1,0:T(8,128)(2,1)S(1)}, bf16[592,256]{1,0:T(8,128)(2,1)}, u32[]{:S(2)}, u32[]{:S(2)}) collective-permute-start(bf16[592,256]{1,0:T(8,128)(2,1)S(1)} %get-tuple-element.23.refs_4_), channel_id=1, source_target_pairs={{0,8},{8,0},{4,12},{12,4},{1,9},{9,1},{5,13},{13,5},{2,10},{10,2},... | collective-permute-start | bytes 909320 | tf_op jit(solution)/shard_map/ppermute | solution.py:61
  24.2 7.9 %collective-permute-start.3 = (bf16[592,512]{1,0:T(8,128)(2,1)S(1)}, bf16[592,512]{1,0:T(8,128)(2,1)}, u32[]{:S(2)}, u32[]{:S(2)}) collective-permute-start(bf16[592,512]{1,0:T(8,128)(2,1)S(1)} %collective-permute-done.1.refs_1_), channel_id=1, source_target_pairs={{0,4},{4,0},{8,12},{12,8},{1,5},{5,1},{9,13},{13,9},{2,6},{6,2},{1... | collective-permute-start | bytes 1818632 | tf_op jit(solution)/shard_map/ppermute | solution.py:63
  25.3 5.4 %collective-permute-start.5 = (bf16[592,256]{1,0:T(8,128)(2,1)S(1)}, bf16[592,256]{1,0:T(8,128)(2,1)S(1)}, u32[]{:S(2)}, u32[]{:S(2)}) collective-permute-start(bf16[592,256]{1,0:T(8,128)(2,1)S(1)} %get-tuple-element.23.refs_4_), channel_id=1, source_target_pairs={{0,4},{4,0},{8,12},{12,8},{1,5},{5,1},{9,13},{13,9},{2,6},{6,2},{1... | collective-permute-start | bytes 909320 | tf_op jit(solution)/shard_map/ppermute | solution.py:62
  30.3 1.8 %collective-permute-start.6 = (bf16[592,256]{1,0:T(8,128)(2,1)}, bf16[592,256]{1,0:T(8,128)(2,1)S(1)}, u32[]{:S(2)}, u32[]{:S(2)}) collective-permute-start(bf16[592,256]{1,0:T(8,128)(2,1)} %collective-permute-done.4.refs_5_), channel_id=1, source_target_pairs={{0,4},{4,0},{8,12},{12,8},{1,5},{5,1},{9,13},{13,9},{2,6},{6,2},{1... | collective-permute-start | bytes 909320 | tf_op jit(solution)/shard_map/ppermute | solution.py:63
  42.4 12.8 %collective-permute-start.7 = (f16[440,512]{1,0:T(8,128)(2,1)S(1)}, f16[440,512]{1,0:T(8,128)(2,1)S(1)}, u32[]{:S(2)}, u32[]{:S(2)}) collective-permute-start(f16[440,512]{1,0:T(8,128)(2,1)S(1)} %convert_element_type.37), channel_id=1, source_target_pairs={{0,1},{1,0},{2,3},{3,2},{4,5},{5,4},{6,7},{7,6},{8,9},{9,8},{10,11... | collective-permute-start | bytes 1351688 | tf_op jit(solution)/shard_map/ppermute | solution.py:423
  44.3 20.3 %collective-permute-start.8 = (f16[440,512]{1,0:T(8,128)(2,1)S(1)}, f16[440,512]{1,0:T(8,128)(2,1)S(1)}, u32[]{:S(2)}, u32[]{:S(2)}) collective-permute-start(f16[440,512]{1,0:T(8,128)(2,1)S(1)} %convert_element_type.38), channel_id=1, source_target_pairs={{0,2},{3,1},{4,6},{7,5},{8,10},{11,9},{12,14},{15,13},{16,18},{19,... | collective-permute-start | bytes 1351688 | tf_op jit(solution)/shard_map/ppermute | solution.py:423
  48.8 15.9 %collective-permute-start.9 = (f16[440,512]{1,0:T(8,128)(2,1)S(1)}, f16[440,512]{1,0:T(8,128)(2,1)S(1)}, u32[]{:S(2)}, u32[]{:S(2)}) collective-permute-start(f16[440,512]{1,0:T(8,128)(2,1)S(1)} %convert_element_type.38), channel_id=1, source_target_pairs={{1,2},{2,1},{5,6},{6,5},{9,10},{10,9},{13,14},{14,13},{17,18},{18,... | collective-permute-start | bytes 1351688 | tf_op jit(solution)/shard_map/ppermute | solution.py:423
  56.0 24.0 %collective-permute-start.10 = (f16[440,512]{1,0:T(8,128)(2,1)S(1)}, f16[440,512]{1,0:T(8,128)(2,1)S(1)}, u32[]{:S(2)}, u32[]{:S(2)}) collective-permute-start(f16[440,512]{1,0:T(8,128)(2,1)S(1)} %convert_element_type.40), channel_id=1, source_target_pairs={{0,1},{3,2},{1,3},{2,0},{4,5},{7,6},{5,7},{6,4},{8,9},{11,10},{9,1... | collective-permute-start | bytes 1351688 | tf_op jit(solution)/shard_map/ppermute | solution.py:423
  81.2 4.4 %collective-permute-start.11 = (f32[32,128]{1,0:T(8,128)S(1)}, f32[32,128]{1,0:T(8,128)S(1)}, u32[]{:S(2)}, u32[]{:S(2)}) collective-permute-start(f32[32,128]{1,0:T(8,128)S(1)} %get-tuple-element.39.refs_0_), channel_id=1, source_target_pairs={{0,1},{1,0},{2,3},{3,2},{4,5},{5,4},{6,7},{7,6},{8,9},{9,8},{10,11... | collective-permute-start | bytes 49160 | tf_op jit(solution)/shard_map/ppermute | solution.py:423
  81.2 4.9 %collective-permute-start.12 = (f32[32,128]{1,0:T(8,128)S(1)}, f32[32,128]{1,0:T(8,128)S(1)}, u32[]{:S(2)}, u32[]{:S(2)}) collective-permute-start(f32[32,128]{1,0:T(8,128)S(1)} %get-tuple-element.39.refs_0_), channel_id=1, source_target_pairs={{0,2},{1,3},{2,0},{3,1},{4,6},{5,7},{6,4},{7,5},{8,10},{9,11},{10,... | collective-permute-start | bytes 49160 | tf_op jit(solution)/shard_map/ppermute | solution.py:423
  84.4 5.5 %collective-permute-start.13 = (f32[32,128]{1,0:T(8,128)S(1)}, f32[32,128]{1,0:T(8,128)S(1)}, u32[]{:S(2)}, u32[]{:S(2)}) collective-permute-start(f32[32,128]{1,0:T(8,128)S(1)} %get-tuple-element.39.refs_0_), channel_id=1, source_target_pairs={{0,3},{1,2},{2,1},{3,0},{4,7},{5,6},{6,5},{7,4},{8,11},{9,10},{10,... | collective-permute-start | bytes 49160 | tf_op jit(solution)/shard_map/ppermute | solution.py:423

commit v6 on v5

--- a/solution.py
+++ b/solution.py
@@ -43,7 +43,7 @@
         in_specs=[smem, hbm],
         out_specs=vmem,
         scratch_shapes=[pltpu.SemaphoreType.DMA],
-        compiler_params=pltpu.CompilerParams(vmem_limit_bytes=4 * 1024 * 1024),
+        compiler_params=pltpu.CompilerParams(vmem_limit_bytes=60 * 1024 * 1024),
         name="give",
     )(switches, block)
     got = lax.ppermute(sent, axis, mate)
@@ -129,8 +129,8 @@
 ):
     halves, refs = refs[: 4 * len(widths)], refs[4 * len(widths) :]
     weight_in, taps, weight_out, onehot, after, before = refs[:6]
-    x_out, dpre_out, gout, small, first, early = refs[6:12]
-    x_vmem, pre, dys, slope, hid, dlog, sem_in, sem_out = refs[12:]
+    x_out, dpre_out, gout, small, first = refs[6:11]
+    x_vmem, pre, dys, slope, hid, dlog, sem_in, sem_out = refs[11:]
     rows = x_vmem.shape[0]
     width = x_vmem.shape[1] // 2
     hidden = weight_in.shape[1]
@@ -282,7 +282,6 @@
     small[17:18, :] = jnp.sum(gout[...] * gout[...], axis=0, keepdims=True)
     if first.shape[0] == sizes.message:
         norm = message(sizes, scalars[3], x_vmem, dpre_out, gout, small, first, True)
-        norm = norm + message(sizes, scalars[4], x_vmem, dpre_out, gout, small, early, True)
         small[18:19, :LANES] = norm
     save.wait()
 
@@ -342,10 +341,10 @@
             jax.ShapeDtypeStruct((rows, hidden), jnp.bfloat16),
             jax.ShapeDtypeStruct((256, hidden), jnp.float32),
             jax.ShapeDtypeStruct((24, hidden), jnp.float32),
-        ]
-        + [jax.ShapeDtypeStruct((sizes.message if sizes.staged else 8, hidden), jnp.float32)] * 2,
+            jax.ShapeDtypeStruct((sizes.message if sizes.staged else 8, hidden), jnp.float32),
+        ],
         in_specs=[pl.BlockSpec(memory_space=pltpu.SMEM)] + [anywhere] * len(halves) + [vmem] * 6,
-        out_specs=[anywhere] + [vmem] * 5,
+        out_specs=[anywhere] + [vmem] * 4,
         scratch_shapes=[
             pltpu.VMEM((rows, wide), jnp.bfloat16),
             pltpu.VMEM((3, chunks, span, LANES), jnp.float32),
@@ -361,8 +360,9 @@
     )(scalars, *halves, weight_in, taps, weight_out, onehot, *masks)
 
 
-def blocks_kernel(sizes, scalars, x, dpre, gout, small, late, own, stats):
-    norm = message(sizes, scalars[5], x, dpre, gout, small, late, True)
+def blocks_kernel(sizes, scalars, x, dpre, gout, small, early, late, own, stats):
+    norm = message(sizes, scalars[4], x, dpre, gout, small, early, True)
+    norm = norm + message(sizes, scalars[5], x, dpre, gout, small, late, True)
     norm = norm + message(sizes, scalars[6], x, dpre, gout, small, own, False)
     stats[...] = jnp.zeros(stats.shape, jnp.float32)
     stats[0:1, :] = norm + small[18:19, :LANES]
@@ -423,18 +423,20 @@
     return lax.ppermute(value, "dp", pairs)
 
 
-def add_kernel(sizes, scalars, mine, theirs, out):
+def add_kernel(sizes, scalars, mine, theirs, own, middle, out, parts):
     depth, group = sizes.depth, sizes.group
     mark = depth + group
     end = (scalars[6] == 0) | (scalars[6] == 3)
+    spans = tuple(enumerate(((0, depth), (depth, mark), (mark, mark + 9))))
 
     @pl.when(end)
     def _():
         out[...] = mine[...]
+        parts[...] = own[...]
 
     @pl.when(jnp.logical_not(end))
     def _():
-        for i, (start, stop) in enumerate(((0, depth), (depth, mark), (mark, mark + 9))):
+        for i, (start, stop) in spans:
             at = mark + 9 + i
             a, b = mine[at : at + 1, :], theirs[at : at + 1, :]
             common = jnp.minimum(a, b)
@@ -442,7 +444,11 @@
                 start:stop, :
             ] * jnp.exp2(common - b)
             out[at : at + 1, :] = common
+            parts[start:stop, :] = own[start:stop, :] + middle[start:stop, :] * jnp.exp2(
+                -middle[at : at + 1, :]
+            )
         out[mark + 12 :, :] = mine[mark + 12 :, :]
+        parts[mark + 9 :, :] = own[mark + 9 :, :]
 
 
 def by_row(sizes, shape, three):
@@ -452,7 +458,7 @@
     )
 
 
-def staged_sums(sizes, me, scalars, xrows, dpre, gout, small, first, early):
+def staged_sums(sizes, me, scalars, xrows, dpre, gout, small, first):
     vmem = pl.BlockSpec(memory_space=pltpu.VMEM)
     smem = pl.BlockSpec(memory_space=pltpu.SMEM)
     hidden = dpre.shape[1]
@@ -460,46 +466,39 @@
     full = jax.ShapeDtypeStruct(shape, jnp.float32)
     lines = jax.ShapeDtypeStruct((8, LANES), jnp.float32)
     half = jnp.float16
-    near = permute(first.astype(half), [(0, 1), (1, 0), (2, 3), (3, 2)])
-    early = early.astype(half)
-    middle = permute(early, [(1, 2), (2, 1)])
-    skip = permute(early, [(0, 2), (3, 1)])
-    late, own, stats = pl.pallas_call(
+    first = first.astype(half)
+    near = permute(first, [(0, 1), (3, 2)])
+    middle = permute(first, [(1, 2), (2, 1)])
+    early, late, own, stats = pl.pallas_call(
         functools.partial(blocks_kernel, sizes),
-        out_shape=[full, full, lines],
+        out_shape=[full, full, full, lines],
         in_specs=[smem] + [vmem] * 4,
-        out_specs=[vmem] * 3,
+        out_specs=[vmem] * 4,
         compiler_params=pltpu.CompilerParams(vmem_limit_bytes=16 * 1024 * 1024),
         cost_estimate=pl.CostEstimate(
-            flops=4 * sizes.depth * dpre.shape[0] * hidden,
-            bytes_accessed=2 * xrows.size + 2 * dpre.size + 8 * sizes.message * hidden,
+            flops=6 * sizes.depth * dpre.shape[0] * hidden,
+            bytes_accessed=2 * xrows.size + 2 * dpre.size + 12 * sizes.message * hidden,
             transcendentals=0,
         ),
         name="blocks",
     )(scalars, xrows, dpre, gout, small)
-    end = (me == 0) | (me == 3)
-    mark = sizes.depth + sizes.group + 9
-    both = pl.pallas_call(
+    outer = permute(early.astype(half), [(0, 2), (3, 1), (1, 0), (2, 3)])
+    both, parts = pl.pallas_call(
         functools.partial(add_kernel, sizes),
-        out_shape=full,
-        in_specs=[smem, vmem, vmem],
-        out_specs=vmem,
+        out_shape=[full, full],
+        in_specs=[smem] + [vmem] * 4,
+        out_specs=[vmem] * 2,
         compiler_params=pltpu.CompilerParams(vmem_limit_bytes=8 * 1024 * 1024),
         name="add",
-    )(scalars, late, near.astype(jnp.float32))
+    )(scalars, late, near.astype(jnp.float32), own, middle.astype(jnp.float32))
     both = both.astype(half)
-    near, skip, middle, _ = lax.optimization_barrier((near, skip, middle, both))
     far = permute(both, [(0, 1), (3, 2), (1, 3), (2, 0)])
-
-    def split(value):
-        return [value[mark + i : mark + i + 1] for i in range(3)]
-
-
-    def decode(value):
-        value = value.astype(jnp.float32)
-        return value * by_row(sizes, shape, [jnp.exp2(-v) for v in split(value)])
-
-    parts = own + decode(jnp.where(end, near, skip)) + decode(middle)
+    outer, _ = lax.optimization_barrier((outer, both))
+    outer = outer.astype(jnp.float32)
+    mark = sizes.depth + sizes.group + 9
+    parts = parts + outer * by_row(
+        sizes, shape, [jnp.exp2(-outer[mark + i : mark + i + 1]) for i in range(3)]
+    )
     return parts, far.astype(jnp.float32), stats
 
 
@@ -518,9 +517,10 @@
     odd = me % 2
     end = (me == 0) | (me == 3)
     step, jump = jnp.where(odd == 0, 1, 2), jnp.where(high, me - 2, me + 2)
-    to = [3 * (1 - odd), jnp.where(end, jump, step), jnp.where(end, step, jump), me]
+    edge = 3 * (1 - odd)
+    to = [jnp.where(end, edge, step), jnp.where(end, jump, edge), jnp.where(end, step, jump), me]
     scalars = jnp.stack([dil, here, core] + to).astype(jnp.int32)
-    xrows, dpre, gout, small, first, early = head_backward(
+    xrows, dpre, gout, small, first = head_backward(
         sizes,
         widths,
         scalars,
@@ -533,7 +533,7 @@
     )
     if not sizes.staged:
         return general_sums(sizes, xrows, dpre, gout, small)
-    parts, last, stats = staged_sums(sizes, me, scalars, xrows, dpre, gout, small, first, early)
+    parts, last, stats = staged_sums(sizes, me, scalars, xrows, dpre, gout, small, first)
     vmem = pl.BlockSpec(memory_space=pltpu.VMEM)
     hidden = dpre.shape[1]
     share_in, share_out, total_taps, line = pl.pallas_call(

time: 90.7 us -> 94.2 us (1.039)
  waiting for transfers between devices: 52 us -> 40.4 us
  starting transfers between devices: 17.9 us -> 27.8 us
  Pallas kernels: 15.2 us -> 18.5 us
  local copies, waits for them, and re-layouts: 1.63 us -> 2.95 us
    ppermute x7, waiting for transfers between devices: 29.6 us -> 19.4 us  [permute(): return lax.ppermute(value, 'dp', pairs)]
    ppermute x7, starting transfers between devices: 13.7 us -> 23.6 us  [permute(): return lax.ppermute(value, 'dp', pairs)]
    pallas_call x1, Pallas kernels: 0.62 us -> 2.92 us  [pieces(): pl.pallas_call(give_kernel, out_shape=jax.ShapeDtypeStruct((rows, width),...]
    unnamed x10 -> x14, local copies, waits for them, and re-layouts: 1.52 us -> 1.92 us
  transfers between devices with their start and end apart: 14 -> 14, of which waited for: 9 -> 8; matrix products, arithmetic and copies ran while one was open for 2% -> 2% of each run, Pallas kernels for 2% -> 2%
where the time goes in v6:
time: 94.2 us; the launch traced here: 94 us
  waiting for transfers between devices  40.4 us (43%)
  starting transfers between devices  27.8 us (30%)
  Pallas kernels  18.5 us (20%)
  local copies, waits for them, and re-layouts  2.95 us (3%)
  between operations  2.42 us (3%)
  other arithmetic  1.96 us (2%)
    ppermute x7, starting transfers between devices, permute(): return lax.ppermute(value, 'dp', pairs)  23.6 us
    ppermute x7, waiting for transfers between devices, permute(): return lax.ppermute(value, 'dp', pairs)  19.4 us
    ppermute x2, waiting for transfers between devices, pieces(): other = lax.ppermute(piece, axis, across)  18.1 us
    pallas_call x1, Pallas kernels, head_backward(): pl.pallas_call(functools.partial(head_kernel, sizes, widths), out_shape=[...  9.86 us
    ppermute x2, starting transfers between devices, pieces(): other = lax.ppermute(piece, axis, across)  3.15 us
    pallas_call x1, Pallas kernels, pieces(): pl.pallas_call(give_kernel, out_shape=jax.ShapeDtypeStruct((rows, width),...  2.92 us
    ppermute x1, waiting for transfers between devices, pieces(): got = lax.ppermute(sent, axis, mate)  2.3 us
    unnamed x14, local copies, waits for them, and re-layouts  1.92 us
  transfers between devices with their start and end apart: 14, of which 8 were waited for; matrix products, arithmetic and copies ran while one was open for 2% of the time, Pallas kernels for 2%

profile of v6, /device:TPU:0, one launch (start us, length us, event | category | flops | bytes accessed | tf_op | source)
XLA Modules:
  0.0 94.0 jit_solution(6496767282924061477)
XLA Ops:
  0.6 0.0 copy-start
  1.5 0.6 pad_add_fusion.switches
  2.0 2.9 %give.1 = bf16[592,768]{1,0:T(8,128)(2,1)} custom-call(s32[2]{0:T(128)} %pad_add_fusion.switches, bf16[592,1536]{1,0:T(8,128)(2,1)} %bitcast.26), custom_call_target="tpu_custom_call" | custom-call | tf_op jit(solution)/shard_map/give/pallas_call | solution.py:40
  5.0 0.0 copy-start.6
  5.0 0.0 copy-start.1
  5.0 0.0 copy-start.4
  5.0 0.5 collective-permute-start
  5.5 2.3 %collective-permute-done.got = bf16[592,768]{1,0:T(8,128)(2,1)S(1)} collective-permute-done((bf16[592,768]{1,0:T(8,128)(2,1)}, bf16[592,768]{1,0:T(8,128)(2,1)S(1)}, u32[]{:S(2)}, u32[]{:S(2)}) %collective-permute-start) | collective-permute-done | bytes 909344 | tf_op jit(solution)/shard_map/ppermute | solution.py:49
  7.8 1.5 %hold.1 = (bf16[592,512]{1,0:T(8,128)(2,1)}, bf16[592,256]{1,0:T(8,128)(2,1)}) custom-call(s32[2]{0:T(128)S(1)} %copy-done.5, bf16[592,1536]{1,0:T(8,128)(2,1)S(1)} %bitcast.27, bf16[592,768]{1,0:T(8,128)(2,1)S(1)} %collective-permute-done.got), custom_call_target="tpu_custom_call" | custom-call | tf_op jit(solution)/shard_map/hold/pallas_call | solution.py:50
  9.4 2.9 %collective-permute-start.1 = (bf16[592,512]{1,0:T(8,128)(2,1)}, bf16[592,512]{1,0:T(8,128)(2,1)S(1)}, u32[]{:S(2)}, u32[]{:S(2)}) collective-permute-start(bf16[592,512]{1,0:T(8,128)(2,1)} %get-tuple-element.22.refs_0_), channel_id=1, source_target_pairs={{0,8},{8,0},{4,12},{12,4},{1,9},{9,1},{5,13},{13,5},{2,10},{10,2},... | collective-permute-start | bytes 1818632 | tf_op jit(solution)/shard_map/ppermute | solution.py:61
  12.3 0.0 collective-permute-start.2
  12.3 0.2 collective-permute-start.4
  12.5 14.4 %collective-permute-done.1.refs_1_ = bf16[592,512]{1,0:T(8,128)(2,1)S(1)} collective-permute-done((bf16[592,512]{1,0:T(8,128)(2,1)}, bf16[592,512]{1,0:T(8,128)(2,1)S(1)}, u32[]{:S(2)}, u32[]{:S(2)}) %collective-permute-start.1) | collective-permute-done | bytes 606240 | tf_op jit(solution)/shard_map/ppermute | solution.py:61
  27.0 0.0 collective-permute-start.3
  27.8 0.9 pad.4.refs_10_
  28.7 0.1 stack.42.scalars
  28.8 0.1 fusion.refs_11_
  28.9 0.5 collective-permute-start.5
  29.4 3.7 %collective-permute-done.4.refs_5_ = bf16[592,256]{1,0:T(8,128)(2,1)} collective-permute-done((bf16[592,256]{1,0:T(8,128)(2,1)}, bf16[592,256]{1,0:T(8,128)(2,1)}, u32[]{:S(2)}, u32[]{:S(2)}) %collective-permute-start.4) | collective-permute-done | bytes 303136 | tf_op jit(solution)/shard_map/ppermute | solution.py:61
  33.1 0.3 fusion.2
  33.4 0.0 collective-permute-done.2.refs_2_
  33.5 0.8 copy-done.2
  34.3 0.6 collective-permute-done.6.refs_7_
  34.9 0.0 collective-permute-done.3.refs_3_
  34.9 1.1 %copy-done.3 = bf16[592,512]{1,0:T(8,128)(2,1)S(1)} copy-done((bf16[592,512]{1,0:T(8,128)(2,1)S(1)}, bf16[592,512]{1,0:T(8,128)(2,1)}, u32[]{:S(2)}) %copy-start.3) | copy-done | bytes 606232
  36.0 9.9 %head.1 = (bf16[592,1536]{1,0:T(8,128)(2,1)S(1)}, bf16[592,512]{1,0:T(8,128)(2,1)S(1)}, f32[256,512]{1,0:T(8,128)S(1)}, f32[24,512]{1,0:T(8,128)S(1)}, f32[440,512]{1,0:T(8,128)S(1)}) custom-call(s32[7]{0:T(128)S(1)} %stack.42.scalars, bf16[592,512]{1,0:T(8,128)(2,1)} %get-tuple-element.22.refs_0_, bf16[592,512]{1,0:T(8,128)(2,1)S(1)} %collective-permute-done.1.refs_1_, ...), custom_call_target="tpu_custom_call" | custom-call | tf_op jit(solution)/shard_map/head/pallas_call | solution.py:337
  45.9 0.1 convert_element_type.37
  45.9 3.8 %collective-permute-start.7 = (f16[440,512]{1,0:T(8,128)(2,1)S(1)}, f16[440,512]{1,0:T(8,128)(2,1)S(1)}, u32[]{:S(2)}, u32[]{:S(2)}) collective-permute-start(f16[440,512]{1,0:T(8,128)(2,1)S(1)} %convert_element_type.37), channel_id=1, source_target_pairs={{0,1},{3,2},{4,5},{7,6},{8,9},{11,10},{12,13},{15,14},{16,17},{19,... | collective-permute-start | bytes 1351688 | tf_op jit(solution)/shard_map/ppermute | solution.py:423
  49.7 0.7 collective-permute-start.8
  50.4 1.7 %blocks.1 = (f32[440,512]{1,0:T(8,128)S(1)}, f32[440,512]{1,0:T(8,128)S(1)}, f32[440,512]{1,0:T(8,128)S(1)}, f32[8,128]{1,0:T(8,128)S(1)}) custom-call(s32[7]{0:T(128)S(1)} %stack.42.scalars, bf16[592,1536]{1,0:T(8,128)(2,1)S(1)} %get-tuple-element.24.x, bf16[592,512]{1,0:T(8,128)(2,1)S(1)} %get-tuple-element.25.dpre, ...), custom_call_target="tpu_custom_call" | custom-call | flops 698351616 | bytes 5128192 | tf_op jit(solution)/shard_map/blocks/pallas_call | solution.py:472
  52.1 0.1 convert_element_type.40
  52.1 2.1 %collective-permute-start.9 = (f16[440,512]{1,0:T(8,128)(2,1)S(1)}, f16[440,512]{1,0:T(8,128)(2,1)S(1)}, u32[]{:S(2)}, u32[]{:S(2)}) collective-permute-start(f16[440,512]{1,0:T(8,128)(2,1)S(1)} %convert_element_type.40), channel_id=1, source_target_pairs={{0,2},{3,1},{1,0},{2,3},{4,6},{7,5},{5,4},{6,7},{8,10},{11,9},{9,8... | collective-permute-start | bytes 1351688 | tf_op jit(solution)/shard_map/ppermute | solution.py:423
  54.3 6.1 %collective-permute-done.7 = f16[440,512]{1,0:T(8,128)(2,1)S(1)} collective-permute-done((f16[440,512]{1,0:T(8,128)(2,1)S(1)}, f16[440,512]{1,0:T(8,128)(2,1)S(1)}, u32[]{:S(2)}, u32[]{:S(2)}) %collective-permute-start.7) | collective-permute-done | bytes 450592 | tf_op jit(solution)/shard_map/ppermute | solution.py:423
  60.4 0.1 convert_element_type.38.theirs
  60.5 0.1 convert_element_type.39.middle
  60.6 0.7 add.50
  61.3 0.1 convert_element_type.41
  61.3 12.7 %collective-permute-start.10 = (f16[440,512]{1,0:T(8,128)(2,1)S(1)}, f16[440,512]{1,0:T(8,128)(2,1)S(1)}, u32[]{:S(2)}, u32[]{:S(2)}) collective-permute-start(f16[440,512]{1,0:T(8,128)(2,1)S(1)} %convert_element_type.41), channel_id=1, source_target_pairs={{0,1},{3,2},{1,3},{2,0},{4,5},{7,6},{5,7},{6,4},{8,9},{11,10},{9,1... | collective-permute-start | bytes 1351688 | tf_op jit(solution)/shard_map/ppermute | solution.py:423
  74.0 0.1 convert_element_type.42
  74.2 0.3 multiply_add_fusion.parts
  74.5 10.4 %collective-permute-done.10 = f16[440,512]{1,0:T(8,128)(2,1)S(1)} collective-permute-done((f16[440,512]{1,0:T(8,128)(2,1)S(1)}, f16[440,512]{1,0:T(8,128)(2,1)S(1)}, u32[]{:S(2)}, u32[]{:S(2)}) %collective-permute-start.10) | collective-permute-done | bytes 450592 | tf_op jit(solution)/shard_map/ppermute | solution.py:423
  84.9 0.1 convert_element_type.43.last
  85.0 1.1 %sums.1 = (f32[384,512]{1,0:T(8,128)}, f32[150,1,128]{2,1,0:T(1,128)}, f32[9,1,512]{2,1,0:T(1,128)}, f32[32,128]{1,0:T(8,128)S(1)}) custom-call(f32[440,512]{1,0:T(8,128)S(1)} %multiply_add_fusion.parts, f32[440,512]{1,0:T(8,128)S(1)} %convert_element_type.43.last, f32[8,128]{1,0:T(8,128)S(1)} %get-tuple-element.35.stats), custom_call_target="tpu_custom_call" | custom-call | tf_op jit(solution)/shard_map/sums/pallas_call | solution.py:539
  86.0 1.7 %collective-permute-start.12 = (f32[32,128]{1,0:T(8,128)S(1)}, f32[32,128]{1,0:T(8,128)S(1)}, u32[]{:S(2)}, u32[]{:S(2)}) collective-permute-start(f32[32,128]{1,0:T(8,128)S(1)} %get-tuple-element.39.refs_0_), channel_id=1, source_target_pairs={{0,2},{1,3},{2,0},{3,1},{4,6},{5,7},{6,4},{7,5},{8,10},{9,11},{10,... | collective-permute-start | bytes 49160 | tf_op jit(solution)/shard_map/ppermute | solution.py:423
  87.8 2.6 %collective-permute-start.13 = (f32[32,128]{1,0:T(8,128)S(1)}, f32[32,128]{1,0:T(8,128)S(1)}, u32[]{:S(2)}, u32[]{:S(2)}) collective-permute-start(f32[32,128]{1,0:T(8,128)S(1)} %get-tuple-element.39.refs_0_), channel_id=1, source_target_pairs={{0,3},{1,2},{2,1},{3,0},{4,7},{5,6},{6,5},{7,4},{8,11},{9,10},{10,... | collective-permute-start | bytes 49160 | tf_op jit(solution)/shard_map/ppermute | solution.py:423
  90.4 0.2 collective-permute-done.12.refs_2_
  90.7 2.6 %collective-permute-done.13.refs_3_ = f32[32,128]{1,0:T(8,128)S(1)} collective-permute-done((f32[32,128]{1,0:T(8,128)S(1)}, f32[32,128]{1,0:T(8,128)S(1)}, u32[]{:S(2)}, u32[]{:S(2)}) %collective-permute-start.13) | collective-permute-done | bytes 16416 | tf_op jit(solution)/shard_map/ppermute | solution.py:423
  93.3 0.7 norms.1
  (19 shorter events, 0.1 us)
Async XLA Ops:
  0.6 7.2 %copy-start = (bf16[1,1,592,1536]{3,2,1,0:T(8,128)(2,1)S(1)}, bf16[1,1,592,1536]{3,2,1,0:T(8,128)(2,1)}, u32[]{:S(2)}) copy-start(bf16[1,1,592,1536]{3,2,1,0:T(8,128)(2,1)} %param.7) | copy-start | bytes 5455876
  2.0 5.8 %copy-start.5 = (s32[2]{0:T(128)S(1)}, s32[2]{0:T(128)}, u32[]{:S(2)}) copy-start(s32[2]{0:T(128)} %pad_add_fusion.switches) | copy-start | bytes 28
  5.0 22.8 %copy-start.6 = (s32[1,592]{1,0:T(1,128)S(1)}, s32[1,592]{1,0:T(1,128)}, u32[]{:S(2)}) copy-start(s32[1,592]{1,0:T(1,128)} %param.10) | copy-start | bytes 7108
  5.0 29.9 %copy-start.1 = (bf16[1,1536,512]{2,1,0:T(8,128)(2,1)S(1)}, bf16[1,1536,512]{2,1,0:T(8,128)(2,1)}, u32[]{:S(2)}) copy-start(bf16[1,1536,512]{2,1,0:T(8,128)(2,1)} %param.11) | copy-start | bytes 4718596
  5.0 29.9 %copy-start.4 = (f32[1,9,512]{2,0,1:T(1,128)S(1)}, f32[1,9,512]{2,0,1:T(1,128)}, u32[]{:S(2)}) copy-start(f32[1,9,512]{2,0,1:T(1,128)} %param.12) | copy-start | bytes 55300
  5.0 2.8 %collective-permute-start = (bf16[592,768]{1,0:T(8,128)(2,1)}, bf16[592,768]{1,0:T(8,128)(2,1)S(1)}, u32[]{:S(2)}, u32[]{:S(2)}) collective-permute-start(bf16[592,768]{1,0:T(8,128)(2,1)} %give.1), channel_id=1, source_target_pairs={{0,4},{4,0},{8,12},{12,8},{1,5},{5,1},{9,13},{13,9},{2,6},{6,2},{1... | collective-permute-start | bytes 2727944 | tf_op jit(solution)/shard_map/ppermute | solution.py:49
  9.4 17.6 %collective-permute-start.1 = (bf16[592,512]{1,0:T(8,128)(2,1)}, bf16[592,512]{1,0:T(8,128)(2,1)S(1)}, u32[]{:S(2)}, u32[]{:S(2)}) collective-permute-start(bf16[592,512]{1,0:T(8,128)(2,1)} %get-tuple-element.22.refs_0_), channel_id=1, source_target_pairs={{0,8},{8,0},{4,12},{12,4},{1,9},{9,1},{5,13},{13,5},{2,10},{10,2},... | collective-permute-start | bytes 1818632 | tf_op jit(solution)/shard_map/ppermute | solution.py:61
  12.3 21.1 %collective-permute-start.2 = (bf16[592,512]{1,0:T(8,128)(2,1)}, bf16[592,512]{1,0:T(8,128)(2,1)S(1)}, u32[]{:S(2)}, u32[]{:S(2)}) collective-permute-start(bf16[592,512]{1,0:T(8,128)(2,1)} %get-tuple-element.22.refs_0_), channel_id=1, source_target_pairs={{0,4},{4,0},{8,12},{12,8},{1,5},{5,1},{9,13},{13,9},{2,6},{6,2},{1... | collective-permute-start | bytes 1818632 | tf_op jit(solution)/shard_map/ppermute | solution.py:62
  12.3 20.8 %collective-permute-start.4 = (bf16[592,256]{1,0:T(8,128)(2,1)}, bf16[592,256]{1,0:T(8,128)(2,1)}, u32[]{:S(2)}, u32[]{:S(2)}) collective-permute-start(bf16[592,256]{1,0:T(8,128)(2,1)} %get-tuple-element.23.refs_4_), channel_id=1, source_target_pairs={{0,8},{8,0},{4,12},{12,4},{1,9},{9,1},{5,13},{13,5},{2,10},{10,2},... | collective-permute-start | bytes 909320 | tf_op jit(solution)/shard_map/ppermute | solution.py:61
  27.0 7.9 %collective-permute-start.3 = (bf16[592,512]{1,0:T(8,128)(2,1)S(1)}, bf16[592,512]{1,0:T(8,128)(2,1)}, u32[]{:S(2)}, u32[]{:S(2)}) collective-permute-start(bf16[592,512]{1,0:T(8,128)(2,1)S(1)} %collective-permute-done.1.refs_1_), channel_id=1, source_target_pairs={{0,4},{4,0},{8,12},{12,8},{1,5},{5,1},{9,13},{13,9},{2,6},{6,2},{1... | collective-permute-start | bytes 1818632 | tf_op jit(solution)/shard_map/ppermute | solution.py:63
  28.9 4.5 %collective-permute-start.5 = (bf16[592,256]{1,0:T(8,128)(2,1)}, bf16[592,256]{1,0:T(8,128)(2,1)S(1)}, u32[]{:S(2)}, u32[]{:S(2)}) collective-permute-start(bf16[592,256]{1,0:T(8,128)(2,1)} %get-tuple-element.23.refs_4_), channel_id=1, source_target_pairs={{0,4},{4,0},{8,12},{12,8},{1,5},{5,1},{9,13},{13,9},{2,6},{6,2},{1... | collective-permute-start | bytes 909320 | tf_op jit(solution)/shard_map/ppermute | solution.py:62
  33.1 1.8 %collective-permute-start.6 = (bf16[592,256]{1,0:T(8,128)(2,1)}, bf16[592,256]{1,0:T(8,128)(2,1)S(1)}, u32[]{:S(2)}, u32[]{:S(2)}) collective-permute-start(bf16[592,256]{1,0:T(8,128)(2,1)} %collective-permute-done.4.refs_5_), channel_id=1, source_target_pairs={{0,4},{4,0},{8,12},{12,8},{1,5},{5,1},{9,13},{13,9},{2,6},{6,2},{1... | collective-permute-start | bytes 909320 | tf_op jit(solution)/shard_map/ppermute | solution.py:63
  33.4 0.8 copy-start.2
  34.9 1.1 %copy-start.3 = (bf16[592,512]{1,0:T(8,128)(2,1)S(1)}, bf16[592,512]{1,0:T(8,128)(2,1)}, u32[]{:S(2)}) copy-start(bf16[592,512]{1,0:T(8,128)(2,1)} %copy-done.2) | copy-start | bytes 1818628
  45.9 14.4 %collective-permute-start.7 = (f16[440,512]{1,0:T(8,128)(2,1)S(1)}, f16[440,512]{1,0:T(8,128)(2,1)S(1)}, u32[]{:S(2)}, u32[]{:S(2)}) collective-permute-start(f16[440,512]{1,0:T(8,128)(2,1)S(1)} %convert_element_type.37), channel_id=1, source_target_pairs={{0,1},{3,2},{4,5},{7,6},{8,9},{11,10},{12,13},{15,14},{16,17},{19,... | collective-permute-start | bytes 1351688 | tf_op jit(solution)/shard_map/ppermute | solution.py:423
  49.7 10.8 %collective-permute-start.8 = (f16[440,512]{1,0:T(8,128)(2,1)S(1)}, f16[440,512]{1,0:T(8,128)(2,1)S(1)}, u32[]{:S(2)}, u32[]{:S(2)}) collective-permute-start(f16[440,512]{1,0:T(8,128)(2,1)S(1)} %convert_element_type.37), channel_id=1, source_target_pairs={{1,2},{2,1},{5,6},{6,5},{9,10},{10,9},{13,14},{14,13},{17,18},{18,... | collective-permute-start | bytes 1351688 | tf_op jit(solution)/shard_map/ppermute | solution.py:423
  52.1 21.9 %collective-permute-start.9 = (f16[440,512]{1,0:T(8,128)(2,1)S(1)}, f16[440,512]{1,0:T(8,128)(2,1)S(1)}, u32[]{:S(2)}, u32[]{:S(2)}) collective-permute-start(f16[440,512]{1,0:T(8,128)(2,1)S(1)} %convert_element_type.40), channel_id=1, source_target_pairs={{0,2},{3,1},{1,0},{2,3},{4,6},{7,5},{5,4},{6,7},{8,10},{11,9},{9,8... | collective-permute-start | bytes 1351688 | tf_op jit(solution)/shard_map/ppermute | solution.py:423
  61.3 23.5 %collective-permute-start.10 = (f16[440,512]{1,0:T(8,128)(2,1)S(1)}, f16[440,512]{1,0:T(8,128)(2,1)S(1)}, u32[]{:S(2)}, u32[]{:S(2)}) collective-permute-start(f16[440,512]{1,0:T(8,128)(2,1)S(1)} %convert_element_type.41), channel_id=1, source_target_pairs={{0,1},{3,2},{1,3},{2,0},{4,5},{7,6},{5,7},{6,4},{8,9},{11,10},{9,1... | collective-permute-start | bytes 1351688 | tf_op jit(solution)/shard_map/ppermute | solution.py:423
  86.0 4.4 %collective-permute-start.11 = (f32[32,128]{1,0:T(8,128)S(1)}, f32[32,128]{1,0:T(8,128)S(1)}, u32[]{:S(2)}, u32[]{:S(2)}) collective-permute-start(f32[32,128]{1,0:T(8,128)S(1)} %get-tuple-element.39.refs_0_), channel_id=1, source_target_pairs={{0,1},{1,0},{2,3},{3,2},{4,5},{5,4},{6,7},{7,6},{8,9},{9,8},{10,11... | collective-permute-start | bytes 49160 | tf_op jit(solution)/shard_map/ppermute | solution.py:423
  86.0 4.6 %collective-permute-start.12 = (f32[32,128]{1,0:T(8,128)S(1)}, f32[32,128]{1,0:T(8,128)S(1)}, u32[]{:S(2)}, u32[]{:S(2)}) collective-permute-start(f32[32,128]{1,0:T(8,128)S(1)} %get-tuple-element.39.refs_0_), channel_id=1, source_target_pairs={{0,2},{1,3},{2,0},{3,1},{4,6},{5,7},{6,4},{7,5},{8,10},{9,11},{10,... | collective-permute-start | bytes 49160 | tf_op jit(solution)/shard_map/ppermute | solution.py:423
  87.8 5.5 %collective-permute-start.13 = (f32[32,128]{1,0:T(8,128)S(1)}, f32[32,128]{1,0:T(8,128)S(1)}, u32[]{:S(2)}, u32[]{:S(2)}) collective-permute-start(f32[32,128]{1,0:T(8,128)S(1)} %get-tuple-element.39.refs_0_), channel_id=1, source_target_pairs={{0,3},{1,2},{2,1},{3,0},{4,7},{5,6},{6,5},{7,4},{8,11},{9,10},{10,... | collective-permute-start | bytes 49160 | tf_op jit(solution)/shard_map/ppermute | solution.py:423

commit v7 on v5

--- a/solution.py
+++ b/solution.py
@@ -31,73 +31,17 @@
     across = [(0, 2), (2, 0), (1, 3), (3, 1)]
     here = ((source // 2) == (me // 2)).astype(jnp.int32)
     widths = split_width(width)
-    rows = block.shape[0]
-    switches = jnp.stack([core, (source % 2 == core).astype(jnp.int32)]).astype(jnp.int32)
-    smem = pl.BlockSpec(memory_space=pltpu.SMEM)
-    vmem = pl.BlockSpec(memory_space=pltpu.VMEM)
-    anywhere = pl.BlockSpec(memory_space=pl.ANY)
-    hbm = pl.BlockSpec(memory_space=pltpu.MemorySpace.HBM)
-    sent = pl.pallas_call(
-        give_kernel,
-        out_shape=jax.ShapeDtypeStruct((rows, width), block.dtype),
-        in_specs=[smem, hbm],
-        out_specs=vmem,
-        scratch_shapes=[pltpu.SemaphoreType.DMA],
-        compiler_params=pltpu.CompilerParams(vmem_limit_bytes=4 * 1024 * 1024),
-        name="give",
-    )(switches, block)
-    got = lax.ppermute(sent, axis, mate)
-    held = pl.pallas_call(
-        functools.partial(hold_kernel, widths),
-        out_shape=[jax.ShapeDtypeStruct((rows, piece), block.dtype) for piece in widths],
-        in_specs=[smem, hbm, anywhere],
-        out_specs=[vmem] * len(widths),
-        scratch_shapes=[pltpu.SemaphoreType.DMA((len(widths),))],
-        compiler_params=pltpu.CompilerParams(vmem_limit_bytes=4 * 1024 * 1024),
-        name="hold",
-    )(switches, block, got)
+    got = lax.ppermute(jnp.where(core == 0, block[:, width:], block[:, :width]), axis, mate)
     values = []
-    for piece in held:
-        other = lax.ppermute(piece, axis, across)
-        back_held = lax.ppermute(piece, axis, mate)
-        back_other = lax.ppermute(other, axis, mate)
-        values += [piece, other, back_held, back_other]
+    at = 0
+    for piece in widths:
+        low, high = block[:, at : at + piece], block[:, width + at : width + at + piece]
+        kept = jnp.where(core == 0, low, high)
+        held = jnp.where(source % 2 == core, kept, got[:, at : at + piece])
+        other = lax.ppermute(held, axis, across)
+        values += [held, other, lax.ppermute(held, axis, mate), lax.ppermute(other, axis, mate)]
+        at += piece
     return here, core, widths, tuple(values)
-
-
-def give_kernel(switches, block, out, sem):
-    width = out.shape[1]
-    column = pl.multiple_of((1 - switches[0]) * width, LANES)
-    copy = pltpu.make_async_copy(block.at[:, pl.ds(column, width)], out, sem)
-    copy.start()
-    copy.wait()
-
-
-def hold_kernel(widths, switches, block, got, *rest):
-    outs, sem = rest[:-1], rest[-1]
-    width = got.shape[1]
-    column = switches[0] * width
-    starts = [sum(widths[:i]) for i in range(len(widths))]
-
-    def copy(i, own):
-        if own:
-            source = block.at[:, pl.ds(pl.multiple_of(column + starts[i], LANES), widths[i])]
-        else:
-            source = got.at[:, pl.ds(starts[i], widths[i])]
-        return pltpu.make_async_copy(source, outs[i], sem.at[i])
-
-    @pl.when(switches[1] == 1)
-    def _():
-        for i in range(len(widths)):
-            copy(i, True).start()
-
-    @pl.when(switches[1] == 0)
-    def _():
-        for i in range(len(widths)):
-            copy(i, False).start()
-
-    for i in range(len(widths)):
-        copy(i, False).wait()
 
 
 def split_width(width):
@@ -107,13 +51,11 @@
 
 
 def gelu_parts(value):
-    inner = 0.7978845608 * (value + 0.044715 * value * value * value)
-    tanh_val = jnp.tanh(inner)
-    out_val = 0.5 * value * (1.0 + tanh_val)
-    slope = 0.5 * (1.0 + tanh_val) + 0.5 * value * (1.0 - tanh_val * tanh_val) * 0.7978845608 * (
-        1.0 + 3.0 * 0.044715 * value * value
-    )
-    return (out_val, slope)
+    square = value * value
+    half = 0.5 + 0.5 * jnp.tanh(value * (0.7978845608 + (0.7978845608 * 0.044715) * square))
+    out_val = value * half
+    rate = 2.0 * 0.7978845608 + (6.0 * 0.7978845608 * 0.044715) * square
+    return (out_val, half + out_val * (1.0 - half) * rate)
 
 
 def exponent(size):
@@ -139,60 +81,54 @@
     dil, here, core = scalars[0], scalars[1], scalars[2]
 
     def fetch(kind, index):
-        place = core if kind < 2 else 1 - core
-        column = pl.multiple_of(place * width + sum(widths[:index]), LANES)
-        target = x_vmem.at[:, pl.ds(column, widths[index])]
+        column = (core if kind < 2 else 1 - core) * width + sum(widths[:index])
+        target = x_vmem.at[:, pl.ds(pl.multiple_of(column, LANES), widths[index])]
         return pltpu.make_async_copy(halves[4 * index + kind], target, sem_in.at[index, kind // 2])
 
-    @pl.when(here == 1)
-    def _():
-        for index in range(len(widths)):
-            fetch(0, index).start()
-            fetch(2, index).start()
-
-    @pl.when(here == 0)
-    def _():
-        for index in range(len(widths)):
-            fetch(1, index).start()
-            fetch(3, index).start()
-
-    for shift in range(3):
-        for c in range(chunks):
-            for ref in (pre, dys):
-                ref[shift, c, :guard, :] = jnp.zeros((guard, LANES), jnp.float32)
-                tail = ref.shape[2] - guard - rows
-                ref[shift, c, guard + rows :, :] = jnp.zeros((tail, LANES), jnp.float32)
+    for away in (0, 1):
+
+        @pl.when(here == 1 - away)
+        def _(away=away):
+            for index in range(len(widths)):
+                fetch(away, index).start()
+                fetch(2 + away, index).start()
+
+    for c in range(chunks):
+        for ref in (pre, dys):
+            ref[c, :guard, :] = jnp.zeros((guard, LANES), jnp.float32)
+            ref[c, guard + rows :, :] = jnp.zeros((guard, LANES), jnp.float32)
     for index in range(len(widths)):
         fetch(0, index).wait()
         fetch(2, index).wait()
     save = pltpu.make_async_copy(x_vmem, x_out, sem_out)
     save.start()
 
-    masks = (after, None, before)
     for n in range(hidden // 256):
         value = jnp.dot(
             x_vmem[...], weight_in[:, 256 * n : 256 * n + 256], preferred_element_type=jnp.float32
         )
         for h in range(2):
-            part = value[:, LANES * h : LANES * h + LANES]
-            for shift in range(3):
-                mask = (before, None, after)[shift]
-                pre[shift, 2 * n + h, guard : guard + rows, :] = (
-                    part if mask is None else part * mask[...]
-                )
+            pre[2 * n + h, guard : guard + rows, :] = value[:, LANES * h : LANES * h + LANES]
 
     starts = [dil * (PC * a + b) for a, b in OFFSETS]
 
+    def column_sums(source, c, row, count, sign):
+        column = slice(LANES * c, LANES * c + LANES)
+        sums = []
+        for b in range(3):
+            total = None
+            for k in (b, 3 + b, 6 + b):
+                at = guard + row + sign * starts[k]
+                term = source[c, pl.ds(at, count), :] * taps[k, :, column]
+                total = term if total is None else total + term
+            sums.append(total)
+        return sums
+
     def forward(row, count):
+        low, high = after[pl.ds(row, count), :], before[pl.ds(row, count), :]
         for c in range(chunks):
-            total = None
-            for k in range(9):
-                term = (
-                    pre[k % 3, c, pl.ds(guard + row + starts[k], count), :]
-                    * taps[k, :, LANES * c : LANES * c + LANES]
-                )
-                total = term if total is None else total + term
-            act, grad = gelu_parts(total)
+            sums = column_sums(pre, c, row, count, 1)
+            act, grad = gelu_parts(sums[1] + low * sums[0] + high * sums[2])
             slope[c, pl.ds(row, count), :] = grad
             hid[pl.ds(row, count), LANES * c : LANES * c + LANES] = act.astype(jnp.bfloat16)
 
@@ -225,10 +161,7 @@
         )
         for h in range(2):
             c = 2 * n + h
-            part = value[:, LANES * h : LANES * h + LANES] * slope[c]
-            for shift in range(3):
-                mask = (after, None, before)[shift]
-                dys[shift, c, guard : guard + rows, :] = part if mask is None else part * mask[...]
+            dys[c, guard : guard + rows, :] = value[:, LANES * h : LANES * h + LANES] * slope[c]
 
     def fold(value):
         return jnp.sum(value.reshape(-1, 8, LANES), axis=0)
@@ -242,15 +175,15 @@
 
         def backward(row, count, carry):
             sums, top = carry
-            dy = dys[1, c, pl.ds(guard + row, count), :]
-            total = None
-            out = []
-            for k in range(9):
-                out.append(sums[k] + fold(dy * pre[k % 3, c, pl.ds(guard + row + starts[k], count), :]))
-                term = (
-                    dys[k % 3, c, pl.ds(guard + row - starts[k], count), :] * taps[k, :, column]
-                )
-                total = term if total is None else total + term
+            low, high = after[pl.ds(row, count), :], before[pl.ds(row, count), :]
+            dy = dys[c, pl.ds(guard + row, count), :]
+            masked = (dy * low, dy, dy * high)
+            out = [
+                sums[k] + fold(masked[k % 3] * pre[c, pl.ds(guard + row + starts[k], count), :])
+                for k in range(9)
+            ]
+            back = column_sums(dys, c, row, count, -1)
+            total = back[1] + high * back[0] + low * back[2]
             dpre_out[pl.ds(row, count), column] = total.astype(jnp.bfloat16)
             size = jnp.max(jnp.abs(total).reshape(-1, 8, LANES), axis=0)
             return tuple(out), jnp.maximum(top, size)
@@ -348,15 +281,15 @@
         out_specs=[anywhere] + [vmem] * 5,
         scratch_shapes=[
             pltpu.VMEM((rows, wide), jnp.bfloat16),
-            pltpu.VMEM((3, chunks, span, LANES), jnp.float32),
-            pltpu.VMEM((3, chunks, span, LANES), jnp.float32),
+            pltpu.VMEM((chunks, span, LANES), jnp.float32),
+            pltpu.VMEM((chunks, span, LANES), jnp.float32),
             pltpu.VMEM((chunks, rows, LANES), jnp.float32),
             pltpu.VMEM((rows, hidden), jnp.bfloat16),
             pltpu.VMEM((rows, 256), jnp.bfloat16),
             pltpu.SemaphoreType.DMA((len(widths), 2)),
             pltpu.SemaphoreType.DMA,
         ],
-        compiler_params=pltpu.CompilerParams(vmem_limit_bytes=30 * 1024 * 1024),
+        compiler_params=pltpu.CompilerParams(vmem_limit_bytes=24 * 1024 * 1024),
         name="head",
     )(scalars, *halves, weight_in, taps, weight_out, onehot, *masks)
 
@@ -398,17 +331,13 @@
     line[24:25, :] = sum(square[:, LANES * c : LANES * c + LANES] for c in range(chunks))
 
 
-def norm_kernel(dp, chunks, *refs):
-    lines, out = refs[:dp], refs[dp]
-    total = lines[0][...]
-    for line in lines[1:]:
-        total = total + line[...]
+def norm_kernel(chunks, line, total, out):
     values = [
         jnp.sum(total[16:17, :]),
         jnp.sum(total[17:18, :]),
         jnp.sum(total[18 : 18 + chunks, :]),
         jnp.sum(total[0:8, :]),
-        jnp.sum(lines[0][24:25, :]),
+        jnp.sum(line[24:25, :]),
         jnp.sum(total[8:16, :]),
     ]
     row = lax.broadcasted_iota(jnp.int32, (8, LANES), 0)
@@ -549,15 +478,17 @@
         compiler_params=pltpu.CompilerParams(vmem_limit_bytes=8 * 1024 * 1024),
         name="sums",
     )(parts, last, stats)
-    lines = [line] + [permute(line, [(i, i ^ s) for i in range(dp)]) for s in range(1, dp)]
+    total = line
+    for step in (1, 2):
+        total = total + permute(total, [(i, i ^ step) for i in range(dp)])
     norms = pl.pallas_call(
-        functools.partial(norm_kernel, dp, chunks),
+        functools.partial(norm_kernel, chunks),
         out_shape=jax.ShapeDtypeStruct((2, 3), jnp.float32),
-        in_specs=[vmem] * dp,
+        in_specs=[vmem] * 2,
         out_specs=vmem,
         compiler_params=pltpu.CompilerParams(vmem_limit_bytes=4 * 1024 * 1024),
         name="norms",
-    )(*lines)
+    )(line, total)
     share_out = jnp.transpose(share_out, (1, 2, 0))
     return (share_in[None], jnp.transpose(total_taps, (1, 0, 2)), share_out, norms[None])
 

time: 90.7 us -> 89.6 us (0.988)
  other arithmetic: 1.66 us -> 5.6 us
  starting transfers between devices: 17.9 us -> 15.3 us
  Pallas kernels: 15.2 us -> 13.7 us
  local copies, waits for them, and re-layouts: 1.63 us -> 0.14 us
    select_n x0 -> x3, other arithmetic: none -> 4.02 us  [the longest x2 2.35 us: pieces(): held = jnp.where(source % 2 == core, kept, got[:, at:at + piece])]
    ppermute x7 -> x6, starting transfers between devices: 13.7 us -> 10.9 us  [permute(): return lax.ppermute(value, 'dp', pairs)]
    ppermute x7 -> x6, waiting for transfers between devices: 29.6 us -> 31.9 us  [permute(): return lax.ppermute(value, 'dp', pairs)]
    ppermute x7, waiting for transfers between devices: 22.3 us -> 20.4 us  [the longest x2 17.4 us: pieces(): other = lax.ppermute(held, axis, across)]
    unnamed x10, local copies, waits for them, and re-layouts: 1.52 us -> 0.03 us
    pallas_call x3 -> x1, Pallas kernels: 1.96 us -> 0.7 us  [per_device(): pl.pallas_call(functools.partial(norm_kernel, chunks), out_shape=jax.Shap...]
  transfers between devices with their start and end apart: 14 -> 13, of which waited for: 9 -> 9; matrix products, arithmetic and copies ran while one was open for 2% -> 3% of each run, Pallas kernels for 2% -> 2%
where the time goes in v7:
time: 89.6 us; the launch traced here: 89.3 us
  waiting for transfers between devices  52.2 us (58%)
  starting transfers between devices  15.3 us (17%)
  Pallas kernels  13.7 us (15%)
  other arithmetic  5.6 us (6%)
  between operations  2.29 us (3%)
    ppermute x6, waiting for transfers between devices, permute(): return lax.ppermute(value, 'dp', pairs)  31.9 us
    ppermute x2, waiting for transfers between devices, pieces(): other = lax.ppermute(held, axis, across)  17.4 us
    ppermute x6, starting transfers between devices, permute(): return lax.ppermute(value, 'dp', pairs)  10.9 us
    pallas_call x1, Pallas kernels, head_backward(): pl.pallas_call(functools.partial(head_kernel, sizes, widths), out_shape=[...  9.92 us
    ppermute x2, starting transfers between devices, pieces(): other = lax.ppermute(held, axis, across)  3.35 us
    select_n x2, other arithmetic, pieces(): held = jnp.where(source % 2 == core, kept, got[:, at:at + piece])  2.35 us
  transfers between devices with their start and end apart: 13, of which 9 were waited for; matrix products, arithmetic and copies ran while one was open for 3% of the time, Pallas kernels for 2%

profile of v7, /device:TPU:0, one launch (start us, length us, event | category | flops | bytes accessed | tf_op | source)
XLA Modules:
  0.0 89.3 jit_solution(13333530268249088096)
XLA Ops:
  0.6 0.0 copy-start.2
  0.7 1.7 %slice_select_fusion = bf16[592,768]{1,0:T(8,128)(2,1)S(1)} fusion(bf16[592,1536]{1,0:T(8,128)(2,1)} %bitcast.30, pred[]{:T(512)S(6)} %eq.50), kind=kLoop, calls=%fused_computation | loop fusion | flops 454656 | bytes 2727937 | tf_op jit(solution)/shard_map/jit(_where)/select_n | solution.py:34
  2.3 0.5 collective-permute-start
  3.5 0.0 copy-start.4
  3.5 0.0 copy-start.3
  3.6 1.5 %collective-permute-done = bf16[592,768]{1,0:T(8,128)(2,1)} collective-permute-done((bf16[592,768]{1,0:T(8,128)(2,1)S(1)}, bf16[592,768]{1,0:T(8,128)(2,1)}, u32[]{:S(2)}, u32[]{:S(2)}) %collective-permute-start) | collective-permute-done | bytes 909344 | tf_op jit(solution)/shard_map/ppermute | solution.py:34
  5.1 1.2 %slice_select_fusion.1.refs_0_ = bf16[592,512]{1,0:T(8,128)(2,1)S(1)} fusion(bf16[592,768]{1,0:T(8,128)(2,1)} %collective-permute-done, bf16[592,1536]{1,0:T(8,128)(2,1)S(1)} %bitcast.32, pred[]{:T(512)S(6)} %eq.50, pred[]{:T(512)S(6)} %eq.49), kind=kLoop, calls=%fused_computation.2 | loop fusion | flops 606208 | bytes 2424834 | tf_op jit(solution)/shard_map/jit(_where)/select_n | solution.py:40
  6.2 0.0 copy-start
  6.2 0.0 copy-start.1
  6.3 2.9 %collective-permute-start.1 = (bf16[592,512]{1,0:T(8,128)(2,1)S(1)}, bf16[592,512]{1,0:T(8,128)(2,1)S(1)}, u32[]{:S(2)}, u32[]{:S(2)}) collective-permute-start(bf16[592,512]{1,0:T(8,128)(2,1)S(1)} %slice_select_fusion.1.refs_0_), channel_id=1, source_target_pairs={{0,8},{8,0},{4,12},{12,4},{1,9},{9,1},{5,13},{13,5},{2,10},{10,2},... | collective-permute-start | bytes 1818632 | tf_op jit(solution)/shard_map/ppermute | solution.py:41
  9.2 0.0 collective-permute-start.2
  9.2 1.2 %slice_select_fusion.3.refs_4_ = bf16[592,256]{1,0:T(8,128)(2,1)S(1)} fusion(bf16[592,768]{1,0:T(8,128)(2,1)} %collective-permute-done, bf16[592,1536]{1,0:T(8,128)(2,1)} %bitcast.31, pred[]{:T(512)S(6)} %eq.50, pred[]{:T(512)S(6)} %eq.49), kind=kLoop, calls=%fused_computation.9 | loop fusion | flops 303104 | bytes 1212418 | tf_op jit(solution)/shard_map/jit(_where)/select_n | solution.py:40
  10.4 0.4 collective-permute-start.4
  10.8 12.8 %collective-permute-done.1.refs_1_ = bf16[592,512]{1,0:T(8,128)(2,1)S(1)} collective-permute-done((bf16[592,512]{1,0:T(8,128)(2,1)S(1)}, bf16[592,512]{1,0:T(8,128)(2,1)S(1)}, u32[]{:S(2)}, u32[]{:S(2)}) %collective-permute-start.1) | collective-permute-done | bytes 606240 | tf_op jit(solution)/shard_map/ppermute | solution.py:41
  23.6 0.0 collective-permute-start.3
  24.4 0.1 stack.32.scalars
  24.5 0.1 fusion.refs_11_
  24.7 0.5 collective-permute-start.5
  25.2 4.6 %collective-permute-done.4.refs_5_ = bf16[592,256]{1,0:T(8,128)(2,1)} collective-permute-done((bf16[592,256]{1,0:T(8,128)(2,1)S(1)}, bf16[592,256]{1,0:T(8,128)(2,1)}, u32[]{:S(2)}, u32[]{:S(2)}) %collective-permute-start.4) | collective-permute-done | bytes 303136 | tf_op jit(solution)/shard_map/ppermute | solution.py:41
  29.8 0.0 collective-permute-start.6
  29.8 0.3 fusion.2
  30.1 0.0 collective-permute-done.5.refs_6_
  30.1 0.0 collective-permute-done.2.refs_2_
  30.1 1.5 %collective-permute-done.6.refs_7_ = bf16[592,256]{1,0:T(8,128)(2,1)S(1)} collective-permute-done((bf16[592,256]{1,0:T(8,128)(2,1)}, bf16[592,256]{1,0:T(8,128)(2,1)S(1)}, u32[]{:S(2)}, u32[]{:S(2)}) %collective-permute-start.6) | collective-permute-done | bytes 303136 | tf_op jit(solution)/shard_map/ppermute | solution.py:42
  31.6 9.9 %head.1 = (bf16[592,1536]{1,0:T(8,128)(2,1)S(1)}, bf16[592,512]{1,0:T(8,128)(2,1)S(1)}, f32[256,512]{1,0:T(8,128)S(1)}, f32[24,512]{1,0:T(8,128)S(1)}, f32[440,512]{1,0:T(8,128)S(1)}, /*index=5*/f32[440,512]{1,0:T(8,128)S(1)}) custom-call(s32[7]{0:T(128)S(1)} %stack.32.scalars, bf16[592,512]{1,0:T(8,128)(2,1)S(1)} %slice_select_fusion.1.refs_0_, ...), custom_call_target="tpu_custom_call" | custom-call | tf_op jit(solution)/shard_map/head/pallas_call | solution.py:271
  41.5 0.1 convert_element_type.36
  41.6 1.9 %collective-permute-start.7 = (f16[440,512]{1,0:T(8,128)(2,1)S(1)}, f16[440,512]{1,0:T(8,128)(2,1)S(1)}, u32[]{:S(2)}, u32[]{:S(2)}) collective-permute-start(f16[440,512]{1,0:T(8,128)(2,1)S(1)} %convert_element_type.36), channel_id=1, source_target_pairs={{0,1},{1,0},{2,3},{3,2},{4,5},{5,4},{6,7},{7,6},{8,9},{9,8},{10,11... | collective-permute-start | bytes 1351688 | tf_op jit(solution)/shard_map/ppermute | solution.py:352
  43.5 0.1 convert_element_type.37
  43.5 4.6 %collective-permute-start.8 = (f16[440,512]{1,0:T(8,128)(2,1)S(1)}, f16[440,512]{1,0:T(8,128)(2,1)S(1)}, u32[]{:S(2)}, u32[]{:S(2)}) collective-permute-start(f16[440,512]{1,0:T(8,128)(2,1)S(1)} %convert_element_type.37), channel_id=1, source_target_pairs={{0,2},{3,1},{4,6},{7,5},{8,10},{11,9},{12,14},{15,13},{16,18},{19,... | collective-permute-start | bytes 1351688 | tf_op jit(solution)/shard_map/ppermute | solution.py:352
  48.1 0.7 collective-permute-start.9
  48.8 1.4 %blocks.1 = (f32[440,512]{1,0:T(8,128)S(1)}, f32[440,512]{1,0:T(8,128)S(1)}, f32[8,128]{1,0:T(8,128)S(1)}) custom-call(s32[7]{0:T(128)S(1)} %stack.32.scalars, bf16[592,1536]{1,0:T(8,128)(2,1)S(1)} %get-tuple-element.20.x, bf16[592,512]{1,0:T(8,128)(2,1)S(1)} %get-tuple-element.21.dpre, f32[256,512]{1,0:T(8,128)S(1)} %get-tuple-element.22.gout, ...), custom_call_target="tpu_custom_call" | custom-call | flops 465567744 | bytes 4227072 | tf_op jit(solution)/shard_map/blocks/pallas_call | solution.py:396
  50.2 4.0 %collective-permute-done.7 = f16[440,512]{1,0:T(8,128)(2,1)S(1)} collective-permute-done((f16[440,512]{1,0:T(8,128)(2,1)S(1)}, f16[440,512]{1,0:T(8,128)(2,1)S(1)}, u32[]{:S(2)}, u32[]{:S(2)}) %collective-permute-start.7) | collective-permute-done | bytes 450592 | tf_op jit(solution)/shard_map/ppermute | solution.py:352
  54.2 0.1 convert_element_type.38.theirs
  54.3 0.6 add.62
  54.9 0.1 convert_element_type.39
  55.0 2.6 %collective-permute-start.10 = (f16[440,512]{1,0:T(8,128)(2,1)S(1)}, f16[440,512]{1,0:T(8,128)(2,1)S(1)}, u32[]{:S(2)}, u32[]{:S(2)}) collective-permute-start(f16[440,512]{1,0:T(8,128)(2,1)S(1)} %convert_element_type.39), channel_id=1, source_target_pairs={{0,1},{3,2},{1,3},{2,0},{4,5},{7,6},{5,7},{6,4},{8,9},{11,10},{9,1... | collective-permute-start | bytes 1351688 | tf_op jit(solution)/shard_map/ppermute | solution.py:352
  57.6 6.3 %collective-permute-done.8 = f16[440,512]{1,0:T(8,128)(2,1)S(1)} collective-permute-done((f16[440,512]{1,0:T(8,128)(2,1)S(1)}, f16[440,512]{1,0:T(8,128)(2,1)S(1)}, u32[]{:S(2)}, u32[]{:S(2)}) %collective-permute-start.8) | collective-permute-done | bytes 450592 | tf_op jit(solution)/shard_map/ppermute | solution.py:352
  63.9 0.1 select_convert_fusion
  64.0 0.1 convert_element_type.41
  64.2 0.4 multiply_add_fusion.parts
  64.6 14.4 %collective-permute-done.10 = f16[440,512]{1,0:T(8,128)(2,1)S(1)} collective-permute-done((f16[440,512]{1,0:T(8,128)(2,1)S(1)}, f16[440,512]{1,0:T(8,128)(2,1)S(1)}, u32[]{:S(2)}, u32[]{:S(2)}) %collective-permute-start.10) | collective-permute-done | bytes 450592 | tf_op jit(solution)/shard_map/ppermute | solution.py:352
  79.0 0.1 convert_element_type.42.last
  79.1 1.1 %sums.1 = (f32[384,512]{1,0:T(8,128)}, f32[150,1,128]{2,1,0:T(1,128)}, f32[9,1,512]{2,1,0:T(1,128)}, f32[32,128]{1,0:T(8,128)S(1)}) custom-call(f32[440,512]{1,0:T(8,128)S(1)} %multiply_add_fusion.parts, f32[440,512]{1,0:T(8,128)S(1)} %convert_element_type.42.last, f32[8,128]{1,0:T(8,128)S(1)} %get-tuple-element.31.stats), custom_call_target="tpu_custom_call" | custom-call | tf_op jit(solution)/shard_map/sums/pallas_call | solution.py:468
  80.2 0.0 collective-permute-start.11
  80.2 3.7 %collective-permute-done.11 = f32[32,128]{1,0:T(8,128)S(1)} collective-permute-done((f32[32,128]{1,0:T(8,128)S(1)}, f32[32,128]{1,0:T(8,128)S(1)}, u32[]{:S(2)}, u32[]{:S(2)}) %collective-permute-start.11) | collective-permute-done | bytes 16416 | tf_op jit(solution)/shard_map/ppermute | solution.py:352
  83.9 1.2 %collective-permute-start.12 = (f32[32,128]{1,0:T(8,128)S(1)}, f32[32,128]{1,0:T(8,128)S(1)}, u32[]{:S(2)}, u32[]{:S(2)}) collective-permute-start(f32[32,128]{1,0:T(8,128)S(1)} %add.56), channel_id=1, source_target_pairs={{0,2},{1,3},{2,0},{3,1},{4,6},{5,7},{6,4},{7,5},{8,10},{9,11},{10,... | collective-permute-start | bytes 49160 | tf_op jit(solution)/shard_map/ppermute | solution.py:352
  85.1 3.5 %collective-permute-done.12 = f32[32,128]{1,0:T(8,128)S(1)} collective-permute-done((f32[32,128]{1,0:T(8,128)S(1)}, f32[32,128]{1,0:T(8,128)S(1)}, u32[]{:S(2)}, u32[]{:S(2)}) %collective-permute-start.12) | collective-permute-done | bytes 16416 | tf_op jit(solution)/shard_map/ppermute | solution.py:352
  88.6 0.7 norms.1
  (16 shorter events, 0.1 us)
Async XLA Ops:
  0.6 4.4 %copy-start.2 = (bf16[1,1,592,1536]{3,2,1,0:T(8,128)(2,1)S(1)}, bf16[1,1,592,1536]{3,2,1,0:T(8,128)(2,1)}, u32[]{:S(2)}) copy-start(bf16[1,1,592,1536]{3,2,1,0:T(8,128)(2,1)} %param.7) | copy-start | bytes 5455876
  2.3 2.7 %collective-permute-start = (bf16[592,768]{1,0:T(8,128)(2,1)S(1)}, bf16[592,768]{1,0:T(8,128)(2,1)}, u32[]{:S(2)}, u32[]{:S(2)}) collective-permute-start(bf16[592,768]{1,0:T(8,128)(2,1)S(1)} %slice_select_fusion), channel_id=1, source_target_pairs={{0,4},{4,0},{8,12},{12,8},{1,5},{5,1},{9,13},{13,9},{2,6},{6,2},{1... | collective-permute-start | bytes 2727944 | tf_op jit(solution)/shard_map/ppermute | solution.py:34
  3.5 20.8 %copy-start.4 = (s32[1,592]{1,0:T(1,128)S(1)}, s32[1,592]{1,0:T(1,128)}, u32[]{:S(2)}) copy-start(s32[1,592]{1,0:T(1,128)} %param.10) | copy-start | bytes 7108
  3.5 20.9 %copy-start.3 = (bf16[1,512,150]{1,2,0:T(8,128)(2,1)S(1)}, bf16[1,512,150]{1,2,0:T(8,128)(2,1)}, u32[]{:S(2)}) copy-start(bf16[1,512,150]{1,2,0:T(8,128)(2,1)} %param.13) | copy-start | bytes 460804
  6.2 25.3 %copy-start = (bf16[1,1536,512]{2,1,0:T(8,128)(2,1)S(1)}, bf16[1,1536,512]{2,1,0:T(8,128)(2,1)}, u32[]{:S(2)}) copy-start(bf16[1,1536,512]{2,1,0:T(8,128)(2,1)} %param.11) | copy-start | bytes 4718596
  6.2 25.3 %copy-start.1 = (f32[1,9,512]{2,0,1:T(1,128)S(1)}, f32[1,9,512]{2,0,1:T(1,128)}, u32[]{:S(2)}) copy-start(f32[1,9,512]{2,0,1:T(1,128)} %param.12) | copy-start | bytes 55300
  6.3 17.4 %collective-permute-start.1 = (bf16[592,512]{1,0:T(8,128)(2,1)S(1)}, bf16[592,512]{1,0:T(8,128)(2,1)S(1)}, u32[]{:S(2)}, u32[]{:S(2)}) collective-permute-start(bf16[592,512]{1,0:T(8,128)(2,1)S(1)} %slice_select_fusion.1.refs_0_), channel_id=1, source_target_pairs={{0,8},{8,0},{4,12},{12,4},{1,9},{9,1},{5,13},{13,5},{2,10},{10,2},... | collective-permute-start | bytes 1818632 | tf_op jit(solution)/shard_map/ppermute | solution.py:41
  9.2 20.9 %collective-permute-start.2 = (bf16[592,512]{1,0:T(8,128)(2,1)S(1)}, bf16[592,512]{1,0:T(8,128)(2,1)}, u32[]{:S(2)}, u32[]{:S(2)}) collective-permute-start(bf16[592,512]{1,0:T(8,128)(2,1)S(1)} %slice_select_fusion.1.refs_0_), channel_id=1, source_target_pairs={{0,4},{4,0},{8,12},{12,8},{1,5},{5,1},{9,13},{13,9},{2,6},{6,2},{1... | collective-permute-start | bytes 1818632 | tf_op jit(solution)/shard_map/ppermute | solution.py:42
  10.4 19.4 %collective-permute-start.4 = (bf16[592,256]{1,0:T(8,128)(2,1)S(1)}, bf16[592,256]{1,0:T(8,128)(2,1)}, u32[]{:S(2)}, u32[]{:S(2)}) collective-permute-start(bf16[592,256]{1,0:T(8,128)(2,1)S(1)} %slice_select_fusion.3.refs_4_), channel_id=1, source_target_pairs={{0,8},{8,0},{4,12},{12,4},{1,9},{9,1},{5,13},{13,5},{2,10},{10,2},... | collective-permute-start | bytes 909320 | tf_op jit(solution)/shard_map/ppermute | solution.py:41
  23.6 7.9 %collective-permute-start.3 = (bf16[592,512]{1,0:T(8,128)(2,1)S(1)}, bf16[592,512]{1,0:T(8,128)(2,1)}, u32[]{:S(2)}, u32[]{:S(2)}) collective-permute-start(bf16[592,512]{1,0:T(8,128)(2,1)S(1)} %collective-permute-done.1.refs_1_), channel_id=1, source_target_pairs={{0,4},{4,0},{8,12},{12,8},{1,5},{5,1},{9,13},{13,9},{2,6},{6,2},{1... | collective-permute-start | bytes 1818632 | tf_op jit(solution)/shard_map/ppermute | solution.py:42
  24.7 5.4 %collective-permute-start.5 = (bf16[592,256]{1,0:T(8,128)(2,1)S(1)}, bf16[592,256]{1,0:T(8,128)(2,1)S(1)}, u32[]{:S(2)}, u32[]{:S(2)}) collective-permute-start(bf16[592,256]{1,0:T(8,128)(2,1)S(1)} %slice_select_fusion.3.refs_4_), channel_id=1, source_target_pairs={{0,4},{4,0},{8,12},{12,8},{1,5},{5,1},{9,13},{13,9},{2,6},{6,2},{1... | collective-permute-start | bytes 909320 | tf_op jit(solution)/shard_map/ppermute | solution.py:42
  29.8 1.8 %collective-permute-start.6 = (bf16[592,256]{1,0:T(8,128)(2,1)}, bf16[592,256]{1,0:T(8,128)(2,1)S(1)}, u32[]{:S(2)}, u32[]{:S(2)}) collective-permute-start(bf16[592,256]{1,0:T(8,128)(2,1)} %collective-permute-done.4.refs_5_), channel_id=1, source_target_pairs={{0,4},{4,0},{8,12},{12,8},{1,5},{5,1},{9,13},{13,9},{2,6},{6,2},{1... | collective-permute-start | bytes 909320 | tf_op jit(solution)/shard_map/ppermute | solution.py:42
  41.6 12.6 %collective-permute-start.7 = (f16[440,512]{1,0:T(8,128)(2,1)S(1)}, f16[440,512]{1,0:T(8,128)(2,1)S(1)}, u32[]{:S(2)}, u32[]{:S(2)}) collective-permute-start(f16[440,512]{1,0:T(8,128)(2,1)S(1)} %convert_element_type.36), channel_id=1, source_target_pairs={{0,1},{1,0},{2,3},{3,2},{4,5},{5,4},{6,7},{7,6},{8,9},{9,8},{10,11... | collective-permute-start | bytes 1351688 | tf_op jit(solution)/shard_map/ppermute | solution.py:352
  43.5 20.4 %collective-permute-start.8 = (f16[440,512]{1,0:T(8,128)(2,1)S(1)}, f16[440,512]{1,0:T(8,128)(2,1)S(1)}, u32[]{:S(2)}, u32[]{:S(2)}) collective-permute-start(f16[440,512]{1,0:T(8,128)(2,1)S(1)} %convert_element_type.37), channel_id=1, source_target_pairs={{0,2},{3,1},{4,6},{7,5},{8,10},{11,9},{12,14},{15,13},{16,18},{19,... | collective-permute-start | bytes 1351688 | tf_op jit(solution)/shard_map/ppermute | solution.py:352
  48.1 15.8 %collective-permute-start.9 = (f16[440,512]{1,0:T(8,128)(2,1)S(1)}, f16[440,512]{1,0:T(8,128)(2,1)S(1)}, u32[]{:S(2)}, u32[]{:S(2)}) collective-permute-start(f16[440,512]{1,0:T(8,128)(2,1)S(1)} %convert_element_type.37), channel_id=1, source_target_pairs={{1,2},{2,1},{5,6},{6,5},{9,10},{10,9},{13,14},{14,13},{17,18},{18,... | collective-permute-start | bytes 1351688 | tf_op jit(solution)/shard_map/ppermute | solution.py:352
  55.0 24.0 %collective-permute-start.10 = (f16[440,512]{1,0:T(8,128)(2,1)S(1)}, f16[440,512]{1,0:T(8,128)(2,1)S(1)}, u32[]{:S(2)}, u32[]{:S(2)}) collective-permute-start(f16[440,512]{1,0:T(8,128)(2,1)S(1)} %convert_element_type.39), channel_id=1, source_target_pairs={{0,1},{3,2},{1,3},{2,0},{4,5},{7,6},{5,7},{6,4},{8,9},{11,10},{9,1... | collective-permute-start | bytes 1351688 | tf_op jit(solution)/shard_map/ppermute | solution.py:352
  80.2 3.7 %collective-permute-start.11 = (f32[32,128]{1,0:T(8,128)S(1)}, f32[32,128]{1,0:T(8,128)S(1)}, u32[]{:S(2)}, u32[]{:S(2)}) collective-permute-start(f32[32,128]{1,0:T(8,128)S(1)} %get-tuple-element.35.line), channel_id=1, source_target_pairs={{0,1},{1,0},{2,3},{3,2},{4,5},{5,4},{6,7},{7,6},{8,9},{9,8},{10,11... | collective-permute-start | bytes 49160 | tf_op jit(solution)/shard_map/ppermute | solution.py:352
  83.9 4.6 %collective-permute-start.12 = (f32[32,128]{1,0:T(8,128)S(1)}, f32[32,128]{1,0:T(8,128)S(1)}, u32[]{:S(2)}, u32[]{:S(2)}) collective-permute-start(f32[32,128]{1,0:T(8,128)S(1)} %add.56), channel_id=1, source_target_pairs={{0,2},{1,3},{2,0},{3,1},{4,6},{5,7},{6,4},{7,5},{8,10},{9,11},{10,... | collective-permute-start | bytes 49160 | tf_op jit(solution)/shard_map/ppermute | solution.py:352

commit v8 on v7

--- a/solution.py
+++ b/solution.py
@@ -10,7 +10,8 @@
 
 PC = 37
 LANES = 128
-STEP = 32
+FORWARD_STEP = 64
+BACKWARD_STEP = 64
 REACH = 4
 OFFSETS = [(a, b) for a in (-1, 0, 1) for b in (-1, 0, 1)]
 X_LIMIT = 6.0
@@ -71,8 +72,8 @@
 ):
     halves, refs = refs[: 4 * len(widths)], refs[4 * len(widths) :]
     weight_in, taps, weight_out, onehot, after, before = refs[:6]
-    x_out, dpre_out, gout, small, first, early = refs[6:12]
-    x_vmem, pre, dys, slope, hid, dlog, sem_in, sem_out = refs[12:]
+    x_vmem, dpre_out, gout, small, first, early = refs[6:12]
+    pre, dys, slope, hid, dlog, sem_in = refs[12:]
     rows = x_vmem.shape[0]
     width = x_vmem.shape[1] // 2
     hidden = weight_in.shape[1]
@@ -100,8 +101,6 @@
     for index in range(len(widths)):
         fetch(0, index).wait()
         fetch(2, index).wait()
-    save = pltpu.make_async_copy(x_vmem, x_out, sem_out)
-    save.start()
 
     for n in range(hidden // 256):
         value = jnp.dot(
@@ -132,15 +131,17 @@
             slope[c, pl.ds(row, count), :] = grad
             hid[pl.ds(row, count), LANES * c : LANES * c + LANES] = act.astype(jnp.bfloat16)
 
-    whole = rows // STEP
-    left = rows - whole * STEP
-
-    @pl.loop(0, whole)
-    def _(i):
-        forward(pl.multiple_of(i * STEP, STEP), STEP)
-
-    if left:
-        forward(whole * STEP, left)
+    def run(step, body):
+        whole = rows // step
+
+        @pl.loop(0, whole)
+        def _(i):
+            body(pl.multiple_of(i * step, step), step)
+
+        if rows > whole * step:
+            body(whole * step, rows - whole * step)
+
+    run(FORWARD_STEP, forward)
 
     logits = lax.dot_general(
         hid[...], weight_out[...], (((1,), (1,)), ((), ())), preferred_element_type=jnp.float32
@@ -189,14 +190,16 @@
             return tuple(out), jnp.maximum(top, size)
 
         zeros = tuple(jnp.zeros((8, LANES), jnp.float32) for _ in range(9))
+        step = BACKWARD_STEP
+        whole = rows // step
         carry = lax.fori_loop(
             0,
             whole,
-            lambda i, carry: backward(pl.multiple_of(i * STEP, STEP), STEP, carry),
+            lambda i, carry, step=step: backward(pl.multiple_of(i * step, step), step, carry),
             (zeros, biggest),
         )
-        if left:
-            carry = backward(whole * STEP, left, carry)
+        if rows > whole * step:
+            carry = backward(whole * step, rows - whole * step, carry)
         sums, biggest = carry
         for k in range(9):
             value = jnp.sum(sums[k], axis=0, keepdims=True)
@@ -217,7 +220,6 @@
         norm = message(sizes, scalars[3], x_vmem, dpre_out, gout, small, first, True)
         norm = norm + message(sizes, scalars[4], x_vmem, dpre_out, gout, small, early, True)
         small[18:19, :LANES] = norm
-    save.wait()
 
 
 def message(sizes, place, x, dpre, gout, small, out, scaled):
@@ -278,16 +280,14 @@
         ]
         + [jax.ShapeDtypeStruct((sizes.message if sizes.staged else 8, hidden), jnp.float32)] * 2,
         in_specs=[pl.BlockSpec(memory_space=pltpu.SMEM)] + [anywhere] * len(halves) + [vmem] * 6,
-        out_specs=[anywhere] + [vmem] * 5,
+        out_specs=[vmem] * 6,
         scratch_shapes=[
-            pltpu.VMEM((rows, wide), jnp.bfloat16),
             pltpu.VMEM((chunks, span, LANES), jnp.float32),
             pltpu.VMEM((chunks, span, LANES), jnp.float32),
             pltpu.VMEM((chunks, rows, LANES), jnp.float32),
             pltpu.VMEM((rows, hidden), jnp.bfloat16),
             pltpu.VMEM((rows, 256), jnp.bfloat16),
             pltpu.SemaphoreType.DMA((len(widths), 2)),
-            pltpu.SemaphoreType.DMA,
         ],
         compiler_params=pltpu.CompilerParams(vmem_limit_bytes=24 * 1024 * 1024),
         name="head",
@@ -304,34 +304,44 @@
         stats[2 + c : 3 + c, :] = small[17:18, LANES * c : LANES * c + LANES]
 
 
-def sum_kernel(sizes, parts, last, stats, share_in, share_out, taps_out, line):
-    depth, chunks = sizes.depth, sizes.chunks
-
+def totals(sizes, parts, last):
+    mark = sizes.depth + sizes.group
+    spans = ((0, sizes.depth), (sizes.depth, mark), (mark, mark + 9))
+    return [
+        parts[start:stop, :] + last[start:stop, :] * jnp.exp2(-last[mark + 9 + i : mark + 10 + i, :])
+        for i, (start, stop) in enumerate(spans)
+    ]
+
+
+def line_kernel(sizes, parts, last, stats, line):
     def fold(value):
         value = jnp.sum(value.reshape(-1, 8, value.shape[1]), axis=0)
-        return sum(value[:, LANES * c : LANES * c + LANES] for c in range(value.shape[1] // LANES))
-
-    mark = depth + sizes.group
-    factors = [jnp.exp2(-last[mark + 9 + i : mark + 10 + i, :]) for i in range(3)]
-    total = parts[:depth, :] + last[:depth, :] * factors[0]
-    share_in[...] = total
-    line[0:8, :] = fold(total * total)
-    total = parts[depth:mark, :] + last[depth:mark, :] * factors[1]
-    line[8:16, :] = fold(total * total)
+        return sum(value[:, LANES * c : LANES * c + LANES] for c in range(sizes.chunks))
+
+    sum_in, sum_out, sum_taps = totals(sizes, parts, last)
+    line[0:8, :] = fold(sum_in * sum_in)
+    line[8:16, :] = fold(sum_out * sum_out)
+    line[16:24, :] = stats[...]
+    line[24:32, :] = jnp.zeros((8, LANES), jnp.float32)
+    square = jnp.sum(sum_taps * sum_taps, axis=0, keepdims=True)
+    line[24:25, :] = sum(square[:, LANES * c : LANES * c + LANES] for c in range(sizes.chunks))
+
+
+def sum_kernel(sizes, parts, last, share_in, share_out, taps_out):
+    sum_in, sum_out, sum_taps = totals(sizes, parts, last)
+    share_in[...] = sum_in
     for start, group in sizes.groups:
         lane = start // sizes.group * LANES
         count = min(group, sizes.classes - start)
-        share_out[start : start + count, 0, :] = total[:count, lane : lane + LANES]
-    total = parts[mark : mark + 9, :] + last[mark : mark + 9, :] * factors[2]
-    square = jnp.sum(total * total, axis=0, keepdims=True)
+        share_out[start : start + count, 0, :] = sum_out[:count, lane : lane + LANES]
     for k in range(9):
-        taps_out[k, :, :] = total[k : k + 1, :]
-    line[16:24, :] = stats[...]
-    line[24:32, :] = jnp.zeros((8, LANES), jnp.float32)
-    line[24:25, :] = sum(square[:, LANES * c : LANES * c + LANES] for c in range(chunks))
-
-
-def norm_kernel(chunks, line, total, out):
+        taps_out[k, :, :] = sum_taps[k : k + 1, :]
+
+
+def norm_kernel(chunks, *refs):
+    lines, out = refs[:-1], refs[-1]
+    total = sum(line[...] for line in lines)
+    line = lines[0]
     values = [
         jnp.sum(total[16:17, :]),
         jnp.sum(total[17:18, :]),
@@ -465,30 +475,39 @@
     parts, last, stats = staged_sums(sizes, me, scalars, xrows, dpre, gout, small, first, early)
     vmem = pl.BlockSpec(memory_space=pltpu.VMEM)
     hidden = dpre.shape[1]
-    share_in, share_out, total_taps, line = pl.pallas_call(
+    small = pltpu.CompilerParams(vmem_limit_bytes=8 * 1024 * 1024)
+    line = pl.pallas_call(
+        functools.partial(line_kernel, sizes),
+        out_shape=jax.ShapeDtypeStruct((32, LANES), jnp.float32),
+        in_specs=[vmem] * 3,
+        out_specs=vmem,
+        compiler_params=small,
+        name="line",
+    )(parts, last, stats)
+    lines = [line] + [permute(line, [(i, i ^ s) for i in range(dp)]) for s in range(1, dp)]
+    share_in, share_out, total_taps = pl.pallas_call(
         functools.partial(sum_kernel, sizes),
         out_shape=[
             jax.ShapeDtypeStruct((sizes.depth, hidden), jnp.float32),
             jax.ShapeDtypeStruct((classes, 1, sizes.depth_out), jnp.float32),
             jax.ShapeDtypeStruct((9, 1, hidden), jnp.float32),
-            jax.ShapeDtypeStruct((32, LANES), jnp.float32),
         ],
-        in_specs=[vmem] * 3,
-        out_specs=[vmem] * 4,
-        compiler_params=pltpu.CompilerParams(vmem_limit_bytes=8 * 1024 * 1024),
+        in_specs=[vmem] * 2,
+        out_specs=[vmem] * 3,
+        compiler_params=small,
+        cost_estimate=pl.CostEstimate(
+            flops=2 * parts.size, bytes_accessed=16 * parts.size, transcendentals=0
+        ),
         name="sums",
-    )(parts, last, stats)
-    total = line
-    for step in (1, 2):
-        total = total + permute(total, [(i, i ^ step) for i in range(dp)])
+    )(parts, last)
     norms = pl.pallas_call(
         functools.partial(norm_kernel, chunks),
         out_shape=jax.ShapeDtypeStruct((2, 3), jnp.float32),
-        in_specs=[vmem] * 2,
+        in_specs=[vmem] * dp,
         out_specs=vmem,
         compiler_params=pltpu.CompilerParams(vmem_limit_bytes=4 * 1024 * 1024),
         name="norms",
-    )(line, total)
+    )(*lines)
     share_out = jnp.transpose(share_out, (1, 2, 0))
     return (share_in[None], jnp.transpose(total_taps, (1, 0, 2)), share_out, norms[None])
 

time: 89.6 us -> 88.3 us (0.985)
  waiting for transfers between devices: 52.2 us -> 48.7 us
  starting transfers between devices: 15.3 us -> 18.4 us
    ppermute x6 -> x7, waiting for transfers between devices: 31.9 us -> 28.3 us  [permute(): return lax.ppermute(value, 'dp', pairs)]
    ppermute x6 -> x7, starting transfers between devices: 10.9 us -> 14 us  [permute(): return lax.ppermute(value, 'dp', pairs)]
    pallas_call x1, Pallas kernels: 9.92 us -> 8.91 us  [head_backward(): pl.pallas_call(functools.partial(head_kernel, sizes, widths), out_shape=[...]
  transfers between devices with their start and end apart: 13 -> 14, of which waited for: 9 -> 8; matrix products, arithmetic and copies ran while one was open for 3% -> 3% of each run, Pallas kernels for 2% -> 3%
where the time goes in v8:
time: 88.3 us; the launch traced here: 88 us
  waiting for transfers between devices  48.7 us (55%)
  starting transfers between devices  18.4 us (21%)
  Pallas kernels  12.9 us (15%)
  other arithmetic  5.59 us (6%)
  between operations  2.31 us (3%)
    ppermute x7, waiting for transfers between devices, permute(): return lax.ppermute(value, 'dp', pairs)  28.3 us
    ppermute x2, waiting for transfers between devices, pieces(): other = lax.ppermute(held, axis, across)  17.4 us
    ppermute x7, starting transfers between devices, permute(): return lax.ppermute(value, 'dp', pairs)  14 us
    pallas_call x1, Pallas kernels, head_backward(): pl.pallas_call(functools.partial(head_kernel, sizes, widths), out_shape=[...  8.91 us
    ppermute x2, starting transfers between devices, pieces(): other = lax.ppermute(held, axis, across)  3.35 us
    select_n x2, other arithmetic, pieces(): held = jnp.where(source % 2 == core, kept, got[:, at:at + piece])  2.35 us
  transfers between devices with their start and end apart: 14, of which 8 were waited for; matrix products, arithmetic and copies ran while one was open for 3% of the time, Pallas kernels for 3%

profile of v8, /device:TPU:0, one launch (start us, length us, event | category | flops | bytes accessed | tf_op | source)
XLA Modules:
  0.0 88.0 jit_solution(5351957722466288833)
XLA Ops:
  0.6 0.0 copy-start.2
  0.7 1.7 %slice_select_fusion = bf16[592,768]{1,0:T(8,128)(2,1)S(1)} fusion(bf16[592,1536]{1,0:T(8,128)(2,1)} %bitcast.30, pred[]{:T(512)S(6)} %eq.50), kind=kLoop, calls=%fused_computation | loop fusion | flops 454656 | bytes 2727937 | tf_op jit(solution)/shard_map/jit(_where)/select_n | solution.py:35
  2.3 0.5 collective-permute-start
  3.5 0.0 copy-start.4
  3.5 0.0 copy-start.3
  3.6 1.5 %collective-permute-done = bf16[592,768]{1,0:T(8,128)(2,1)} collective-permute-done((bf16[592,768]{1,0:T(8,128)(2,1)S(1)}, bf16[592,768]{1,0:T(8,128)(2,1)}, u32[]{:S(2)}, u32[]{:S(2)}) %collective-permute-start) | collective-permute-done | bytes 909344 | tf_op jit(solution)/shard_map/ppermute | solution.py:35
  5.1 1.2 %slice_select_fusion.1.refs_0_ = bf16[592,512]{1,0:T(8,128)(2,1)S(1)} fusion(bf16[592,768]{1,0:T(8,128)(2,1)} %collective-permute-done, bf16[592,1536]{1,0:T(8,128)(2,1)S(1)} %bitcast.32, pred[]{:T(512)S(6)} %eq.50, pred[]{:T(512)S(6)} %eq.49), kind=kLoop, calls=%fused_computation.2 | loop fusion | flops 606208 | bytes 2424834 | tf_op jit(solution)/shard_map/jit(_where)/select_n | solution.py:41
  6.2 0.0 copy-start
  6.2 0.0 copy-start.1
  6.3 2.9 %collective-permute-start.1 = (bf16[592,512]{1,0:T(8,128)(2,1)S(1)}, bf16[592,512]{1,0:T(8,128)(2,1)S(1)}, u32[]{:S(2)}, u32[]{:S(2)}) collective-permute-start(bf16[592,512]{1,0:T(8,128)(2,1)S(1)} %slice_select_fusion.1.refs_0_), channel_id=1, source_target_pairs={{0,8},{8,0},{4,12},{12,4},{1,9},{9,1},{5,13},{13,5},{2,10},{10,2},... | collective-permute-start | bytes 1818632 | tf_op jit(solution)/shard_map/ppermute | solution.py:42
  9.2 1.2 %slice_select_fusion.3.refs_4_ = bf16[592,256]{1,0:T(8,128)(2,1)S(1)} fusion(bf16[592,768]{1,0:T(8,128)(2,1)} %collective-permute-done, bf16[592,1536]{1,0:T(8,128)(2,1)} %bitcast.31, pred[]{:T(512)S(6)} %eq.50, pred[]{:T(512)S(6)} %eq.49), kind=kLoop, calls=%fused_computation.9 | loop fusion | flops 303104 | bytes 1212418 | tf_op jit(solution)/shard_map/jit(_where)/select_n | solution.py:41
  10.4 0.4 collective-permute-start.4
  10.8 12.8 %collective-permute-done.1.refs_1_ = bf16[592,512]{1,0:T(8,128)(2,1)S(1)} collective-permute-done((bf16[592,512]{1,0:T(8,128)(2,1)S(1)}, bf16[592,512]{1,0:T(8,128)(2,1)S(1)}, u32[]{:S(2)}, u32[]{:S(2)}) %collective-permute-start.1) | collective-permute-done | bytes 606240 | tf_op jit(solution)/shard_map/ppermute | solution.py:42
  24.5 0.1 stack.32.scalars
  24.5 0.1 fusion.refs_11_
  24.7 0.5 collective-permute-start.5
  25.2 4.6 %collective-permute-done.4.refs_5_ = bf16[592,256]{1,0:T(8,128)(2,1)} collective-permute-done((bf16[592,256]{1,0:T(8,128)(2,1)S(1)}, bf16[592,256]{1,0:T(8,128)(2,1)}, u32[]{:S(2)}, u32[]{:S(2)}) %collective-permute-start.4) | collective-permute-done | bytes 303136 | tf_op jit(solution)/shard_map/ppermute | solution.py:42
  29.8 0.3 fusion.2
  30.1 0.0 collective-permute-done.2.refs_2_
  30.1 1.5 %collective-permute-done.6.refs_7_ = bf16[592,256]{1,0:T(8,128)(2,1)S(1)} collective-permute-done((bf16[592,256]{1,0:T(8,128)(2,1)}, bf16[592,256]{1,0:T(8,128)(2,1)S(1)}, u32[]{:S(2)}, u32[]{:S(2)}) %collective-permute-start.6) | collective-permute-done | bytes 303136 | tf_op jit(solution)/shard_map/ppermute | solution.py:43
  31.6 8.9 %head.1 = (bf16[592,1536]{1,0:T(8,128)(2,1)S(1)}, bf16[592,512]{1,0:T(8,128)(2,1)S(1)}, f32[256,512]{1,0:T(8,128)S(1)}, f32[24,512]{1,0:T(8,128)S(1)}, f32[440,512]{1,0:T(8,128)S(1)}, /*index=5*/f32[440,512]{1,0:T(8,128)S(1)}) custom-call(s32[7]{0:T(128)S(1)} %stack.32.scalars, bf16[592,512]{1,0:T(8,128)(2,1)S(1)} %slice_select_fusion.1.refs_0_, ...), custom_call_target="tpu_custom_call" | custom-call | tf_op jit(solution)/shard_map/head/pallas_call | solution.py:273
  40.5 0.1 convert_element_type.36
  40.6 2.0 %collective-permute-start.7 = (f16[440,512]{1,0:T(8,128)(2,1)S(1)}, f16[440,512]{1,0:T(8,128)(2,1)S(1)}, u32[]{:S(2)}, u32[]{:S(2)}) collective-permute-start(f16[440,512]{1,0:T(8,128)(2,1)S(1)} %convert_element_type.36), channel_id=1, source_target_pairs={{0,1},{1,0},{2,3},{3,2},{4,5},{5,4},{6,7},{7,6},{8,9},{9,8},{10,11... | collective-permute-start | bytes 1351688 | tf_op jit(solution)/shard_map/ppermute | solution.py:362
  42.5 0.1 convert_element_type.37
  42.6 4.4 %collective-permute-start.8 = (f16[440,512]{1,0:T(8,128)(2,1)S(1)}, f16[440,512]{1,0:T(8,128)(2,1)S(1)}, u32[]{:S(2)}, u32[]{:S(2)}) collective-permute-start(f16[440,512]{1,0:T(8,128)(2,1)S(1)} %convert_element_type.37), channel_id=1, source_target_pairs={{0,2},{3,1},{4,6},{7,5},{8,10},{11,9},{12,14},{15,13},{16,18},{19,... | collective-permute-start | bytes 1351688 | tf_op jit(solution)/shard_map/ppermute | solution.py:362
  47.0 0.7 collective-permute-start.9
  47.7 1.4 %blocks.1 = (f32[440,512]{1,0:T(8,128)S(1)}, f32[440,512]{1,0:T(8,128)S(1)}, f32[8,128]{1,0:T(8,128)S(1)}) custom-call(s32[7]{0:T(128)S(1)} %stack.32.scalars, bf16[592,1536]{1,0:T(8,128)(2,1)S(1)} %get-tuple-element.19.x, bf16[592,512]{1,0:T(8,128)(2,1)S(1)} %get-tuple-element.20.dpre, f32[256,512]{1,0:T(8,128)S(1)} %get-tuple-element.21.gout, ...), custom_call_target="tpu_custom_call" | custom-call | flops 465567744 | bytes 4227072 | tf_op jit(solution)/shard_map/blocks/pallas_call | solution.py:406
  49.1 4.2 %collective-permute-done.7 = f16[440,512]{1,0:T(8,128)(2,1)S(1)} collective-permute-done((f16[440,512]{1,0:T(8,128)(2,1)S(1)}, f16[440,512]{1,0:T(8,128)(2,1)S(1)}, u32[]{:S(2)}, u32[]{:S(2)}) %collective-permute-start.7) | collective-permute-done | bytes 450592 | tf_op jit(solution)/shard_map/ppermute | solution.py:362
  53.3 0.1 convert_element_type.38.theirs
  53.4 0.6 add.54
  54.1 0.1 convert_element_type.39
  54.1 2.5 %collective-permute-start.10 = (f16[440,512]{1,0:T(8,128)(2,1)S(1)}, f16[440,512]{1,0:T(8,128)(2,1)S(1)}, u32[]{:S(2)}, u32[]{:S(2)}) collective-permute-start(f16[440,512]{1,0:T(8,128)(2,1)S(1)} %convert_element_type.39), channel_id=1, source_target_pairs={{0,1},{3,2},{1,3},{2,0},{4,5},{7,6},{5,7},{6,4},{8,9},{11,10},{9,1... | collective-permute-start | bytes 1351688 | tf_op jit(solution)/shard_map/ppermute | solution.py:362
  56.6 6.3 %collective-permute-done.8 = f16[440,512]{1,0:T(8,128)(2,1)S(1)} collective-permute-done((f16[440,512]{1,0:T(8,128)(2,1)S(1)}, f16[440,512]{1,0:T(8,128)(2,1)S(1)}, u32[]{:S(2)}, u32[]{:S(2)}) %collective-permute-start.8) | collective-permute-done | bytes 450592 | tf_op jit(solution)/shard_map/ppermute | solution.py:362
  62.9 0.0 collective-permute-done.9
  62.9 0.1 select_convert_fusion
  63.1 0.1 convert_element_type.41
  63.2 0.4 multiply_add_fusion.parts
  63.6 14.5 %collective-permute-done.10 = f16[440,512]{1,0:T(8,128)(2,1)S(1)} collective-permute-done((f16[440,512]{1,0:T(8,128)(2,1)S(1)}, f16[440,512]{1,0:T(8,128)(2,1)S(1)}, u32[]{:S(2)}, u32[]{:S(2)}) %collective-permute-start.10) | collective-permute-done | bytes 450592 | tf_op jit(solution)/shard_map/ppermute | solution.py:362
  78.1 0.1 convert_element_type.42.last
  78.2 0.3 line.1.refs_0_
  78.5 0.1 collective-permute-start.11
  78.6 3.2 %collective-permute-start.12 = (f32[32,128]{1,0:T(8,128)S(1)}, f32[32,128]{1,0:T(8,128)S(1)}, u32[]{:S(2)}, u32[]{:S(2)}) collective-permute-start(f32[32,128]{1,0:T(8,128)S(1)} %line.1.refs_0_), channel_id=1, source_target_pairs={{0,2},{1,3},{2,0},{3,1},{4,6},{5,7},{6,4},{7,5},{8,10},{9,11},{10,... | collective-permute-start | bytes 49160 | tf_op jit(solution)/shard_map/ppermute | solution.py:362
  81.8 1.2 %collective-permute-start.13 = (f32[32,128]{1,0:T(8,128)S(1)}, f32[32,128]{1,0:T(8,128)S(1)}, u32[]{:S(2)}, u32[]{:S(2)}) collective-permute-start(f32[32,128]{1,0:T(8,128)S(1)} %line.1.refs_0_), channel_id=1, source_target_pairs={{0,3},{1,2},{2,1},{3,0},{4,7},{5,6},{6,5},{7,4},{8,11},{9,10},{10,... | collective-permute-start | bytes 49160 | tf_op jit(solution)/shard_map/ppermute | solution.py:362
  83.0 1.0 %sums.1 = (f32[384,512]{1,0:T(8,128)}, f32[150,1,128]{2,1,0:T(1,128)}, f32[9,1,512]{2,1,0:T(1,128)}) custom-call(f32[440,512]{1,0:T(8,128)S(1)} %multiply_add_fusion.parts, f32[440,512]{1,0:T(8,128)S(1)} %convert_element_type.42.last), custom_call_target="tpu_custom_call" | custom-call | flops 450560 | bytes 3604480 | tf_op jit(solution)/shard_map/sums/pallas_call | solution.py:488
  84.0 0.0 collective-permute-done.11.refs_1_
  84.0 0.0 collective-permute-done.12.refs_2_
  84.0 3.3 %collective-permute-done.13.refs_3_ = f32[32,128]{1,0:T(8,128)S(1)} collective-permute-done((f32[32,128]{1,0:T(8,128)S(1)}, f32[32,128]{1,0:T(8,128)S(1)}, u32[]{:S(2)}, u32[]{:S(2)}) %collective-permute-start.13) | collective-permute-done | bytes 16416 | tf_op jit(solution)/shard_map/ppermute | solution.py:362
  87.3 0.7 norms.1
  (17 shorter events, 0.1 us)
Async XLA Ops:
  0.6 4.4 %copy-start.2 = (bf16[1,1,592,1536]{3,2,1,0:T(8,128)(2,1)S(1)}, bf16[1,1,592,1536]{3,2,1,0:T(8,128)(2,1)}, u32[]{:S(2)}) copy-start(bf16[1,1,592,1536]{3,2,1,0:T(8,128)(2,1)} %param.7) | copy-start | bytes 5455876
  2.3 2.7 %collective-permute-start = (bf16[592,768]{1,0:T(8,128)(2,1)S(1)}, bf16[592,768]{1,0:T(8,128)(2,1)}, u32[]{:S(2)}, u32[]{:S(2)}) collective-permute-start(bf16[592,768]{1,0:T(8,128)(2,1)S(1)} %slice_select_fusion), channel_id=1, source_target_pairs={{0,4},{4,0},{8,12},{12,8},{1,5},{5,1},{9,13},{13,9},{2,6},{6,2},{1... | collective-permute-start | bytes 2727944 | tf_op jit(solution)/shard_map/ppermute | solution.py:35
  3.5 20.9 %copy-start.4 = (s32[1,592]{1,0:T(1,128)S(1)}, s32[1,592]{1,0:T(1,128)}, u32[]{:S(2)}) copy-start(s32[1,592]{1,0:T(1,128)} %param.10) | copy-start | bytes 7108
  3.5 20.9 %copy-start.3 = (bf16[1,512,150]{1,2,0:T(8,128)(2,1)S(1)}, bf16[1,512,150]{1,2,0:T(8,128)(2,1)}, u32[]{:S(2)}) copy-start(bf16[1,512,150]{1,2,0:T(8,128)(2,1)} %param.13) | copy-start | bytes 460804
  6.2 25.3 %copy-start = (bf16[1,1536,512]{2,1,0:T(8,128)(2,1)S(1)}, bf16[1,1536,512]{2,1,0:T(8,128)(2,1)}, u32[]{:S(2)}) copy-start(bf16[1,1536,512]{2,1,0:T(8,128)(2,1)} %param.11) | copy-start | bytes 4718596
  6.2 25.3 %copy-start.1 = (f32[1,9,512]{2,0,1:T(1,128)S(1)}, f32[1,9,512]{2,0,1:T(1,128)}, u32[]{:S(2)}) copy-start(f32[1,9,512]{2,0,1:T(1,128)} %param.12) | copy-start | bytes 55300
  6.3 17.4 %collective-permute-start.1 = (bf16[592,512]{1,0:T(8,128)(2,1)S(1)}, bf16[592,512]{1,0:T(8,128)(2,1)S(1)}, u32[]{:S(2)}, u32[]{:S(2)}) collective-permute-start(bf16[592,512]{1,0:T(8,128)(2,1)S(1)} %slice_select_fusion.1.refs_0_), channel_id=1, source_target_pairs={{0,8},{8,0},{4,12},{12,4},{1,9},{9,1},{5,13},{13,5},{2,10},{10,2},... | collective-permute-start | bytes 1818632 | tf_op jit(solution)/shard_map/ppermute | solution.py:42
  9.2 20.9 %collective-permute-start.2 = (bf16[592,512]{1,0:T(8,128)(2,1)S(1)}, bf16[592,512]{1,0:T(8,128)(2,1)}, u32[]{:S(2)}, u32[]{:S(2)}) collective-permute-start(bf16[592,512]{1,0:T(8,128)(2,1)S(1)} %slice_select_fusion.1.refs_0_), channel_id=1, source_target_pairs={{0,4},{4,0},{8,12},{12,8},{1,5},{5,1},{9,13},{13,9},{2,6},{6,2},{1... | collective-permute-start | bytes 1818632 | tf_op jit(solution)/shard_map/ppermute | solution.py:43
  10.4 19.4 %collective-permute-start.4 = (bf16[592,256]{1,0:T(8,128)(2,1)S(1)}, bf16[592,256]{1,0:T(8,128)(2,1)}, u32[]{:S(2)}, u32[]{:S(2)}) collective-permute-start(bf16[592,256]{1,0:T(8,128)(2,1)S(1)} %slice_select_fusion.3.refs_4_), channel_id=1, source_target_pairs={{0,8},{8,0},{4,12},{12,4},{1,9},{9,1},{5,13},{13,5},{2,10},{10,2},... | collective-permute-start | bytes 909320 | tf_op jit(solution)/shard_map/ppermute | solution.py:42
  23.6 7.9 %collective-permute-start.3 = (bf16[592,512]{1,0:T(8,128)(2,1)S(1)}, bf16[592,512]{1,0:T(8,128)(2,1)}, u32[]{:S(2)}, u32[]{:S(2)}) collective-permute-start(bf16[592,512]{1,0:T(8,128)(2,1)S(1)} %collective-permute-done.1.refs_1_), channel_id=1, source_target_pairs={{0,4},{4,0},{8,12},{12,8},{1,5},{5,1},{9,13},{13,9},{2,6},{6,2},{1... | collective-permute-start | bytes 1818632 | tf_op jit(solution)/shard_map/ppermute | solution.py:43
  24.7 5.4 %collective-permute-start.5 = (bf16[592,256]{1,0:T(8,128)(2,1)S(1)}, bf16[592,256]{1,0:T(8,128)(2,1)S(1)}, u32[]{:S(2)}, u32[]{:S(2)}) collective-permute-start(bf16[592,256]{1,0:T(8,128)(2,1)S(1)} %slice_select_fusion.3.refs_4_), channel_id=1, source_target_pairs={{0,4},{4,0},{8,12},{12,8},{1,5},{5,1},{9,13},{13,9},{2,6},{6,2},{1... | collective-permute-start | bytes 909320 | tf_op jit(solution)/shard_map/ppermute | solution.py:43
  29.8 1.8 %collective-permute-start.6 = (bf16[592,256]{1,0:T(8,128)(2,1)}, bf16[592,256]{1,0:T(8,128)(2,1)S(1)}, u32[]{:S(2)}, u32[]{:S(2)}) collective-permute-start(bf16[592,256]{1,0:T(8,128)(2,1)} %collective-permute-done.4.refs_5_), channel_id=1, source_target_pairs={{0,4},{4,0},{8,12},{12,8},{1,5},{5,1},{9,13},{13,9},{2,6},{6,2},{1... | collective-permute-start | bytes 909320 | tf_op jit(solution)/shard_map/ppermute | solution.py:43
  40.6 12.8 %collective-permute-start.7 = (f16[440,512]{1,0:T(8,128)(2,1)S(1)}, f16[440,512]{1,0:T(8,128)(2,1)S(1)}, u32[]{:S(2)}, u32[]{:S(2)}) collective-permute-start(f16[440,512]{1,0:T(8,128)(2,1)S(1)} %convert_element_type.36), channel_id=1, source_target_pairs={{0,1},{1,0},{2,3},{3,2},{4,5},{5,4},{6,7},{7,6},{8,9},{9,8},{10,11... | collective-permute-start | bytes 1351688 | tf_op jit(solution)/shard_map/ppermute | solution.py:362
  42.6 20.3 %collective-permute-start.8 = (f16[440,512]{1,0:T(8,128)(2,1)S(1)}, f16[440,512]{1,0:T(8,128)(2,1)S(1)}, u32[]{:S(2)}, u32[]{:S(2)}) collective-permute-start(f16[440,512]{1,0:T(8,128)(2,1)S(1)} %convert_element_type.37), channel_id=1, source_target_pairs={{0,2},{3,1},{4,6},{7,5},{8,10},{11,9},{12,14},{15,13},{16,18},{19,... | collective-permute-start | bytes 1351688 | tf_op jit(solution)/shard_map/ppermute | solution.py:362
  47.0 15.9 %collective-permute-start.9 = (f16[440,512]{1,0:T(8,128)(2,1)S(1)}, f16[440,512]{1,0:T(8,128)(2,1)S(1)}, u32[]{:S(2)}, u32[]{:S(2)}) collective-permute-start(f16[440,512]{1,0:T(8,128)(2,1)S(1)} %convert_element_type.37), channel_id=1, source_target_pairs={{1,2},{2,1},{5,6},{6,5},{9,10},{10,9},{13,14},{14,13},{17,18},{18,... | collective-permute-start | bytes 1351688 | tf_op jit(solution)/shard_map/ppermute | solution.py:362
  54.1 24.0 %collective-permute-start.10 = (f16[440,512]{1,0:T(8,128)(2,1)S(1)}, f16[440,512]{1,0:T(8,128)(2,1)S(1)}, u32[]{:S(2)}, u32[]{:S(2)}) collective-permute-start(f16[440,512]{1,0:T(8,128)(2,1)S(1)} %convert_element_type.39), channel_id=1, source_target_pairs={{0,1},{3,2},{1,3},{2,0},{4,5},{7,6},{5,7},{6,4},{8,9},{11,10},{9,1... | collective-permute-start | bytes 1351688 | tf_op jit(solution)/shard_map/ppermute | solution.py:362
  78.5 5.5 %collective-permute-start.11 = (f32[32,128]{1,0:T(8,128)S(1)}, f32[32,128]{1,0:T(8,128)S(1)}, u32[]{:S(2)}, u32[]{:S(2)}) collective-permute-start(f32[32,128]{1,0:T(8,128)S(1)} %line.1.refs_0_), channel_id=1, source_target_pairs={{0,1},{1,0},{2,3},{3,2},{4,5},{5,4},{6,7},{7,6},{8,9},{9,8},{10,11... | collective-permute-start | bytes 49160 | tf_op jit(solution)/shard_map/ppermute | solution.py:362
  78.6 5.4 %collective-permute-start.12 = (f32[32,128]{1,0:T(8,128)S(1)}, f32[32,128]{1,0:T(8,128)S(1)}, u32[]{:S(2)}, u32[]{:S(2)}) collective-permute-start(f32[32,128]{1,0:T(8,128)S(1)} %line.1.refs_0_), channel_id=1, source_target_pairs={{0,2},{1,3},{2,0},{3,1},{4,6},{5,7},{6,4},{7,5},{8,10},{9,11},{10,... | collective-permute-start | bytes 49160 | tf_op jit(solution)/shard_map/ppermute | solution.py:362
  81.8 5.5 %collective-permute-start.13 = (f32[32,128]{1,0:T(8,128)S(1)}, f32[32,128]{1,0:T(8,128)S(1)}, u32[]{:S(2)}, u32[]{:S(2)}) collective-permute-start(f32[32,128]{1,0:T(8,128)S(1)} %line.1.refs_0_), channel_id=1, source_target_pairs={{0,3},{1,2},{2,1},{3,0},{4,7},{5,6},{6,5},{7,4},{8,11},{9,10},{10,... | collective-permute-start | bytes 49160 | tf_op jit(solution)/shard_map/ppermute | solution.py:362

commit v9 on v8

--- a/solution.py
+++ b/solution.py
@@ -304,21 +304,24 @@
         stats[2 + c : 3 + c, :] = small[17:18, LANES * c : LANES * c + LANES]
 
 
-def totals(sizes, parts, last):
+def totals(sizes, parts, messages):
     mark = sizes.depth + sizes.group
     spans = ((0, sizes.depth), (sizes.depth, mark), (mark, mark + 9))
-    return [
-        parts[start:stop, :] + last[start:stop, :] * jnp.exp2(-last[mark + 9 + i : mark + 10 + i, :])
-        for i, (start, stop) in enumerate(spans)
-    ]
-
-
-def line_kernel(sizes, parts, last, stats, line):
+    sums = []
+    for i, (start, stop) in enumerate(spans):
+        total = parts[start:stop, :]
+        for value in messages:
+            total = total + value[start:stop, :] * jnp.exp2(-value[mark + 9 + i : mark + 10 + i, :])
+        sums.append(total)
+    return sums
+
+
+def line_kernel(sizes, parts, far, edge, stats, line):
     def fold(value):
         value = jnp.sum(value.reshape(-1, 8, value.shape[1]), axis=0)
         return sum(value[:, LANES * c : LANES * c + LANES] for c in range(sizes.chunks))
 
-    sum_in, sum_out, sum_taps = totals(sizes, parts, last)
+    sum_in, sum_out, sum_taps = totals(sizes, parts, (far, edge))
     line[0:8, :] = fold(sum_in * sum_in)
     line[8:16, :] = fold(sum_out * sum_out)
     line[16:24, :] = stats[...]
@@ -327,8 +330,8 @@
     line[24:25, :] = sum(square[:, LANES * c : LANES * c + LANES] for c in range(sizes.chunks))
 
 
-def sum_kernel(sizes, parts, last, share_in, share_out, taps_out):
-    sum_in, sum_out, sum_taps = totals(sizes, parts, last)
+def sum_kernel(sizes, parts, far, edge, share_in, share_out, taps_out):
+    sum_in, sum_out, sum_taps = totals(sizes, parts, (far, edge))
     share_in[...] = sum_in
     for start, group in sizes.groups:
         lane = start // sizes.group * LANES
@@ -402,7 +405,6 @@
     near = permute(first.astype(half), [(0, 1), (1, 0), (2, 3), (3, 2)])
     early = early.astype(half)
     middle = permute(early, [(1, 2), (2, 1)])
-    skip = permute(early, [(0, 2), (3, 1)])
     late, own, stats = pl.pallas_call(
         functools.partial(blocks_kernel, sizes),
         out_shape=[full, full, lines],
@@ -427,19 +429,15 @@
         name="add",
     )(scalars, late, near.astype(jnp.float32))
     both = both.astype(half)
-    near, skip, middle, _ = lax.optimization_barrier((near, skip, middle, both))
-    far = permute(both, [(0, 1), (3, 2), (1, 3), (2, 0)])
-
-    def split(value):
-        return [value[mark + i : mark + i + 1] for i in range(3)]
-
-
-    def decode(value):
-        value = value.astype(jnp.float32)
-        return value * by_row(sizes, shape, [jnp.exp2(-v) for v in split(value)])
-
-    parts = own + decode(jnp.where(end, near, skip)) + decode(middle)
-    return parts, far.astype(jnp.float32), stats
+    far = permute(both, [(0, 2), (2, 0), (1, 3), (3, 1)])
+    early, _ = lax.optimization_barrier((early, both))
+    near, middle, _ = lax.optimization_barrier((near, middle, both))
+    edge = permute(early, [(0, 1), (3, 2)])
+    value = jnp.where(end, near, middle).astype(jnp.float32)
+    parts = own + value * by_row(
+        sizes, shape, [jnp.exp2(-value[mark + i : mark + i + 1]) for i in range(3)]
+    )
+    return parts, far.astype(jnp.float32), edge.astype(jnp.float32), stats
 
 
 def per_device(sizes, dp, trials, features, owner, dilation_index, labels, input_weight, taps, output_weight):
@@ -455,9 +453,8 @@
     weight_out = jnp.pad(output_weight[0].T, ((0, 256 - classes), (0, 0)))
     high = me >= 2
     odd = me % 2
-    end = (me == 0) | (me == 3)
     step, jump = jnp.where(odd == 0, 1, 2), jnp.where(high, me - 2, me + 2)
-    to = [3 * (1 - odd), jnp.where(end, jump, step), jnp.where(end, step, jump), me]
+    to = [3 * (1 - odd), step, jump, me]
     scalars = jnp.stack([dil, here, core] + to).astype(jnp.int32)
     xrows, dpre, gout, small, first, early = head_backward(
         sizes,
@@ -472,18 +469,18 @@
     )
     if not sizes.staged:
         return general_sums(sizes, xrows, dpre, gout, small)
-    parts, last, stats = staged_sums(sizes, me, scalars, xrows, dpre, gout, small, first, early)
+    parts, far, edge, stats = staged_sums(sizes, me, scalars, xrows, dpre, gout, small, first, early)
     vmem = pl.BlockSpec(memory_space=pltpu.VMEM)
     hidden = dpre.shape[1]
     small = pltpu.CompilerParams(vmem_limit_bytes=8 * 1024 * 1024)
     line = pl.pallas_call(
         functools.partial(line_kernel, sizes),
         out_shape=jax.ShapeDtypeStruct((32, LANES), jnp.float32),
-        in_specs=[vmem] * 3,
+        in_specs=[vmem] * 4,
         out_specs=vmem,
         compiler_params=small,
         name="line",
-    )(parts, last, stats)
+    )(parts, far, edge, stats)
     lines = [line] + [permute(line, [(i, i ^ s) for i in range(dp)]) for s in range(1, dp)]
     share_in, share_out, total_taps = pl.pallas_call(
         functools.partial(sum_kernel, sizes),
@@ -492,14 +489,14 @@
             jax.ShapeDtypeStruct((classes, 1, sizes.depth_out), jnp.float32),
             jax.ShapeDtypeStruct((9, 1, hidden), jnp.float32),
         ],
-        in_specs=[vmem] * 2,
+        in_specs=[vmem] * 3,
         out_specs=[vmem] * 3,
         compiler_params=small,
         cost_estimate=pl.CostEstimate(
             flops=2 * parts.size, bytes_accessed=16 * parts.size, transcendentals=0
         ),
         name="sums",
-    )(parts, last)
+    )(parts, far, edge)
     norms = pl.pallas_call(
         functools.partial(norm_kernel, chunks),
         out_shape=jax.ShapeDtypeStruct((2, 3), jnp.float32),

time: 88.3 us -> 94.2 us (1.067)
  local copies, waits for them, and re-layouts: 0.14 us -> 9.27 us
  waiting for transfers between devices: 48.7 us -> 45.3 us
    unnamed x10 -> x34, local copies, waits for them, and re-layouts: 0.03 us -> 9.16 us
    ppermute x7, waiting for transfers between devices: 28.3 us -> 26 us  [permute(): return lax.ppermute(value, 'dp', pairs)]
    ppermute x2, waiting for transfers between devices: 1.46 us -> 0.43 us  [pieces(): lax.ppermute(other, axis, mate)]
  transfers between devices with their start and end apart: 14 -> 14, of which waited for: 8 -> 9; matrix products, arithmetic and copies ran while one was open for 3% -> 3% of each run, Pallas kernels for 3% -> 3%
where the time goes in v9:
time: 94.2 us; the launch traced here: 93.7 us
  waiting for transfers between devices  45.3 us (48%)
  starting transfers between devices  18.3 us (19%)
  Pallas kernels  12.2 us (13%)
  local copies, waits for them, and re-layouts  9.27 us (10%)
  other arithmetic  6.25 us (7%)
  between operations  2.36 us (3%)
    ppermute x7, waiting for transfers between devices, permute(): return lax.ppermute(value, 'dp', pairs)  26 us
    ppermute x2, waiting for transfers between devices, pieces(): other = lax.ppermute(held, axis, across)  17.4 us
    ppermute x7, starting transfers between devices, permute(): return lax.ppermute(value, 'dp', pairs)  14.1 us
    unnamed x34, local copies, waits for them, and re-layouts  9.16 us
    pallas_call x1, Pallas kernels, head_backward(): pl.pallas_call(functools.partial(head_kernel, sizes, widths), out_shape=[...  8.09 us
    ppermute x2, starting transfers between devices, pieces(): other = lax.ppermute(held, axis, across)  3.22 us
    select_n x2, other arithmetic, pieces(): held = jnp.where(source % 2 == core, kept, got[:, at:at + piece])  2.35 us
  transfers between devices with their start and end apart: 14, of which 9 were waited for; matrix products, arithmetic and copies ran while one was open for 3% of the time, Pallas kernels for 3%

profile of v9, /device:TPU:0, one launch (start us, length us, event | category | flops | bytes accessed | tf_op | source)
XLA Modules:
  0.0 93.7 jit_solution(10107485839738843746)
XLA Ops:
  0.7 1.7 %slice_select_fusion = bf16[592,768]{1,0:T(8,128)(2,1)S(1)} fusion(bf16[592,1536]{1,0:T(8,128)(2,1)} %bitcast.27, pred[]{:T(512)S(6)} %eq.46), kind=kLoop, calls=%fused_computation | loop fusion | flops 454656 | bytes 2727937 | tf_op jit(solution)/shard_map/jit(_where)/select_n | solution.py:35
  2.3 0.5 collective-permute-start
  3.6 1.5 %collective-permute-done = bf16[592,768]{1,0:T(8,128)(2,1)} collective-permute-done((bf16[592,768]{1,0:T(8,128)(2,1)S(1)}, bf16[592,768]{1,0:T(8,128)(2,1)}, u32[]{:S(2)}, u32[]{:S(2)}) %collective-permute-start) | collective-permute-done | bytes 909344 | tf_op jit(solution)/shard_map/ppermute | solution.py:35
  5.1 1.2 %slice_select_fusion.1.refs_0_ = bf16[592,512]{1,0:T(8,128)(2,1)S(1)} fusion(bf16[592,768]{1,0:T(8,128)(2,1)} %collective-permute-done, bf16[592,1536]{1,0:T(8,128)(2,1)S(1)} %bitcast.29, pred[]{:T(512)S(6)} %eq.46, pred[]{:T(512)S(6)} %eq.45), kind=kLoop, calls=%fused_computation.2 | loop fusion | flops 606208 | bytes 2424834 | tf_op jit(solution)/shard_map/jit(_where)/select_n | solution.py:41
  6.2 2.9 %collective-permute-start.1 = (bf16[592,512]{1,0:T(8,128)(2,1)S(1)}, bf16[592,512]{1,0:T(8,128)(2,1)S(1)}, u32[]{:S(2)}, u32[]{:S(2)}) collective-permute-start(bf16[592,512]{1,0:T(8,128)(2,1)S(1)} %slice_select_fusion.1.refs_0_), channel_id=1, source_target_pairs={{0,8},{8,0},{4,12},{12,4},{1,9},{9,1},{5,13},{13,5},{2,10},{10,2},... | collective-permute-start | bytes 1818632 | tf_op jit(solution)/shard_map/ppermute | solution.py:42
  9.2 1.2 %slice_select_fusion.3.refs_4_ = bf16[592,256]{1,0:T(8,128)(2,1)S(1)} fusion(bf16[592,768]{1,0:T(8,128)(2,1)} %collective-permute-done, bf16[592,1536]{1,0:T(8,128)(2,1)} %bitcast.28, pred[]{:T(512)S(6)} %eq.46, pred[]{:T(512)S(6)} %eq.45), kind=kLoop, calls=%fused_computation.9 | loop fusion | flops 303104 | bytes 1212418 | tf_op jit(solution)/shard_map/jit(_where)/select_n | solution.py:41
  10.4 0.3 collective-permute-start.4
  10.7 13.0 %collective-permute-done.1.refs_1_ = bf16[592,512]{1,0:T(8,128)(2,1)S(1)} collective-permute-done((bf16[592,512]{1,0:T(8,128)(2,1)S(1)}, bf16[592,512]{1,0:T(8,128)(2,1)S(1)}, u32[]{:S(2)}, u32[]{:S(2)}) %collective-permute-start.1) | collective-permute-done | bytes 606240 | tf_op jit(solution)/shard_map/ppermute | solution.py:42
  24.5 0.1 stack.32.scalars
  24.6 0.1 fusion.refs_11_
  24.7 0.5 collective-permute-start.5
  25.2 4.4 %collective-permute-done.4.refs_5_ = bf16[592,256]{1,0:T(8,128)(2,1)S(1)} collective-permute-done((bf16[592,256]{1,0:T(8,128)(2,1)S(1)}, bf16[592,256]{1,0:T(8,128)(2,1)S(1)}, u32[]{:S(2)}, u32[]{:S(2)}) %collective-permute-start.4) | collective-permute-done | bytes 303136 | tf_op jit(solution)/shard_map/ppermute | solution.py:42
  29.7 0.3 fusion.2
  30.0 0.8 copy-done.3
  30.8 0.4 collective-permute-done.6.refs_7_
  31.2 0.9 copy-done.5
  32.1 1.4 %copy-done = bf16[1,1536,512]{2,1,0:T(8,128)(2,1)S(1)} copy-done((bf16[1,1536,512]{2,1,0:T(8,128)(2,1)S(1)}, bf16[1,1536,512]{2,1,0:T(8,128)(2,1)}, u32[]{:S(2)}) %copy-start) | copy-done | bytes 1572888
  33.5 1.1 %copy-done.2 = bf16[592,512]{1,0:T(8,128)(2,1)S(1)} copy-done((bf16[592,512]{1,0:T(8,128)(2,1)S(1)}, bf16[592,512]{1,0:T(8,128)(2,1)}, u32[]{:S(2)}) %copy-start.2) | copy-done | bytes 606232
  34.6 1.1 %copy-done.4 = bf16[592,512]{1,0:T(8,128)(2,1)S(1)} copy-done((bf16[592,512]{1,0:T(8,128)(2,1)S(1)}, bf16[592,512]{1,0:T(8,128)(2,1)}, u32[]{:S(2)}) %copy-start.4) | copy-done | bytes 606232
  35.7 1.1 %copy-done.6 = bf16[592,512]{1,0:T(8,128)(2,1)S(1)} copy-done((bf16[592,512]{1,0:T(8,128)(2,1)S(1)}, bf16[592,512]{1,0:T(8,128)(2,1)}, u32[]{:S(2)}) %copy-start.6) | copy-done | bytes 606232
  36.7 1.0 %copy-done.10 = bf16[592,256]{1,0:T(8,128)(2,1)S(1)} copy-done((bf16[592,256]{1,0:T(8,128)(2,1)S(1)}, bf16[592,256]{1,0:T(8,128)(2,1)}, u32[]{:S(2)}) %copy-start.10) | copy-done | bytes 303128
  37.7 8.1 %head.1 = (bf16[592,1536]{1,0:T(8,128)(2,1)S(1)}, bf16[592,512]{1,0:T(8,128)(2,1)S(1)}, f32[256,512]{1,0:T(8,128)S(1)}, f32[24,512]{1,0:T(8,128)S(1)}, f32[440,512]{1,0:T(8,128)S(1)}, /*index=5*/f32[440,512]{1,0:T(8,128)S(1)}) custom-call(s32[7]{0:T(128)S(1)} %stack.32.scalars, bf16[592,512]{1,0:T(8,128)(2,1)S(1)} %slice_select_fusion.1.refs_0_, ...), custom_call_target="tpu_custom_call" | custom-call | tf_op jit(solution)/shard_map/head/pallas_call | solution.py:273
  45.8 0.9 convert_element_type.36
  46.7 1.8 %collective-permute-start.7 = (f16[440,512]{1,0:T(8,128)(2,1)}, f16[440,512]{1,0:T(8,128)(2,1)S(1)}, u32[]{:S(2)}, u32[]{:S(2)}) collective-permute-start(f16[440,512]{1,0:T(8,128)(2,1)} %convert_element_type.36), channel_id=1, source_target_pairs={{0,1},{1,0},{2,3},{3,2},{4,5},{5,4},{6,7},{7,6},{8,9},{9,8},{10,11... | collective-permute-start | bytes 1351688 | tf_op jit(solution)/shard_map/ppermute | solution.py:365
  48.6 1.4 %collective-permute-start.8 = (f16[440,512]{1,0:T(8,128)(2,1)S(1)}, f16[440,512]{1,0:T(8,128)(2,1)}, u32[]{:S(2)}, u32[]{:S(2)}) collective-permute-start(f16[440,512]{1,0:T(8,128)(2,1)S(1)} %convert_element_type.37), channel_id=1, source_target_pairs={{1,2},{2,1},{5,6},{6,5},{9,10},{10,9},{13,14},{14,13},{17,18},{18,... | collective-permute-start | bytes 1351688 | tf_op jit(solution)/shard_map/ppermute | solution.py:365
  50.1 1.1 %copy-done.8 = bf16[592,512]{1,0:T(8,128)(2,1)S(1)} copy-done((bf16[592,512]{1,0:T(8,128)(2,1)S(1)}, bf16[592,512]{1,0:T(8,128)(2,1)}, u32[]{:S(2)}) %copy-start.8) | copy-done | bytes 606232
  51.2 0.8 copy-done.12
  52.0 1.4 %blocks.1 = (f32[440,512]{1,0:T(8,128)S(1)}, f32[440,512]{1,0:T(8,128)S(1)}, f32[8,128]{1,0:T(8,128)S(1)}) custom-call(s32[7]{0:T(128)S(1)} %stack.32.scalars, bf16[592,1536]{1,0:T(8,128)(2,1)S(1)} %get-tuple-element.19.x, bf16[592,512]{1,0:T(8,128)(2,1)S(1)} %copy-done.8, f32[256,512]{1,0:T(8,128)S(1)} %get-tuple-element.21.gout, f32[24,512]{1,0:T(8,128)S(1)} %copy-done.12), custom_call_target="tpu_custom_call" | custom-call | flops 465567744 | bytes 4227072 | tf_op jit(solution)/shard_map/blocks/pallas_call | solution.py:408
  53.3 6.1 %collective-permute-done.7 = f16[440,512]{1,0:T(8,128)(2,1)S(1)} collective-permute-done((f16[440,512]{1,0:T(8,128)(2,1)}, f16[440,512]{1,0:T(8,128)(2,1)S(1)}, u32[]{:S(2)}, u32[]{:S(2)}) %collective-permute-start.7) | collective-permute-done | bytes 450592 | tf_op jit(solution)/shard_map/ppermute | solution.py:365
  59.5 0.1 convert_element_type.38.theirs
  59.6 0.6 add.49
  60.2 0.1 convert_element_type.39
  60.3 2.9 %collective-permute-start.9 = (f16[440,512]{1,0:T(8,128)(2,1)S(1)}, f16[440,512]{1,0:T(8,128)(2,1)S(1)}, u32[]{:S(2)}, u32[]{:S(2)}) collective-permute-start(f16[440,512]{1,0:T(8,128)(2,1)S(1)} %convert_element_type.39), channel_id=1, source_target_pairs={{0,2},{2,0},{1,3},{3,1},{4,6},{6,4},{5,7},{7,5},{8,10},{10,8},{9,1... | collective-permute-start | bytes 1351688 | tf_op jit(solution)/shard_map/ppermute | solution.py:365
  63.2 3.4 %collective-permute-start.10 = (f16[440,512]{1,0:T(8,128)(2,1)S(1)}, f16[440,512]{1,0:T(8,128)(2,1)S(1)}, u32[]{:S(2)}, u32[]{:S(2)}) collective-permute-start(f16[440,512]{1,0:T(8,128)(2,1)S(1)} %convert_element_type.37), channel_id=1, source_target_pairs={{0,1},{3,2},{4,5},{7,6},{8,9},{11,10},{12,13},{15,14},{16,17},{19,... | collective-permute-start | bytes 1351688 | tf_op jit(solution)/shard_map/ppermute | solution.py:365
  66.6 0.1 select_convert_fusion
  66.8 0.2 multiply_add_fusion.parts
  67.0 15.1 %collective-permute-done.10 = f16[440,512]{1,0:T(8,128)(2,1)S(1)} collective-permute-done((f16[440,512]{1,0:T(8,128)(2,1)S(1)}, f16[440,512]{1,0:T(8,128)(2,1)S(1)}, u32[]{:S(2)}, u32[]{:S(2)}) %collective-permute-start.10) | collective-permute-done | bytes 450592 | tf_op jit(solution)/shard_map/ppermute | solution.py:365
  82.1 0.1 convert_element_type.42.edge
  82.3 0.6 collective-permute-done.9
  82.9 0.1 convert_element_type.41.far
  83.0 0.4 line.1.refs_0_
  83.4 1.9 %collective-permute-start.11 = (f32[32,128]{1,0:T(8,128)S(1)}, f32[32,128]{1,0:T(8,128)S(1)}, u32[]{:S(2)}, u32[]{:S(2)}) collective-permute-start(f32[32,128]{1,0:T(8,128)S(1)} %line.1.refs_0_), channel_id=1, source_target_pairs={{0,1},{1,0},{2,3},{3,2},{4,5},{5,4},{6,7},{7,6},{8,9},{9,8},{10,11... | collective-permute-start | bytes 49160 | tf_op jit(solution)/shard_map/ppermute | solution.py:365
  85.3 2.1 %collective-permute-start.12 = (f32[32,128]{1,0:T(8,128)S(1)}, f32[32,128]{1,0:T(8,128)S(1)}, u32[]{:S(2)}, u32[]{:S(2)}) collective-permute-start(f32[32,128]{1,0:T(8,128)S(1)} %line.1.refs_0_), channel_id=1, source_target_pairs={{0,2},{1,3},{2,0},{3,1},{4,6},{5,7},{6,4},{7,5},{8,10},{9,11},{10,... | collective-permute-start | bytes 49160 | tf_op jit(solution)/shard_map/ppermute | solution.py:365
  87.5 0.4 collective-permute-start.13
  87.8 1.1 %sums.1 = (f32[384,512]{1,0:T(8,128)}, f32[150,1,128]{2,1,0:T(1,128)}, f32[9,1,512]{2,1,0:T(1,128)}) custom-call(f32[440,512]{1,0:T(8,128)S(1)} %multiply_add_fusion.parts, f32[440,512]{1,0:T(8,128)S(1)} %convert_element_type.41.far, f32[440,512]{1,0:T(8,128)S(1)} %convert_element_type.42.edge), custom_call_target="tpu_custom_call" | custom-call | flops 450560 | bytes 3604480 | tf_op jit(solution)/shard_map/sums/pallas_call | solution.py:485
  88.9 1.0 %collective-permute-done.12.refs_2_ = f32[32,128]{1,0:T(8,128)S(1)} collective-permute-done((f32[32,128]{1,0:T(8,128)S(1)}, f32[32,128]{1,0:T(8,128)S(1)}, u32[]{:S(2)}, u32[]{:S(2)}) %collective-permute-start.12) | collective-permute-done | bytes 16416 | tf_op jit(solution)/shard_map/ppermute | solution.py:365
  89.9 3.0 %collective-permute-done.13.refs_3_ = f32[32,128]{1,0:T(8,128)S(1)} collective-permute-done((f32[32,128]{1,0:T(8,128)S(1)}, f32[32,128]{1,0:T(8,128)S(1)}, u32[]{:S(2)}, u32[]{:S(2)}) %collective-permute-start.13) | collective-permute-done | bytes 16416 | tf_op jit(solution)/shard_map/ppermute | solution.py:365
  93.0 0.7 norms.1
  (40 shorter events, 0.2 us)
Async XLA Ops:
  0.6 4.4 %copy-start.14 = (bf16[1,1,592,1536]{3,2,1,0:T(8,128)(2,1)S(1)}, bf16[1,1,592,1536]{3,2,1,0:T(8,128)(2,1)}, u32[]{:S(2)}) copy-start(bf16[1,1,592,1536]{3,2,1,0:T(8,128)(2,1)} %param.7) | copy-start | bytes 5455876
  2.3 2.7 %collective-permute-start = (bf16[592,768]{1,0:T(8,128)(2,1)S(1)}, bf16[592,768]{1,0:T(8,128)(2,1)}, u32[]{:S(2)}, u32[]{:S(2)}) collective-permute-start(bf16[592,768]{1,0:T(8,128)(2,1)S(1)} %slice_select_fusion), channel_id=1, source_target_pairs={{0,4},{4,0},{8,12},{12,8},{1,5},{5,1},{9,13},{13,9},{2,6},{6,2},{1... | collective-permute-start | bytes 2727944 | tf_op jit(solution)/shard_map/ppermute | solution.py:35
  3.5 20.9 %copy-start.16 = (s32[1,592]{1,0:T(1,128)S(1)}, s32[1,592]{1,0:T(1,128)}, u32[]{:S(2)}) copy-start(s32[1,592]{1,0:T(1,128)} %param.10) | copy-start | bytes 7108
  3.5 20.9 %copy-start.15 = (bf16[1,512,150]{1,2,0:T(8,128)(2,1)S(1)}, bf16[1,512,150]{1,2,0:T(8,128)(2,1)}, u32[]{:S(2)}) copy-start(bf16[1,512,150]{1,2,0:T(8,128)(2,1)} %param.13) | copy-start | bytes 460804
  6.2 25.9 %copy-start.13 = (f32[1,9,512]{2,0,1:T(1,128)S(1)}, f32[1,9,512]{2,0,1:T(1,128)}, u32[]{:S(2)}) copy-start(f32[1,9,512]{2,0,1:T(1,128)} %param.12) | copy-start | bytes 55300
  6.2 17.4 %collective-permute-start.1 = (bf16[592,512]{1,0:T(8,128)(2,1)S(1)}, bf16[592,512]{1,0:T(8,128)(2,1)S(1)}, u32[]{:S(2)}, u32[]{:S(2)}) collective-permute-start(bf16[592,512]{1,0:T(8,128)(2,1)S(1)} %slice_select_fusion.1.refs_0_), channel_id=1, source_target_pairs={{0,8},{8,0},{4,12},{12,4},{1,9},{9,1},{5,13},{13,5},{2,10},{10,2},... | collective-permute-start | bytes 1818632 | tf_op jit(solution)/shard_map/ppermute | solution.py:42
  9.2 20.8 %collective-permute-start.2 = (bf16[592,512]{1,0:T(8,128)(2,1)S(1)}, bf16[592,512]{1,0:T(8,128)(2,1)S(1)}, u32[]{:S(2)}, u32[]{:S(2)}) collective-permute-start(bf16[592,512]{1,0:T(8,128)(2,1)S(1)} %slice_select_fusion.1.refs_0_), channel_id=1, source_target_pairs={{0,4},{4,0},{8,12},{12,8},{1,5},{5,1},{9,13},{13,9},{2,6},{6,2},{1... | collective-permute-start | bytes 1818632 | tf_op jit(solution)/shard_map/ppermute | solution.py:43
  10.4 19.3 %collective-permute-start.4 = (bf16[592,256]{1,0:T(8,128)(2,1)S(1)}, bf16[592,256]{1,0:T(8,128)(2,1)S(1)}, u32[]{:S(2)}, u32[]{:S(2)}) collective-permute-start(bf16[592,256]{1,0:T(8,128)(2,1)S(1)} %slice_select_fusion.3.refs_4_), channel_id=1, source_target_pairs={{0,8},{8,0},{4,12},{12,4},{1,9},{9,1},{5,13},{13,5},{2,10},{10,2},... | collective-permute-start | bytes 909320 | tf_op jit(solution)/shard_map/ppermute | solution.py:42
  23.6 8.5 %copy-start.1 = (bf16[592,512]{1,0:T(8,128)(2,1)}, bf16[592,512]{1,0:T(8,128)(2,1)S(1)}, u32[]{:S(2)}) copy-start(bf16[592,512]{1,0:T(8,128)(2,1)S(1)} %collective-permute-done.1.refs_1_) | copy-start | bytes 1818628
  23.6 7.6 %collective-permute-start.3 = (bf16[592,512]{1,0:T(8,128)(2,1)S(1)}, bf16[592,512]{1,0:T(8,128)(2,1)S(1)}, u32[]{:S(2)}, u32[]{:S(2)}) collective-permute-start(bf16[592,512]{1,0:T(8,128)(2,1)S(1)} %collective-permute-done.1.refs_1_), channel_id=1, source_target_pairs={{0,4},{4,0},{8,12},{12,8},{1,5},{5,1},{9,13},{13,9},{2,6},{6,2},{1... | collective-permute-start | bytes 1818632 | tf_op jit(solution)/shard_map/ppermute | solution.py:43
  24.7 5.3 %collective-permute-start.5 = (bf16[592,256]{1,0:T(8,128)(2,1)S(1)}, bf16[592,256]{1,0:T(8,128)(2,1)S(1)}, u32[]{:S(2)}, u32[]{:S(2)}) collective-permute-start(bf16[592,256]{1,0:T(8,128)(2,1)S(1)} %slice_select_fusion.3.refs_4_), channel_id=1, source_target_pairs={{0,4},{4,0},{8,12},{12,8},{1,5},{5,1},{9,13},{13,9},{2,6},{6,2},{1... | collective-permute-start | bytes 909320 | tf_op jit(solution)/shard_map/ppermute | solution.py:43
  29.6 2.5 %copy-start.9 = (bf16[592,256]{1,0:T(8,128)(2,1)}, bf16[592,256]{1,0:T(8,128)(2,1)S(1)}, u32[]{:S(2)}) copy-start(bf16[592,256]{1,0:T(8,128)(2,1)S(1)} %collective-permute-done.4.refs_5_) | copy-start | bytes 909316
  29.6 1.6 %collective-permute-start.6 = (bf16[592,256]{1,0:T(8,128)(2,1)S(1)}, bf16[592,256]{1,0:T(8,128)(2,1)S(1)}, u32[]{:S(2)}, u32[]{:S(2)}) collective-permute-start(bf16[592,256]{1,0:T(8,128)(2,1)S(1)} %collective-permute-done.4.refs_5_), channel_id=1, source_target_pairs={{0,4},{4,0},{8,12},{12,8},{1,5},{5,1},{9,13},{13,9},{2,6},{6,2},{1... | collective-permute-start | bytes 909320 | tf_op jit(solution)/shard_map/ppermute | solution.py:43
  30.0 0.8 copy-start.3
  31.2 0.9 copy-start.5
  32.1 1.4 %copy-start = (bf16[1,1536,512]{2,1,0:T(8,128)(2,1)S(1)}, bf16[1,1536,512]{2,1,0:T(8,128)(2,1)}, u32[]{:S(2)}) copy-start(bf16[1,1536,512]{2,1,0:T(8,128)(2,1)} %param.11) | copy-start | bytes 4718596
  33.5 1.1 %copy-start.2 = (bf16[592,512]{1,0:T(8,128)(2,1)S(1)}, bf16[592,512]{1,0:T(8,128)(2,1)}, u32[]{:S(2)}) copy-start(bf16[592,512]{1,0:T(8,128)(2,1)} %copy-done.1) | copy-start | bytes 1818628
  34.6 1.1 %copy-start.4 = (bf16[592,512]{1,0:T(8,128)(2,1)S(1)}, bf16[592,512]{1,0:T(8,128)(2,1)}, u32[]{:S(2)}) copy-start(bf16[592,512]{1,0:T(8,128)(2,1)} %copy-done.3) | copy-start | bytes 1818628
  35.7 1.1 %copy-start.6 = (bf16[592,512]{1,0:T(8,128)(2,1)S(1)}, bf16[592,512]{1,0:T(8,128)(2,1)}, u32[]{:S(2)}) copy-start(bf16[592,512]{1,0:T(8,128)(2,1)} %copy-done.5) | copy-start | bytes 1818628
  36.7 1.0 %copy-start.10 = (bf16[592,256]{1,0:T(8,128)(2,1)S(1)}, bf16[592,256]{1,0:T(8,128)(2,1)}, u32[]{:S(2)}) copy-start(bf16[592,256]{1,0:T(8,128)(2,1)} %copy-done.9) | copy-start | bytes 909316
  45.8 2.8 %copy-start.7 = (bf16[592,512]{1,0:T(8,128)(2,1)}, bf16[592,512]{1,0:T(8,128)(2,1)S(1)}, u32[]{:S(2)}) copy-start(bf16[592,512]{1,0:T(8,128)(2,1)S(1)} %get-tuple-element.20.dpre) | copy-start | bytes 1818628
  45.8 2.8 %copy-start.11 = (f32[24,512]{1,0:T(8,128)}, f32[24,512]{1,0:T(8,128)S(1)}, u32[]{:S(2)}) copy-start(f32[24,512]{1,0:T(8,128)S(1)} %get-tuple-element.22.small) | copy-start | bytes 147460
  46.7 12.7 %collective-permute-start.7 = (f16[440,512]{1,0:T(8,128)(2,1)}, f16[440,512]{1,0:T(8,128)(2,1)S(1)}, u32[]{:S(2)}, u32[]{:S(2)}) collective-permute-start(f16[440,512]{1,0:T(8,128)(2,1)} %convert_element_type.36), channel_id=1, source_target_pairs={{0,1},{1,0},{2,3},{3,2},{4,5},{5,4},{6,7},{7,6},{8,9},{9,8},{10,11... | collective-permute-start | bytes 1351688 | tf_op jit(solution)/shard_map/ppermute | solution.py:365
  48.6 18.0 %collective-permute-start.8 = (f16[440,512]{1,0:T(8,128)(2,1)S(1)}, f16[440,512]{1,0:T(8,128)(2,1)}, u32[]{:S(2)}, u32[]{:S(2)}) collective-permute-start(f16[440,512]{1,0:T(8,128)(2,1)S(1)} %convert_element_type.37), channel_id=1, source_target_pairs={{1,2},{2,1},{5,6},{6,5},{9,10},{10,9},{13,14},{14,13},{17,18},{18,... | collective-permute-start | bytes 1351688 | tf_op jit(solution)/shard_map/ppermute | solution.py:365
  50.1 1.1 %copy-start.8 = (bf16[592,512]{1,0:T(8,128)(2,1)S(1)}, bf16[592,512]{1,0:T(8,128)(2,1)}, u32[]{:S(2)}) copy-start(bf16[592,512]{1,0:T(8,128)(2,1)} %copy-done.7) | copy-start | bytes 1818628
  51.2 0.8 copy-start.12
  60.3 22.6 %collective-permute-start.9 = (f16[440,512]{1,0:T(8,128)(2,1)S(1)}, f16[440,512]{1,0:T(8,128)(2,1)S(1)}, u32[]{:S(2)}, u32[]{:S(2)}) collective-permute-start(f16[440,512]{1,0:T(8,128)(2,1)S(1)} %convert_element_type.39), channel_id=1, source_target_pairs={{0,2},{2,0},{1,3},{3,1},{4,6},{6,4},{5,7},{7,5},{8,10},{10,8},{9,1... | collective-permute-start | bytes 1351688 | tf_op jit(solution)/shard_map/ppermute | solution.py:365
  63.2 19.0 %collective-permute-start.10 = (f16[440,512]{1,0:T(8,128)(2,1)S(1)}, f16[440,512]{1,0:T(8,128)(2,1)S(1)}, u32[]{:S(2)}, u32[]{:S(2)}) collective-permute-start(f16[440,512]{1,0:T(8,128)(2,1)S(1)} %convert_element_type.37), channel_id=1, source_target_pairs={{0,1},{3,2},{4,5},{7,6},{8,9},{11,10},{12,13},{15,14},{16,17},{19,... | collective-permute-start | bytes 1351688 | tf_op jit(solution)/shard_map/ppermute | solution.py:365
  83.4 5.5 %collective-permute-start.11 = (f32[32,128]{1,0:T(8,128)S(1)}, f32[32,128]{1,0:T(8,128)S(1)}, u32[]{:S(2)}, u32[]{:S(2)}) collective-permute-start(f32[32,128]{1,0:T(8,128)S(1)} %line.1.refs_0_), channel_id=1, source_target_pairs={{0,1},{1,0},{2,3},{3,2},{4,5},{5,4},{6,7},{7,6},{8,9},{9,8},{10,11... | collective-permute-start | bytes 49160 | tf_op jit(solution)/shard_map/ppermute | solution.py:365
  85.3 4.6 %collective-permute-start.12 = (f32[32,128]{1,0:T(8,128)S(1)}, f32[32,128]{1,0:T(8,128)S(1)}, u32[]{:S(2)}, u32[]{:S(2)}) collective-permute-start(f32[32,128]{1,0:T(8,128)S(1)} %line.1.refs_0_), channel_id=1, source_target_pairs={{0,2},{1,3},{2,0},{3,1},{4,6},{5,7},{6,4},{7,5},{8,10},{9,11},{10,... | collective-permute-start | bytes 49160 | tf_op jit(solution)/shard_map/ppermute | solution.py:365
  87.5 5.5 %collective-permute-start.13 = (f32[32,128]{1,0:T(8,128)S(1)}, f32[32,128]{1,0:T(8,128)S(1)}, u32[]{:S(2)}, u32[]{:S(2)}) collective-permute-start(f32[32,128]{1,0:T(8,128)S(1)} %line.1.refs_0_), channel_id=1, source_target_pairs={{0,3},{1,2},{2,1},{3,0},{4,7},{5,6},{6,5},{7,4},{8,11},{9,10},{10,... | collective-permute-start | bytes 49160 | tf_op jit(solution)/shard_map/ppermute | solution.py:365

commit v10 on v8

--- a/solution.py
+++ b/solution.py
@@ -402,7 +402,6 @@
     near = permute(first.astype(half), [(0, 1), (1, 0), (2, 3), (3, 2)])
     early = early.astype(half)
     middle = permute(early, [(1, 2), (2, 1)])
-    skip = permute(early, [(0, 2), (3, 1)])
     late, own, stats = pl.pallas_call(
         functools.partial(blocks_kernel, sizes),
         out_shape=[full, full, lines],
@@ -427,8 +426,10 @@
         name="add",
     )(scalars, late, near.astype(jnp.float32))
     both = both.astype(half)
-    near, skip, middle, _ = lax.optimization_barrier((near, skip, middle, both))
     far = permute(both, [(0, 1), (3, 2), (1, 3), (2, 0)])
+    early, _ = lax.optimization_barrier((early, both))
+    near, middle, _ = lax.optimization_barrier((near, middle, both))
+    skip = permute(early, [(0, 2), (3, 1)])
 
     def split(value):
         return [value[mark + i : mark + i + 1] for i in range(3)]
@@ -438,7 +439,7 @@
         value = value.astype(jnp.float32)
         return value * by_row(sizes, shape, [jnp.exp2(-v) for v in split(value)])
 
-    parts = own + decode(jnp.where(end, near, skip)) + decode(middle)
+    parts = own + decode(jnp.where(end, near, middle)) + decode(skip)
     return parts, far.astype(jnp.float32), stats
 
 

time: 88.3 us -> 87.9 us (level)
  no operation moved by 1% of the time
where the time goes in v10:
time: 87.9 us
  waiting for transfers between devices  49.2 us (56%)
  starting transfers between devices  17.8 us (20%)
  Pallas kernels  12.9 us (15%)
  other arithmetic  5.59 us (6%)
  between operations  2.31 us (3%)
    ppermute x7, waiting for transfers between devices, permute(): return lax.ppermute(value, 'dp', pairs)  28.8 us
    ppermute x2, waiting for transfers between devices, pieces(): other = lax.ppermute(held, axis, across)  17.4 us
    ppermute x7, starting transfers between devices, permute(): return lax.ppermute(value, 'dp', pairs)  13.4 us
    pallas_call x1, Pallas kernels, head_backward(): pl.pallas_call(functools.partial(head_kernel, sizes, widths), out_shape=[...  8.91 us
    ppermute x2, starting transfers between devices, pieces(): other = lax.ppermute(held, axis, across)  3.35 us
    select_n x2, other arithmetic, pieces(): held = jnp.where(source % 2 == core, kept, got[:, at:at + piece])  2.35 us
  transfers between devices with their start and end apart: 14, of which 8 were waited for; matrix products, arithmetic and copies ran while one was open for 3% of the time, Pallas kernels for 3%

profile of v10, /device:TPU:0, one launch (start us, length us, event | category | flops | bytes accessed | tf_op | source)
XLA Modules:
  0.0 87.9 jit_solution(3500722339099690559)
XLA Ops:
  0.6 0.0 copy-start.2
  0.7 1.7 %slice_select_fusion = bf16[592,768]{1,0:T(8,128)(2,1)S(1)} fusion(bf16[592,1536]{1,0:T(8,128)(2,1)} %bitcast.30, pred[]{:T(512)S(6)} %eq.50), kind=kLoop, calls=%fused_computation | loop fusion | flops 454656 | bytes 2727937 | tf_op jit(solution)/shard_map/jit(_where)/select_n | solution.py:35
  2.3 0.5 collective-permute-start
  3.5 0.0 copy-start.4
  3.5 0.0 copy-start.3
  3.6 1.5 %collective-permute-done = bf16[592,768]{1,0:T(8,128)(2,1)} collective-permute-done((bf16[592,768]{1,0:T(8,128)(2,1)S(1)}, bf16[592,768]{1,0:T(8,128)(2,1)}, u32[]{:S(2)}, u32[]{:S(2)}) %collective-permute-start) | collective-permute-done | bytes 909344 | tf_op jit(solution)/shard_map/ppermute | solution.py:35
  5.1 1.2 %slice_select_fusion.1.refs_0_ = bf16[592,512]{1,0:T(8,128)(2,1)S(1)} fusion(bf16[592,768]{1,0:T(8,128)(2,1)} %collective-permute-done, bf16[592,1536]{1,0:T(8,128)(2,1)S(1)} %bitcast.32, pred[]{:T(512)S(6)} %eq.50, pred[]{:T(512)S(6)} %eq.49), kind=kLoop, calls=%fused_computation.2 | loop fusion | flops 606208 | bytes 2424834 | tf_op jit(solution)/shard_map/jit(_where)/select_n | solution.py:41
  6.2 0.0 copy-start
  6.2 0.0 copy-start.1
  6.3 2.9 %collective-permute-start.1 = (bf16[592,512]{1,0:T(8,128)(2,1)S(1)}, bf16[592,512]{1,0:T(8,128)(2,1)S(1)}, u32[]{:S(2)}, u32[]{:S(2)}) collective-permute-start(bf16[592,512]{1,0:T(8,128)(2,1)S(1)} %slice_select_fusion.1.refs_0_), channel_id=1, source_target_pairs={{0,8},{8,0},{4,12},{12,4},{1,9},{9,1},{5,13},{13,5},{2,10},{10,2},... | collective-permute-start | bytes 1818632 | tf_op jit(solution)/shard_map/ppermute | solution.py:42
  9.2 0.0 collective-permute-start.2
  9.2 1.2 %slice_select_fusion.3.refs_4_ = bf16[592,256]{1,0:T(8,128)(2,1)S(1)} fusion(bf16[592,768]{1,0:T(8,128)(2,1)} %collective-permute-done, bf16[592,1536]{1,0:T(8,128)(2,1)} %bitcast.31, pred[]{:T(512)S(6)} %eq.50, pred[]{:T(512)S(6)} %eq.49), kind=kLoop, calls=%fused_computation.9 | loop fusion | flops 303104 | bytes 1212418 | tf_op jit(solution)/shard_map/jit(_where)/select_n | solution.py:41
  10.4 0.4 collective-permute-start.4
  10.8 12.8 %collective-permute-done.1.refs_1_ = bf16[592,512]{1,0:T(8,128)(2,1)S(1)} collective-permute-done((bf16[592,512]{1,0:T(8,128)(2,1)S(1)}, bf16[592,512]{1,0:T(8,128)(2,1)S(1)}, u32[]{:S(2)}, u32[]{:S(2)}) %collective-permute-start.1) | collective-permute-done | bytes 606240 | tf_op jit(solution)/shard_map/ppermute | solution.py:42
  23.6 0.0 collective-permute-start.3
  24.5 0.1 stack.32.scalars
  24.5 0.1 fusion.refs_11_
  24.7 0.5 collective-permute-start.5
  25.2 4.6 %collective-permute-done.4.refs_5_ = bf16[592,256]{1,0:T(8,128)(2,1)} collective-permute-done((bf16[592,256]{1,0:T(8,128)(2,1)S(1)}, bf16[592,256]{1,0:T(8,128)(2,1)}, u32[]{:S(2)}, u32[]{:S(2)}) %collective-permute-start.4) | collective-permute-done | bytes 303136 | tf_op jit(solution)/shard_map/ppermute | solution.py:42
  29.8 0.0 collective-permute-start.6
  29.8 0.3 fusion.2
  30.1 0.0 collective-permute-done.5.refs_6_
  30.1 1.5 %collective-permute-done.6.refs_7_ = bf16[592,256]{1,0:T(8,128)(2,1)S(1)} collective-permute-done((bf16[592,256]{1,0:T(8,128)(2,1)}, bf16[592,256]{1,0:T(8,128)(2,1)S(1)}, u32[]{:S(2)}, u32[]{:S(2)}) %collective-permute-start.6) | collective-permute-done | bytes 303136 | tf_op jit(solution)/shard_map/ppermute | solution.py:43
  31.6 8.9 %head.1 = (bf16[592,1536]{1,0:T(8,128)(2,1)S(1)}, bf16[592,512]{1,0:T(8,128)(2,1)S(1)}, f32[256,512]{1,0:T(8,128)S(1)}, f32[24,512]{1,0:T(8,128)S(1)}, f32[440,512]{1,0:T(8,128)S(1)}, /*index=5*/f32[440,512]{1,0:T(8,128)S(1)}) custom-call(s32[7]{0:T(128)S(1)} %stack.32.scalars, bf16[592,512]{1,0:T(8,128)(2,1)S(1)} %slice_select_fusion.1.refs_0_, ...), custom_call_target="tpu_custom_call" | custom-call | tf_op jit(solution)/shard_map/head/pallas_call | solution.py:273
  40.5 0.1 convert_element_type.36
  40.6 1.9 %collective-permute-start.7 = (f16[440,512]{1,0:T(8,128)(2,1)S(1)}, f16[440,512]{1,0:T(8,128)(2,1)S(1)}, u32[]{:S(2)}, u32[]{:S(2)}) collective-permute-start(f16[440,512]{1,0:T(8,128)(2,1)S(1)} %convert_element_type.36), channel_id=1, source_target_pairs={{0,1},{1,0},{2,3},{3,2},{4,5},{5,4},{6,7},{7,6},{8,9},{9,8},{10,11... | collective-permute-start | bytes 1351688 | tf_op jit(solution)/shard_map/ppermute | solution.py:362
  42.4 0.1 convert_element_type.37
  42.5 0.7 collective-permute-start.8
  43.2 1.4 %blocks.1 = (f32[440,512]{1,0:T(8,128)S(1)}, f32[440,512]{1,0:T(8,128)S(1)}, f32[8,128]{1,0:T(8,128)S(1)}) custom-call(s32[7]{0:T(128)S(1)} %stack.32.scalars, bf16[592,1536]{1,0:T(8,128)(2,1)S(1)} %get-tuple-element.19.x, bf16[592,512]{1,0:T(8,128)(2,1)S(1)} %get-tuple-element.20.dpre, f32[256,512]{1,0:T(8,128)S(1)} %get-tuple-element.21.gout, ...), custom_call_target="tpu_custom_call" | custom-call | flops 465567744 | bytes 4227072 | tf_op jit(solution)/shard_map/blocks/pallas_call | solution.py:405
  44.6 8.6 %collective-permute-done.7 = f16[440,512]{1,0:T(8,128)(2,1)S(1)} collective-permute-done((f16[440,512]{1,0:T(8,128)(2,1)S(1)}, f16[440,512]{1,0:T(8,128)(2,1)S(1)}, u32[]{:S(2)}, u32[]{:S(2)}) %collective-permute-start.7) | collective-permute-done | bytes 450592 | tf_op jit(solution)/shard_map/ppermute | solution.py:362
  53.2 0.1 convert_element_type.38.theirs
  53.3 0.6 add.54
  54.0 0.1 convert_element_type.39
  54.0 1.8 %collective-permute-start.10 = (f16[440,512]{1,0:T(8,128)(2,1)S(1)}, f16[440,512]{1,0:T(8,128)(2,1)S(1)}, u32[]{:S(2)}, u32[]{:S(2)}) collective-permute-start(f16[440,512]{1,0:T(8,128)(2,1)S(1)} %convert_element_type.39), channel_id=1, source_target_pairs={{0,1},{3,2},{1,3},{2,0},{4,5},{7,6},{5,7},{6,4},{8,9},{11,10},{9,1... | collective-permute-start | bytes 1351688 | tf_op jit(solution)/shard_map/ppermute | solution.py:362
  55.9 3.1 %collective-permute-start.9 = (f16[440,512]{1,0:T(8,128)(2,1)S(1)}, f16[440,512]{1,0:T(8,128)(2,1)S(1)}, u32[]{:S(2)}, u32[]{:S(2)}) collective-permute-start(f16[440,512]{1,0:T(8,128)(2,1)S(1)} %convert_element_type.37), channel_id=1, source_target_pairs={{0,2},{3,1},{4,6},{7,5},{8,10},{11,9},{12,14},{15,13},{16,18},{19,... | collective-permute-start | bytes 1351688 | tf_op jit(solution)/shard_map/ppermute | solution.py:362
  59.0 0.1 select_convert_fusion
  59.1 15.7 %collective-permute-done.9 = f16[440,512]{1,0:T(8,128)(2,1)S(1)} collective-permute-done((f16[440,512]{1,0:T(8,128)(2,1)S(1)}, f16[440,512]{1,0:T(8,128)(2,1)S(1)}, u32[]{:S(2)}, u32[]{:S(2)}) %collective-permute-start.9) | collective-permute-done | bytes 450592 | tf_op jit(solution)/shard_map/ppermute | solution.py:362
  74.8 0.1 convert_element_type.41
  75.0 0.1 convert_element_type.42.last
  75.1 0.4 multiply_add_fusion.parts
  75.5 0.3 line.1.refs_0_
  75.8 3.5 %collective-permute-start.11 = (f32[32,128]{1,0:T(8,128)S(1)}, f32[32,128]{1,0:T(8,128)S(1)}, u32[]{:S(2)}, u32[]{:S(2)}) collective-permute-start(f32[32,128]{1,0:T(8,128)S(1)} %line.1.refs_0_), channel_id=1, source_target_pairs={{0,1},{1,0},{2,3},{3,2},{4,5},{5,4},{6,7},{7,6},{8,9},{9,8},{10,11... | collective-permute-start | bytes 49160 | tf_op jit(solution)/shard_map/ppermute | solution.py:362
  79.3 2.3 %collective-permute-start.12 = (f32[32,128]{1,0:T(8,128)S(1)}, f32[32,128]{1,0:T(8,128)S(1)}, u32[]{:S(2)}, u32[]{:S(2)}) collective-permute-start(f32[32,128]{1,0:T(8,128)S(1)} %line.1.refs_0_), channel_id=1, source_target_pairs={{0,2},{1,3},{2,0},{3,1},{4,6},{5,7},{6,4},{7,5},{8,10},{9,11},{10,... | collective-permute-start | bytes 49160 | tf_op jit(solution)/shard_map/ppermute | solution.py:362
  81.7 0.1 collective-permute-start.13
  81.7 1.0 %sums.1 = (f32[384,512]{1,0:T(8,128)}, f32[150,1,128]{2,1,0:T(1,128)}, f32[9,1,512]{2,1,0:T(1,128)}) custom-call(f32[440,512]{1,0:T(8,128)S(1)} %multiply_add_fusion.parts, f32[440,512]{1,0:T(8,128)S(1)} %convert_element_type.42.last), custom_call_target="tpu_custom_call" | custom-call | flops 450560 | bytes 3604480 | tf_op jit(solution)/shard_map/sums/pallas_call | solution.py:489
  82.8 1.2 %collective-permute-done.12.refs_2_ = f32[32,128]{1,0:T(8,128)S(1)} collective-permute-done((f32[32,128]{1,0:T(8,128)S(1)}, f32[32,128]{1,0:T(8,128)S(1)}, u32[]{:S(2)}, u32[]{:S(2)}) %collective-permute-start.12) | collective-permute-done | bytes 16416 | tf_op jit(solution)/shard_map/ppermute | solution.py:362
  83.9 3.2 %collective-permute-done.13.refs_3_ = f32[32,128]{1,0:T(8,128)S(1)} collective-permute-done((f32[32,128]{1,0:T(8,128)S(1)}, f32[32,128]{1,0:T(8,128)S(1)}, u32[]{:S(2)}, u32[]{:S(2)}) %collective-permute-start.13) | collective-permute-done | bytes 16416 | tf_op jit(solution)/shard_map/ppermute | solution.py:362
  87.2 0.7 norms.1
  (17 shorter events, 0.1 us)
Async XLA Ops:
  0.6 4.4 %copy-start.2 = (bf16[1,1,592,1536]{3,2,1,0:T(8,128)(2,1)S(1)}, bf16[1,1,592,1536]{3,2,1,0:T(8,128)(2,1)}, u32[]{:S(2)}) copy-start(bf16[1,1,592,1536]{3,2,1,0:T(8,128)(2,1)} %param.7) | copy-start | bytes 5455876
  2.3 2.7 %collective-permute-start = (bf16[592,768]{1,0:T(8,128)(2,1)S(1)}, bf16[592,768]{1,0:T(8,128)(2,1)}, u32[]{:S(2)}, u32[]{:S(2)}) collective-permute-start(bf16[592,768]{1,0:T(8,128)(2,1)S(1)} %slice_select_fusion), channel_id=1, source_target_pairs={{0,4},{4,0},{8,12},{12,8},{1,5},{5,1},{9,13},{13,9},{2,6},{6,2},{1... | collective-permute-start | bytes 2727944 | tf_op jit(solution)/shard_map/ppermute | solution.py:35
  3.5 20.9 %copy-start.4 = (s32[1,592]{1,0:T(1,128)S(1)}, s32[1,592]{1,0:T(1,128)}, u32[]{:S(2)}) copy-start(s32[1,592]{1,0:T(1,128)} %param.10) | copy-start | bytes 7108
  3.5 20.9 %copy-start.3 = (bf16[1,512,150]{1,2,0:T(8,128)(2,1)S(1)}, bf16[1,512,150]{1,2,0:T(8,128)(2,1)}, u32[]{:S(2)}) copy-start(bf16[1,512,150]{1,2,0:T(8,128)(2,1)} %param.13) | copy-start | bytes 460804
  6.2 25.3 %copy-start = (bf16[1,1536,512]{2,1,0:T(8,128)(2,1)S(1)}, bf16[1,1536,512]{2,1,0:T(8,128)(2,1)}, u32[]{:S(2)}) copy-start(bf16[1,1536,512]{2,1,0:T(8,128)(2,1)} %param.11) | copy-start | bytes 4718596
  6.2 25.3 %copy-start.1 = (f32[1,9,512]{2,0,1:T(1,128)S(1)}, f32[1,9,512]{2,0,1:T(1,128)}, u32[]{:S(2)}) copy-start(f32[1,9,512]{2,0,1:T(1,128)} %param.12) | copy-start | bytes 55300
  6.3 17.4 %collective-permute-start.1 = (bf16[592,512]{1,0:T(8,128)(2,1)S(1)}, bf16[592,512]{1,0:T(8,128)(2,1)S(1)}, u32[]{:S(2)}, u32[]{:S(2)}) collective-permute-start(bf16[592,512]{1,0:T(8,128)(2,1)S(1)} %slice_select_fusion.1.refs_0_), channel_id=1, source_target_pairs={{0,8},{8,0},{4,12},{12,4},{1,9},{9,1},{5,13},{13,5},{2,10},{10,2},... | collective-permute-start | bytes 1818632 | tf_op jit(solution)/shard_map/ppermute | solution.py:42
  9.2 20.9 %collective-permute-start.2 = (bf16[592,512]{1,0:T(8,128)(2,1)S(1)}, bf16[592,512]{1,0:T(8,128)(2,1)}, u32[]{:S(2)}, u32[]{:S(2)}) collective-permute-start(bf16[592,512]{1,0:T(8,128)(2,1)S(1)} %slice_select_fusion.1.refs_0_), channel_id=1, source_target_pairs={{0,4},{4,0},{8,12},{12,8},{1,5},{5,1},{9,13},{13,9},{2,6},{6,2},{1... | collective-permute-start | bytes 1818632 | tf_op jit(solution)/shard_map/ppermute | solution.py:43
  10.4 19.4 %collective-permute-start.4 = (bf16[592,256]{1,0:T(8,128)(2,1)S(1)}, bf16[592,256]{1,0:T(8,128)(2,1)}, u32[]{:S(2)}, u32[]{:S(2)}) collective-permute-start(bf16[592,256]{1,0:T(8,128)(2,1)S(1)} %slice_select_fusion.3.refs_4_), channel_id=1, source_target_pairs={{0,8},{8,0},{4,12},{12,4},{1,9},{9,1},{5,13},{13,5},{2,10},{10,2},... | collective-permute-start | bytes 909320 | tf_op jit(solution)/shard_map/ppermute | solution.py:42
  23.6 7.9 %collective-permute-start.3 = (bf16[592,512]{1,0:T(8,128)(2,1)S(1)}, bf16[592,512]{1,0:T(8,128)(2,1)}, u32[]{:S(2)}, u32[]{:S(2)}) collective-permute-start(bf16[592,512]{1,0:T(8,128)(2,1)S(1)} %collective-permute-done.1.refs_1_), channel_id=1, source_target_pairs={{0,4},{4,0},{8,12},{12,8},{1,5},{5,1},{9,13},{13,9},{2,6},{6,2},{1... | collective-permute-start | bytes 1818632 | tf_op jit(solution)/shard_map/ppermute | solution.py:43
  24.7 5.4 %collective-permute-start.5 = (bf16[592,256]{1,0:T(8,128)(2,1)S(1)}, bf16[592,256]{1,0:T(8,128)(2,1)S(1)}, u32[]{:S(2)}, u32[]{:S(2)}) collective-permute-start(bf16[592,256]{1,0:T(8,128)(2,1)S(1)} %slice_select_fusion.3.refs_4_), channel_id=1, source_target_pairs={{0,4},{4,0},{8,12},{12,8},{1,5},{5,1},{9,13},{13,9},{2,6},{6,2},{1... | collective-permute-start | bytes 909320 | tf_op jit(solution)/shard_map/ppermute | solution.py:43
  29.8 1.8 %collective-permute-start.6 = (bf16[592,256]{1,0:T(8,128)(2,1)}, bf16[592,256]{1,0:T(8,128)(2,1)S(1)}, u32[]{:S(2)}, u32[]{:S(2)}) collective-permute-start(bf16[592,256]{1,0:T(8,128)(2,1)} %collective-permute-done.4.refs_5_), channel_id=1, source_target_pairs={{0,4},{4,0},{8,12},{12,8},{1,5},{5,1},{9,13},{13,9},{2,6},{6,2},{1... | collective-permute-start | bytes 909320 | tf_op jit(solution)/shard_map/ppermute | solution.py:43
  40.6 12.7 %collective-permute-start.7 = (f16[440,512]{1,0:T(8,128)(2,1)S(1)}, f16[440,512]{1,0:T(8,128)(2,1)S(1)}, u32[]{:S(2)}, u32[]{:S(2)}) collective-permute-start(f16[440,512]{1,0:T(8,128)(2,1)S(1)} %convert_element_type.36), channel_id=1, source_target_pairs={{0,1},{1,0},{2,3},{3,2},{4,5},{5,4},{6,7},{7,6},{8,9},{9,8},{10,11... | collective-permute-start | bytes 1351688 | tf_op jit(solution)/shard_map/ppermute | solution.py:362
  42.5 16.4 %collective-permute-start.8 = (f16[440,512]{1,0:T(8,128)(2,1)S(1)}, f16[440,512]{1,0:T(8,128)(2,1)S(1)}, u32[]{:S(2)}, u32[]{:S(2)}) collective-permute-start(f16[440,512]{1,0:T(8,128)(2,1)S(1)} %convert_element_type.37), channel_id=1, source_target_pairs={{1,2},{2,1},{5,6},{6,5},{9,10},{10,9},{13,14},{14,13},{17,18},{18,... | collective-permute-start | bytes 1351688 | tf_op jit(solution)/shard_map/ppermute | solution.py:362
  54.0 20.9 %collective-permute-start.10 = (f16[440,512]{1,0:T(8,128)(2,1)S(1)}, f16[440,512]{1,0:T(8,128)(2,1)S(1)}, u32[]{:S(2)}, u32[]{:S(2)}) collective-permute-start(f16[440,512]{1,0:T(8,128)(2,1)S(1)} %convert_element_type.39), channel_id=1, source_target_pairs={{0,1},{3,2},{1,3},{2,0},{4,5},{7,6},{5,7},{6,4},{8,9},{11,10},{9,1... | collective-permute-start | bytes 1351688 | tf_op jit(solution)/shard_map/ppermute | solution.py:362
  55.9 18.9 %collective-permute-start.9 = (f16[440,512]{1,0:T(8,128)(2,1)S(1)}, f16[440,512]{1,0:T(8,128)(2,1)S(1)}, u32[]{:S(2)}, u32[]{:S(2)}) collective-permute-start(f16[440,512]{1,0:T(8,128)(2,1)S(1)} %convert_element_type.37), channel_id=1, source_target_pairs={{0,2},{3,1},{4,6},{7,5},{8,10},{11,9},{12,14},{15,13},{16,18},{19,... | collective-permute-start | bytes 1351688 | tf_op jit(solution)/shard_map/ppermute | solution.py:362
  75.8 7.0 %collective-permute-start.11 = (f32[32,128]{1,0:T(8,128)S(1)}, f32[32,128]{1,0:T(8,128)S(1)}, u32[]{:S(2)}, u32[]{:S(2)}) collective-permute-start(f32[32,128]{1,0:T(8,128)S(1)} %line.1.refs_0_), channel_id=1, source_target_pairs={{0,1},{1,0},{2,3},{3,2},{4,5},{5,4},{6,7},{7,6},{8,9},{9,8},{10,11... | collective-permute-start | bytes 49160 | tf_op jit(solution)/shard_map/ppermute | solution.py:362
  79.3 4.6 %collective-permute-start.12 = (f32[32,128]{1,0:T(8,128)S(1)}, f32[32,128]{1,0:T(8,128)S(1)}, u32[]{:S(2)}, u32[]{:S(2)}) collective-permute-start(f32[32,128]{1,0:T(8,128)S(1)} %line.1.refs_0_), channel_id=1, source_target_pairs={{0,2},{1,3},{2,0},{3,1},{4,6},{5,7},{6,4},{7,5},{8,10},{9,11},{10,... | collective-permute-start | bytes 49160 | tf_op jit(solution)/shard_map/ppermute | solution.py:362
  81.7 5.5 %collective-permute-start.13 = (f32[32,128]{1,0:T(8,128)S(1)}, f32[32,128]{1,0:T(8,128)S(1)}, u32[]{:S(2)}, u32[]{:S(2)}) collective-permute-start(f32[32,128]{1,0:T(8,128)S(1)} %line.1.refs_0_), channel_id=1, source_target_pairs={{0,3},{1,2},{2,1},{3,0},{4,7},{5,6},{6,5},{7,4},{8,11},{9,10},{10,... | collective-permute-start | bytes 49160 | tf_op jit(solution)/shard_map/ppermute | solution.py:362

commit v11 on v10

--- a/solution.py
+++ b/solution.py
@@ -485,7 +485,7 @@
         compiler_params=small,
         name="line",
     )(parts, last, stats)
-    lines = [line] + [permute(line, [(i, i ^ s) for i in range(dp)]) for s in range(1, dp)]
+    lines = [line] + [permute(line, [(i, i ^ s) for i in range(dp)]) for s in (3, 2, 1)]
     share_in, share_out, total_taps = pl.pallas_call(
         functools.partial(sum_kernel, sizes),
         out_shape=[

time: 87.9 us -> 86.5 us (0.984)
  waiting for transfers between devices: 49.2 us -> 47.6 us
    ppermute x7, waiting for transfers between devices: 28.8 us -> 27.2 us  [permute(): return lax.ppermute(value, 'dp', pairs)]
where the time goes in v11:
time: 86.5 us; the launch traced here: 86.2 us
  waiting for transfers between devices  47.6 us (55%)
  starting transfers between devices  17.7 us (20%)
  Pallas kernels  12.9 us (15%)
  other arithmetic  5.59 us (6%)
  between operations  2.31 us (3%)
    ppermute x7, waiting for transfers between devices, permute(): return lax.ppermute(value, 'dp', pairs)  27.2 us
    ppermute x2, waiting for transfers between devices, pieces(): other = lax.ppermute(held, axis, across)  17.4 us
    ppermute x7, starting transfers between devices, permute(): return lax.ppermute(value, 'dp', pairs)  13.3 us
    pallas_call x1, Pallas kernels, head_backward(): pl.pallas_call(functools.partial(head_kernel, sizes, widths), out_shape=[...  8.91 us
    ppermute x2, starting transfers between devices, pieces(): other = lax.ppermute(held, axis, across)  3.35 us
    select_n x2, other arithmetic, pieces(): held = jnp.where(source % 2 == core, kept, got[:, at:at + piece])  2.35 us
  transfers between devices with their start and end apart: 14, of which 8 were waited for; matrix products, arithmetic and copies ran while one was open for 3% of the time, Pallas kernels for 3%

profile of v11, /device:TPU:0, one launch (start us, length us, event | category | flops | bytes accessed | tf_op | source)
XLA Modules:
  0.0 86.2 jit_solution(9296501086350326756)
XLA Ops:
  0.6 0.0 copy-start.2
  0.7 1.7 %slice_select_fusion = bf16[592,768]{1,0:T(8,128)(2,1)S(1)} fusion(bf16[592,1536]{1,0:T(8,128)(2,1)} %bitcast.30, pred[]{:T(512)S(6)} %eq.50), kind=kLoop, calls=%fused_computation | loop fusion | flops 454656 | bytes 2727937 | tf_op jit(solution)/shard_map/jit(_where)/select_n | solution.py:35
  2.3 0.5 collective-permute-start
  3.5 0.0 copy-start.4
  3.5 0.0 copy-start.3
  3.6 1.5 %collective-permute-done = bf16[592,768]{1,0:T(8,128)(2,1)} collective-permute-done((bf16[592,768]{1,0:T(8,128)(2,1)S(1)}, bf16[592,768]{1,0:T(8,128)(2,1)}, u32[]{:S(2)}, u32[]{:S(2)}) %collective-permute-start) | collective-permute-done | bytes 909344 | tf_op jit(solution)/shard_map/ppermute | solution.py:35
  5.1 1.2 %slice_select_fusion.1.refs_0_ = bf16[592,512]{1,0:T(8,128)(2,1)S(1)} fusion(bf16[592,768]{1,0:T(8,128)(2,1)} %collective-permute-done, bf16[592,1536]{1,0:T(8,128)(2,1)S(1)} %bitcast.32, pred[]{:T(512)S(6)} %eq.50, pred[]{:T(512)S(6)} %eq.49), kind=kLoop, calls=%fused_computation.2 | loop fusion | flops 606208 | bytes 2424834 | tf_op jit(solution)/shard_map/jit(_where)/select_n | solution.py:41
  6.2 0.0 copy-start
  6.2 0.0 copy-start.1
  6.3 2.9 %collective-permute-start.1 = (bf16[592,512]{1,0:T(8,128)(2,1)S(1)}, bf16[592,512]{1,0:T(8,128)(2,1)S(1)}, u32[]{:S(2)}, u32[]{:S(2)}) collective-permute-start(bf16[592,512]{1,0:T(8,128)(2,1)S(1)} %slice_select_fusion.1.refs_0_), channel_id=1, source_target_pairs={{0,8},{8,0},{4,12},{12,4},{1,9},{9,1},{5,13},{13,5},{2,10},{10,2},... | collective-permute-start | bytes 1818632 | tf_op jit(solution)/shard_map/ppermute | solution.py:42
  9.2 0.0 collective-permute-start.2
  9.2 1.2 %slice_select_fusion.3.refs_4_ = bf16[592,256]{1,0:T(8,128)(2,1)S(1)} fusion(bf16[592,768]{1,0:T(8,128)(2,1)} %collective-permute-done, bf16[592,1536]{1,0:T(8,128)(2,1)} %bitcast.31, pred[]{:T(512)S(6)} %eq.50, pred[]{:T(512)S(6)} %eq.49), kind=kLoop, calls=%fused_computation.9 | loop fusion | flops 303104 | bytes 1212418 | tf_op jit(solution)/shard_map/jit(_where)/select_n | solution.py:41
  10.4 0.4 collective-permute-start.4
  10.8 12.8 %collective-permute-done.1.refs_1_ = bf16[592,512]{1,0:T(8,128)(2,1)S(1)} collective-permute-done((bf16[592,512]{1,0:T(8,128)(2,1)S(1)}, bf16[592,512]{1,0:T(8,128)(2,1)S(1)}, u32[]{:S(2)}, u32[]{:S(2)}) %collective-permute-start.1) | collective-permute-done | bytes 606240 | tf_op jit(solution)/shard_map/ppermute | solution.py:42
  23.6 0.0 collective-permute-start.3
  24.5 0.1 stack.32.scalars
  24.5 0.1 fusion.refs_11_
  24.7 0.5 collective-permute-start.5
  25.2 4.6 %collective-permute-done.4.refs_5_ = bf16[592,256]{1,0:T(8,128)(2,1)} collective-permute-done((bf16[592,256]{1,0:T(8,128)(2,1)S(1)}, bf16[592,256]{1,0:T(8,128)(2,1)}, u32[]{:S(2)}, u32[]{:S(2)}) %collective-permute-start.4) | collective-permute-done | bytes 303136 | tf_op jit(solution)/shard_map/ppermute | solution.py:42
  29.8 0.3 fusion.2
  30.1 0.0 collective-permute-done.5.refs_6_
  30.1 0.0 collective-permute-done.2.refs_2_
  30.1 1.5 %collective-permute-done.6.refs_7_ = bf16[592,256]{1,0:T(8,128)(2,1)S(1)} collective-permute-done((bf16[592,256]{1,0:T(8,128)(2,1)}, bf16[592,256]{1,0:T(8,128)(2,1)S(1)}, u32[]{:S(2)}, u32[]{:S(2)}) %collective-permute-start.6) | collective-permute-done | bytes 303136 | tf_op jit(solution)/shard_map/ppermute | solution.py:43
  31.6 0.0 collective-permute-done.3.refs_3_
  31.6 8.9 %head.1 = (bf16[592,1536]{1,0:T(8,128)(2,1)S(1)}, bf16[592,512]{1,0:T(8,128)(2,1)S(1)}, f32[256,512]{1,0:T(8,128)S(1)}, f32[24,512]{1,0:T(8,128)S(1)}, f32[440,512]{1,0:T(8,128)S(1)}, /*index=5*/f32[440,512]{1,0:T(8,128)S(1)}) custom-call(s32[7]{0:T(128)S(1)} %stack.32.scalars, bf16[592,512]{1,0:T(8,128)(2,1)S(1)} %slice_select_fusion.1.refs_0_, ...), custom_call_target="tpu_custom_call" | custom-call | tf_op jit(solution)/shard_map/head/pallas_call | solution.py:273
  40.5 0.1 convert_element_type.36
  40.6 2.0 %collective-permute-start.7 = (f16[440,512]{1,0:T(8,128)(2,1)S(1)}, f16[440,512]{1,0:T(8,128)(2,1)S(1)}, u32[]{:S(2)}, u32[]{:S(2)}) collective-permute-start(f16[440,512]{1,0:T(8,128)(2,1)S(1)} %convert_element_type.36), channel_id=1, source_target_pairs={{0,1},{1,0},{2,3},{3,2},{4,5},{5,4},{6,7},{7,6},{8,9},{9,8},{10,11... | collective-permute-start | bytes 1351688 | tf_op jit(solution)/shard_map/ppermute | solution.py:362
  42.5 0.1 convert_element_type.37
  42.6 0.7 collective-permute-start.8
  43.3 1.4 %blocks.1 = (f32[440,512]{1,0:T(8,128)S(1)}, f32[440,512]{1,0:T(8,128)S(1)}, f32[8,128]{1,0:T(8,128)S(1)}) custom-call(s32[7]{0:T(128)S(1)} %stack.32.scalars, bf16[592,1536]{1,0:T(8,128)(2,1)S(1)} %get-tuple-element.19.x, bf16[592,512]{1,0:T(8,128)(2,1)S(1)} %get-tuple-element.20.dpre, f32[256,512]{1,0:T(8,128)S(1)} %get-tuple-element.21.gout, ...), custom_call_target="tpu_custom_call" | custom-call | flops 465567744 | bytes 4227072 | tf_op jit(solution)/shard_map/blocks/pallas_call | solution.py:405
  44.7 8.6 %collective-permute-done.7 = f16[440,512]{1,0:T(8,128)(2,1)S(1)} collective-permute-done((f16[440,512]{1,0:T(8,128)(2,1)S(1)}, f16[440,512]{1,0:T(8,128)(2,1)S(1)}, u32[]{:S(2)}, u32[]{:S(2)}) %collective-permute-start.7) | collective-permute-done | bytes 450592 | tf_op jit(solution)/shard_map/ppermute | solution.py:362
  53.2 0.1 convert_element_type.38.theirs
  53.4 0.6 add.54
  54.0 0.1 convert_element_type.39
  54.1 1.8 %collective-permute-start.10 = (f16[440,512]{1,0:T(8,128)(2,1)S(1)}, f16[440,512]{1,0:T(8,128)(2,1)S(1)}, u32[]{:S(2)}, u32[]{:S(2)}) collective-permute-start(f16[440,512]{1,0:T(8,128)(2,1)S(1)} %convert_element_type.39), channel_id=1, source_target_pairs={{0,1},{3,2},{1,3},{2,0},{4,5},{7,6},{5,7},{6,4},{8,9},{11,10},{9,1... | collective-permute-start | bytes 1351688 | tf_op jit(solution)/shard_map/ppermute | solution.py:362
  55.9 3.1 %collective-permute-start.9 = (f16[440,512]{1,0:T(8,128)(2,1)S(1)}, f16[440,512]{1,0:T(8,128)(2,1)S(1)}, u32[]{:S(2)}, u32[]{:S(2)}) collective-permute-start(f16[440,512]{1,0:T(8,128)(2,1)S(1)} %convert_element_type.37), channel_id=1, source_target_pairs={{0,2},{3,1},{4,6},{7,5},{8,10},{11,9},{12,14},{15,13},{16,18},{19,... | collective-permute-start | bytes 1351688 | tf_op jit(solution)/shard_map/ppermute | solution.py:362
  59.0 0.1 select_convert_fusion
  59.1 15.6 %collective-permute-done.9 = f16[440,512]{1,0:T(8,128)(2,1)S(1)} collective-permute-done((f16[440,512]{1,0:T(8,128)(2,1)S(1)}, f16[440,512]{1,0:T(8,128)(2,1)S(1)}, u32[]{:S(2)}, u32[]{:S(2)}) %collective-permute-start.9) | collective-permute-done | bytes 450592 | tf_op jit(solution)/shard_map/ppermute | solution.py:362
  74.8 0.1 convert_element_type.41
  74.9 0.1 convert_element_type.42.last
  75.0 0.4 multiply_add_fusion.parts
  75.5 0.3 line.1.refs_0_
  75.7 5.1 %collective-permute-start.11 = (f32[32,128]{1,0:T(8,128)S(1)}, f32[32,128]{1,0:T(8,128)S(1)}, u32[]{:S(2)}, u32[]{:S(2)}) collective-permute-start(f32[32,128]{1,0:T(8,128)S(1)} %line.1.refs_0_), channel_id=1, source_target_pairs={{0,3},{1,2},{2,1},{3,0},{4,7},{5,6},{6,5},{7,4},{8,11},{9,10},{10,... | collective-permute-start | bytes 49160 | tf_op jit(solution)/shard_map/ppermute | solution.py:362
  80.9 0.6 collective-permute-start.13
  81.5 1.0 %sums.1 = (f32[384,512]{1,0:T(8,128)}, f32[150,1,128]{2,1,0:T(1,128)}, f32[9,1,512]{2,1,0:T(1,128)}) custom-call(f32[440,512]{1,0:T(8,128)S(1)} %multiply_add_fusion.parts, f32[440,512]{1,0:T(8,128)S(1)} %convert_element_type.42.last), custom_call_target="tpu_custom_call" | custom-call | flops 450560 | bytes 3604480 | tf_op jit(solution)/shard_map/sums/pallas_call | solution.py:489
  82.5 0.1 collective-permute-done.11.refs_1_
  82.6 2.9 %collective-permute-done.12.refs_2_ = f32[32,128]{1,0:T(8,128)S(1)} collective-permute-done((f32[32,128]{1,0:T(8,128)S(1)}, f32[32,128]{1,0:T(8,128)S(1)}, u32[]{:S(2)}, u32[]{:S(2)}) %collective-permute-start.12) | collective-permute-done | bytes 16416 | tf_op jit(solution)/shard_map/ppermute | solution.py:362
  85.5 0.7 norms.1
  (17 shorter events, 0.1 us)
Async XLA Ops:
  0.6 4.4 %copy-start.2 = (bf16[1,1,592,1536]{3,2,1,0:T(8,128)(2,1)S(1)}, bf16[1,1,592,1536]{3,2,1,0:T(8,128)(2,1)}, u32[]{:S(2)}) copy-start(bf16[1,1,592,1536]{3,2,1,0:T(8,128)(2,1)} %param.7) | copy-start | bytes 5455876
  2.3 2.7 %collective-permute-start = (bf16[592,768]{1,0:T(8,128)(2,1)S(1)}, bf16[592,768]{1,0:T(8,128)(2,1)}, u32[]{:S(2)}, u32[]{:S(2)}) collective-permute-start(bf16[592,768]{1,0:T(8,128)(2,1)S(1)} %slice_select_fusion), channel_id=1, source_target_pairs={{0,4},{4,0},{8,12},{12,8},{1,5},{5,1},{9,13},{13,9},{2,6},{6,2},{1... | collective-permute-start | bytes 2727944 | tf_op jit(solution)/shard_map/ppermute | solution.py:35
  3.5 20.9 %copy-start.4 = (s32[1,592]{1,0:T(1,128)S(1)}, s32[1,592]{1,0:T(1,128)}, u32[]{:S(2)}) copy-start(s32[1,592]{1,0:T(1,128)} %param.10) | copy-start | bytes 7108
  3.5 20.9 %copy-start.3 = (bf16[1,512,150]{1,2,0:T(8,128)(2,1)S(1)}, bf16[1,512,150]{1,2,0:T(8,128)(2,1)}, u32[]{:S(2)}) copy-start(bf16[1,512,150]{1,2,0:T(8,128)(2,1)} %param.13) | copy-start | bytes 460804
  6.2 25.3 %copy-start = (bf16[1,1536,512]{2,1,0:T(8,128)(2,1)S(1)}, bf16[1,1536,512]{2,1,0:T(8,128)(2,1)}, u32[]{:S(2)}) copy-start(bf16[1,1536,512]{2,1,0:T(8,128)(2,1)} %param.11) | copy-start | bytes 4718596
  6.2 25.3 %copy-start.1 = (f32[1,9,512]{2,0,1:T(1,128)S(1)}, f32[1,9,512]{2,0,1:T(1,128)}, u32[]{:S(2)}) copy-start(f32[1,9,512]{2,0,1:T(1,128)} %param.12) | copy-start | bytes 55300
  6.3 17.4 %collective-permute-start.1 = (bf16[592,512]{1,0:T(8,128)(2,1)S(1)}, bf16[592,512]{1,0:T(8,128)(2,1)S(1)}, u32[]{:S(2)}, u32[]{:S(2)}) collective-permute-start(bf16[592,512]{1,0:T(8,128)(2,1)S(1)} %slice_select_fusion.1.refs_0_), channel_id=1, source_target_pairs={{0,8},{8,0},{4,12},{12,4},{1,9},{9,1},{5,13},{13,5},{2,10},{10,2},... | collective-permute-start | bytes 1818632 | tf_op jit(solution)/shard_map/ppermute | solution.py:42
  9.2 20.9 %collective-permute-start.2 = (bf16[592,512]{1,0:T(8,128)(2,1)S(1)}, bf16[592,512]{1,0:T(8,128)(2,1)}, u32[]{:S(2)}, u32[]{:S(2)}) collective-permute-start(bf16[592,512]{1,0:T(8,128)(2,1)S(1)} %slice_select_fusion.1.refs_0_), channel_id=1, source_target_pairs={{0,4},{4,0},{8,12},{12,8},{1,5},{5,1},{9,13},{13,9},{2,6},{6,2},{1... | collective-permute-start | bytes 1818632 | tf_op jit(solution)/shard_map/ppermute | solution.py:43
  10.4 19.4 %collective-permute-start.4 = (bf16[592,256]{1,0:T(8,128)(2,1)S(1)}, bf16[592,256]{1,0:T(8,128)(2,1)}, u32[]{:S(2)}, u32[]{:S(2)}) collective-permute-start(bf16[592,256]{1,0:T(8,128)(2,1)S(1)} %slice_select_fusion.3.refs_4_), channel_id=1, source_target_pairs={{0,8},{8,0},{4,12},{12,4},{1,9},{9,1},{5,13},{13,5},{2,10},{10,2},... | collective-permute-start | bytes 909320 | tf_op jit(solution)/shard_map/ppermute | solution.py:42
  23.6 7.9 %collective-permute-start.3 = (bf16[592,512]{1,0:T(8,128)(2,1)S(1)}, bf16[592,512]{1,0:T(8,128)(2,1)}, u32[]{:S(2)}, u32[]{:S(2)}) collective-permute-start(bf16[592,512]{1,0:T(8,128)(2,1)S(1)} %collective-permute-done.1.refs_1_), channel_id=1, source_target_pairs={{0,4},{4,0},{8,12},{12,8},{1,5},{5,1},{9,13},{13,9},{2,6},{6,2},{1... | collective-permute-start | bytes 1818632 | tf_op jit(solution)/shard_map/ppermute | solution.py:43
  24.7 5.4 %collective-permute-start.5 = (bf16[592,256]{1,0:T(8,128)(2,1)S(1)}, bf16[592,256]{1,0:T(8,128)(2,1)S(1)}, u32[]{:S(2)}, u32[]{:S(2)}) collective-permute-start(bf16[592,256]{1,0:T(8,128)(2,1)S(1)} %slice_select_fusion.3.refs_4_), channel_id=1, source_target_pairs={{0,4},{4,0},{8,12},{12,8},{1,5},{5,1},{9,13},{13,9},{2,6},{6,2},{1... | collective-permute-start | bytes 909320 | tf_op jit(solution)/shard_map/ppermute | solution.py:43
  29.8 1.8 %collective-permute-start.6 = (bf16[592,256]{1,0:T(8,128)(2,1)}, bf16[592,256]{1,0:T(8,128)(2,1)S(1)}, u32[]{:S(2)}, u32[]{:S(2)}) collective-permute-start(bf16[592,256]{1,0:T(8,128)(2,1)} %collective-permute-done.4.refs_5_), channel_id=1, source_target_pairs={{0,4},{4,0},{8,12},{12,8},{1,5},{5,1},{9,13},{13,9},{2,6},{6,2},{1... | collective-permute-start | bytes 909320 | tf_op jit(solution)/shard_map/ppermute | solution.py:43
  40.6 12.7 %collective-permute-start.7 = (f16[440,512]{1,0:T(8,128)(2,1)S(1)}, f16[440,512]{1,0:T(8,128)(2,1)S(1)}, u32[]{:S(2)}, u32[]{:S(2)}) collective-permute-start(f16[440,512]{1,0:T(8,128)(2,1)S(1)} %convert_element_type.36), channel_id=1, source_target_pairs={{0,1},{1,0},{2,3},{3,2},{4,5},{5,4},{6,7},{7,6},{8,9},{9,8},{10,11... | collective-permute-start | bytes 1351688 | tf_op jit(solution)/shard_map/ppermute | solution.py:362
  42.6 16.4 %collective-permute-start.8 = (f16[440,512]{1,0:T(8,128)(2,1)S(1)}, f16[440,512]{1,0:T(8,128)(2,1)S(1)}, u32[]{:S(2)}, u32[]{:S(2)}) collective-permute-start(f16[440,512]{1,0:T(8,128)(2,1)S(1)} %convert_element_type.37), channel_id=1, source_target_pairs={{1,2},{2,1},{5,6},{6,5},{9,10},{10,9},{13,14},{14,13},{17,18},{18,... | collective-permute-start | bytes 1351688 | tf_op jit(solution)/shard_map/ppermute | solution.py:362
  54.1 20.9 %collective-permute-start.10 = (f16[440,512]{1,0:T(8,128)(2,1)S(1)}, f16[440,512]{1,0:T(8,128)(2,1)S(1)}, u32[]{:S(2)}, u32[]{:S(2)}) collective-permute-start(f16[440,512]{1,0:T(8,128)(2,1)S(1)} %convert_element_type.39), channel_id=1, source_target_pairs={{0,1},{3,2},{1,3},{2,0},{4,5},{7,6},{5,7},{6,4},{8,9},{11,10},{9,1... | collective-permute-start | bytes 1351688 | tf_op jit(solution)/shard_map/ppermute | solution.py:362
  55.9 18.9 %collective-permute-start.9 = (f16[440,512]{1,0:T(8,128)(2,1)S(1)}, f16[440,512]{1,0:T(8,128)(2,1)S(1)}, u32[]{:S(2)}, u32[]{:S(2)}) collective-permute-start(f16[440,512]{1,0:T(8,128)(2,1)S(1)} %convert_element_type.37), channel_id=1, source_target_pairs={{0,2},{3,1},{4,6},{7,5},{8,10},{11,9},{12,14},{15,13},{16,18},{19,... | collective-permute-start | bytes 1351688 | tf_op jit(solution)/shard_map/ppermute | solution.py:362
  75.7 6.9 %collective-permute-start.11 = (f32[32,128]{1,0:T(8,128)S(1)}, f32[32,128]{1,0:T(8,128)S(1)}, u32[]{:S(2)}, u32[]{:S(2)}) collective-permute-start(f32[32,128]{1,0:T(8,128)S(1)} %line.1.refs_0_), channel_id=1, source_target_pairs={{0,3},{1,2},{2,1},{3,0},{4,7},{5,6},{6,5},{7,4},{8,11},{9,10},{10,... | collective-permute-start | bytes 49160 | tf_op jit(solution)/shard_map/ppermute | solution.py:362
  80.9 4.6 %collective-permute-start.12 = (f32[32,128]{1,0:T(8,128)S(1)}, f32[32,128]{1,0:T(8,128)S(1)}, u32[]{:S(2)}, u32[]{:S(2)}) collective-permute-start(f32[32,128]{1,0:T(8,128)S(1)} %line.1.refs_0_), channel_id=1, source_target_pairs={{0,2},{1,3},{2,0},{3,1},{4,6},{5,7},{6,4},{7,5},{8,10},{9,11},{10,... | collective-permute-start | bytes 49160 | tf_op jit(solution)/shard_map/ppermute | solution.py:362
  80.9 4.6 %collective-permute-start.13 = (f32[32,128]{1,0:T(8,128)S(1)}, f32[32,128]{1,0:T(8,128)S(1)}, u32[]{:S(2)}, u32[]{:S(2)}) collective-permute-start(f32[32,128]{1,0:T(8,128)S(1)} %line.1.refs_0_), channel_id=1, source_target_pairs={{0,1},{1,0},{2,3},{3,2},{4,5},{5,4},{6,7},{7,6},{8,9},{9,8},{10,11... | collective-permute-start | bytes 49160 | tf_op jit(solution)/shard_map/ppermute | solution.py:362

commit v12 on v11

--- a/solution.py
+++ b/solution.py
@@ -15,40 +15,47 @@
 REACH = 4
 OFFSETS = [(a, b) for a in (-1, 0, 1) for b in (-1, 0, 1)]
 X_LIMIT = 6.0
+OTHER_REFS = 18
 ROOM = 16384.0
 
 
 def pieces(block, axis, size, source):
-    width = block.shape[1] // 2
+    wide = block.shape[1]
     if size != 4:
         block = jnp.where(lax.axis_index(axis) == source, block, jnp.zeros_like(block))
         block = lax.psum(block, axis)
-        low, high = block[:, :width], block[:, width:]
+        low, high = block[:, : wide // 2], block[:, wide // 2 :]
         zero = jnp.int32(0)
-        return zero + 1, zero, (width,), (low, low, high, high)
+        return zero, zero, (wide // 2,), (low, low, high, high)
     me = lax.axis_index(axis)
     core = me % 2
     mate = [(0, 1), (1, 0), (2, 3), (3, 2)]
     across = [(0, 2), (2, 0), (1, 3), (3, 1)]
-    here = ((source // 2) == (me // 2)).astype(jnp.int32)
-    widths = split_width(width)
-    got = lax.ppermute(jnp.where(core == 0, block[:, width:], block[:, :width]), axis, mate)
+    widths, width = split_width(wide)
+    shared = block[:, 2 * width :]
+    shared_other = lax.ppermute(shared, axis, across)
+    got = lax.ppermute(jnp.where(core == 0, block[:, width : 2 * width], block[:, :width]), axis, mate)
     values = []
     at = 0
     for piece in widths:
+        if at:
+            block, shared_other, _ = lax.optimization_barrier((block, shared_other, values[0]))
         low, high = block[:, at : at + piece], block[:, width + at : width + at + piece]
         kept = jnp.where(core == 0, low, high)
         held = jnp.where(source % 2 == core, kept, got[:, at : at + piece])
         other = lax.ppermute(held, axis, across)
         values += [held, other, lax.ppermute(held, axis, mate), lax.ppermute(other, axis, mate)]
         at += piece
-    return here, core, widths, tuple(values)
-
-
-def split_width(width):
-    tiles = width // LANES
-    last = max(tiles // 3, 1)
-    return tuple(LANES * n for n in (tiles - last, last) if n > 0)
+    values += [shared, lax.ppermute(shared, axis, mate)]
+    values += [shared_other, lax.ppermute(shared_other, axis, mate)]
+    return (source ^ me).astype(jnp.int32), core, widths, tuple(values)
+
+
+def split_width(wide):
+    tiles = wide // LANES
+    half = (tiles - 2) // 2
+    last = max(half * 2 // 5, 1)
+    return tuple(LANES * n for n in (half - last, last) if n > 0), LANES * half
 
 
 def gelu_parts(value):
@@ -70,29 +77,36 @@
     scalars,
     *refs,
 ):
-    halves, refs = refs[: 4 * len(widths)], refs[4 * len(widths) :]
+    count = len(refs) - OTHER_REFS
+    halves, refs = refs[:count], refs[count:]
+    shared = halves[4 * len(widths) :]
     weight_in, taps, weight_out, onehot, after, before = refs[:6]
     x_vmem, dpre_out, gout, small, first, early = refs[6:12]
     pre, dys, slope, hid, dlog, sem_in = refs[12:]
     rows = x_vmem.shape[0]
-    width = x_vmem.shape[1] // 2
+    width = sum(widths)
     hidden = weight_in.shape[1]
     chunks = hidden // LANES
     guard = REACH * (PC + 1)
-    dil, here, core = scalars[0], scalars[1], scalars[2]
+    dil, where, core = scalars[0], scalars[1], scalars[2]
 
     def fetch(kind, index):
         column = (core if kind < 2 else 1 - core) * width + sum(widths[:index])
         target = x_vmem.at[:, pl.ds(pl.multiple_of(column, LANES), widths[index])]
         return pltpu.make_async_copy(halves[4 * index + kind], target, sem_in.at[index, kind // 2])
 
-    for away in (0, 1):
-
-        @pl.when(here == 1 - away)
-        def _(away=away):
+    def fetch_shared(kind):
+        return pltpu.make_async_copy(shared[kind], x_vmem.at[:, 2 * width :], sem_in.at[len(widths), 0])
+
+    for kind in range(4):
+
+        @pl.when(where == kind)
+        def _(kind=kind):
             for index in range(len(widths)):
-                fetch(away, index).start()
-                fetch(2 + away, index).start()
+                fetch(kind // 2, index).start()
+                fetch(2 + kind // 2, index).start()
+            if shared:
+                fetch_shared(kind).start()
 
     for c in range(chunks):
         for ref in (pre, dys):
@@ -101,6 +115,8 @@
     for index in range(len(widths)):
         fetch(0, index).wait()
         fetch(2, index).wait()
+    if shared:
+        fetch_shared(0).wait()
 
     for n in range(hidden // 256):
         value = jnp.dot(
@@ -287,7 +303,7 @@
             pltpu.VMEM((chunks, rows, LANES), jnp.float32),
             pltpu.VMEM((rows, hidden), jnp.bfloat16),
             pltpu.VMEM((rows, 256), jnp.bfloat16),
-            pltpu.SemaphoreType.DMA((len(widths), 2)),
+            pltpu.SemaphoreType.DMA((len(widths) + 1, 2)),
         ],
         compiler_params=pltpu.CompilerParams(vmem_limit_bytes=24 * 1024 * 1024),
         name="head",
@@ -444,7 +460,7 @@
 
 
 def per_device(sizes, dp, trials, features, owner, dilation_index, labels, input_weight, taps, output_weight):
-    here, core, widths, halves = pieces(features[0, 0], "trial", trials, owner[0])
+    where, core, widths, halves = pieces(features[0, 0], "trial", trials, owner[0])
     me = lax.axis_index("dp")
     dil = dilation_index[0] + 1
     rows = features.shape[2]
@@ -459,7 +475,7 @@
     end = (me == 0) | (me == 3)
     step, jump = jnp.where(odd == 0, 1, 2), jnp.where(high, me - 2, me + 2)
     to = [3 * (1 - odd), jnp.where(end, jump, step), jnp.where(end, step, jump), me]
-    scalars = jnp.stack([dil, here, core] + to).astype(jnp.int32)
+    scalars = jnp.stack([dil, where, core] + to).astype(jnp.int32)
     xrows, dpre, gout, small, first, early = head_backward(
         sizes,
         widths,

time: 86.5 us -> 85.8 us (level)
  waiting for transfers between devices: 47.6 us -> 44.8 us
  starting transfers between devices: 17.7 us -> 20 us
    ppermute x2, waiting for transfers between devices: 17.4 us -> 12.2 us  [pieces(): other = lax.ppermute(held, axis, across)]
    ppermute x1 -> x4, starting transfers between devices: 0.52 us -> 3.31 us  [the longest x1 2.55 us: pieces(): shared_other = lax.ppermute(shared, axis, across)]
    ppermute x1 -> x4, waiting for transfers between devices: 1.52 us -> 4.26 us  [the longest x1 4.26 us: pieces(): shared_other = lax.ppermute(shared, axis, across)]
  transfers between devices with their start and end apart: 14 -> 17, of which waited for: 8 -> 8; matrix products, arithmetic and copies ran while one was open for 3% -> 4% of each run, Pallas kernels for 3% -> 4%
where the time goes in v12:
time: 85.8 us; the launch traced here: 85.6 us
  waiting for transfers between devices  44.8 us (52%)
  starting transfers between devices  20 us (23%)
  Pallas kernels  12.1 us (14%)
  other arithmetic  6.28 us (7%)
  between operations  2.27 us (3%)
    ppermute x7, waiting for transfers between devices, permute(): return lax.ppermute(value, 'dp', pairs)  27.1 us
    ppermute x7, starting transfers between devices, permute(): return lax.ppermute(value, 'dp', pairs)  13.4 us
    ppermute x2, waiting for transfers between devices, pieces(): other = lax.ppermute(held, axis, across)  12.2 us
    pallas_call x1, Pallas kernels, head_backward(): pl.pallas_call(functools.partial(head_kernel, sizes, widths), out_shape=[...  8.09 us
    ppermute x1, waiting for transfers between devices, pieces(): shared_other = lax.ppermute(shared, axis, across)  4.26 us
    ppermute x2, starting transfers between devices, pieces(): other = lax.ppermute(held, axis, across)  2.79 us
    ppermute x1, starting transfers between devices, pieces(): shared_other = lax.ppermute(shared, axis, across)  2.55 us
    select_n x1, other arithmetic, pieces(): jnp.where(core == 0, block[:, width:2 * width], block[:, :width])  2.44 us
  transfers between devices with their start and end apart: 17, of which 8 were waited for; matrix products, arithmetic and copies ran while one was open for 4% of the time, Pallas kernels for 4%

profile of v12, /device:TPU:0, one launch (start us, length us, event | category | flops | bytes accessed | tf_op | source)
XLA Modules:
  0.0 85.6 jit_solution(16089861637398040248)
XLA Ops:
  0.7 2.4 %slice_select_fusion = bf16[592,640]{1,0:T(8,128)(2,1)} fusion(bf16[592,1536]{1,0:T(8,128)(2,1)} %bitcast.30, pred[]{:T(512)S(6)} %eq.46), kind=kLoop, calls=%fused_computation.1 | loop fusion | flops 378880 | bytes 2273281 | tf_op jit(solution)/shard_map/jit(_where)/select_n | solution.py:37
  3.1 0.5 collective-permute-start
  3.6 2.6 %collective-permute-start.4 = (bf16[592,256]{1,0:T(8,128)(2,1)S(1)}, bf16[592,256]{1,0:T(8,128)(2,1)S(1)}, u32[]{:S(2)}, u32[]{:S(2)}) collective-permute-start(bf16[592,256]{1,0:T(8,128)(2,1)S(1)} %slice.65.refs_8_), channel_id=1, source_target_pairs={{0,8},{8,0},{4,12},{12,4},{1,9},{9,1},{5,13},{13,5},{2,10},{10,2},... | collective-permute-start | bytes 909320 | tf_op jit(solution)/shard_map/ppermute | solution.py:36
  6.2 0.2 collective-permute-start.8
  7.8 0.1 stack.28.scalars
  7.9 1.2 %slice_select_fusion.1.refs_0_ = bf16[592,384]{1,0:T(8,128)(2,1)S(1)} fusion(bf16[592,640]{1,0:T(8,128)(2,1)} %collective-permute-done, bf16[592,1536]{1,0:T(8,128)(2,1)S(1)} %bitcast.32, pred[]{:T(512)S(6)} %eq.46, pred[]{:T(512)S(6)} %eq.45), kind=kLoop, calls=%fused_computation.4 | loop fusion | flops 454656 | bytes 1818626 | tf_op jit(solution)/shard_map/jit(_where)/select_n | solution.py:45
  9.2 0.8 collective-permute-start.1
  9.9 4.3 %collective-permute-done.4.refs_10_ = bf16[592,256]{1,0:T(8,128)(2,1)S(1)} collective-permute-done((bf16[592,256]{1,0:T(8,128)(2,1)S(1)}, bf16[592,256]{1,0:T(8,128)(2,1)S(1)}, u32[]{:S(2)}, u32[]{:S(2)}) %collective-permute-start.4) | collective-permute-done | bytes 303136 | tf_op jit(solution)/shard_map/ppermute | solution.py:36
  14.2 1.0 %slice_select_fusion.3.refs_4_ = bf16[592,256]{1,0:T(8,128)(2,1)S(1)} fusion(bf16[592,640]{1,0:T(8,128)(2,1)} %collective-permute-done, bf16[592,1536]{1,0:T(8,128)(2,1)S(1)} %bitcast.33, pred[]{:T(512)S(6)} %eq.46, pred[]{:T(512)S(6)} %eq.45), kind=kLoop, calls=%fused_computation.9 | loop fusion | flops 303104 | bytes 1212418 | tf_op jit(solution)/shard_map/jit(_where)/select_n | solution.py:45
  15.2 2.0 %collective-permute-start.5 = (bf16[592,256]{1,0:T(8,128)(2,1)S(1)}, bf16[592,256]{1,0:T(8,128)(2,1)S(1)}, u32[]{:S(2)}, u32[]{:S(2)}) collective-permute-start(bf16[592,256]{1,0:T(8,128)(2,1)S(1)} %slice_select_fusion.3.refs_4_), channel_id=1, source_target_pairs={{0,8},{8,0},{4,12},{12,4},{1,9},{9,1},{5,13},{13,5},{2,10},{10,2},... | collective-permute-start | bytes 909320 | tf_op jit(solution)/shard_map/ppermute | solution.py:46
  17.2 0.1 fusion.refs_15_
  17.4 0.1 collective-permute-start.2
  17.5 6.5 %collective-permute-done.1.refs_1_ = bf16[592,384]{1,0:T(8,128)(2,1)S(1)} collective-permute-done((bf16[592,384]{1,0:T(8,128)(2,1)S(1)}, bf16[592,384]{1,0:T(8,128)(2,1)S(1)}, u32[]{:S(2)}, u32[]{:S(2)}) %collective-permute-start.1) | collective-permute-done | bytes 454688 | tf_op jit(solution)/shard_map/ppermute | solution.py:46
  23.9 0.5 collective-permute-start.6
  24.5 0.0 collective-permute-done.8.refs_9_
  24.5 0.1 collective-permute-start.9
  24.5 5.7 %collective-permute-done.5.refs_5_ = bf16[592,256]{1,0:T(8,128)(2,1)S(1)} collective-permute-done((bf16[592,256]{1,0:T(8,128)(2,1)S(1)}, bf16[592,256]{1,0:T(8,128)(2,1)S(1)}, u32[]{:S(2)}, u32[]{:S(2)}) %collective-permute-start.5) | collective-permute-done | bytes 303136 | tf_op jit(solution)/shard_map/ppermute | solution.py:46
  30.2 0.0 collective-permute-start.7
  30.3 0.3 fusion.2
  30.6 0.0 collective-permute-done.6.refs_6_
  30.6 0.0 collective-permute-done.2.refs_2_
  30.6 1.2 %collective-permute-done.7.refs_7_ = bf16[592,256]{1,0:T(8,128)(2,1)S(1)} collective-permute-done((bf16[592,256]{1,0:T(8,128)(2,1)S(1)}, bf16[592,256]{1,0:T(8,128)(2,1)S(1)}, u32[]{:S(2)}, u32[]{:S(2)}) %collective-permute-start.7) | collective-permute-done | bytes 303136 | tf_op jit(solution)/shard_map/ppermute | solution.py:47
  31.8 0.0 collective-permute-done.3.refs_3_
  31.9 8.1 %head.1 = (bf16[592,1536]{1,0:T(8,128)(2,1)S(1)}, bf16[592,512]{1,0:T(8,128)(2,1)S(1)}, f32[256,512]{1,0:T(8,128)S(1)}, f32[24,512]{1,0:T(8,128)S(1)}, f32[440,512]{1,0:T(8,128)S(1)}, /*index=5*/f32[440,512]{1,0:T(8,128)S(1)}) custom-call(s32[7]{0:T(128)S(1)} %stack.28.scalars, bf16[592,384]{1,0:T(8,128)(2,1)S(1)} %slice_select_fusion.1.refs_0_, ...), custom_call_target="tpu_custom_call" | custom-call | tf_op jit(solution)/shard_map/head/pallas_call | solution.py:289
  40.0 0.1 convert_element_type.35
  40.0 1.9 %collective-permute-start.10 = (f16[440,512]{1,0:T(8,128)(2,1)S(1)}, f16[440,512]{1,0:T(8,128)(2,1)S(1)}, u32[]{:S(2)}, u32[]{:S(2)}) collective-permute-start(f16[440,512]{1,0:T(8,128)(2,1)S(1)} %convert_element_type.35), channel_id=1, source_target_pairs={{0,1},{1,0},{2,3},{3,2},{4,5},{5,4},{6,7},{7,6},{8,9},{9,8},{10,11... | collective-permute-start | bytes 1351688 | tf_op jit(solution)/shard_map/ppermute | solution.py:378
  41.9 0.1 convert_element_type.36
  42.0 0.7 collective-permute-start.11
  42.7 1.4 %blocks.1 = (f32[440,512]{1,0:T(8,128)S(1)}, f32[440,512]{1,0:T(8,128)S(1)}, f32[8,128]{1,0:T(8,128)S(1)}) custom-call(s32[7]{0:T(128)S(1)} %stack.28.scalars, bf16[592,1536]{1,0:T(8,128)(2,1)S(1)} %get-tuple-element.23.x, bf16[592,512]{1,0:T(8,128)(2,1)S(1)} %get-tuple-element.24.dpre, f32[256,512]{1,0:T(8,128)S(1)} %get-tuple-element.25.gout, ...), custom_call_target="tpu_custom_call" | custom-call | flops 465567744 | bytes 4227072 | tf_op jit(solution)/shard_map/blocks/pallas_call | solution.py:421
  44.1 8.5 %collective-permute-done.10 = f16[440,512]{1,0:T(8,128)(2,1)S(1)} collective-permute-done((f16[440,512]{1,0:T(8,128)(2,1)S(1)}, f16[440,512]{1,0:T(8,128)(2,1)S(1)}, u32[]{:S(2)}, u32[]{:S(2)}) %collective-permute-start.10) | collective-permute-done | bytes 450592 | tf_op jit(solution)/shard_map/ppermute | solution.py:378
  52.6 0.1 convert_element_type.37.theirs
  52.7 0.6 add.52
  53.4 0.1 convert_element_type.38
  53.4 1.8 %collective-permute-start.13 = (f16[440,512]{1,0:T(8,128)(2,1)S(1)}, f16[440,512]{1,0:T(8,128)(2,1)S(1)}, u32[]{:S(2)}, u32[]{:S(2)}) collective-permute-start(f16[440,512]{1,0:T(8,128)(2,1)S(1)} %convert_element_type.38), channel_id=1, source_target_pairs={{0,1},{3,2},{1,3},{2,0},{4,5},{7,6},{5,7},{6,4},{8,9},{11,10},{9,1... | collective-permute-start | bytes 1351688 | tf_op jit(solution)/shard_map/ppermute | solution.py:378
  55.3 3.1 %collective-permute-start.12 = (f16[440,512]{1,0:T(8,128)(2,1)S(1)}, f16[440,512]{1,0:T(8,128)(2,1)S(1)}, u32[]{:S(2)}, u32[]{:S(2)}) collective-permute-start(f16[440,512]{1,0:T(8,128)(2,1)S(1)} %convert_element_type.36), channel_id=1, source_target_pairs={{0,2},{3,1},{4,6},{7,5},{8,10},{11,9},{12,14},{15,13},{16,18},{19,... | collective-permute-start | bytes 1351688 | tf_op jit(solution)/shard_map/ppermute | solution.py:378
  58.3 0.1 select_convert_fusion
  58.5 15.6 %collective-permute-done.12 = f16[440,512]{1,0:T(8,128)(2,1)S(1)} collective-permute-done((f16[440,512]{1,0:T(8,128)(2,1)S(1)}, f16[440,512]{1,0:T(8,128)(2,1)S(1)}, u32[]{:S(2)}, u32[]{:S(2)}) %collective-permute-start.12) | collective-permute-done | bytes 450592 | tf_op jit(solution)/shard_map/ppermute | solution.py:378
  74.1 0.1 convert_element_type.40
  74.3 0.1 convert_element_type.41.last
  74.4 0.4 multiply_add_fusion.parts
  74.8 0.3 line.1.refs_0_
  75.0 5.2 %collective-permute-start.14 = (f32[32,128]{1,0:T(8,128)S(1)}, f32[32,128]{1,0:T(8,128)S(1)}, u32[]{:S(2)}, u32[]{:S(2)}) collective-permute-start(f32[32,128]{1,0:T(8,128)S(1)} %line.1.refs_0_), channel_id=1, source_target_pairs={{0,3},{1,2},{2,1},{3,0},{4,7},{5,6},{6,5},{7,4},{8,11},{9,10},{10,... | collective-permute-start | bytes 49160 | tf_op jit(solution)/shard_map/ppermute | solution.py:378
  80.3 0.0 collective-permute-start.15
  80.3 0.6 collective-permute-start.16
  80.9 1.0 %sums.1 = (f32[384,512]{1,0:T(8,128)}, f32[150,1,128]{2,1,0:T(1,128)}, f32[9,1,512]{2,1,0:T(1,128)}) custom-call(f32[440,512]{1,0:T(8,128)S(1)} %multiply_add_fusion.parts, f32[440,512]{1,0:T(8,128)S(1)} %convert_element_type.41.last), custom_call_target="tpu_custom_call" | custom-call | flops 450560 | bytes 3604480 | tf_op jit(solution)/shard_map/sums/pallas_call | solution.py:505
  81.9 0.1 collective-permute-done.14.refs_1_
  82.0 2.9 %collective-permute-done.15.refs_2_ = f32[32,128]{1,0:T(8,128)S(1)} collective-permute-done((f32[32,128]{1,0:T(8,128)S(1)}, f32[32,128]{1,0:T(8,128)S(1)}, u32[]{:S(2)}, u32[]{:S(2)}) %collective-permute-start.15) | collective-permute-done | bytes 16416 | tf_op jit(solution)/shard_map/ppermute | solution.py:378
  84.9 0.7 norms.1
  (24 shorter events, 0.2 us)
Async XLA Ops:
  0.6 2.9 %copy-start.2 = (bf16[1,1,592,1536]{3,2,1,0:T(8,128)(2,1)S(1)}, bf16[1,1,592,1536]{3,2,1,0:T(8,128)(2,1)}, u32[]{:S(2)}) copy-start(bf16[1,1,592,1536]{3,2,1,0:T(8,128)(2,1)} %param.7) | copy-start | bytes 5455876
  0.6 7.1 %copy-start.4 = (s32[1,592]{1,0:T(1,128)S(1)}, s32[1,592]{1,0:T(1,128)}, u32[]{:S(2)}) copy-start(s32[1,592]{1,0:T(1,128)} %param.10) | copy-start | bytes 7108
  0.7 7.1 %copy-start.3 = (bf16[1,512,150]{1,2,0:T(8,128)(2,1)S(1)}, bf16[1,512,150]{1,2,0:T(8,128)(2,1)}, u32[]{:S(2)}) copy-start(bf16[1,512,150]{1,2,0:T(8,128)(2,1)} %param.13) | copy-start | bytes 460804
  3.1 4.8 %collective-permute-start = (bf16[592,640]{1,0:T(8,128)(2,1)}, bf16[592,640]{1,0:T(8,128)(2,1)}, u32[]{:S(2)}, u32[]{:S(2)}) collective-permute-start(bf16[592,640]{1,0:T(8,128)(2,1)} %slice_select_fusion), channel_id=1, source_target_pairs={{0,4},{4,0},{8,12},{12,8},{1,5},{5,1},{9,13},{13,9},{2,6},{6,2},{1... | collective-permute-start | bytes 2273288 | tf_op jit(solution)/shard_map/ppermute | solution.py:37
  3.6 10.6 %collective-permute-start.4 = (bf16[592,256]{1,0:T(8,128)(2,1)S(1)}, bf16[592,256]{1,0:T(8,128)(2,1)S(1)}, u32[]{:S(2)}, u32[]{:S(2)}) collective-permute-start(bf16[592,256]{1,0:T(8,128)(2,1)S(1)} %slice.65.refs_8_), channel_id=1, source_target_pairs={{0,8},{8,0},{4,12},{12,4},{1,9},{9,1},{5,13},{13,5},{2,10},{10,2},... | collective-permute-start | bytes 909320 | tf_op jit(solution)/shard_map/ppermute | solution.py:36
  6.2 18.3 %collective-permute-start.8 = (bf16[592,256]{1,0:T(8,128)(2,1)S(1)}, bf16[592,256]{1,0:T(8,128)(2,1)S(1)}, u32[]{:S(2)}, u32[]{:S(2)}) collective-permute-start(bf16[592,256]{1,0:T(8,128)(2,1)S(1)} %slice.65.refs_8_), channel_id=1, source_target_pairs={{0,4},{4,0},{8,12},{12,8},{1,5},{5,1},{9,13},{13,9},{2,6},{6,2},{1... | collective-permute-start | bytes 909320 | tf_op jit(solution)/shard_map/ppermute | solution.py:49
  7.9 23.9 %copy-start = (bf16[1,1536,512]{2,1,0:T(8,128)(2,1)S(1)}, bf16[1,1536,512]{2,1,0:T(8,128)(2,1)}, u32[]{:S(2)}) copy-start(bf16[1,1536,512]{2,1,0:T(8,128)(2,1)} %param.11) | copy-start | bytes 4718596
  7.9 24.0 %copy-start.1 = (f32[1,9,512]{2,0,1:T(1,128)S(1)}, f32[1,9,512]{2,0,1:T(1,128)}, u32[]{:S(2)}) copy-start(f32[1,9,512]{2,0,1:T(1,128)} %param.12) | copy-start | bytes 55300
  9.2 14.8 %collective-permute-start.1 = (bf16[592,384]{1,0:T(8,128)(2,1)S(1)}, bf16[592,384]{1,0:T(8,128)(2,1)S(1)}, u32[]{:S(2)}, u32[]{:S(2)}) collective-permute-start(bf16[592,384]{1,0:T(8,128)(2,1)S(1)} %slice_select_fusion.1.refs_0_), channel_id=1, source_target_pairs={{0,8},{8,0},{4,12},{12,4},{1,9},{9,1},{5,13},{13,5},{2,10},{10,2},... | collective-permute-start | bytes 1363976 | tf_op jit(solution)/shard_map/ppermute | solution.py:46
  15.2 15.0 %collective-permute-start.5 = (bf16[592,256]{1,0:T(8,128)(2,1)S(1)}, bf16[592,256]{1,0:T(8,128)(2,1)S(1)}, u32[]{:S(2)}, u32[]{:S(2)}) collective-permute-start(bf16[592,256]{1,0:T(8,128)(2,1)S(1)} %slice_select_fusion.3.refs_4_), channel_id=1, source_target_pairs={{0,8},{8,0},{4,12},{12,4},{1,9},{9,1},{5,13},{13,5},{2,10},{10,2},... | collective-permute-start | bytes 909320 | tf_op jit(solution)/shard_map/ppermute | solution.py:46
  17.4 13.2 %collective-permute-start.2 = (bf16[592,384]{1,0:T(8,128)(2,1)S(1)}, bf16[592,384]{1,0:T(8,128)(2,1)S(1)}, u32[]{:S(2)}, u32[]{:S(2)}) collective-permute-start(bf16[592,384]{1,0:T(8,128)(2,1)S(1)} %slice_select_fusion.1.refs_0_), channel_id=1, source_target_pairs={{0,4},{4,0},{8,12},{12,8},{1,5},{5,1},{9,13},{13,9},{2,6},{6,2},{1... | collective-permute-start | bytes 1363976 | tf_op jit(solution)/shard_map/ppermute | solution.py:47
  23.9 7.9 %collective-permute-start.3 = (bf16[592,384]{1,0:T(8,128)(2,1)S(1)}, bf16[592,384]{1,0:T(8,128)(2,1)S(1)}, u32[]{:S(2)}, u32[]{:S(2)}) collective-permute-start(bf16[592,384]{1,0:T(8,128)(2,1)S(1)} %collective-permute-done.1.refs_1_), channel_id=1, source_target_pairs={{0,4},{4,0},{8,12},{12,8},{1,5},{5,1},{9,13},{13,9},{2,6},{6,2},{1... | collective-permute-start | bytes 1363976 | tf_op jit(solution)/shard_map/ppermute | solution.py:47
  23.9 6.6 %collective-permute-start.6 = (bf16[592,256]{1,0:T(8,128)(2,1)S(1)}, bf16[592,256]{1,0:T(8,128)(2,1)S(1)}, u32[]{:S(2)}, u32[]{:S(2)}) collective-permute-start(bf16[592,256]{1,0:T(8,128)(2,1)S(1)} %slice_select_fusion.3.refs_4_), channel_id=1, source_target_pairs={{0,4},{4,0},{8,12},{12,8},{1,5},{5,1},{9,13},{13,9},{2,6},{6,2},{1... | collective-permute-start | bytes 909320 | tf_op jit(solution)/shard_map/ppermute | solution.py:47
  24.5 6.1 %collective-permute-start.9 = (bf16[592,256]{1,0:T(8,128)(2,1)S(1)}, bf16[592,256]{1,0:T(8,128)(2,1)S(1)}, u32[]{:S(2)}, u32[]{:S(2)}) collective-permute-start(bf16[592,256]{1,0:T(8,128)(2,1)S(1)} %collective-permute-done.4.refs_10_), channel_id=1, source_target_pairs={{0,4},{4,0},{8,12},{12,8},{1,5},{5,1},{9,13},{13,9},{2,6},{6,2},{1... | collective-permute-start | bytes 909320 | tf_op jit(solution)/shard_map/ppermute | solution.py:50
  30.2 1.6 %collective-permute-start.7 = (bf16[592,256]{1,0:T(8,128)(2,1)S(1)}, bf16[592,256]{1,0:T(8,128)(2,1)S(1)}, u32[]{:S(2)}, u32[]{:S(2)}) collective-permute-start(bf16[592,256]{1,0:T(8,128)(2,1)S(1)} %collective-permute-done.5.refs_5_), channel_id=1, source_target_pairs={{0,4},{4,0},{8,12},{12,8},{1,5},{5,1},{9,13},{13,9},{2,6},{6,2},{1... | collective-permute-start | bytes 909320 | tf_op jit(solution)/shard_map/ppermute | solution.py:47
  40.0 12.6 %collective-permute-start.10 = (f16[440,512]{1,0:T(8,128)(2,1)S(1)}, f16[440,512]{1,0:T(8,128)(2,1)S(1)}, u32[]{:S(2)}, u32[]{:S(2)}) collective-permute-start(f16[440,512]{1,0:T(8,128)(2,1)S(1)} %convert_element_type.35), channel_id=1, source_target_pairs={{0,1},{1,0},{2,3},{3,2},{4,5},{5,4},{6,7},{7,6},{8,9},{9,8},{10,11... | collective-permute-start | bytes 1351688 | tf_op jit(solution)/shard_map/ppermute | solution.py:378
  42.0 16.4 %collective-permute-start.11 = (f16[440,512]{1,0:T(8,128)(2,1)S(1)}, f16[440,512]{1,0:T(8,128)(2,1)S(1)}, u32[]{:S(2)}, u32[]{:S(2)}) collective-permute-start(f16[440,512]{1,0:T(8,128)(2,1)S(1)} %convert_element_type.36), channel_id=1, source_target_pairs={{1,2},{2,1},{5,6},{6,5},{9,10},{10,9},{13,14},{14,13},{17,18},{18,... | collective-permute-start | bytes 1351688 | tf_op jit(solution)/shard_map/ppermute | solution.py:378
  53.4 20.8 %collective-permute-start.13 = (f16[440,512]{1,0:T(8,128)(2,1)S(1)}, f16[440,512]{1,0:T(8,128)(2,1)S(1)}, u32[]{:S(2)}, u32[]{:S(2)}) collective-permute-start(f16[440,512]{1,0:T(8,128)(2,1)S(1)} %convert_element_type.38), channel_id=1, source_target_pairs={{0,1},{3,2},{1,3},{2,0},{4,5},{7,6},{5,7},{6,4},{8,9},{11,10},{9,1... | collective-permute-start | bytes 1351688 | tf_op jit(solution)/shard_map/ppermute | solution.py:378
  55.3 18.8 %collective-permute-start.12 = (f16[440,512]{1,0:T(8,128)(2,1)S(1)}, f16[440,512]{1,0:T(8,128)(2,1)S(1)}, u32[]{:S(2)}, u32[]{:S(2)}) collective-permute-start(f16[440,512]{1,0:T(8,128)(2,1)S(1)} %convert_element_type.36), channel_id=1, source_target_pairs={{0,2},{3,1},{4,6},{7,5},{8,10},{11,9},{12,14},{15,13},{16,18},{19,... | collective-permute-start | bytes 1351688 | tf_op jit(solution)/shard_map/ppermute | solution.py:378
  75.0 7.0 %collective-permute-start.14 = (f32[32,128]{1,0:T(8,128)S(1)}, f32[32,128]{1,0:T(8,128)S(1)}, u32[]{:S(2)}, u32[]{:S(2)}) collective-permute-start(f32[32,128]{1,0:T(8,128)S(1)} %line.1.refs_0_), channel_id=1, source_target_pairs={{0,3},{1,2},{2,1},{3,0},{4,7},{5,6},{6,5},{7,4},{8,11},{9,10},{10,... | collective-permute-start | bytes 49160 | tf_op jit(solution)/shard_map/ppermute | solution.py:378
  80.3 4.6 %collective-permute-start.15 = (f32[32,128]{1,0:T(8,128)S(1)}, f32[32,128]{1,0:T(8,128)S(1)}, u32[]{:S(2)}, u32[]{:S(2)}) collective-permute-start(f32[32,128]{1,0:T(8,128)S(1)} %line.1.refs_0_), channel_id=1, source_target_pairs={{0,2},{1,3},{2,0},{3,1},{4,6},{5,7},{6,4},{7,5},{8,10},{9,11},{10,... | collective-permute-start | bytes 49160 | tf_op jit(solution)/shard_map/ppermute | solution.py:378
  80.3 4.6 %collective-permute-start.16 = (f32[32,128]{1,0:T(8,128)S(1)}, f32[32,128]{1,0:T(8,128)S(1)}, u32[]{:S(2)}, u32[]{:S(2)}) collective-permute-start(f32[32,128]{1,0:T(8,128)S(1)} %line.1.refs_0_), channel_id=1, source_target_pairs={{0,1},{1,0},{2,3},{3,2},{4,5},{5,4},{6,7},{7,6},{8,9},{9,8},{10,11... | collective-permute-start | bytes 49160 | tf_op jit(solution)/shard_map/ppermute | solution.py:378

commit v13 on v12

--- a/solution.py
+++ b/solution.py
@@ -354,10 +354,7 @@
         taps_out[k, :, :] = sum_taps[k : k + 1, :]
 
 
-def norm_kernel(chunks, *refs):
-    lines, out = refs[:-1], refs[-1]
-    total = sum(line[...] for line in lines)
-    line = lines[0]
+def norm_kernel(chunks, line, total, out):
     values = [
         jnp.sum(total[16:17, :]),
         jnp.sum(total[17:18, :]),
@@ -501,7 +498,9 @@
         compiler_params=small,
         name="line",
     )(parts, last, stats)
-    lines = [line] + [permute(line, [(i, i ^ s) for i in range(dp)]) for s in (3, 2, 1)]
+    total = line
+    for step in (1, 2):
+        total = total + permute(total, [(i, i ^ step) for i in range(dp)])
     share_in, share_out, total_taps = pl.pallas_call(
         functools.partial(sum_kernel, sizes),
         out_shape=[
@@ -520,11 +519,11 @@
     norms = pl.pallas_call(
         functools.partial(norm_kernel, chunks),
         out_shape=jax.ShapeDtypeStruct((2, 3), jnp.float32),
-        in_specs=[vmem] * dp,
+        in_specs=[vmem] * 2,
         out_specs=vmem,
         compiler_params=pltpu.CompilerParams(vmem_limit_bytes=4 * 1024 * 1024),
         name="norms",
-    )(*lines)
+    )(line, total)
     share_out = jnp.transpose(share_out, (1, 2, 0))
     return (share_in[None], jnp.transpose(total_taps, (1, 0, 2)), share_out, norms[None])
 

time: 85.8 us -> 85.8 us (level)
    ppermute x7 -> x6, waiting for transfers between devices: 27.1 us -> 26.9 us  [permute(): return lax.ppermute(value, 'dp', pairs)]
    ppermute x7 -> x6, starting transfers between devices: 13.4 us -> 13.3 us  [permute(): return lax.ppermute(value, 'dp', pairs)]
  transfers between devices with their start and end apart: 17 -> 16, of which waited for: 8 -> 8; matrix products, arithmetic and copies ran while one was open for 4% -> 4% of each run, Pallas kernels for 4% -> 4%
where the time goes in v13:
time: 85.8 us; the launch traced here: 85.4 us
  waiting for transfers between devices  44.6 us (52%)
  starting transfers between devices  20 us (23%)
  Pallas kernels  12.2 us (14%)
  other arithmetic  6.29 us (7%)
  between operations  2.27 us (3%)
    ppermute x6, waiting for transfers between devices, permute(): return lax.ppermute(value, 'dp', pairs)  26.9 us
    ppermute x6, starting transfers between devices, permute(): return lax.ppermute(value, 'dp', pairs)  13.3 us
    ppermute x2, waiting for transfers between devices, pieces(): other = lax.ppermute(held, axis, across)  12.2 us
    pallas_call x1, Pallas kernels, head_backward(): pl.pallas_call(functools.partial(head_kernel, sizes, widths), out_shape=[...  8.19 us
    ppermute x1, waiting for transfers between devices, pieces(): shared_other = lax.ppermute(shared, axis, across)  4.26 us
    ppermute x2, starting transfers between devices, pieces(): other = lax.ppermute(held, axis, across)  2.79 us
    ppermute x1, starting transfers between devices, pieces(): shared_other = lax.ppermute(shared, axis, across)  2.55 us
    select_n x1, other arithmetic, pieces(): jnp.where(core == 0, block[:, width:2 * width], block[:, :width])  2.44 us
  transfers between devices with their start and end apart: 16, of which 8 were waited for; matrix products, arithmetic and copies ran while one was open for 4% of the time, Pallas kernels for 4%

profile of v13, /device:TPU:0, one launch (start us, length us, event | category | flops | bytes accessed | tf_op | source)
XLA Modules:
  0.0 85.4 jit_solution(6392348069279841191)
XLA Ops:
  0.7 2.4 %slice_select_fusion = bf16[592,640]{1,0:T(8,128)(2,1)} fusion(bf16[592,1536]{1,0:T(8,128)(2,1)} %bitcast.30, pred[]{:T(512)S(6)} %eq.46), kind=kLoop, calls=%fused_computation.1 | loop fusion | flops 378880 | bytes 2273281 | tf_op jit(solution)/shard_map/jit(_where)/select_n | solution.py:37
  3.1 0.5 collective-permute-start
  3.6 2.6 %collective-permute-start.4 = (bf16[592,256]{1,0:T(8,128)(2,1)S(1)}, bf16[592,256]{1,0:T(8,128)(2,1)S(1)}, u32[]{:S(2)}, u32[]{:S(2)}) collective-permute-start(bf16[592,256]{1,0:T(8,128)(2,1)S(1)} %slice.65.refs_8_), channel_id=1, source_target_pairs={{0,8},{8,0},{4,12},{12,4},{1,9},{9,1},{5,13},{13,5},{2,10},{10,2},... | collective-permute-start | bytes 909320 | tf_op jit(solution)/shard_map/ppermute | solution.py:36
  6.2 0.2 collective-permute-start.8
  7.8 0.1 stack.28.scalars
  7.9 0.0 collective-permute-done
  7.9 1.2 %slice_select_fusion.1.refs_0_ = bf16[592,384]{1,0:T(8,128)(2,1)S(1)} fusion(bf16[592,640]{1,0:T(8,128)(2,1)} %collective-permute-done, bf16[592,1536]{1,0:T(8,128)(2,1)S(1)} %bitcast.32, pred[]{:T(512)S(6)} %eq.46, pred[]{:T(512)S(6)} %eq.45), kind=kLoop, calls=%fused_computation.4 | loop fusion | flops 454656 | bytes 1818626 | tf_op jit(solution)/shard_map/jit(_where)/select_n | solution.py:45
  9.2 0.8 collective-permute-start.1
  9.9 4.3 %collective-permute-done.4.refs_10_ = bf16[592,256]{1,0:T(8,128)(2,1)S(1)} collective-permute-done((bf16[592,256]{1,0:T(8,128)(2,1)S(1)}, bf16[592,256]{1,0:T(8,128)(2,1)S(1)}, u32[]{:S(2)}, u32[]{:S(2)}) %collective-permute-start.4) | collective-permute-done | bytes 303136 | tf_op jit(solution)/shard_map/ppermute | solution.py:36
  14.2 1.0 %slice_select_fusion.3.refs_4_ = bf16[592,256]{1,0:T(8,128)(2,1)S(1)} fusion(bf16[592,640]{1,0:T(8,128)(2,1)} %collective-permute-done, bf16[592,1536]{1,0:T(8,128)(2,1)S(1)} %bitcast.33, pred[]{:T(512)S(6)} %eq.46, pred[]{:T(512)S(6)} %eq.45), kind=kLoop, calls=%fused_computation.9 | loop fusion | flops 303104 | bytes 1212418 | tf_op jit(solution)/shard_map/jit(_where)/select_n | solution.py:45
  15.2 2.0 %collective-permute-start.5 = (bf16[592,256]{1,0:T(8,128)(2,1)S(1)}, bf16[592,256]{1,0:T(8,128)(2,1)S(1)}, u32[]{:S(2)}, u32[]{:S(2)}) collective-permute-start(bf16[592,256]{1,0:T(8,128)(2,1)S(1)} %slice_select_fusion.3.refs_4_), channel_id=1, source_target_pairs={{0,8},{8,0},{4,12},{12,4},{1,9},{9,1},{5,13},{13,5},{2,10},{10,2},... | collective-permute-start | bytes 909320 | tf_op jit(solution)/shard_map/ppermute | solution.py:46
  17.2 0.1 fusion.refs_15_
  17.4 0.1 collective-permute-start.2
  17.5 6.5 %collective-permute-done.1.refs_1_ = bf16[592,384]{1,0:T(8,128)(2,1)S(1)} collective-permute-done((bf16[592,384]{1,0:T(8,128)(2,1)S(1)}, bf16[592,384]{1,0:T(8,128)(2,1)S(1)}, u32[]{:S(2)}, u32[]{:S(2)}) %collective-permute-start.1) | collective-permute-done | bytes 454688 | tf_op jit(solution)/shard_map/ppermute | solution.py:46
  23.9 0.0 collective-permute-start.3
  23.9 0.5 collective-permute-start.6
  24.5 0.1 collective-permute-start.9
  24.5 5.7 %collective-permute-done.5.refs_5_ = bf16[592,256]{1,0:T(8,128)(2,1)S(1)} collective-permute-done((bf16[592,256]{1,0:T(8,128)(2,1)S(1)}, bf16[592,256]{1,0:T(8,128)(2,1)S(1)}, u32[]{:S(2)}, u32[]{:S(2)}) %collective-permute-start.5) | collective-permute-done | bytes 303136 | tf_op jit(solution)/shard_map/ppermute | solution.py:46
  30.3 0.3 fusion.2
  30.6 0.0 collective-permute-done.9.refs_11_
  30.6 0.0 collective-permute-done.2.refs_2_
  30.6 1.2 %collective-permute-done.7.refs_7_ = bf16[592,256]{1,0:T(8,128)(2,1)S(1)} collective-permute-done((bf16[592,256]{1,0:T(8,128)(2,1)S(1)}, bf16[592,256]{1,0:T(8,128)(2,1)S(1)}, u32[]{:S(2)}, u32[]{:S(2)}) %collective-permute-start.7) | collective-permute-done | bytes 303136 | tf_op jit(solution)/shard_map/ppermute | solution.py:47
  31.9 8.2 %head.1 = (bf16[592,1536]{1,0:T(8,128)(2,1)S(1)}, bf16[592,512]{1,0:T(8,128)(2,1)S(1)}, f32[256,512]{1,0:T(8,128)S(1)}, f32[24,512]{1,0:T(8,128)S(1)}, f32[440,512]{1,0:T(8,128)S(1)}, /*index=5*/f32[440,512]{1,0:T(8,128)S(1)}) custom-call(s32[7]{0:T(128)S(1)} %stack.28.scalars, bf16[592,384]{1,0:T(8,128)(2,1)S(1)} %slice_select_fusion.1.refs_0_, ...), custom_call_target="tpu_custom_call" | custom-call | tf_op jit(solution)/shard_map/head/pallas_call | solution.py:289
  40.1 0.1 convert_element_type.35
  40.1 1.9 %collective-permute-start.10 = (f16[440,512]{1,0:T(8,128)(2,1)S(1)}, f16[440,512]{1,0:T(8,128)(2,1)S(1)}, u32[]{:S(2)}, u32[]{:S(2)}) collective-permute-start(f16[440,512]{1,0:T(8,128)(2,1)S(1)} %convert_element_type.35), channel_id=1, source_target_pairs={{0,1},{1,0},{2,3},{3,2},{4,5},{5,4},{6,7},{7,6},{8,9},{9,8},{10,11... | collective-permute-start | bytes 1351688 | tf_op jit(solution)/shard_map/ppermute | solution.py:375
  42.0 0.1 convert_element_type.36
  42.1 0.7 collective-permute-start.11
  42.8 1.4 %blocks.1 = (f32[440,512]{1,0:T(8,128)S(1)}, f32[440,512]{1,0:T(8,128)S(1)}, f32[8,128]{1,0:T(8,128)S(1)}) custom-call(s32[7]{0:T(128)S(1)} %stack.28.scalars, bf16[592,1536]{1,0:T(8,128)(2,1)S(1)} %get-tuple-element.23.x, bf16[592,512]{1,0:T(8,128)(2,1)S(1)} %get-tuple-element.24.dpre, f32[256,512]{1,0:T(8,128)S(1)} %get-tuple-element.25.gout, ...), custom_call_target="tpu_custom_call" | custom-call | flops 465567744 | bytes 4227072 | tf_op jit(solution)/shard_map/blocks/pallas_call | solution.py:418
  44.2 8.4 %collective-permute-done.10 = f16[440,512]{1,0:T(8,128)(2,1)S(1)} collective-permute-done((f16[440,512]{1,0:T(8,128)(2,1)S(1)}, f16[440,512]{1,0:T(8,128)(2,1)S(1)}, u32[]{:S(2)}, u32[]{:S(2)}) %collective-permute-start.10) | collective-permute-done | bytes 450592 | tf_op jit(solution)/shard_map/ppermute | solution.py:375
  52.6 0.1 convert_element_type.37.theirs
  52.7 0.6 add.60
  53.3 0.1 convert_element_type.38
  53.4 1.8 %collective-permute-start.13 = (f16[440,512]{1,0:T(8,128)(2,1)S(1)}, f16[440,512]{1,0:T(8,128)(2,1)S(1)}, u32[]{:S(2)}, u32[]{:S(2)}) collective-permute-start(f16[440,512]{1,0:T(8,128)(2,1)S(1)} %convert_element_type.38), channel_id=1, source_target_pairs={{0,1},{3,2},{1,3},{2,0},{4,5},{7,6},{5,7},{6,4},{8,9},{11,10},{9,1... | collective-permute-start | bytes 1351688 | tf_op jit(solution)/shard_map/ppermute | solution.py:375
  55.2 3.1 %collective-permute-start.12 = (f16[440,512]{1,0:T(8,128)(2,1)S(1)}, f16[440,512]{1,0:T(8,128)(2,1)S(1)}, u32[]{:S(2)}, u32[]{:S(2)}) collective-permute-start(f16[440,512]{1,0:T(8,128)(2,1)S(1)} %convert_element_type.36), channel_id=1, source_target_pairs={{0,2},{3,1},{4,6},{7,5},{8,10},{11,9},{12,14},{15,13},{16,18},{19,... | collective-permute-start | bytes 1351688 | tf_op jit(solution)/shard_map/ppermute | solution.py:375
  58.3 0.0 collective-permute-done.11
  58.3 0.1 select_convert_fusion
  58.4 15.4 %collective-permute-done.12 = f16[440,512]{1,0:T(8,128)(2,1)S(1)} collective-permute-done((f16[440,512]{1,0:T(8,128)(2,1)S(1)}, f16[440,512]{1,0:T(8,128)(2,1)S(1)}, u32[]{:S(2)}, u32[]{:S(2)}) %collective-permute-start.12) | collective-permute-done | bytes 450592 | tf_op jit(solution)/shard_map/ppermute | solution.py:375
  73.8 0.1 convert_element_type.40
  74.0 0.0 collective-permute-done.13
  74.0 0.1 convert_element_type.41.last
  74.1 0.4 multiply_add_fusion.parts
  74.5 0.3 line.1
  74.8 3.5 %collective-permute-start.14 = (f32[32,128]{1,0:T(8,128)S(1)}, f32[32,128]{1,0:T(8,128)S(1)}, u32[]{:S(2)}, u32[]{:S(2)}) collective-permute-start(f32[32,128]{1,0:T(8,128)S(1)} %line.1), channel_id=1, source_target_pairs={{0,1},{1,0},{2,3},{3,2},{4,5},{5,4},{6,7},{7,6},{8,9},{9,8},{10,11... | collective-permute-start | bytes 49160 | tf_op jit(solution)/shard_map/ppermute | solution.py:375
  78.3 1.7 %collective-permute-done.14 = f32[32,128]{1,0:T(8,128)S(1)} collective-permute-done((f32[32,128]{1,0:T(8,128)S(1)}, f32[32,128]{1,0:T(8,128)S(1)}, u32[]{:S(2)}, u32[]{:S(2)}) %collective-permute-start.14) | collective-permute-done | bytes 16416 | tf_op jit(solution)/shard_map/ppermute | solution.py:375
  80.0 2.3 %collective-permute-start.15 = (f32[32,128]{1,0:T(8,128)S(1)}, f32[32,128]{1,0:T(8,128)S(1)}, u32[]{:S(2)}, u32[]{:S(2)}) collective-permute-start(f32[32,128]{1,0:T(8,128)S(1)} %add.54), channel_id=1, source_target_pairs={{0,2},{1,3},{2,0},{3,1},{4,6},{5,7},{6,4},{7,5},{8,10},{9,11},{10,... | collective-permute-start | bytes 49160 | tf_op jit(solution)/shard_map/ppermute | solution.py:375
  82.3 1.0 %sums.1 = (f32[384,512]{1,0:T(8,128)}, f32[150,1,128]{2,1,0:T(1,128)}, f32[9,1,512]{2,1,0:T(1,128)}) custom-call(f32[440,512]{1,0:T(8,128)S(1)} %multiply_add_fusion.parts, f32[440,512]{1,0:T(8,128)S(1)} %convert_element_type.41.last), custom_call_target="tpu_custom_call" | custom-call | flops 450560 | bytes 3604480 | tf_op jit(solution)/shard_map/sums/pallas_call | solution.py:504
  83.3 1.4 %collective-permute-done.15 = f32[32,128]{1,0:T(8,128)S(1)} collective-permute-done((f32[32,128]{1,0:T(8,128)S(1)}, f32[32,128]{1,0:T(8,128)S(1)}, u32[]{:S(2)}, u32[]{:S(2)}) %collective-permute-start.15) | collective-permute-done | bytes 16416 | tf_op jit(solution)/shard_map/ppermute | solution.py:375
  84.7 0.7 norms.1
  (24 shorter events, 0.2 us)
Async XLA Ops:
  0.6 2.9 %copy-start.2 = (bf16[1,1,592,1536]{3,2,1,0:T(8,128)(2,1)S(1)}, bf16[1,1,592,1536]{3,2,1,0:T(8,128)(2,1)}, u32[]{:S(2)}) copy-start(bf16[1,1,592,1536]{3,2,1,0:T(8,128)(2,1)} %param.7) | copy-start | bytes 5455876
  0.6 7.1 %copy-start.4 = (s32[1,592]{1,0:T(1,128)S(1)}, s32[1,592]{1,0:T(1,128)}, u32[]{:S(2)}) copy-start(s32[1,592]{1,0:T(1,128)} %param.10) | copy-start | bytes 7108
  0.7 7.1 %copy-start.3 = (bf16[1,512,150]{1,2,0:T(8,128)(2,1)S(1)}, bf16[1,512,150]{1,2,0:T(8,128)(2,1)}, u32[]{:S(2)}) copy-start(bf16[1,512,150]{1,2,0:T(8,128)(2,1)} %param.13) | copy-start | bytes 460804
  3.1 4.8 %collective-permute-start = (bf16[592,640]{1,0:T(8,128)(2,1)}, bf16[592,640]{1,0:T(8,128)(2,1)}, u32[]{:S(2)}, u32[]{:S(2)}) collective-permute-start(bf16[592,640]{1,0:T(8,128)(2,1)} %slice_select_fusion), channel_id=1, source_target_pairs={{0,4},{4,0},{8,12},{12,8},{1,5},{5,1},{9,13},{13,9},{2,6},{6,2},{1... | collective-permute-start | bytes 2273288 | tf_op jit(solution)/shard_map/ppermute | solution.py:37
  3.6 10.6 %collective-permute-start.4 = (bf16[592,256]{1,0:T(8,128)(2,1)S(1)}, bf16[592,256]{1,0:T(8,128)(2,1)S(1)}, u32[]{:S(2)}, u32[]{:S(2)}) collective-permute-start(bf16[592,256]{1,0:T(8,128)(2,1)S(1)} %slice.65.refs_8_), channel_id=1, source_target_pairs={{0,8},{8,0},{4,12},{12,4},{1,9},{9,1},{5,13},{13,5},{2,10},{10,2},... | collective-permute-start | bytes 909320 | tf_op jit(solution)/shard_map/ppermute | solution.py:36
  6.2 18.3 %collective-permute-start.8 = (bf16[592,256]{1,0:T(8,128)(2,1)S(1)}, bf16[592,256]{1,0:T(8,128)(2,1)S(1)}, u32[]{:S(2)}, u32[]{:S(2)}) collective-permute-start(bf16[592,256]{1,0:T(8,128)(2,1)S(1)} %slice.65.refs_8_), channel_id=1, source_target_pairs={{0,4},{4,0},{8,12},{12,8},{1,5},{5,1},{9,13},{13,9},{2,6},{6,2},{1... | collective-permute-start | bytes 909320 | tf_op jit(solution)/shard_map/ppermute | solution.py:49
  7.9 23.9 %copy-start = (bf16[1,1536,512]{2,1,0:T(8,128)(2,1)S(1)}, bf16[1,1536,512]{2,1,0:T(8,128)(2,1)}, u32[]{:S(2)}) copy-start(bf16[1,1536,512]{2,1,0:T(8,128)(2,1)} %param.11) | copy-start | bytes 4718596
  7.9 24.0 %copy-start.1 = (f32[1,9,512]{2,0,1:T(1,128)S(1)}, f32[1,9,512]{2,0,1:T(1,128)}, u32[]{:S(2)}) copy-start(f32[1,9,512]{2,0,1:T(1,128)} %param.12) | copy-start | bytes 55300
  9.2 14.8 %collective-permute-start.1 = (bf16[592,384]{1,0:T(8,128)(2,1)S(1)}, bf16[592,384]{1,0:T(8,128)(2,1)S(1)}, u32[]{:S(2)}, u32[]{:S(2)}) collective-permute-start(bf16[592,384]{1,0:T(8,128)(2,1)S(1)} %slice_select_fusion.1.refs_0_), channel_id=1, source_target_pairs={{0,8},{8,0},{4,12},{12,4},{1,9},{9,1},{5,13},{13,5},{2,10},{10,2},... | collective-permute-start | bytes 1363976 | tf_op jit(solution)/shard_map/ppermute | solution.py:46
  15.2 15.0 %collective-permute-start.5 = (bf16[592,256]{1,0:T(8,128)(2,1)S(1)}, bf16[592,256]{1,0:T(8,128)(2,1)S(1)}, u32[]{:S(2)}, u32[]{:S(2)}) collective-permute-start(bf16[592,256]{1,0:T(8,128)(2,1)S(1)} %slice_select_fusion.3.refs_4_), channel_id=1, source_target_pairs={{0,8},{8,0},{4,12},{12,4},{1,9},{9,1},{5,13},{13,5},{2,10},{10,2},... | collective-permute-start | bytes 909320 | tf_op jit(solution)/shard_map/ppermute | solution.py:46
  17.4 13.2 %collective-permute-start.2 = (bf16[592,384]{1,0:T(8,128)(2,1)S(1)}, bf16[592,384]{1,0:T(8,128)(2,1)S(1)}, u32[]{:S(2)}, u32[]{:S(2)}) collective-permute-start(bf16[592,384]{1,0:T(8,128)(2,1)S(1)} %slice_select_fusion.1.refs_0_), channel_id=1, source_target_pairs={{0,4},{4,0},{8,12},{12,8},{1,5},{5,1},{9,13},{13,9},{2,6},{6,2},{1... | collective-permute-start | bytes 1363976 | tf_op jit(solution)/shard_map/ppermute | solution.py:47
  23.9 7.9 %collective-permute-start.3 = (bf16[592,384]{1,0:T(8,128)(2,1)S(1)}, bf16[592,384]{1,0:T(8,128)(2,1)S(1)}, u32[]{:S(2)}, u32[]{:S(2)}) collective-permute-start(bf16[592,384]{1,0:T(8,128)(2,1)S(1)} %collective-permute-done.1.refs_1_), channel_id=1, source_target_pairs={{0,4},{4,0},{8,12},{12,8},{1,5},{5,1},{9,13},{13,9},{2,6},{6,2},{1... | collective-permute-start | bytes 1363976 | tf_op jit(solution)/shard_map/ppermute | solution.py:47
  23.9 6.6 %collective-permute-start.6 = (bf16[592,256]{1,0:T(8,128)(2,1)S(1)}, bf16[592,256]{1,0:T(8,128)(2,1)S(1)}, u32[]{:S(2)}, u32[]{:S(2)}) collective-permute-start(bf16[592,256]{1,0:T(8,128)(2,1)S(1)} %slice_select_fusion.3.refs_4_), channel_id=1, source_target_pairs={{0,4},{4,0},{8,12},{12,8},{1,5},{5,1},{9,13},{13,9},{2,6},{6,2},{1... | collective-permute-start | bytes 909320 | tf_op jit(solution)/shard_map/ppermute | solution.py:47
  24.5 6.1 %collective-permute-start.9 = (bf16[592,256]{1,0:T(8,128)(2,1)S(1)}, bf16[592,256]{1,0:T(8,128)(2,1)S(1)}, u32[]{:S(2)}, u32[]{:S(2)}) collective-permute-start(bf16[592,256]{1,0:T(8,128)(2,1)S(1)} %collective-permute-done.4.refs_10_), channel_id=1, source_target_pairs={{0,4},{4,0},{8,12},{12,8},{1,5},{5,1},{9,13},{13,9},{2,6},{6,2},{1... | collective-permute-start | bytes 909320 | tf_op jit(solution)/shard_map/ppermute | solution.py:50
  30.2 1.6 %collective-permute-start.7 = (bf16[592,256]{1,0:T(8,128)(2,1)S(1)}, bf16[592,256]{1,0:T(8,128)(2,1)S(1)}, u32[]{:S(2)}, u32[]{:S(2)}) collective-permute-start(bf16[592,256]{1,0:T(8,128)(2,1)S(1)} %collective-permute-done.5.refs_5_), channel_id=1, source_target_pairs={{0,4},{4,0},{8,12},{12,8},{1,5},{5,1},{9,13},{13,9},{2,6},{6,2},{1... | collective-permute-start | bytes 909320 | tf_op jit(solution)/shard_map/ppermute | solution.py:47
  40.1 12.4 %collective-permute-start.10 = (f16[440,512]{1,0:T(8,128)(2,1)S(1)}, f16[440,512]{1,0:T(8,128)(2,1)S(1)}, u32[]{:S(2)}, u32[]{:S(2)}) collective-permute-start(f16[440,512]{1,0:T(8,128)(2,1)S(1)} %convert_element_type.35), channel_id=1, source_target_pairs={{0,1},{1,0},{2,3},{3,2},{4,5},{5,4},{6,7},{7,6},{8,9},{9,8},{10,11... | collective-permute-start | bytes 1351688 | tf_op jit(solution)/shard_map/ppermute | solution.py:375
  42.1 16.2 %collective-permute-start.11 = (f16[440,512]{1,0:T(8,128)(2,1)S(1)}, f16[440,512]{1,0:T(8,128)(2,1)S(1)}, u32[]{:S(2)}, u32[]{:S(2)}) collective-permute-start(f16[440,512]{1,0:T(8,128)(2,1)S(1)} %convert_element_type.36), channel_id=1, source_target_pairs={{1,2},{2,1},{5,6},{6,5},{9,10},{10,9},{13,14},{14,13},{17,18},{18,... | collective-permute-start | bytes 1351688 | tf_op jit(solution)/shard_map/ppermute | solution.py:375
  53.4 20.6 %collective-permute-start.13 = (f16[440,512]{1,0:T(8,128)(2,1)S(1)}, f16[440,512]{1,0:T(8,128)(2,1)S(1)}, u32[]{:S(2)}, u32[]{:S(2)}) collective-permute-start(f16[440,512]{1,0:T(8,128)(2,1)S(1)} %convert_element_type.38), channel_id=1, source_target_pairs={{0,1},{3,2},{1,3},{2,0},{4,5},{7,6},{5,7},{6,4},{8,9},{11,10},{9,1... | collective-permute-start | bytes 1351688 | tf_op jit(solution)/shard_map/ppermute | solution.py:375
  55.2 18.6 %collective-permute-start.12 = (f16[440,512]{1,0:T(8,128)(2,1)S(1)}, f16[440,512]{1,0:T(8,128)(2,1)S(1)}, u32[]{:S(2)}, u32[]{:S(2)}) collective-permute-start(f16[440,512]{1,0:T(8,128)(2,1)S(1)} %convert_element_type.36), channel_id=1, source_target_pairs={{0,2},{3,1},{4,6},{7,5},{8,10},{11,9},{12,14},{15,13},{16,18},{19,... | collective-permute-start | bytes 1351688 | tf_op jit(solution)/shard_map/ppermute | solution.py:375
  74.8 5.3 %collective-permute-start.14 = (f32[32,128]{1,0:T(8,128)S(1)}, f32[32,128]{1,0:T(8,128)S(1)}, u32[]{:S(2)}, u32[]{:S(2)}) collective-permute-start(f32[32,128]{1,0:T(8,128)S(1)} %line.1), channel_id=1, source_target_pairs={{0,1},{1,0},{2,3},{3,2},{4,5},{5,4},{6,7},{7,6},{8,9},{9,8},{10,11... | collective-permute-start | bytes 49160 | tf_op jit(solution)/shard_map/ppermute | solution.py:375
  80.0 4.6 %collective-permute-start.15 = (f32[32,128]{1,0:T(8,128)S(1)}, f32[32,128]{1,0:T(8,128)S(1)}, u32[]{:S(2)}, u32[]{:S(2)}) collective-permute-start(f32[32,128]{1,0:T(8,128)S(1)} %add.54), channel_id=1, source_target_pairs={{0,2},{1,3},{2,0},{3,1},{4,6},{5,7},{6,4},{7,5},{8,10},{9,11},{10,... | collective-permute-start | bytes 49160 | tf_op jit(solution)/shard_map/ppermute | solution.py:375

commit v14 on v13

--- a/solution.py
+++ b/solution.py
@@ -33,6 +33,7 @@
     across = [(0, 2), (2, 0), (1, 3), (3, 1)]
     widths, width = split_width(wide)
     shared = block[:, 2 * width :]
+    block, shared = lax.optimization_barrier((block, shared))
     shared_other = lax.ppermute(shared, axis, across)
     got = lax.ppermute(jnp.where(core == 0, block[:, width : 2 * width], block[:, :width]), axis, mate)
     values = []
@@ -440,7 +441,7 @@
     )(scalars, late, near.astype(jnp.float32))
     both = both.astype(half)
     far = permute(both, [(0, 1), (3, 2), (1, 3), (2, 0)])
-    early, _ = lax.optimization_barrier((early, both))
+    early, _ = lax.optimization_barrier((early, near))
     near, middle, _ = lax.optimization_barrier((near, middle, both))
     skip = permute(early, [(0, 2), (3, 1)])
 

time: 85.8 us -> 88.8 us (1.035)
  waiting for transfers between devices: 44.6 us -> 50.6 us
  starting transfers between devices: 20 us -> 16.2 us
  local copies, waits for them, and re-layouts: 0.15 us -> 1.25 us
    ppermute x6, waiting for transfers between devices: 26.9 us -> 33.4 us  [permute(): return lax.ppermute(value, 'dp', pairs)]
    ppermute x6, starting transfers between devices: 13.3 us -> 9.19 us  [permute(): return lax.ppermute(value, 'dp', pairs)]
    slice x1, local copies, waits for them, and re-layouts: 0.02 us -> 1.12 us  [pieces(): shared = block[:, 2 * width:]]
  transfers between devices with their start and end apart: 16 -> 16, of which waited for: 8 -> 9; matrix products, arithmetic and copies ran while one was open for 4% -> 4% of each run, Pallas kernels for 4% -> 3%
where the time goes in v14:
time: 88.8 us; the launch traced here: 88.7 us
  waiting for transfers between devices  50.6 us (57%)
  starting transfers between devices  16.2 us (18%)
  Pallas kernels  12.1 us (14%)
  other arithmetic  6.16 us (7%)
  between operations  2.28 us (3%)
  local copies, waits for them, and re-layouts  1.25 us (1%)
    ppermute x6, waiting for transfers between devices, permute(): return lax.ppermute(value, 'dp', pairs)  33.4 us
    ppermute x2, waiting for transfers between devices, pieces(): other = lax.ppermute(held, axis, across)  12.2 us
    ppermute x6, starting transfers between devices, permute(): return lax.ppermute(value, 'dp', pairs)  9.19 us
    pallas_call x1, Pallas kernels, head_backward(): pl.pallas_call(functools.partial(head_kernel, sizes, widths), out_shape=[...  8.15 us
    ppermute x1, waiting for transfers between devices, pieces(): shared_other = lax.ppermute(shared, axis, across)  3.83 us
    ppermute x2, starting transfers between devices, pieces(): other = lax.ppermute(held, axis, across)  3.21 us
    ppermute x1, starting transfers between devices, pieces(): shared_other = lax.ppermute(shared, axis, across)  2.49 us
    select_n x1, other arithmetic, pieces(): jnp.where(core == 0, block[:, width:2 * width], block[:, :width])  2.31 us
  transfers between devices with their start and end apart: 16, of which 9 were waited for; matrix products, arithmetic and copies ran while one was open for 4% of the time, Pallas kernels for 3%

profile of v14, /device:TPU:0, one launch (start us, length us, event | category | flops | bytes accessed | tf_op | source)
XLA Modules:
  0.0 88.7 jit_solution(13005650041286754378)
XLA Ops:
  0.6 0.0 copy-start.2
  0.7 1.1 %slice.60.refs_8_ = bf16[592,256]{1,0:T(8,128)(2,1)S(1)} slice(bf16[592,1536]{1,0:T(8,128)(2,1)} %bitcast.30), slice={[0:592], [1280:1536]} | slice | bytes 606208 | tf_op jit(solution)/shard_map/slice | solution.py:35
  1.8 2.3 %slice_select_fusion = bf16[592,640]{1,0:T(8,128)(2,1)} fusion(bf16[592,1536]{1,0:T(8,128)(2,1)} %bitcast.31, pred[]{:T(512)S(6)} %eq.46), kind=kLoop, calls=%fused_computation.1 | loop fusion | flops 378880 | bytes 2273281 | tf_op jit(solution)/shard_map/jit(_where)/select_n | solution.py:38
  4.1 0.5 collective-permute-start
  4.6 2.5 %collective-permute-start.4 = (bf16[592,256]{1,0:T(8,128)(2,1)S(1)}, bf16[592,256]{1,0:T(8,128)(2,1)S(1)}, u32[]{:S(2)}, u32[]{:S(2)}) collective-permute-start(bf16[592,256]{1,0:T(8,128)(2,1)S(1)} %slice.60.refs_8_), channel_id=1, source_target_pairs={{0,8},{8,0},{4,12},{12,4},{1,9},{9,1},{5,13},{13,5},{2,10},{10,2},... | collective-permute-start | bytes 909320 | tf_op jit(solution)/shard_map/ppermute | solution.py:37
  7.1 0.2 collective-permute-start.8
  8.7 0.1 stack.28.scalars
  8.8 0.0 collective-permute-done
  8.8 1.2 %slice_select_fusion.1.refs_0_ = bf16[592,384]{1,0:T(8,128)(2,1)S(1)} fusion(bf16[592,640]{1,0:T(8,128)(2,1)} %collective-permute-done, bf16[592,1536]{1,0:T(8,128)(2,1)S(1)} %bitcast.32, pred[]{:T(512)S(6)} %eq.46, pred[]{:T(512)S(6)} %eq.45), kind=kLoop, calls=%fused_computation.4 | loop fusion | flops 454656 | bytes 1818626 | tf_op jit(solution)/shard_map/jit(_where)/select_n | solution.py:46
  10.1 1.2 %collective-permute-start.1 = (bf16[592,384]{1,0:T(8,128)(2,1)S(1)}, bf16[592,384]{1,0:T(8,128)(2,1)S(1)}, u32[]{:S(2)}, u32[]{:S(2)}) collective-permute-start(bf16[592,384]{1,0:T(8,128)(2,1)S(1)} %slice_select_fusion.1.refs_0_), channel_id=1, source_target_pairs={{0,8},{8,0},{4,12},{12,4},{1,9},{9,1},{5,13},{13,5},{2,10},{10,2},... | collective-permute-start | bytes 1363976 | tf_op jit(solution)/shard_map/ppermute | solution.py:47
  11.3 3.8 %collective-permute-done.4.refs_10_ = bf16[592,256]{1,0:T(8,128)(2,1)S(1)} collective-permute-done((bf16[592,256]{1,0:T(8,128)(2,1)S(1)}, bf16[592,256]{1,0:T(8,128)(2,1)S(1)}, u32[]{:S(2)}, u32[]{:S(2)}) %collective-permute-start.4) | collective-permute-done | bytes 303136 | tf_op jit(solution)/shard_map/ppermute | solution.py:37
  15.1 1.0 %slice_select_fusion.2.refs_4_ = bf16[592,256]{1,0:T(8,128)(2,1)S(1)} fusion(bf16[592,640]{1,0:T(8,128)(2,1)} %collective-permute-done, bf16[592,1536]{1,0:T(8,128)(2,1)S(1)} %bitcast.33, pred[]{:T(512)S(6)} %eq.46, pred[]{:T(512)S(6)} %eq.45), kind=kLoop, calls=%fused_computation.8 | loop fusion | flops 303104 | bytes 1212418 | tf_op jit(solution)/shard_map/jit(_where)/select_n | solution.py:46
  16.1 2.0 %collective-permute-start.5 = (bf16[592,256]{1,0:T(8,128)(2,1)S(1)}, bf16[592,256]{1,0:T(8,128)(2,1)S(1)}, u32[]{:S(2)}, u32[]{:S(2)}) collective-permute-start(bf16[592,256]{1,0:T(8,128)(2,1)S(1)} %slice_select_fusion.2.refs_4_), channel_id=1, source_target_pairs={{0,8},{8,0},{4,12},{12,4},{1,9},{9,1},{5,13},{13,5},{2,10},{10,2},... | collective-permute-start | bytes 909320 | tf_op jit(solution)/shard_map/ppermute | solution.py:47
  18.1 0.1 fusion.refs_15_
  18.3 0.1 collective-permute-start.2
  18.4 6.5 %collective-permute-done.1.refs_1_ = bf16[592,384]{1,0:T(8,128)(2,1)S(1)} collective-permute-done((bf16[592,384]{1,0:T(8,128)(2,1)S(1)}, bf16[592,384]{1,0:T(8,128)(2,1)S(1)}, u32[]{:S(2)}, u32[]{:S(2)}) %collective-permute-start.1) | collective-permute-done | bytes 454688 | tf_op jit(solution)/shard_map/ppermute | solution.py:47
  24.8 0.0 collective-permute-start.3
  24.8 0.5 collective-permute-start.6
  25.4 0.0 collective-permute-done.8.refs_9_
  25.4 0.1 collective-permute-start.9
  25.4 5.7 %collective-permute-done.5.refs_5_ = bf16[592,256]{1,0:T(8,128)(2,1)S(1)} collective-permute-done((bf16[592,256]{1,0:T(8,128)(2,1)S(1)}, bf16[592,256]{1,0:T(8,128)(2,1)S(1)}, u32[]{:S(2)}, u32[]{:S(2)}) %collective-permute-start.5) | collective-permute-done | bytes 303136 | tf_op jit(solution)/shard_map/ppermute | solution.py:47
  31.2 0.3 fusion.2
  31.5 1.2 %collective-permute-done.7.refs_7_ = bf16[592,256]{1,0:T(8,128)(2,1)S(1)} collective-permute-done((bf16[592,256]{1,0:T(8,128)(2,1)S(1)}, bf16[592,256]{1,0:T(8,128)(2,1)S(1)}, u32[]{:S(2)}, u32[]{:S(2)}) %collective-permute-start.7) | collective-permute-done | bytes 303136 | tf_op jit(solution)/shard_map/ppermute | solution.py:48
  32.8 8.2 %head.1 = (bf16[592,1536]{1,0:T(8,128)(2,1)S(1)}, bf16[592,512]{1,0:T(8,128)(2,1)S(1)}, f32[256,512]{1,0:T(8,128)S(1)}, f32[24,512]{1,0:T(8,128)S(1)}, f32[440,512]{1,0:T(8,128)S(1)}, /*index=5*/f32[440,512]{1,0:T(8,128)S(1)}) custom-call(s32[7]{0:T(128)S(1)} %stack.28.scalars, bf16[592,384]{1,0:T(8,128)(2,1)S(1)} %slice_select_fusion.1.refs_0_, ...), custom_call_target="tpu_custom_call" | custom-call | tf_op jit(solution)/shard_map/head/pallas_call | solution.py:290
  40.9 0.1 convert_element_type.35
  41.0 1.9 %collective-permute-start.10 = (f16[440,512]{1,0:T(8,128)(2,1)S(1)}, f16[440,512]{1,0:T(8,128)(2,1)S(1)}, u32[]{:S(2)}, u32[]{:S(2)}) collective-permute-start(f16[440,512]{1,0:T(8,128)(2,1)S(1)} %convert_element_type.35), channel_id=1, source_target_pairs={{0,1},{1,0},{2,3},{3,2},{4,5},{5,4},{6,7},{7,6},{8,9},{9,8},{10,11... | collective-permute-start | bytes 1351688 | tf_op jit(solution)/shard_map/ppermute | solution.py:376
  42.9 0.1 convert_element_type.36
  42.9 0.7 collective-permute-start.11
  43.7 1.4 %blocks.1 = (f32[440,512]{1,0:T(8,128)S(1)}, f32[440,512]{1,0:T(8,128)S(1)}, f32[8,128]{1,0:T(8,128)S(1)}) custom-call(s32[7]{0:T(128)S(1)} %stack.28.scalars, bf16[592,1536]{1,0:T(8,128)(2,1)S(1)} %get-tuple-element.27.x, bf16[592,512]{1,0:T(8,128)(2,1)S(1)} %get-tuple-element.28.dpre, f32[256,512]{1,0:T(8,128)S(1)} %get-tuple-element.29.gout, ...), custom_call_target="tpu_custom_call" | custom-call | flops 465567744 | bytes 4227072 | tf_op jit(solution)/shard_map/blocks/pallas_call | solution.py:419
  45.0 8.5 %collective-permute-done.10 = f16[440,512]{1,0:T(8,128)(2,1)S(1)} collective-permute-done((f16[440,512]{1,0:T(8,128)(2,1)S(1)}, f16[440,512]{1,0:T(8,128)(2,1)S(1)}, u32[]{:S(2)}, u32[]{:S(2)}) %collective-permute-start.10) | collective-permute-done | bytes 450592 | tf_op jit(solution)/shard_map/ppermute | solution.py:376
  53.5 4.7 %collective-permute-start.12 = (f16[440,512]{1,0:T(8,128)(2,1)S(1)}, f16[440,512]{1,0:T(8,128)(2,1)S(1)}, u32[]{:S(2)}, u32[]{:S(2)}) collective-permute-start(f16[440,512]{1,0:T(8,128)(2,1)S(1)} %convert_element_type.36), channel_id=1, source_target_pairs={{0,2},{3,1},{4,6},{7,5},{8,10},{11,9},{12,14},{15,13},{16,18},{19,... | collective-permute-start | bytes 1351688 | tf_op jit(solution)/shard_map/ppermute | solution.py:376
  58.2 0.1 convert_element_type.37.theirs
  58.4 0.6 add.60
  59.0 0.1 convert_element_type.38
  59.0 0.1 collective-permute-start.13
  59.1 0.1 select_convert_fusion
  59.3 9.8 %collective-permute-done.12 = f16[440,512]{1,0:T(8,128)(2,1)S(1)} collective-permute-done((f16[440,512]{1,0:T(8,128)(2,1)S(1)}, f16[440,512]{1,0:T(8,128)(2,1)S(1)}, u32[]{:S(2)}, u32[]{:S(2)}) %collective-permute-start.12) | collective-permute-done | bytes 450592 | tf_op jit(solution)/shard_map/ppermute | solution.py:376
  69.0 0.1 convert_element_type.40
  69.2 9.6 %collective-permute-done.13 = f16[440,512]{1,0:T(8,128)(2,1)S(1)} collective-permute-done((f16[440,512]{1,0:T(8,128)(2,1)S(1)}, f16[440,512]{1,0:T(8,128)(2,1)S(1)}, u32[]{:S(2)}, u32[]{:S(2)}) %collective-permute-start.13) | collective-permute-done | bytes 450592 | tf_op jit(solution)/shard_map/ppermute | solution.py:376
  78.7 0.1 convert_element_type.41.last
  78.9 0.4 multiply_add_fusion.parts
  79.3 0.3 line.1
  79.5 0.8 collective-permute-start.14
  80.4 3.0 %collective-permute-done.14 = f32[32,128]{1,0:T(8,128)S(1)} collective-permute-done((f32[32,128]{1,0:T(8,128)S(1)}, f32[32,128]{1,0:T(8,128)S(1)}, u32[]{:S(2)}, u32[]{:S(2)}) %collective-permute-start.14) | collective-permute-done | bytes 16416 | tf_op jit(solution)/shard_map/ppermute | solution.py:376
  83.3 1.0 %collective-permute-start.15 = (f32[32,128]{1,0:T(8,128)S(1)}, f32[32,128]{1,0:T(8,128)S(1)}, u32[]{:S(2)}, u32[]{:S(2)}) collective-permute-start(f32[32,128]{1,0:T(8,128)S(1)} %add.54), channel_id=1, source_target_pairs={{0,2},{1,3},{2,0},{3,1},{4,6},{5,7},{6,4},{7,5},{8,10},{9,11},{10,... | collective-permute-start | bytes 49160 | tf_op jit(solution)/shard_map/ppermute | solution.py:376
  84.4 1.0 %sums.1 = (f32[384,512]{1,0:T(8,128)}, f32[150,1,128]{2,1,0:T(1,128)}, f32[9,1,512]{2,1,0:T(1,128)}) custom-call(f32[440,512]{1,0:T(8,128)S(1)} %multiply_add_fusion.parts, f32[440,512]{1,0:T(8,128)S(1)} %convert_element_type.41.last), custom_call_target="tpu_custom_call" | custom-call | flops 450560 | bytes 3604480 | tf_op jit(solution)/shard_map/sums/pallas_call | solution.py:505
  85.4 2.6 %collective-permute-done.15 = f32[32,128]{1,0:T(8,128)S(1)} collective-permute-done((f32[32,128]{1,0:T(8,128)S(1)}, f32[32,128]{1,0:T(8,128)S(1)}, u32[]{:S(2)}, u32[]{:S(2)}) %collective-permute-start.15) | collective-permute-done | bytes 16416 | tf_op jit(solution)/shard_map/ppermute | solution.py:376
  88.0 0.7 norms.1
  (24 shorter events, 0.2 us)
Async XLA Ops:
  0.6 8.2 %copy-start.2 = (bf16[1,1,592,1536]{3,2,1,0:T(8,128)(2,1)S(1)}, bf16[1,1,592,1536]{3,2,1,0:T(8,128)(2,1)}, u32[]{:S(2)}) copy-start(bf16[1,1,592,1536]{3,2,1,0:T(8,128)(2,1)} %param.7) | copy-start | bytes 5455876
  0.6 8.0 %copy-start.4 = (s32[1,592]{1,0:T(1,128)S(1)}, s32[1,592]{1,0:T(1,128)}, u32[]{:S(2)}) copy-start(s32[1,592]{1,0:T(1,128)} %param.10) | copy-start | bytes 7108
  0.7 8.0 %copy-start.3 = (bf16[1,512,150]{1,2,0:T(8,128)(2,1)S(1)}, bf16[1,512,150]{1,2,0:T(8,128)(2,1)}, u32[]{:S(2)}) copy-start(bf16[1,512,150]{1,2,0:T(8,128)(2,1)} %param.13) | copy-start | bytes 460804
  4.1 4.7 %collective-permute-start = (bf16[592,640]{1,0:T(8,128)(2,1)}, bf16[592,640]{1,0:T(8,128)(2,1)}, u32[]{:S(2)}, u32[]{:S(2)}) collective-permute-start(bf16[592,640]{1,0:T(8,128)(2,1)} %slice_select_fusion), channel_id=1, source_target_pairs={{0,4},{4,0},{8,12},{12,8},{1,5},{5,1},{9,13},{13,9},{2,6},{6,2},{1... | collective-permute-start | bytes 2273288 | tf_op jit(solution)/shard_map/ppermute | solution.py:38
  4.6 10.5 %collective-permute-start.4 = (bf16[592,256]{1,0:T(8,128)(2,1)S(1)}, bf16[592,256]{1,0:T(8,128)(2,1)S(1)}, u32[]{:S(2)}, u32[]{:S(2)}) collective-permute-start(bf16[592,256]{1,0:T(8,128)(2,1)S(1)} %slice.60.refs_8_), channel_id=1, source_target_pairs={{0,8},{8,0},{4,12},{12,4},{1,9},{9,1},{5,13},{13,5},{2,10},{10,2},... | collective-permute-start | bytes 909320 | tf_op jit(solution)/shard_map/ppermute | solution.py:37
  7.1 18.3 %collective-permute-start.8 = (bf16[592,256]{1,0:T(8,128)(2,1)S(1)}, bf16[592,256]{1,0:T(8,128)(2,1)S(1)}, u32[]{:S(2)}, u32[]{:S(2)}) collective-permute-start(bf16[592,256]{1,0:T(8,128)(2,1)S(1)} %slice.60.refs_8_), channel_id=1, source_target_pairs={{0,4},{4,0},{8,12},{12,8},{1,5},{5,1},{9,13},{13,9},{2,6},{6,2},{1... | collective-permute-start | bytes 909320 | tf_op jit(solution)/shard_map/ppermute | solution.py:50
  8.8 23.9 %copy-start = (bf16[1,1536,512]{2,1,0:T(8,128)(2,1)S(1)}, bf16[1,1536,512]{2,1,0:T(8,128)(2,1)}, u32[]{:S(2)}) copy-start(bf16[1,1536,512]{2,1,0:T(8,128)(2,1)} %param.11) | copy-start | bytes 4718596
  8.8 23.9 %copy-start.1 = (f32[1,9,512]{2,0,1:T(1,128)S(1)}, f32[1,9,512]{2,0,1:T(1,128)}, u32[]{:S(2)}) copy-start(f32[1,9,512]{2,0,1:T(1,128)} %param.12) | copy-start | bytes 55300
  10.1 14.8 %collective-permute-start.1 = (bf16[592,384]{1,0:T(8,128)(2,1)S(1)}, bf16[592,384]{1,0:T(8,128)(2,1)S(1)}, u32[]{:S(2)}, u32[]{:S(2)}) collective-permute-start(bf16[592,384]{1,0:T(8,128)(2,1)S(1)} %slice_select_fusion.1.refs_0_), channel_id=1, source_target_pairs={{0,8},{8,0},{4,12},{12,4},{1,9},{9,1},{5,13},{13,5},{2,10},{10,2},... | collective-permute-start | bytes 1363976 | tf_op jit(solution)/shard_map/ppermute | solution.py:47
  16.1 15.0 %collective-permute-start.5 = (bf16[592,256]{1,0:T(8,128)(2,1)S(1)}, bf16[592,256]{1,0:T(8,128)(2,1)S(1)}, u32[]{:S(2)}, u32[]{:S(2)}) collective-permute-start(bf16[592,256]{1,0:T(8,128)(2,1)S(1)} %slice_select_fusion.2.refs_4_), channel_id=1, source_target_pairs={{0,8},{8,0},{4,12},{12,4},{1,9},{9,1},{5,13},{13,5},{2,10},{10,2},... | collective-permute-start | bytes 909320 | tf_op jit(solution)/shard_map/ppermute | solution.py:47
  18.3 13.2 %collective-permute-start.2 = (bf16[592,384]{1,0:T(8,128)(2,1)S(1)}, bf16[592,384]{1,0:T(8,128)(2,1)S(1)}, u32[]{:S(2)}, u32[]{:S(2)}) collective-permute-start(bf16[592,384]{1,0:T(8,128)(2,1)S(1)} %slice_select_fusion.1.refs_0_), channel_id=1, source_target_pairs={{0,4},{4,0},{8,12},{12,8},{1,5},{5,1},{9,13},{13,9},{2,6},{6,2},{1... | collective-permute-start | bytes 1363976 | tf_op jit(solution)/shard_map/ppermute | solution.py:48
  24.8 7.9 %collective-permute-start.3 = (bf16[592,384]{1,0:T(8,128)(2,1)S(1)}, bf16[592,384]{1,0:T(8,128)(2,1)S(1)}, u32[]{:S(2)}, u32[]{:S(2)}) collective-permute-start(bf16[592,384]{1,0:T(8,128)(2,1)S(1)} %collective-permute-done.1.refs_1_), channel_id=1, source_target_pairs={{0,4},{4,0},{8,12},{12,8},{1,5},{5,1},{9,13},{13,9},{2,6},{6,2},{1... | collective-permute-start | bytes 1363976 | tf_op jit(solution)/shard_map/ppermute | solution.py:48
  24.8 6.6 %collective-permute-start.6 = (bf16[592,256]{1,0:T(8,128)(2,1)S(1)}, bf16[592,256]{1,0:T(8,128)(2,1)S(1)}, u32[]{:S(2)}, u32[]{:S(2)}) collective-permute-start(bf16[592,256]{1,0:T(8,128)(2,1)S(1)} %slice_select_fusion.2.refs_4_), channel_id=1, source_target_pairs={{0,4},{4,0},{8,12},{12,8},{1,5},{5,1},{9,13},{13,9},{2,6},{6,2},{1... | collective-permute-start | bytes 909320 | tf_op jit(solution)/shard_map/ppermute | solution.py:48
  25.4 6.1 %collective-permute-start.9 = (bf16[592,256]{1,0:T(8,128)(2,1)S(1)}, bf16[592,256]{1,0:T(8,128)(2,1)S(1)}, u32[]{:S(2)}, u32[]{:S(2)}) collective-permute-start(bf16[592,256]{1,0:T(8,128)(2,1)S(1)} %collective-permute-done.4.refs_10_), channel_id=1, source_target_pairs={{0,4},{4,0},{8,12},{12,8},{1,5},{5,1},{9,13},{13,9},{2,6},{6,2},{1... | collective-permute-start | bytes 909320 | tf_op jit(solution)/shard_map/ppermute | solution.py:51
  31.1 1.6 %collective-permute-start.7 = (bf16[592,256]{1,0:T(8,128)(2,1)S(1)}, bf16[592,256]{1,0:T(8,128)(2,1)S(1)}, u32[]{:S(2)}, u32[]{:S(2)}) collective-permute-start(bf16[592,256]{1,0:T(8,128)(2,1)S(1)} %collective-permute-done.5.refs_5_), channel_id=1, source_target_pairs={{0,4},{4,0},{8,12},{12,8},{1,5},{5,1},{9,13},{13,9},{2,6},{6,2},{1... | collective-permute-start | bytes 909320 | tf_op jit(solution)/shard_map/ppermute | solution.py:48
  41.0 12.6 %collective-permute-start.10 = (f16[440,512]{1,0:T(8,128)(2,1)S(1)}, f16[440,512]{1,0:T(8,128)(2,1)S(1)}, u32[]{:S(2)}, u32[]{:S(2)}) collective-permute-start(f16[440,512]{1,0:T(8,128)(2,1)S(1)} %convert_element_type.35), channel_id=1, source_target_pairs={{0,1},{1,0},{2,3},{3,2},{4,5},{5,4},{6,7},{7,6},{8,9},{9,8},{10,11... | collective-permute-start | bytes 1351688 | tf_op jit(solution)/shard_map/ppermute | solution.py:376
  42.9 16.2 %collective-permute-start.11 = (f16[440,512]{1,0:T(8,128)(2,1)S(1)}, f16[440,512]{1,0:T(8,128)(2,1)S(1)}, u32[]{:S(2)}, u32[]{:S(2)}) collective-permute-start(f16[440,512]{1,0:T(8,128)(2,1)S(1)} %convert_element_type.36), channel_id=1, source_target_pairs={{1,2},{2,1},{5,6},{6,5},{9,10},{10,9},{13,14},{14,13},{17,18},{18,... | collective-permute-start | bytes 1351688 | tf_op jit(solution)/shard_map/ppermute | solution.py:376
  53.5 15.5 %collective-permute-start.12 = (f16[440,512]{1,0:T(8,128)(2,1)S(1)}, f16[440,512]{1,0:T(8,128)(2,1)S(1)}, u32[]{:S(2)}, u32[]{:S(2)}) collective-permute-start(f16[440,512]{1,0:T(8,128)(2,1)S(1)} %convert_element_type.36), channel_id=1, source_target_pairs={{0,2},{3,1},{4,6},{7,5},{8,10},{11,9},{12,14},{15,13},{16,18},{19,... | collective-permute-start | bytes 1351688 | tf_op jit(solution)/shard_map/ppermute | solution.py:376
  59.0 19.7 %collective-permute-start.13 = (f16[440,512]{1,0:T(8,128)(2,1)S(1)}, f16[440,512]{1,0:T(8,128)(2,1)S(1)}, u32[]{:S(2)}, u32[]{:S(2)}) collective-permute-start(f16[440,512]{1,0:T(8,128)(2,1)S(1)} %convert_element_type.38), channel_id=1, source_target_pairs={{0,1},{3,2},{1,3},{2,0},{4,5},{7,6},{5,7},{6,4},{8,9},{11,10},{9,1... | collective-permute-start | bytes 1351688 | tf_op jit(solution)/shard_map/ppermute | solution.py:376
  79.5 3.8 %collective-permute-start.14 = (f32[32,128]{1,0:T(8,128)S(1)}, f32[32,128]{1,0:T(8,128)S(1)}, u32[]{:S(2)}, u32[]{:S(2)}) collective-permute-start(f32[32,128]{1,0:T(8,128)S(1)} %line.1), channel_id=1, source_target_pairs={{0,1},{1,0},{2,3},{3,2},{4,5},{5,4},{6,7},{7,6},{8,9},{9,8},{10,11... | collective-permute-start | bytes 49160 | tf_op jit(solution)/shard_map/ppermute | solution.py:376
  83.3 4.6 %collective-permute-start.15 = (f32[32,128]{1,0:T(8,128)S(1)}, f32[32,128]{1,0:T(8,128)S(1)}, u32[]{:S(2)}, u32[]{:S(2)}) collective-permute-start(f32[32,128]{1,0:T(8,128)S(1)} %add.54), channel_id=1, source_target_pairs={{0,2},{1,3},{2,0},{3,1},{4,6},{5,7},{6,4},{7,5},{8,10},{9,11},{10,... | collective-permute-start | bytes 49160 | tf_op jit(solution)/shard_map/ppermute | solution.py:376

commit v15 on v13

--- a/solution.py
+++ b/solution.py
@@ -15,7 +15,7 @@
 REACH = 4
 OFFSETS = [(a, b) for a in (-1, 0, 1) for b in (-1, 0, 1)]
 X_LIMIT = 6.0
-OTHER_REFS = 18
+OTHER_REFS = 17
 ROOM = 16384.0
 
 
@@ -81,8 +81,8 @@
     halves, refs = refs[:count], refs[count:]
     shared = halves[4 * len(widths) :]
     weight_in, taps, weight_out, onehot, after, before = refs[:6]
-    x_vmem, dpre_out, gout, small, first, early = refs[6:12]
-    pre, dys, slope, hid, dlog, sem_in = refs[12:]
+    x_vmem, dpre_out, gout, small, first = refs[6:11]
+    pre, dys, slope, hid, dlog, sem_in = refs[11:]
     rows = x_vmem.shape[0]
     width = sum(widths)
     hidden = weight_in.shape[1]
@@ -234,7 +234,6 @@
     small[17:18, :] = jnp.sum(gout[...] * gout[...], axis=0, keepdims=True)
     if first.shape[0] == sizes.message:
         norm = message(sizes, scalars[3], x_vmem, dpre_out, gout, small, first, True)
-        norm = norm + message(sizes, scalars[4], x_vmem, dpre_out, gout, small, early, True)
         small[18:19, :LANES] = norm
 
 
@@ -294,9 +293,9 @@
             jax.ShapeDtypeStruct((256, hidden), jnp.float32),
             jax.ShapeDtypeStruct((24, hidden), jnp.float32),
         ]
-        + [jax.ShapeDtypeStruct((sizes.message if sizes.staged else 8, hidden), jnp.float32)] * 2,
+        + [jax.ShapeDtypeStruct((sizes.message if sizes.staged else 8, hidden), jnp.float32)],
         in_specs=[pl.BlockSpec(memory_space=pltpu.SMEM)] + [anywhere] * len(halves) + [vmem] * 6,
-        out_specs=[vmem] * 6,
+        out_specs=[vmem] * 5,
         scratch_shapes=[
             pltpu.VMEM((chunks, span, LANES), jnp.float32),
             pltpu.VMEM((chunks, span, LANES), jnp.float32),
@@ -310,11 +309,16 @@
     )(scalars, *halves, weight_in, taps, weight_out, onehot, *masks)
 
 
-def blocks_kernel(sizes, scalars, x, dpre, gout, small, late, own, stats):
+def step_kernel(sizes, scalars, x, dpre, gout, small, early, norm):
+    norm[...] = jnp.zeros(norm.shape, jnp.float32)
+    norm[0:1, :] = message(sizes, scalars[4], x, dpre, gout, small, early, True)
+
+
+def blocks_kernel(sizes, scalars, x, dpre, gout, small, step_norm, late, own, stats):
     norm = message(sizes, scalars[5], x, dpre, gout, small, late, True)
     norm = norm + message(sizes, scalars[6], x, dpre, gout, small, own, False)
     stats[...] = jnp.zeros(stats.shape, jnp.float32)
-    stats[0:1, :] = norm + small[18:19, :LANES]
+    stats[0:1, :] = norm + small[18:19, :LANES] + step_norm[0:1, :]
     stats[1:2, :] = small[16:17, :LANES]
     for c in range(sizes.chunks):
         stats[2 + c : 3 + c, :] = small[17:18, LANES * c : LANES * c + LANES]
@@ -404,7 +408,7 @@
     )
 
 
-def staged_sums(sizes, me, scalars, xrows, dpre, gout, small, first, early):
+def staged_sums(sizes, me, scalars, xrows, dpre, gout, small, first):
     vmem = pl.BlockSpec(memory_space=pltpu.VMEM)
     smem = pl.BlockSpec(memory_space=pltpu.SMEM)
     hidden = dpre.shape[1]
@@ -413,12 +417,25 @@
     lines = jax.ShapeDtypeStruct((8, LANES), jnp.float32)
     half = jnp.float16
     near = permute(first.astype(half), [(0, 1), (1, 0), (2, 3), (3, 2)])
+    early, step_norm = pl.pallas_call(
+        functools.partial(step_kernel, sizes),
+        out_shape=[full, lines],
+        in_specs=[smem] + [vmem] * 4,
+        out_specs=[vmem] * 2,
+        compiler_params=pltpu.CompilerParams(vmem_limit_bytes=16 * 1024 * 1024),
+        cost_estimate=pl.CostEstimate(
+            flops=2 * sizes.depth * dpre.shape[0] * hidden,
+            bytes_accessed=2 * xrows.size + 2 * dpre.size + 4 * sizes.message * hidden,
+            transcendentals=0,
+        ),
+        name="step",
+    )(scalars, xrows, dpre, gout, small)
     early = early.astype(half)
     middle = permute(early, [(1, 2), (2, 1)])
     late, own, stats = pl.pallas_call(
         functools.partial(blocks_kernel, sizes),
         out_shape=[full, full, lines],
-        in_specs=[smem] + [vmem] * 4,
+        in_specs=[smem] + [vmem] * 5,
         out_specs=[vmem] * 3,
         compiler_params=pltpu.CompilerParams(vmem_limit_bytes=16 * 1024 * 1024),
         cost_estimate=pl.CostEstimate(
@@ -427,7 +444,7 @@
             transcendentals=0,
         ),
         name="blocks",
-    )(scalars, xrows, dpre, gout, small)
+    )(scalars, xrows, dpre, gout, small, step_norm)
     end = (me == 0) | (me == 3)
     mark = sizes.depth + sizes.group + 9
     both = pl.pallas_call(
@@ -473,7 +490,7 @@
     step, jump = jnp.where(odd == 0, 1, 2), jnp.where(high, me - 2, me + 2)
     to = [3 * (1 - odd), jnp.where(end, jump, step), jnp.where(end, step, jump), me]
     scalars = jnp.stack([dil, where, core] + to).astype(jnp.int32)
-    xrows, dpre, gout, small, first, early = head_backward(
+    xrows, dpre, gout, small, first = head_backward(
         sizes,
         widths,
         scalars,
@@ -486,7 +503,7 @@
     )
     if not sizes.staged:
         return general_sums(sizes, xrows, dpre, gout, small)
-    parts, last, stats = staged_sums(sizes, me, scalars, xrows, dpre, gout, small, first, early)
+    parts, last, stats = staged_sums(sizes, me, scalars, xrows, dpre, gout, small, first)
     vmem = pl.BlockSpec(memory_space=pltpu.VMEM)
     hidden = dpre.shape[1]
     small = pltpu.CompilerParams(vmem_limit_bytes=8 * 1024 * 1024)

time: 85.8 us -> 87.1 us (1.015)
  waiting for transfers between devices: 44.6 us -> 49.5 us
  starting transfers between devices: 20 us -> 15.9 us
    ppermute x6, waiting for transfers between devices: 26.9 us -> 31.8 us  [permute(): return lax.ppermute(value, 'dp', pairs)]
    ppermute x6, starting transfers between devices: 13.3 us -> 9.21 us  [permute(): return lax.ppermute(value, 'dp', pairs)]
    pallas_call x0 -> x1, Pallas kernels: none -> 1.07 us  [staged_sums(): pl.pallas_call(functools.partial(step_kernel, sizes), out_shape=[full, li...]
  transfers between devices with their start and end apart: 16 -> 16, of which waited for: 8 -> 9; matrix products, arithmetic and copies ran while one was open for 4% -> 4% of each run, Pallas kernels for 4% -> 5%
where the time goes in v15:
time: 87.1 us; the launch traced here: 87 us
  waiting for transfers between devices  49.5 us (57%)
  starting transfers between devices  15.9 us (18%)
  Pallas kernels  12.9 us (15%)
  other arithmetic  6.28 us (7%)
  between operations  2.28 us (3%)
    ppermute x6, waiting for transfers between devices, permute(): return lax.ppermute(value, 'dp', pairs)  31.8 us
    ppermute x2, waiting for transfers between devices, pieces(): other = lax.ppermute(held, axis, across)  12.2 us
    ppermute x6, starting transfers between devices, permute(): return lax.ppermute(value, 'dp', pairs)  9.21 us
    pallas_call x1, Pallas kernels, head_backward(): pl.pallas_call(functools.partial(head_kernel, sizes, widths), out_shape=[...  7.82 us
    ppermute x1, waiting for transfers between devices, pieces(): shared_other = lax.ppermute(shared, axis, across)  4.26 us
    ppermute x2, starting transfers between devices, pieces(): other = lax.ppermute(held, axis, across)  2.79 us
    ppermute x1, starting transfers between devices, pieces(): shared_other = lax.ppermute(shared, axis, across)  2.55 us
    select_n x1, other arithmetic, pieces(): jnp.where(core == 0, block[:, width:2 * width], block[:, :width])  2.44 us
  transfers between devices with their start and end apart: 16, of which 9 were waited for; matrix products, arithmetic and copies ran while one was open for 4% of the time, Pallas kernels for 5%

profile of v15, /device:TPU:0, one launch (start us, length us, event | category | flops | bytes accessed | tf_op | source)
XLA Modules:
  0.0 87.0 jit_solution(7649785140060975607)
XLA Ops:
  0.7 2.4 %slice_select_fusion = bf16[592,640]{1,0:T(8,128)(2,1)} fusion(bf16[592,1536]{1,0:T(8,128)(2,1)} %bitcast.30, pred[]{:T(512)S(6)} %eq.46), kind=kLoop, calls=%fused_computation.1 | loop fusion | flops 378880 | bytes 2273281 | tf_op jit(solution)/shard_map/jit(_where)/select_n | solution.py:37
  3.1 0.5 collective-permute-start
  3.6 2.6 %collective-permute-start.4 = (bf16[592,256]{1,0:T(8,128)(2,1)S(1)}, bf16[592,256]{1,0:T(8,128)(2,1)S(1)}, u32[]{:S(2)}, u32[]{:S(2)}) collective-permute-start(bf16[592,256]{1,0:T(8,128)(2,1)S(1)} %slice.65.refs_8_), channel_id=1, source_target_pairs={{0,8},{8,0},{4,12},{12,4},{1,9},{9,1},{5,13},{13,5},{2,10},{10,2},... | collective-permute-start | bytes 909320 | tf_op jit(solution)/shard_map/ppermute | solution.py:36
  6.2 0.2 collective-permute-start.8
  7.8 0.1 stack.28.scalars
  7.9 1.2 %slice_select_fusion.1.refs_0_ = bf16[592,384]{1,0:T(8,128)(2,1)S(1)} fusion(bf16[592,640]{1,0:T(8,128)(2,1)} %collective-permute-done, bf16[592,1536]{1,0:T(8,128)(2,1)S(1)} %bitcast.32, pred[]{:T(512)S(6)} %eq.46, pred[]{:T(512)S(6)} %eq.45), kind=kLoop, calls=%fused_computation.4 | loop fusion | flops 454656 | bytes 1818626 | tf_op jit(solution)/shard_map/jit(_where)/select_n | solution.py:45
  9.2 0.8 collective-permute-start.1
  9.9 4.3 %collective-permute-done.4.refs_10_ = bf16[592,256]{1,0:T(8,128)(2,1)S(1)} collective-permute-done((bf16[592,256]{1,0:T(8,128)(2,1)S(1)}, bf16[592,256]{1,0:T(8,128)(2,1)S(1)}, u32[]{:S(2)}, u32[]{:S(2)}) %collective-permute-start.4) | collective-permute-done | bytes 303136 | tf_op jit(solution)/shard_map/ppermute | solution.py:36
  14.2 1.0 %slice_select_fusion.3.refs_4_ = bf16[592,256]{1,0:T(8,128)(2,1)S(1)} fusion(bf16[592,640]{1,0:T(8,128)(2,1)} %collective-permute-done, bf16[592,1536]{1,0:T(8,128)(2,1)S(1)} %bitcast.33, pred[]{:T(512)S(6)} %eq.46, pred[]{:T(512)S(6)} %eq.45), kind=kLoop, calls=%fused_computation.9 | loop fusion | flops 303104 | bytes 1212418 | tf_op jit(solution)/shard_map/jit(_where)/select_n | solution.py:45
  15.2 2.0 %collective-permute-start.5 = (bf16[592,256]{1,0:T(8,128)(2,1)S(1)}, bf16[592,256]{1,0:T(8,128)(2,1)S(1)}, u32[]{:S(2)}, u32[]{:S(2)}) collective-permute-start(bf16[592,256]{1,0:T(8,128)(2,1)S(1)} %slice_select_fusion.3.refs_4_), channel_id=1, source_target_pairs={{0,8},{8,0},{4,12},{12,4},{1,9},{9,1},{5,13},{13,5},{2,10},{10,2},... | collective-permute-start | bytes 909320 | tf_op jit(solution)/shard_map/ppermute | solution.py:46
  17.2 0.1 fusion.refs_15_
  17.4 0.1 collective-permute-start.2
  17.5 6.5 %collective-permute-done.1.refs_1_ = bf16[592,384]{1,0:T(8,128)(2,1)S(1)} collective-permute-done((bf16[592,384]{1,0:T(8,128)(2,1)S(1)}, bf16[592,384]{1,0:T(8,128)(2,1)S(1)}, u32[]{:S(2)}, u32[]{:S(2)}) %collective-permute-start.1) | collective-permute-done | bytes 454688 | tf_op jit(solution)/shard_map/ppermute | solution.py:46
  23.9 0.5 collective-permute-start.6
  24.5 0.0 collective-permute-done.8.refs_9_
  24.5 0.1 collective-permute-start.9
  24.5 5.7 %collective-permute-done.5.refs_5_ = bf16[592,256]{1,0:T(8,128)(2,1)S(1)} collective-permute-done((bf16[592,256]{1,0:T(8,128)(2,1)S(1)}, bf16[592,256]{1,0:T(8,128)(2,1)S(1)}, u32[]{:S(2)}, u32[]{:S(2)}) %collective-permute-start.5) | collective-permute-done | bytes 303136 | tf_op jit(solution)/shard_map/ppermute | solution.py:46
  30.2 0.0 collective-permute-start.7
  30.3 0.3 fusion.2
  30.6 0.0 collective-permute-done.6.refs_6_
  30.6 0.0 collective-permute-done.9.refs_11_
  30.6 1.2 %collective-permute-done.7.refs_7_ = bf16[592,256]{1,0:T(8,128)(2,1)S(1)} collective-permute-done((bf16[592,256]{1,0:T(8,128)(2,1)S(1)}, bf16[592,256]{1,0:T(8,128)(2,1)S(1)}, u32[]{:S(2)}, u32[]{:S(2)}) %collective-permute-start.7) | collective-permute-done | bytes 303136 | tf_op jit(solution)/shard_map/ppermute | solution.py:47
  31.9 7.8 %head.1 = (bf16[592,1536]{1,0:T(8,128)(2,1)S(1)}, bf16[592,512]{1,0:T(8,128)(2,1)S(1)}, f32[256,512]{1,0:T(8,128)S(1)}, f32[24,512]{1,0:T(8,128)S(1)}, f32[440,512]{1,0:T(8,128)S(1)}) custom-call(s32[7]{0:T(128)S(1)} %stack.28.scalars, bf16[592,384]{1,0:T(8,128)(2,1)S(1)} %slice_select_fusion.1.refs_0_, bf16[592,384]{1,0:T(8,128)(2,1)S(1)} %collective-permute-done.1.refs_1_, ...), custom_call_target="tpu_custom_call" | custom-call | tf_op jit(solution)/shard_map/head/pallas_call | solution.py:288
  39.7 0.1 convert_element_type.35
  39.8 1.9 %collective-permute-start.10 = (f16[440,512]{1,0:T(8,128)(2,1)S(1)}, f16[440,512]{1,0:T(8,128)(2,1)S(1)}, u32[]{:S(2)}, u32[]{:S(2)}) collective-permute-start(f16[440,512]{1,0:T(8,128)(2,1)S(1)} %convert_element_type.35), channel_id=1, source_target_pairs={{0,1},{1,0},{2,3},{3,2},{4,5},{5,4},{6,7},{7,6},{8,9},{9,8},{10,11... | collective-permute-start | bytes 1351688 | tf_op jit(solution)/shard_map/ppermute | solution.py:379
  41.6 1.1 %step.1 = (f32[440,512]{1,0:T(8,128)S(1)}, f32[8,128]{1,0:T(8,128)S(1)}) custom-call(s32[7]{0:T(128)S(1)} %stack.28.scalars, bf16[592,1536]{1,0:T(8,128)(2,1)S(1)} %get-tuple-element.24.x, bf16[592,512]{1,0:T(8,128)(2,1)S(1)} %get-tuple-element.25.dpre, f32[256,512]{1,0:T(8,128)S(1)} %get-tuple-element.26.gout, f32[24,512]{1,0:T(8,128)S(1)} %get-tuple-element.27.small), custom_call_target="tpu_custom_call" | custom-call | flops 232783872 | bytes 3325952 | tf_op jit(solution)/shard_map/step/pallas_call | solution.py:420
  42.7 0.1 convert_element_type.36
  42.8 0.7 collective-permute-start.11
  43.5 1.4 %blocks.1 = (f32[440,512]{1,0:T(8,128)S(1)}, f32[440,512]{1,0:T(8,128)S(1)}, f32[8,128]{1,0:T(8,128)S(1)}) custom-call(s32[7]{0:T(128)S(1)} %stack.28.scalars, bf16[592,1536]{1,0:T(8,128)(2,1)S(1)} %get-tuple-element.24.x, bf16[592,512]{1,0:T(8,128)(2,1)S(1)} %get-tuple-element.25.dpre, f32[256,512]{1,0:T(8,128)S(1)} %get-tuple-element.26.gout, ...), custom_call_target="tpu_custom_call" | custom-call | flops 465567744 | bytes 4227072 | tf_op jit(solution)/shard_map/blocks/pallas_call | solution.py:435
  44.9 7.4 %collective-permute-done.10 = f16[440,512]{1,0:T(8,128)(2,1)S(1)} collective-permute-done((f16[440,512]{1,0:T(8,128)(2,1)S(1)}, f16[440,512]{1,0:T(8,128)(2,1)S(1)}, u32[]{:S(2)}, u32[]{:S(2)}) %collective-permute-start.10) | collective-permute-done | bytes 450592 | tf_op jit(solution)/shard_map/ppermute | solution.py:379
  52.3 0.1 convert_element_type.37.theirs
  52.4 0.6 add.60
  53.0 0.1 convert_element_type.38
  53.1 1.8 %collective-permute-start.13 = (f16[440,512]{1,0:T(8,128)(2,1)S(1)}, f16[440,512]{1,0:T(8,128)(2,1)S(1)}, u32[]{:S(2)}, u32[]{:S(2)}) collective-permute-start(f16[440,512]{1,0:T(8,128)(2,1)S(1)} %convert_element_type.38), channel_id=1, source_target_pairs={{0,1},{3,2},{1,3},{2,0},{4,5},{7,6},{5,7},{6,4},{8,9},{11,10},{9,1... | collective-permute-start | bytes 1351688 | tf_op jit(solution)/shard_map/ppermute | solution.py:379
  54.9 3.1 %collective-permute-start.12 = (f16[440,512]{1,0:T(8,128)(2,1)S(1)}, f16[440,512]{1,0:T(8,128)(2,1)S(1)}, u32[]{:S(2)}, u32[]{:S(2)}) collective-permute-start(f16[440,512]{1,0:T(8,128)(2,1)S(1)} %convert_element_type.36), channel_id=1, source_target_pairs={{0,2},{3,1},{4,6},{7,5},{8,10},{11,9},{12,14},{15,13},{16,18},{19,... | collective-permute-start | bytes 1351688 | tf_op jit(solution)/shard_map/ppermute | solution.py:379
  58.0 0.1 select_convert_fusion
  58.2 15.5 %collective-permute-done.12 = f16[440,512]{1,0:T(8,128)(2,1)S(1)} collective-permute-done((f16[440,512]{1,0:T(8,128)(2,1)S(1)}, f16[440,512]{1,0:T(8,128)(2,1)S(1)}, u32[]{:S(2)}, u32[]{:S(2)}) %collective-permute-start.12) | collective-permute-done | bytes 450592 | tf_op jit(solution)/shard_map/ppermute | solution.py:379
  73.7 0.1 convert_element_type.40
  73.8 3.1 %collective-permute-done.13 = f16[440,512]{1,0:T(8,128)(2,1)S(1)} collective-permute-done((f16[440,512]{1,0:T(8,128)(2,1)S(1)}, f16[440,512]{1,0:T(8,128)(2,1)S(1)}, u32[]{:S(2)}, u32[]{:S(2)}) %collective-permute-start.13) | collective-permute-done | bytes 450592 | tf_op jit(solution)/shard_map/ppermute | solution.py:379
  76.9 0.1 convert_element_type.41.last
  77.0 0.4 multiply_add_fusion.parts
  77.4 0.3 line.1
  77.7 0.6 collective-permute-start.14
  78.3 3.2 %collective-permute-done.14 = f32[32,128]{1,0:T(8,128)S(1)} collective-permute-done((f32[32,128]{1,0:T(8,128)S(1)}, f32[32,128]{1,0:T(8,128)S(1)}, u32[]{:S(2)}, u32[]{:S(2)}) %collective-permute-start.14) | collective-permute-done | bytes 16416 | tf_op jit(solution)/shard_map/ppermute | solution.py:379
  81.5 1.2 %collective-permute-start.15 = (f32[32,128]{1,0:T(8,128)S(1)}, f32[32,128]{1,0:T(8,128)S(1)}, u32[]{:S(2)}, u32[]{:S(2)}) collective-permute-start(f32[32,128]{1,0:T(8,128)S(1)} %add.54), channel_id=1, source_target_pairs={{0,2},{1,3},{2,0},{3,1},{4,6},{5,7},{6,4},{7,5},{8,10},{9,11},{10,... | collective-permute-start | bytes 49160 | tf_op jit(solution)/shard_map/ppermute | solution.py:379
  82.7 1.0 %sums.1 = (f32[384,512]{1,0:T(8,128)}, f32[150,1,128]{2,1,0:T(1,128)}, f32[9,1,512]{2,1,0:T(1,128)}) custom-call(f32[440,512]{1,0:T(8,128)S(1)} %multiply_add_fusion.parts, f32[440,512]{1,0:T(8,128)S(1)} %convert_element_type.41.last), custom_call_target="tpu_custom_call" | custom-call | flops 450560 | bytes 3604480 | tf_op jit(solution)/shard_map/sums/pallas_call | solution.py:521
  83.7 2.5 %collective-permute-done.15 = f32[32,128]{1,0:T(8,128)S(1)} collective-permute-done((f32[32,128]{1,0:T(8,128)S(1)}, f32[32,128]{1,0:T(8,128)S(1)}, u32[]{:S(2)}, u32[]{:S(2)}) %collective-permute-start.15) | collective-permute-done | bytes 16416 | tf_op jit(solution)/shard_map/ppermute | solution.py:379
  86.3 0.7 norms.1
  (25 shorter events, 0.2 us)
Async XLA Ops:
  0.6 2.9 %copy-start.2 = (bf16[1,1,592,1536]{3,2,1,0:T(8,128)(2,1)S(1)}, bf16[1,1,592,1536]{3,2,1,0:T(8,128)(2,1)}, u32[]{:S(2)}) copy-start(bf16[1,1,592,1536]{3,2,1,0:T(8,128)(2,1)} %param.7) | copy-start | bytes 5455876
  0.6 7.1 %copy-start.4 = (s32[1,592]{1,0:T(1,128)S(1)}, s32[1,592]{1,0:T(1,128)}, u32[]{:S(2)}) copy-start(s32[1,592]{1,0:T(1,128)} %param.10) | copy-start | bytes 7108
  0.7 7.1 %copy-start.3 = (bf16[1,512,150]{1,2,0:T(8,128)(2,1)S(1)}, bf16[1,512,150]{1,2,0:T(8,128)(2,1)}, u32[]{:S(2)}) copy-start(bf16[1,512,150]{1,2,0:T(8,128)(2,1)} %param.13) | copy-start | bytes 460804
  3.1 4.8 %collective-permute-start = (bf16[592,640]{1,0:T(8,128)(2,1)}, bf16[592,640]{1,0:T(8,128)(2,1)}, u32[]{:S(2)}, u32[]{:S(2)}) collective-permute-start(bf16[592,640]{1,0:T(8,128)(2,1)} %slice_select_fusion), channel_id=1, source_target_pairs={{0,4},{4,0},{8,12},{12,8},{1,5},{5,1},{9,13},{13,9},{2,6},{6,2},{1... | collective-permute-start | bytes 2273288 | tf_op jit(solution)/shard_map/ppermute | solution.py:37
  3.6 10.6 %collective-permute-start.4 = (bf16[592,256]{1,0:T(8,128)(2,1)S(1)}, bf16[592,256]{1,0:T(8,128)(2,1)S(1)}, u32[]{:S(2)}, u32[]{:S(2)}) collective-permute-start(bf16[592,256]{1,0:T(8,128)(2,1)S(1)} %slice.65.refs_8_), channel_id=1, source_target_pairs={{0,8},{8,0},{4,12},{12,4},{1,9},{9,1},{5,13},{13,5},{2,10},{10,2},... | collective-permute-start | bytes 909320 | tf_op jit(solution)/shard_map/ppermute | solution.py:36
  6.2 18.3 %collective-permute-start.8 = (bf16[592,256]{1,0:T(8,128)(2,1)S(1)}, bf16[592,256]{1,0:T(8,128)(2,1)S(1)}, u32[]{:S(2)}, u32[]{:S(2)}) collective-permute-start(bf16[592,256]{1,0:T(8,128)(2,1)S(1)} %slice.65.refs_8_), channel_id=1, source_target_pairs={{0,4},{4,0},{8,12},{12,8},{1,5},{5,1},{9,13},{13,9},{2,6},{6,2},{1... | collective-permute-start | bytes 909320 | tf_op jit(solution)/shard_map/ppermute | solution.py:49
  7.9 23.9 %copy-start = (bf16[1,1536,512]{2,1,0:T(8,128)(2,1)S(1)}, bf16[1,1536,512]{2,1,0:T(8,128)(2,1)}, u32[]{:S(2)}) copy-start(bf16[1,1536,512]{2,1,0:T(8,128)(2,1)} %param.11) | copy-start | bytes 4718596
  7.9 24.0 %copy-start.1 = (f32[1,9,512]{2,0,1:T(1,128)S(1)}, f32[1,9,512]{2,0,1:T(1,128)}, u32[]{:S(2)}) copy-start(f32[1,9,512]{2,0,1:T(1,128)} %param.12) | copy-start | bytes 55300
  9.2 14.8 %collective-permute-start.1 = (bf16[592,384]{1,0:T(8,128)(2,1)S(1)}, bf16[592,384]{1,0:T(8,128)(2,1)S(1)}, u32[]{:S(2)}, u32[]{:S(2)}) collective-permute-start(bf16[592,384]{1,0:T(8,128)(2,1)S(1)} %slice_select_fusion.1.refs_0_), channel_id=1, source_target_pairs={{0,8},{8,0},{4,12},{12,4},{1,9},{9,1},{5,13},{13,5},{2,10},{10,2},... | collective-permute-start | bytes 1363976 | tf_op jit(solution)/shard_map/ppermute | solution.py:46
  15.2 15.0 %collective-permute-start.5 = (bf16[592,256]{1,0:T(8,128)(2,1)S(1)}, bf16[592,256]{1,0:T(8,128)(2,1)S(1)}, u32[]{:S(2)}, u32[]{:S(2)}) collective-permute-start(bf16[592,256]{1,0:T(8,128)(2,1)S(1)} %slice_select_fusion.3.refs_4_), channel_id=1, source_target_pairs={{0,8},{8,0},{4,12},{12,4},{1,9},{9,1},{5,13},{13,5},{2,10},{10,2},... | collective-permute-start | bytes 909320 | tf_op jit(solution)/shard_map/ppermute | solution.py:46
  17.4 13.2 %collective-permute-start.2 = (bf16[592,384]{1,0:T(8,128)(2,1)S(1)}, bf16[592,384]{1,0:T(8,128)(2,1)S(1)}, u32[]{:S(2)}, u32[]{:S(2)}) collective-permute-start(bf16[592,384]{1,0:T(8,128)(2,1)S(1)} %slice_select_fusion.1.refs_0_), channel_id=1, source_target_pairs={{0,4},{4,0},{8,12},{12,8},{1,5},{5,1},{9,13},{13,9},{2,6},{6,2},{1... | collective-permute-start | bytes 1363976 | tf_op jit(solution)/shard_map/ppermute | solution.py:47
  23.9 7.9 %collective-permute-start.3 = (bf16[592,384]{1,0:T(8,128)(2,1)S(1)}, bf16[592,384]{1,0:T(8,128)(2,1)S(1)}, u32[]{:S(2)}, u32[]{:S(2)}) collective-permute-start(bf16[592,384]{1,0:T(8,128)(2,1)S(1)} %collective-permute-done.1.refs_1_), channel_id=1, source_target_pairs={{0,4},{4,0},{8,12},{12,8},{1,5},{5,1},{9,13},{13,9},{2,6},{6,2},{1... | collective-permute-start | bytes 1363976 | tf_op jit(solution)/shard_map/ppermute | solution.py:47
  23.9 6.6 %collective-permute-start.6 = (bf16[592,256]{1,0:T(8,128)(2,1)S(1)}, bf16[592,256]{1,0:T(8,128)(2,1)S(1)}, u32[]{:S(2)}, u32[]{:S(2)}) collective-permute-start(bf16[592,256]{1,0:T(8,128)(2,1)S(1)} %slice_select_fusion.3.refs_4_), channel_id=1, source_target_pairs={{0,4},{4,0},{8,12},{12,8},{1,5},{5,1},{9,13},{13,9},{2,6},{6,2},{1... | collective-permute-start | bytes 909320 | tf_op jit(solution)/shard_map/ppermute | solution.py:47
  24.5 6.1 %collective-permute-start.9 = (bf16[592,256]{1,0:T(8,128)(2,1)S(1)}, bf16[592,256]{1,0:T(8,128)(2,1)S(1)}, u32[]{:S(2)}, u32[]{:S(2)}) collective-permute-start(bf16[592,256]{1,0:T(8,128)(2,1)S(1)} %collective-permute-done.4.refs_10_), channel_id=1, source_target_pairs={{0,4},{4,0},{8,12},{12,8},{1,5},{5,1},{9,13},{13,9},{2,6},{6,2},{1... | collective-permute-start | bytes 909320 | tf_op jit(solution)/shard_map/ppermute | solution.py:50
  30.2 1.6 %collective-permute-start.7 = (bf16[592,256]{1,0:T(8,128)(2,1)S(1)}, bf16[592,256]{1,0:T(8,128)(2,1)S(1)}, u32[]{:S(2)}, u32[]{:S(2)}) collective-permute-start(bf16[592,256]{1,0:T(8,128)(2,1)S(1)} %collective-permute-done.5.refs_5_), channel_id=1, source_target_pairs={{0,4},{4,0},{8,12},{12,8},{1,5},{5,1},{9,13},{13,9},{2,6},{6,2},{1... | collective-permute-start | bytes 909320 | tf_op jit(solution)/shard_map/ppermute | solution.py:47
  39.8 12.5 %collective-permute-start.10 = (f16[440,512]{1,0:T(8,128)(2,1)S(1)}, f16[440,512]{1,0:T(8,128)(2,1)S(1)}, u32[]{:S(2)}, u32[]{:S(2)}) collective-permute-start(f16[440,512]{1,0:T(8,128)(2,1)S(1)} %convert_element_type.35), channel_id=1, source_target_pairs={{0,1},{1,0},{2,3},{3,2},{4,5},{5,4},{6,7},{7,6},{8,9},{9,8},{10,11... | collective-permute-start | bytes 1351688 | tf_op jit(solution)/shard_map/ppermute | solution.py:379
  42.8 15.2 %collective-permute-start.11 = (f16[440,512]{1,0:T(8,128)(2,1)S(1)}, f16[440,512]{1,0:T(8,128)(2,1)S(1)}, u32[]{:S(2)}, u32[]{:S(2)}) collective-permute-start(f16[440,512]{1,0:T(8,128)(2,1)S(1)} %convert_element_type.36), channel_id=1, source_target_pairs={{1,2},{2,1},{5,6},{6,5},{9,10},{10,9},{13,14},{14,13},{17,18},{18,... | collective-permute-start | bytes 1351688 | tf_op jit(solution)/shard_map/ppermute | solution.py:379
  53.1 23.8 %collective-permute-start.13 = (f16[440,512]{1,0:T(8,128)(2,1)S(1)}, f16[440,512]{1,0:T(8,128)(2,1)S(1)}, u32[]{:S(2)}, u32[]{:S(2)}) collective-permute-start(f16[440,512]{1,0:T(8,128)(2,1)S(1)} %convert_element_type.38), channel_id=1, source_target_pairs={{0,1},{3,2},{1,3},{2,0},{4,5},{7,6},{5,7},{6,4},{8,9},{11,10},{9,1... | collective-permute-start | bytes 1351688 | tf_op jit(solution)/shard_map/ppermute | solution.py:379
  54.9 18.8 %collective-permute-start.12 = (f16[440,512]{1,0:T(8,128)(2,1)S(1)}, f16[440,512]{1,0:T(8,128)(2,1)S(1)}, u32[]{:S(2)}, u32[]{:S(2)}) collective-permute-start(f16[440,512]{1,0:T(8,128)(2,1)S(1)} %convert_element_type.36), channel_id=1, source_target_pairs={{0,2},{3,1},{4,6},{7,5},{8,10},{11,9},{12,14},{15,13},{16,18},{19,... | collective-permute-start | bytes 1351688 | tf_op jit(solution)/shard_map/ppermute | solution.py:379
  77.7 3.8 %collective-permute-start.14 = (f32[32,128]{1,0:T(8,128)S(1)}, f32[32,128]{1,0:T(8,128)S(1)}, u32[]{:S(2)}, u32[]{:S(2)}) collective-permute-start(f32[32,128]{1,0:T(8,128)S(1)} %line.1), channel_id=1, source_target_pairs={{0,1},{1,0},{2,3},{3,2},{4,5},{5,4},{6,7},{7,6},{8,9},{9,8},{10,11... | collective-permute-start | bytes 49160 | tf_op jit(solution)/shard_map/ppermute | solution.py:379
  81.5 4.7 %collective-permute-start.15 = (f32[32,128]{1,0:T(8,128)S(1)}, f32[32,128]{1,0:T(8,128)S(1)}, u32[]{:S(2)}, u32[]{:S(2)}) collective-permute-start(f32[32,128]{1,0:T(8,128)S(1)} %add.54), channel_id=1, source_target_pairs={{0,2},{1,3},{2,0},{3,1},{4,6},{5,7},{6,4},{7,5},{8,10},{9,11},{10,... | collective-permute-start | bytes 49160 | tf_op jit(solution)/shard_map/ppermute | solution.py:379

commit v16 on v13

--- a/solution.py
+++ b/solution.py
@@ -452,7 +452,8 @@
         value = value.astype(jnp.float32)
         return value * by_row(sizes, shape, [jnp.exp2(-v) for v in split(value)])
 
-    parts = own + decode(jnp.where(end, near, middle)) + decode(skip)
+    parts = lax.optimization_barrier(own + decode(jnp.where(end, near, middle)))
+    parts = parts + decode(skip)
     return parts, far.astype(jnp.float32), stats
 
 

time: 85.8 us -> 85.6 us (level)
  no operation moved by 1% of the time
where the time goes in v16:
time: 85.6 us; the launch traced here: 85.4 us
  waiting for transfers between devices  44.6 us (52%)
  starting transfers between devices  19.9 us (23%)
  Pallas kernels  12 us (14%)
  other arithmetic  6.43 us (8%)
  between operations  2.27 us (3%)
    ppermute x6, waiting for transfers between devices, permute(): return lax.ppermute(value, 'dp', pairs)  26.9 us
    ppermute x6, starting transfers between devices, permute(): return lax.ppermute(value, 'dp', pairs)  13.3 us
    ppermute x2, waiting for transfers between devices, pieces(): other = lax.ppermute(held, axis, across)  12.2 us
    pallas_call x1, Pallas kernels, head_backward(): pl.pallas_call(functools.partial(head_kernel, sizes, widths), out_shape=[...  8.09 us
    ppermute x1, waiting for transfers between devices, pieces(): shared_other = lax.ppermute(shared, axis, across)  4.26 us
    ppermute x2, starting transfers between devices, pieces(): other = lax.ppermute(held, axis, across)  2.79 us
    ppermute x1, starting transfers between devices, pieces(): shared_other = lax.ppermute(shared, axis, across)  2.55 us
    select_n x1, other arithmetic, pieces(): jnp.where(core == 0, block[:, width:2 * width], block[:, :width])  2.44 us
  transfers between devices with their start and end apart: 16, of which 8 were waited for; matrix products, arithmetic and copies ran while one was open for 4% of the time, Pallas kernels for 4%

profile of v16, /device:TPU:0, one launch (start us, length us, event | category | flops | bytes accessed | tf_op | source)
XLA Modules:
  0.0 85.4 jit_solution(12514372838718879474)
XLA Ops:
  0.7 2.4 %slice_select_fusion = bf16[592,640]{1,0:T(8,128)(2,1)} fusion(bf16[592,1536]{1,0:T(8,128)(2,1)} %bitcast.30, pred[]{:T(512)S(6)} %eq.46), kind=kLoop, calls=%fused_computation.2 | loop fusion | flops 378880 | bytes 2273281 | tf_op jit(solution)/shard_map/jit(_where)/select_n | solution.py:37
  3.1 0.5 collective-permute-start
  3.6 2.6 %collective-permute-start.4 = (bf16[592,256]{1,0:T(8,128)(2,1)S(1)}, bf16[592,256]{1,0:T(8,128)(2,1)S(1)}, u32[]{:S(2)}, u32[]{:S(2)}) collective-permute-start(bf16[592,256]{1,0:T(8,128)(2,1)S(1)} %slice.65.refs_8_), channel_id=1, source_target_pairs={{0,8},{8,0},{4,12},{12,4},{1,9},{9,1},{5,13},{13,5},{2,10},{10,2},... | collective-permute-start | bytes 909320 | tf_op jit(solution)/shard_map/ppermute | solution.py:36
  6.2 0.2 collective-permute-start.8
  7.8 0.1 stack.28.scalars
  7.9 1.2 %slice_select_fusion.1.refs_0_ = bf16[592,384]{1,0:T(8,128)(2,1)S(1)} fusion(bf16[592,640]{1,0:T(8,128)(2,1)} %collective-permute-done, bf16[592,1536]{1,0:T(8,128)(2,1)S(1)} %bitcast.32, pred[]{:T(512)S(6)} %eq.46, pred[]{:T(512)S(6)} %eq.45), kind=kLoop, calls=%fused_computation.5 | loop fusion | flops 454656 | bytes 1818626 | tf_op jit(solution)/shard_map/jit(_where)/select_n | solution.py:45
  9.2 0.8 collective-permute-start.1
  9.9 4.3 %collective-permute-done.4.refs_10_ = bf16[592,256]{1,0:T(8,128)(2,1)S(1)} collective-permute-done((bf16[592,256]{1,0:T(8,128)(2,1)S(1)}, bf16[592,256]{1,0:T(8,128)(2,1)S(1)}, u32[]{:S(2)}, u32[]{:S(2)}) %collective-permute-start.4) | collective-permute-done | bytes 303136 | tf_op jit(solution)/shard_map/ppermute | solution.py:36
  14.2 1.0 %slice_select_fusion.3.refs_4_ = bf16[592,256]{1,0:T(8,128)(2,1)S(1)} fusion(bf16[592,640]{1,0:T(8,128)(2,1)} %collective-permute-done, bf16[592,1536]{1,0:T(8,128)(2,1)S(1)} %bitcast.33, pred[]{:T(512)S(6)} %eq.46, pred[]{:T(512)S(6)} %eq.45), kind=kLoop, calls=%fused_computation.10 | loop fusion | flops 303104 | bytes 1212418 | tf_op jit(solution)/shard_map/jit(_where)/select_n | solution.py:45
  15.2 2.0 %collective-permute-start.5 = (bf16[592,256]{1,0:T(8,128)(2,1)S(1)}, bf16[592,256]{1,0:T(8,128)(2,1)S(1)}, u32[]{:S(2)}, u32[]{:S(2)}) collective-permute-start(bf16[592,256]{1,0:T(8,128)(2,1)S(1)} %slice_select_fusion.3.refs_4_), channel_id=1, source_target_pairs={{0,8},{8,0},{4,12},{12,4},{1,9},{9,1},{5,13},{13,5},{2,10},{10,2},... | collective-permute-start | bytes 909320 | tf_op jit(solution)/shard_map/ppermute | solution.py:46
  17.2 0.1 fusion.refs_15_
  17.4 0.1 collective-permute-start.2
  17.5 6.5 %collective-permute-done.1.refs_1_ = bf16[592,384]{1,0:T(8,128)(2,1)S(1)} collective-permute-done((bf16[592,384]{1,0:T(8,128)(2,1)S(1)}, bf16[592,384]{1,0:T(8,128)(2,1)S(1)}, u32[]{:S(2)}, u32[]{:S(2)}) %collective-permute-start.1) | collective-permute-done | bytes 454688 | tf_op jit(solution)/shard_map/ppermute | solution.py:46
  23.9 0.0 collective-permute-start.3
  23.9 0.5 collective-permute-start.6
  24.5 0.0 collective-permute-done.8.refs_9_
  24.5 0.1 collective-permute-start.9
  24.5 5.7 %collective-permute-done.5.refs_5_ = bf16[592,256]{1,0:T(8,128)(2,1)S(1)} collective-permute-done((bf16[592,256]{1,0:T(8,128)(2,1)S(1)}, bf16[592,256]{1,0:T(8,128)(2,1)S(1)}, u32[]{:S(2)}, u32[]{:S(2)}) %collective-permute-start.5) | collective-permute-done | bytes 303136 | tf_op jit(solution)/shard_map/ppermute | solution.py:46
  30.2 0.0 collective-permute-start.7
  30.3 0.3 fusion.2
  30.6 0.0 collective-permute-done.6.refs_6_
  30.6 0.0 collective-permute-done.9.refs_11_
  30.6 1.2 %collective-permute-done.7.refs_7_ = bf16[592,256]{1,0:T(8,128)(2,1)S(1)} collective-permute-done((bf16[592,256]{1,0:T(8,128)(2,1)S(1)}, bf16[592,256]{1,0:T(8,128)(2,1)S(1)}, u32[]{:S(2)}, u32[]{:S(2)}) %collective-permute-start.7) | collective-permute-done | bytes 303136 | tf_op jit(solution)/shard_map/ppermute | solution.py:47
  31.9 8.1 %head.1 = (bf16[592,1536]{1,0:T(8,128)(2,1)S(1)}, bf16[592,512]{1,0:T(8,128)(2,1)S(1)}, f32[256,512]{1,0:T(8,128)S(1)}, f32[24,512]{1,0:T(8,128)S(1)}, f32[440,512]{1,0:T(8,128)S(1)}, /*index=5*/f32[440,512]{1,0:T(8,128)S(1)}) custom-call(s32[7]{0:T(128)S(1)} %stack.28.scalars, bf16[592,384]{1,0:T(8,128)(2,1)S(1)} %slice_select_fusion.1.refs_0_, ...), custom_call_target="tpu_custom_call" | custom-call | tf_op jit(solution)/shard_map/head/pallas_call | solution.py:289
  40.0 0.1 convert_element_type.35
  40.0 1.9 %collective-permute-start.10 = (f16[440,512]{1,0:T(8,128)(2,1)S(1)}, f16[440,512]{1,0:T(8,128)(2,1)S(1)}, u32[]{:S(2)}, u32[]{:S(2)}) collective-permute-start(f16[440,512]{1,0:T(8,128)(2,1)S(1)} %convert_element_type.35), channel_id=1, source_target_pairs={{0,1},{1,0},{2,3},{3,2},{4,5},{5,4},{6,7},{7,6},{8,9},{9,8},{10,11... | collective-permute-start | bytes 1351688 | tf_op jit(solution)/shard_map/ppermute | solution.py:375
  41.9 0.1 convert_element_type.36
  42.0 0.7 collective-permute-start.11
  42.7 1.4 %blocks.1 = (f32[440,512]{1,0:T(8,128)S(1)}, f32[440,512]{1,0:T(8,128)S(1)}, f32[8,128]{1,0:T(8,128)S(1)}) custom-call(s32[7]{0:T(128)S(1)} %stack.28.scalars, bf16[592,1536]{1,0:T(8,128)(2,1)S(1)} %get-tuple-element.23.x, bf16[592,512]{1,0:T(8,128)(2,1)S(1)} %get-tuple-element.24.dpre, f32[256,512]{1,0:T(8,128)S(1)} %get-tuple-element.25.gout, ...), custom_call_target="tpu_custom_call" | custom-call | flops 465567744 | bytes 4227072 | tf_op jit(solution)/shard_map/blocks/pallas_call | solution.py:418
  44.1 8.6 %collective-permute-done.10 = f16[440,512]{1,0:T(8,128)(2,1)S(1)} collective-permute-done((f16[440,512]{1,0:T(8,128)(2,1)S(1)}, f16[440,512]{1,0:T(8,128)(2,1)S(1)}, u32[]{:S(2)}, u32[]{:S(2)}) %collective-permute-start.10) | collective-permute-done | bytes 450592 | tf_op jit(solution)/shard_map/ppermute | solution.py:375
  52.6 0.1 convert_element_type.37.theirs
  52.7 0.6 add.60
  53.4 0.1 convert_element_type.38
  53.4 1.8 %collective-permute-start.13 = (f16[440,512]{1,0:T(8,128)(2,1)S(1)}, f16[440,512]{1,0:T(8,128)(2,1)S(1)}, u32[]{:S(2)}, u32[]{:S(2)}) collective-permute-start(f16[440,512]{1,0:T(8,128)(2,1)S(1)} %convert_element_type.38), channel_id=1, source_target_pairs={{0,1},{3,2},{1,3},{2,0},{4,5},{7,6},{5,7},{6,4},{8,9},{11,10},{9,1... | collective-permute-start | bytes 1351688 | tf_op jit(solution)/shard_map/ppermute | solution.py:375
  55.3 3.1 %collective-permute-start.12 = (f16[440,512]{1,0:T(8,128)(2,1)S(1)}, f16[440,512]{1,0:T(8,128)(2,1)S(1)}, u32[]{:S(2)}, u32[]{:S(2)}) collective-permute-start(f16[440,512]{1,0:T(8,128)(2,1)S(1)} %convert_element_type.36), channel_id=1, source_target_pairs={{0,2},{3,1},{4,6},{7,5},{8,10},{11,9},{12,14},{15,13},{16,18},{19,... | collective-permute-start | bytes 1351688 | tf_op jit(solution)/shard_map/ppermute | solution.py:375
  58.3 0.2 select_convert_fusion
  58.6 0.2 multiply_add_fusion.1
  58.8 15.3 %collective-permute-done.12 = f16[440,512]{1,0:T(8,128)(2,1)S(1)} collective-permute-done((f16[440,512]{1,0:T(8,128)(2,1)S(1)}, f16[440,512]{1,0:T(8,128)(2,1)S(1)}, u32[]{:S(2)}, u32[]{:S(2)}) %collective-permute-start.12) | collective-permute-done | bytes 450592 | tf_op jit(solution)/shard_map/ppermute | solution.py:375
  74.1 0.1 convert_element_type.40
  74.3 0.1 convert_element_type.41.last
  74.4 0.2 multiply_add_fusion.parts
  74.6 0.2 line.1
  74.9 3.5 %collective-permute-start.14 = (f32[32,128]{1,0:T(8,128)S(1)}, f32[32,128]{1,0:T(8,128)S(1)}, u32[]{:S(2)}, u32[]{:S(2)}) collective-permute-start(f32[32,128]{1,0:T(8,128)S(1)} %line.1), channel_id=1, source_target_pairs={{0,1},{1,0},{2,3},{3,2},{4,5},{5,4},{6,7},{7,6},{8,9},{9,8},{10,11... | collective-permute-start | bytes 49160 | tf_op jit(solution)/shard_map/ppermute | solution.py:375
  78.4 1.7 %collective-permute-done.14 = f32[32,128]{1,0:T(8,128)S(1)} collective-permute-done((f32[32,128]{1,0:T(8,128)S(1)}, f32[32,128]{1,0:T(8,128)S(1)}, u32[]{:S(2)}, u32[]{:S(2)}) %collective-permute-start.14) | collective-permute-done | bytes 16416 | tf_op jit(solution)/shard_map/ppermute | solution.py:375
  80.1 2.3 %collective-permute-start.15 = (f32[32,128]{1,0:T(8,128)S(1)}, f32[32,128]{1,0:T(8,128)S(1)}, u32[]{:S(2)}, u32[]{:S(2)}) collective-permute-start(f32[32,128]{1,0:T(8,128)S(1)} %add.54), channel_id=1, source_target_pairs={{0,2},{1,3},{2,0},{3,1},{4,6},{5,7},{6,4},{7,5},{8,10},{9,11},{10,... | collective-permute-start | bytes 49160 | tf_op jit(solution)/shard_map/ppermute | solution.py:375
  82.4 1.0 %sums.1 = (f32[384,512]{1,0:T(8,128)}, f32[150,1,128]{2,1,0:T(1,128)}, f32[9,1,512]{2,1,0:T(1,128)}) custom-call(f32[440,512]{1,0:T(8,128)S(1)} %multiply_add_fusion.parts, f32[440,512]{1,0:T(8,128)S(1)} %convert_element_type.41.last), custom_call_target="tpu_custom_call" | custom-call | flops 450560 | bytes 3604480 | tf_op jit(solution)/shard_map/sums/pallas_call | solution.py:505
  83.4 1.3 %collective-permute-done.15 = f32[32,128]{1,0:T(8,128)S(1)} collective-permute-done((f32[32,128]{1,0:T(8,128)S(1)}, f32[32,128]{1,0:T(8,128)S(1)}, u32[]{:S(2)}, u32[]{:S(2)}) %collective-permute-start.15) | collective-permute-done | bytes 16416 | tf_op jit(solution)/shard_map/ppermute | solution.py:375
  84.7 0.7 norms.1
  (25 shorter events, 0.2 us)
Async XLA Ops:
  0.6 2.9 %copy-start.2 = (bf16[1,1,592,1536]{3,2,1,0:T(8,128)(2,1)S(1)}, bf16[1,1,592,1536]{3,2,1,0:T(8,128)(2,1)}, u32[]{:S(2)}) copy-start(bf16[1,1,592,1536]{3,2,1,0:T(8,128)(2,1)} %param.7) | copy-start | bytes 5455876
  0.6 7.1 %copy-start.4 = (s32[1,592]{1,0:T(1,128)S(1)}, s32[1,592]{1,0:T(1,128)}, u32[]{:S(2)}) copy-start(s32[1,592]{1,0:T(1,128)} %param.10) | copy-start | bytes 7108
  0.7 7.1 %copy-start.3 = (bf16[1,512,150]{1,2,0:T(8,128)(2,1)S(1)}, bf16[1,512,150]{1,2,0:T(8,128)(2,1)}, u32[]{:S(2)}) copy-start(bf16[1,512,150]{1,2,0:T(8,128)(2,1)} %param.13) | copy-start | bytes 460804
  3.1 4.8 %collective-permute-start = (bf16[592,640]{1,0:T(8,128)(2,1)}, bf16[592,640]{1,0:T(8,128)(2,1)}, u32[]{:S(2)}, u32[]{:S(2)}) collective-permute-start(bf16[592,640]{1,0:T(8,128)(2,1)} %slice_select_fusion), channel_id=1, source_target_pairs={{0,4},{4,0},{8,12},{12,8},{1,5},{5,1},{9,13},{13,9},{2,6},{6,2},{1... | collective-permute-start | bytes 2273288 | tf_op jit(solution)/shard_map/ppermute | solution.py:37
  3.6 10.6 %collective-permute-start.4 = (bf16[592,256]{1,0:T(8,128)(2,1)S(1)}, bf16[592,256]{1,0:T(8,128)(2,1)S(1)}, u32[]{:S(2)}, u32[]{:S(2)}) collective-permute-start(bf16[592,256]{1,0:T(8,128)(2,1)S(1)} %slice.65.refs_8_), channel_id=1, source_target_pairs={{0,8},{8,0},{4,12},{12,4},{1,9},{9,1},{5,13},{13,5},{2,10},{10,2},... | collective-permute-start | bytes 909320 | tf_op jit(solution)/shard_map/ppermute | solution.py:36
  6.2 18.3 %collective-permute-start.8 = (bf16[592,256]{1,0:T(8,128)(2,1)S(1)}, bf16[592,256]{1,0:T(8,128)(2,1)S(1)}, u32[]{:S(2)}, u32[]{:S(2)}) collective-permute-start(bf16[592,256]{1,0:T(8,128)(2,1)S(1)} %slice.65.refs_8_), channel_id=1, source_target_pairs={{0,4},{4,0},{8,12},{12,8},{1,5},{5,1},{9,13},{13,9},{2,6},{6,2},{1... | collective-permute-start | bytes 909320 | tf_op jit(solution)/shard_map/ppermute | solution.py:49
  7.9 23.9 %copy-start = (bf16[1,1536,512]{2,1,0:T(8,128)(2,1)S(1)}, bf16[1,1536,512]{2,1,0:T(8,128)(2,1)}, u32[]{:S(2)}) copy-start(bf16[1,1536,512]{2,1,0:T(8,128)(2,1)} %param.11) | copy-start | bytes 4718596
  7.9 24.0 %copy-start.1 = (f32[1,9,512]{2,0,1:T(1,128)S(1)}, f32[1,9,512]{2,0,1:T(1,128)}, u32[]{:S(2)}) copy-start(f32[1,9,512]{2,0,1:T(1,128)} %param.12) | copy-start | bytes 55300
  9.2 14.8 %collective-permute-start.1 = (bf16[592,384]{1,0:T(8,128)(2,1)S(1)}, bf16[592,384]{1,0:T(8,128)(2,1)S(1)}, u32[]{:S(2)}, u32[]{:S(2)}) collective-permute-start(bf16[592,384]{1,0:T(8,128)(2,1)S(1)} %slice_select_fusion.1.refs_0_), channel_id=1, source_target_pairs={{0,8},{8,0},{4,12},{12,4},{1,9},{9,1},{5,13},{13,5},{2,10},{10,2},... | collective-permute-start | bytes 1363976 | tf_op jit(solution)/shard_map/ppermute | solution.py:46
  15.2 15.0 %collective-permute-start.5 = (bf16[592,256]{1,0:T(8,128)(2,1)S(1)}, bf16[592,256]{1,0:T(8,128)(2,1)S(1)}, u32[]{:S(2)}, u32[]{:S(2)}) collective-permute-start(bf16[592,256]{1,0:T(8,128)(2,1)S(1)} %slice_select_fusion.3.refs_4_), channel_id=1, source_target_pairs={{0,8},{8,0},{4,12},{12,4},{1,9},{9,1},{5,13},{13,5},{2,10},{10,2},... | collective-permute-start | bytes 909320 | tf_op jit(solution)/shard_map/ppermute | solution.py:46
  17.4 13.2 %collective-permute-start.2 = (bf16[592,384]{1,0:T(8,128)(2,1)S(1)}, bf16[592,384]{1,0:T(8,128)(2,1)S(1)}, u32[]{:S(2)}, u32[]{:S(2)}) collective-permute-start(bf16[592,384]{1,0:T(8,128)(2,1)S(1)} %slice_select_fusion.1.refs_0_), channel_id=1, source_target_pairs={{0,4},{4,0},{8,12},{12,8},{1,5},{5,1},{9,13},{13,9},{2,6},{6,2},{1... | collective-permute-start | bytes 1363976 | tf_op jit(solution)/shard_map/ppermute | solution.py:47
  23.9 7.9 %collective-permute-start.3 = (bf16[592,384]{1,0:T(8,128)(2,1)S(1)}, bf16[592,384]{1,0:T(8,128)(2,1)S(1)}, u32[]{:S(2)}, u32[]{:S(2)}) collective-permute-start(bf16[592,384]{1,0:T(8,128)(2,1)S(1)} %collective-permute-done.1.refs_1_), channel_id=1, source_target_pairs={{0,4},{4,0},{8,12},{12,8},{1,5},{5,1},{9,13},{13,9},{2,6},{6,2},{1... | collective-permute-start | bytes 1363976 | tf_op jit(solution)/shard_map/ppermute | solution.py:47
  23.9 6.6 %collective-permute-start.6 = (bf16[592,256]{1,0:T(8,128)(2,1)S(1)}, bf16[592,256]{1,0:T(8,128)(2,1)S(1)}, u32[]{:S(2)}, u32[]{:S(2)}) collective-permute-start(bf16[592,256]{1,0:T(8,128)(2,1)S(1)} %slice_select_fusion.3.refs_4_), channel_id=1, source_target_pairs={{0,4},{4,0},{8,12},{12,8},{1,5},{5,1},{9,13},{13,9},{2,6},{6,2},{1... | collective-permute-start | bytes 909320 | tf_op jit(solution)/shard_map/ppermute | solution.py:47
  24.5 6.1 %collective-permute-start.9 = (bf16[592,256]{1,0:T(8,128)(2,1)S(1)}, bf16[592,256]{1,0:T(8,128)(2,1)S(1)}, u32[]{:S(2)}, u32[]{:S(2)}) collective-permute-start(bf16[592,256]{1,0:T(8,128)(2,1)S(1)} %collective-permute-done.4.refs_10_), channel_id=1, source_target_pairs={{0,4},{4,0},{8,12},{12,8},{1,5},{5,1},{9,13},{13,9},{2,6},{6,2},{1... | collective-permute-start | bytes 909320 | tf_op jit(solution)/shard_map/ppermute | solution.py:50
  30.2 1.6 %collective-permute-start.7 = (bf16[592,256]{1,0:T(8,128)(2,1)S(1)}, bf16[592,256]{1,0:T(8,128)(2,1)S(1)}, u32[]{:S(2)}, u32[]{:S(2)}) collective-permute-start(bf16[592,256]{1,0:T(8,128)(2,1)S(1)} %collective-permute-done.5.refs_5_), channel_id=1, source_target_pairs={{0,4},{4,0},{8,12},{12,8},{1,5},{5,1},{9,13},{13,9},{2,6},{6,2},{1... | collective-permute-start | bytes 909320 | tf_op jit(solution)/shard_map/ppermute | solution.py:47
  40.0 12.6 %collective-permute-start.10 = (f16[440,512]{1,0:T(8,128)(2,1)S(1)}, f16[440,512]{1,0:T(8,128)(2,1)S(1)}, u32[]{:S(2)}, u32[]{:S(2)}) collective-permute-start(f16[440,512]{1,0:T(8,128)(2,1)S(1)} %convert_element_type.35), channel_id=1, source_target_pairs={{0,1},{1,0},{2,3},{3,2},{4,5},{5,4},{6,7},{7,6},{8,9},{9,8},{10,11... | collective-permute-start | bytes 1351688 | tf_op jit(solution)/shard_map/ppermute | solution.py:375
  42.0 16.4 %collective-permute-start.11 = (f16[440,512]{1,0:T(8,128)(2,1)S(1)}, f16[440,512]{1,0:T(8,128)(2,1)S(1)}, u32[]{:S(2)}, u32[]{:S(2)}) collective-permute-start(f16[440,512]{1,0:T(8,128)(2,1)S(1)} %convert_element_type.36), channel_id=1, source_target_pairs={{1,2},{2,1},{5,6},{6,5},{9,10},{10,9},{13,14},{14,13},{17,18},{18,... | collective-permute-start | bytes 1351688 | tf_op jit(solution)/shard_map/ppermute | solution.py:375
  53.4 20.8 %collective-permute-start.13 = (f16[440,512]{1,0:T(8,128)(2,1)S(1)}, f16[440,512]{1,0:T(8,128)(2,1)S(1)}, u32[]{:S(2)}, u32[]{:S(2)}) collective-permute-start(f16[440,512]{1,0:T(8,128)(2,1)S(1)} %convert_element_type.38), channel_id=1, source_target_pairs={{0,1},{3,2},{1,3},{2,0},{4,5},{7,6},{5,7},{6,4},{8,9},{11,10},{9,1... | collective-permute-start | bytes 1351688 | tf_op jit(solution)/shard_map/ppermute | solution.py:375
  55.3 18.8 %collective-permute-start.12 = (f16[440,512]{1,0:T(8,128)(2,1)S(1)}, f16[440,512]{1,0:T(8,128)(2,1)S(1)}, u32[]{:S(2)}, u32[]{:S(2)}) collective-permute-start(f16[440,512]{1,0:T(8,128)(2,1)S(1)} %convert_element_type.36), channel_id=1, source_target_pairs={{0,2},{3,1},{4,6},{7,5},{8,10},{11,9},{12,14},{15,13},{16,18},{19,... | collective-permute-start | bytes 1351688 | tf_op jit(solution)/shard_map/ppermute | solution.py:375
  74.9 5.2 %collective-permute-start.14 = (f32[32,128]{1,0:T(8,128)S(1)}, f32[32,128]{1,0:T(8,128)S(1)}, u32[]{:S(2)}, u32[]{:S(2)}) collective-permute-start(f32[32,128]{1,0:T(8,128)S(1)} %line.1), channel_id=1, source_target_pairs={{0,1},{1,0},{2,3},{3,2},{4,5},{5,4},{6,7},{7,6},{8,9},{9,8},{10,11... | collective-permute-start | bytes 49160 | tf_op jit(solution)/shard_map/ppermute | solution.py:375
  80.1 4.6 %collective-permute-start.15 = (f32[32,128]{1,0:T(8,128)S(1)}, f32[32,128]{1,0:T(8,128)S(1)}, u32[]{:S(2)}, u32[]{:S(2)}) collective-permute-start(f32[32,128]{1,0:T(8,128)S(1)} %add.54), channel_id=1, source_target_pairs={{0,2},{1,3},{2,0},{3,1},{4,6},{5,7},{6,4},{7,5},{8,10},{9,11},{10,... | collective-permute-start | bytes 49160 | tf_op jit(solution)/shard_map/ppermute | solution.py:375
